TPU v7x, 32 devices: a whole 2x2x4 slice. The times are simulated.
32 devices in a mesh: fsdp: 4 (over z), ctx: 4 (over x, core), tensor: 2 (over y).
Axes of the slice: x: 2, y: 2, z: 4, core: 2. Of those that a mesh axis runs over, the one named last changes fastest.
Arguments:
- tokens_in: bfloat16 [16384, 2048], P(('fsdp', 'ctx', 'tensor')), may hold values from -6 to 6
- attn_gain: float32 [2048], replicated, may hold values from 0.5 to 1.5
- query_weight: bfloat16 [2048, 2048], P('fsdp', 'tensor'), may hold values from -0.1875 to 0.1875
- key_weight: bfloat16 [2048, 2048], P('fsdp', 'tensor'), may hold values from -0.1875 to 0.1875
- value_weight: bfloat16 [2048, 2048], P('fsdp', 'tensor'), may hold values from -0.125 to 0.125
- output_weight: bfloat16 [2048, 2048], P('fsdp', 'tensor'), may hold values from -1 to 1
- mlp_gain: float32 [2048], replicated, may hold values from 0.5 to 1.5
- gate_weight: bfloat16 [2048, 8192], P('fsdp', 'tensor'), may hold values from -0.125 to 0.125
- up_weight: bfloat16 [2048, 8192], P('fsdp', 'tensor'), may hold values from -0.125 to 0.125
- down_weight: bfloat16 [2048, 8192], P('fsdp', 'tensor'), may hold values from -0.0625 to 0.0625
- seg_lengths: int32 [4, 20], P('fsdp'), may hold values from 1 to 128, 1920 in all within a row
- leaf_parent: int32 [4, 16], P('fsdp'), may hold values from 1 to 4
- cotangent: bfloat16 [16384, 2048], P(('fsdp', 'ctx', 'tensor')), may hold values from -6 to 6
Outputs:
- block_out: bfloat16 [16384, 2048], P(('fsdp', 'ctx', 'tensor'))
- input_grad: bfloat16 [16384, 2048], P(('fsdp', 'ctx', 'tensor'))
- attn_gain_grad: float32 [2048], P(('fsdp', 'ctx', 'tensor'))
- query_grad: float32 [2048, 2048], P(('fsdp', 'ctx'), 'tensor')
- key_grad: float32 [2048, 2048], P(('fsdp', 'ctx'), 'tensor')
- value_grad: float32 [2048, 2048], P(('fsdp', 'ctx'), 'tensor')
- output_grad: float32 [2048, 2048], P(('fsdp', 'ctx'), 'tensor')
- mlp_gain_grad: float32 [2048], P(('fsdp', 'ctx', 'tensor'))
- gate_grad: float32 [2048, 8192], P(('fsdp', 'ctx'), 'tensor')
- up_grad: float32 [2048, 8192], P(('fsdp', 'ctx'), 'tensor')
- down_grad: float32 [2048, 8192], P(('fsdp', 'ctx'), 'tensor')
Inputs may be any that keep to these rules, and one draw needn't show every extreme that they name: `seg_lengths`: row t gives the token counts of tree t's 4 branches and then its 16 leaves, which follow its trunk of 2176 tokens in this order; each row sums to 1920 and its largest entry is 128. `leaf_parent`: the branch, numbered 1 to 4, that each leaf hangs from.
All inputs are finite; a program needn't handle non-finite values.
Results may differ from a plain program's by a relative error of at most 0.02.
Values may be sent and summed in bfloat16 or wider, within the bound.
A program may use at most 448 MiB of HBM per device.

v0:
```python
import jax
import jax.numpy as jnp
from jax import lax
from jax.sharding import PartitionSpec as P

HEAD_DIM = 64
TRUNK = 2176


ROPE_BASE = 130000.0
EPSILON = 1e-05
NEG_LARGE = -1e30


def pick_table(onehot, table):
    return jnp.sum(jnp.where(onehot, table[None, :], 0), axis=1)


def tree_tables(lengths_row, parent_row, tree_len):
    branches = lengths_row.shape[0] - parent_row.shape[0]
    ends = TRUNK + jnp.cumsum(lengths_row)
    starts = ends - lengths_row
    matches = parent_row[:, None] - 1 == jnp.arange(branches, dtype=jnp.int32)[None, :]
    parent_len = jnp.sum(jnp.where(matches, lengths_row[None, :branches], 0), axis=1)
    zero_one = jnp.zeros((1,), jnp.int32)
    seg_start = jnp.concatenate([zero_one, starts])
    seg_base = jnp.concatenate(
        [zero_one, jnp.full((branches,), TRUNK, jnp.int32), TRUNK + parent_len]
    )
    seg_parent = jnp.concatenate([zero_one, jnp.zeros((branches,), jnp.int32), parent_row])
    positions = jnp.arange(tree_len, dtype=jnp.int32)
    above = jnp.sum((ends[None, :] <= positions[:, None]).astype(jnp.int32), axis=1)
    segment = (positions >= TRUNK).astype(jnp.int32) + above
    onehot = segment[:, None] == jnp.arange(seg_start.shape[0], dtype=jnp.int32)[None, :]
    depth = positions - pick_table(onehot, seg_start) + pick_table(onehot, seg_base)
    parent = pick_table(onehot, seg_parent)
    return (segment, parent, depth)


def rotate(values, depth, sign):
    count = values.shape[0]
    width = values.shape[1]
    heads = width // HEAD_DIM
    half = HEAD_DIM // 2
    freqs = jnp.power(ROPE_BASE, -(2.0 * jnp.arange(half, dtype=jnp.float32)) / HEAD_DIM)
    angles = depth.astype(jnp.float32)[:, None] * freqs[None, :]
    cosine = jnp.cos(angles)[:, None, :]
    sine = sign * jnp.sin(angles)[:, None, :]
    shaped = values.reshape(count, heads, HEAD_DIM)
    first = shaped[..., :half]
    second = shaped[..., half:]
    turned = jnp.concatenate(
        [first * cosine - second * sine, second * cosine + first * sine], axis=-1
    )
    return turned.reshape(count, width)


def normalize(rows):
    norm_inv = lax.rsqrt(jnp.mean(rows * rows, axis=1, keepdims=True) + EPSILON)
    return (rows * norm_inv, norm_inv)


def norm_backward(grad_rows, scaled, norm_inv, gain):
    weighted = grad_rows * gain[None, :]
    inner = jnp.mean(weighted * scaled, axis=1, keepdims=True)
    return (norm_inv * (weighted - scaled * inner), jnp.sum(grad_rows * scaled, axis=0))


def spread_rows(rows):
    return lax.all_gather(rows, "tensor", axis=0, tiled=True)


def reduce_rows(rows):
    return lax.psum_scatter(rows, "tensor", scatter_dimension=0, tiled=True)


def contract_first(left, right):
    return lax.dot_general(
        left, right, (((0,), (0,)), ((), ())), preferred_element_type=jnp.float32
    )


def contract_last(left, right):
    return lax.dot_general(
        left, right, (((1,), (1,)), ((), ())), preferred_element_type=jnp.float32
    )


def body(
    tokens_in,
    attn_gain,
    query_weight,
    key_weight,
    value_weight,
    output_weight,
    mlp_gain,
    gate_weight,
    up_weight,
    down_weight,
    seg_lengths,
    leaf_parent,
    cotangent,
):
    local_rows = tokens_in.shape[0]
    piece = local_rows * lax.axis_size("tensor")
    blocks = lax.axis_size("ctx")
    tree_len = piece * blocks
    score_scale = HEAD_DIM ** (-0.5)
    segment, parent, depth = tree_tables(seg_lengths[0], leaf_parent[0], tree_len)
    first_row = lax.axis_index("ctx") * piece
    query_seg = lax.dynamic_slice_in_dim(segment, first_row, piece)
    query_par = lax.dynamic_slice_in_dim(parent, first_row, piece)
    query_depth = lax.dynamic_slice_in_dim(depth, first_row, piece)
    query_index = first_row + jnp.arange(piece, dtype=jnp.int32)
    key_seg = segment.reshape(blocks, piece)
    key_index = jnp.arange(tree_len, dtype=jnp.int32).reshape(blocks, piece)
    wq_full, wk_full, wv_full, wo_full = (
        lax.all_gather(query_weight, "fsdp", axis=0, tiled=True),
        lax.all_gather(key_weight, "fsdp", axis=0, tiled=True),
        lax.all_gather(value_weight, "fsdp", axis=0, tiled=True),
        lax.all_gather(output_weight, "fsdp", axis=0, tiled=True),
    )
    wg_full, wu_full, wd_full = (
        lax.all_gather(gate_weight, "fsdp", axis=0, tiled=True),
        lax.all_gather(up_weight, "fsdp", axis=0, tiled=True),
        lax.all_gather(down_weight, "fsdp", axis=0, tiled=True),
    )
    x_rows = tokens_in.astype(jnp.float32)
    attn_scaled, attn_inv = normalize(x_rows)
    attn_in = spread_rows((attn_scaled * attn_gain[None, :]).astype(jnp.bfloat16))
    query_pre = jnp.dot(attn_in, wq_full, preferred_element_type=jnp.float32)
    key_pre = jnp.dot(attn_in, wk_full, preferred_element_type=jnp.float32)
    value_pre = jnp.dot(attn_in, wv_full, preferred_element_type=jnp.float32)
    query_rows = rotate(query_pre, query_depth, 1.0).astype(jnp.bfloat16)
    key_rows = rotate(key_pre, query_depth, 1.0).astype(jnp.bfloat16)
    value_rows = value_pre.astype(jnp.bfloat16)
    key_all, value_all = (
        lax.all_gather(key_rows, "ctx", axis=0, tiled=True),
        lax.all_gather(value_rows, "ctx", axis=0, tiled=True),
    )
    width = query_rows.shape[1]
    heads = width // HEAD_DIM
    query_heads = query_rows.reshape(piece, heads, HEAD_DIM)
    key_blocks = key_all.reshape(blocks, piece, heads, HEAD_DIM)
    value_blocks = value_all.reshape(blocks, piece, heads, HEAD_DIM)

    def block_scores(key_block, seg_block, index_block):
        raw = (
            jnp.einsum("qhd,khd->hqk", query_heads, key_block, preferred_element_type=jnp.float32)
            * score_scale
        )
        seen = (
            (seg_block[None, :] == query_seg[:, None])
            | (seg_block[None, :] == 0)
            | (seg_block[None, :] == query_par[:, None])
        ) & (index_block[None, :] <= query_index[:, None])
        return jnp.where(seen[None], raw, NEG_LARGE)

    def total_step(running, inputs):
        largest, total = running
        key_block, seg_block, index_block = inputs
        scores = block_scores(key_block, seg_block, index_block)
        newest = jnp.maximum(largest, jnp.max(scores, axis=2, keepdims=True))
        total = total * jnp.exp(largest - newest) + jnp.sum(
            jnp.exp(scores - newest), axis=2, keepdims=True
        )
        return ((newest, total), None)

    start_max = jnp.full((heads, piece, 1), NEG_LARGE, jnp.float32)
    start_total = jnp.zeros((heads, piece, 1), jnp.float32)
    (largest, total), unused = lax.scan(
        total_step, (start_max, start_total), (key_blocks, key_seg, key_index)
    )
    log_total = largest + jnp.log(total)

    def output_step(weighted, inputs):
        key_block, value_block, seg_block, index_block = inputs
        probs = jnp.exp(block_scores(key_block, seg_block, index_block) - log_total).astype(
            jnp.bfloat16
        )
        return (
            weighted
            + jnp.einsum("hqk,khd->qhd", probs, value_block, preferred_element_type=jnp.float32),
            None,
        )

    key_inputs = (key_blocks, value_blocks, key_seg, key_index)
    weighted, unused = lax.scan(
        output_step, jnp.zeros((piece, heads, HEAD_DIM), jnp.float32), key_inputs
    )
    attn_out = weighted.reshape(piece, width).astype(jnp.bfloat16)
    mid_rows = x_rows + reduce_rows(contract_last(attn_out, wo_full))
    mlp_scaled, mlp_inv = normalize(mid_rows)
    mlp_in = spread_rows((mlp_scaled * mlp_gain[None, :]).astype(jnp.bfloat16))
    gate = jnp.dot(mlp_in, wg_full, preferred_element_type=jnp.float32)
    up_proj = jnp.dot(mlp_in, wu_full, preferred_element_type=jnp.float32)
    hidden = (jax.nn.silu(gate) * up_proj).astype(jnp.bfloat16)
    final_rows = mid_rows + reduce_rows(contract_last(hidden, wd_full))
    block_out = final_rows.astype(jnp.bfloat16)
    out_grad_all = spread_rows(cotangent)
    down_grad = contract_first(out_grad_all, hidden)
    hidden_grad = jnp.dot(out_grad_all, wd_full, preferred_element_type=jnp.float32)
    sigmoid_gate = jax.nn.sigmoid(gate)
    gate_rows_grad = (
        hidden_grad * up_proj * sigmoid_gate * (1.0 + gate * (1.0 - sigmoid_gate))
    ).astype(jnp.bfloat16)
    up_rows_grad = (hidden_grad * gate * sigmoid_gate).astype(jnp.bfloat16)
    gate_grad = contract_first(mlp_in, gate_rows_grad)
    up_grad = contract_first(mlp_in, up_rows_grad)
    mlp_in_grad = reduce_rows(
        contract_last(gate_rows_grad, wg_full) + contract_last(up_rows_grad, wu_full)
    )
    mlp_back, mlp_gain_part = norm_backward(mlp_in_grad, mlp_scaled, mlp_inv, mlp_gain)
    mid_grad = cotangent.astype(jnp.float32) + mlp_back
    mid_all = spread_rows(mid_grad.astype(jnp.bfloat16))
    output_grad = contract_first(mid_all, attn_out)
    out_heads_grad = (
        jnp.dot(mid_all, wo_full, preferred_element_type=jnp.float32)
        .astype(jnp.bfloat16)
        .reshape(piece, heads, HEAD_DIM)
    )

    def delta_step(delta, inputs):
        key_block, value_block, seg_block, index_block = inputs
        attn_prob = jnp.exp(block_scores(key_block, seg_block, index_block) - log_total)
        prob_grad = jnp.einsum(
            "qhd,khd->hqk", out_heads_grad, value_block, preferred_element_type=jnp.float32
        )
        return (delta + jnp.sum(attn_prob * prob_grad, axis=2, keepdims=True), None)

    delta, unused = lax.scan(delta_step, jnp.zeros((heads, piece, 1), jnp.float32), key_inputs)

    def grad_step(query_total, inputs):
        key_block, value_block, seg_block, index_block = inputs
        attn_prob = jnp.exp(block_scores(key_block, seg_block, index_block) - log_total)
        prob_grad = jnp.einsum(
            "qhd,khd->hqk", out_heads_grad, value_block, preferred_element_type=jnp.float32
        )
        score_grad = (attn_prob * (prob_grad - delta)).astype(jnp.bfloat16)
        query_total = (
            query_total
            + jnp.einsum("hqk,khd->qhd", score_grad, key_block, preferred_element_type=jnp.float32)
            * score_scale
        )
        key_part = (
            jnp.einsum("hqk,qhd->khd", score_grad, query_heads, preferred_element_type=jnp.float32)
            * score_scale
        )
        value_part = jnp.einsum(
            "hqk,qhd->khd",
            attn_prob.astype(jnp.bfloat16),
            out_heads_grad,
            preferred_element_type=jnp.float32,
        )
        return (query_total, (key_part, value_part))

    query_sum, (key_parts, value_parts) = lax.scan(
        grad_step, jnp.zeros((piece, heads, HEAD_DIM), jnp.float32), key_inputs
    )
    key_sum, value_sum = (
        lax.psum_scatter(
            key_parts.reshape(tree_len, width).astype(jnp.bfloat16),
            "ctx",
            scatter_dimension=0,
            tiled=True,
        ).astype(jnp.float32),
        lax.psum_scatter(
            value_parts.reshape(tree_len, width).astype(jnp.bfloat16),
            "ctx",
            scatter_dimension=0,
            tiled=True,
        ).astype(jnp.float32),
    )
    query_pre_grad = rotate(query_sum.reshape(piece, width), query_depth, -1.0).astype(jnp.bfloat16)
    key_pre_grad = rotate(key_sum, query_depth, -1.0).astype(jnp.bfloat16)
    value_pre_grad = value_sum.astype(jnp.bfloat16)
    query_grad = contract_first(attn_in, query_pre_grad)
    key_grad = contract_first(attn_in, key_pre_grad)
    value_grad = contract_first(attn_in, value_pre_grad)
    attn_in_grad = reduce_rows(
        contract_last(query_pre_grad, wq_full)
        + contract_last(key_pre_grad, wk_full)
        + contract_last(value_pre_grad, wv_full)
    )
    attn_back, attn_gain_part = norm_backward(attn_in_grad, attn_scaled, attn_inv, attn_gain)
    input_grad = (mid_grad + attn_back).astype(jnp.bfloat16)
    attn_gain_grad, mlp_gain_grad = (
        lax.psum_scatter(
            attn_gain_part, ("fsdp", "ctx", "tensor"), scatter_dimension=0, tiled=True
        ),
        lax.psum_scatter(mlp_gain_part, ("fsdp", "ctx", "tensor"), scatter_dimension=0, tiled=True),
    )
    query_out, key_out, value_out, output_out, gate_out, up_out, down_out = (
        lax.psum_scatter(
            query_grad.astype(jnp.bfloat16), ("fsdp", "ctx"), scatter_dimension=0, tiled=True
        ).astype(jnp.float32),
        lax.psum_scatter(
            key_grad.astype(jnp.bfloat16), ("fsdp", "ctx"), scatter_dimension=0, tiled=True
        ).astype(jnp.float32),
        lax.psum_scatter(
            value_grad.astype(jnp.bfloat16), ("fsdp", "ctx"), scatter_dimension=0, tiled=True
        ).astype(jnp.float32),
        lax.psum_scatter(
            output_grad.astype(jnp.bfloat16), ("fsdp", "ctx"), scatter_dimension=0, tiled=True
        ).astype(jnp.float32),
        lax.psum_scatter(
            gate_grad.astype(jnp.bfloat16), ("fsdp", "ctx"), scatter_dimension=0, tiled=True
        ).astype(jnp.float32),
        lax.psum_scatter(
            up_grad.astype(jnp.bfloat16), ("fsdp", "ctx"), scatter_dimension=0, tiled=True
        ).astype(jnp.float32),
        lax.psum_scatter(
            down_grad.astype(jnp.bfloat16), ("fsdp", "ctx"), scatter_dimension=0, tiled=True
        ).astype(jnp.float32),
    )
    return (
        block_out,
        input_grad,
        attn_gain_grad,
        query_out,
        key_out,
        value_out,
        output_out,
        mlp_gain_grad,
        gate_out,
        up_out,
        down_out,
    )


def solution(mesh):
    in_specs = (
        P(("fsdp", "ctx", "tensor"), None),
        P(),
        P("fsdp", "tensor"),
        P("fsdp", "tensor"),
        P("fsdp", "tensor"),
        P("fsdp", "tensor"),
        P(),
        P("fsdp", "tensor"),
        P("fsdp", "tensor"),
        P("fsdp", "tensor"),
        P("fsdp", None),
        P("fsdp", None),
        P(("fsdp", "ctx", "tensor"), None),
    )
    out_specs = (
        P(("fsdp", "ctx", "tensor"), None),
        P(("fsdp", "ctx", "tensor"), None),
        P(("fsdp", "ctx", "tensor")),
        P(("fsdp", "ctx"), "tensor"),
        P(("fsdp", "ctx"), "tensor"),
        P(("fsdp", "ctx"), "tensor"),
        P(("fsdp", "ctx"), "tensor"),
        P(("fsdp", "ctx", "tensor")),
        P(("fsdp", "ctx"), "tensor"),
        P(("fsdp", "ctx"), "tensor"),
        P(("fsdp", "ctx"), "tensor"),
    )
    return jax.shard_map(body, mesh=mesh, in_specs=in_specs, out_specs=out_specs, check_vma=False)
```

profile of v0, /device:TPU:0, one launch (start us, length us, event | category | flops | bytes accessed | tf_op | source)
XLA Modules:
  0.0 4075.0 jit_solution(14927405452069166986)
XLA Ops:
  17.7 55.3 %all-gather.14.cloned.1.call-done = bf16[1024,2048]{1,0:T(8,128)(2,1)} async-done(((bf16[512,2048]{1,0:T(8,128)(2,1)}), bf16[1024,2048]{1,0:T(8,128)(2,1)}) %all-gather.14.cloned.1.call-update) | async-done | bytes 4194320 | tf_op jit(solution)/shard_map/all_gather | solution.py:70
  73.0 82.4 %all-gather.24.cloned.1.call-done = bf16[2048,1024]{1,0:T(8,128)(2,1)} async-done(((bf16[512,1024]{1,0:T(8,128)(2,1)}), bf16[2048,1024]{1,0:T(8,128)(2,1)}) %all-gather.24.cloned.1.call-update) | async-done | bytes 4194320 | tf_op jit(solution)/shard_map/all_gather | solution.py:118
  165.4 70.9 %all-gather.20.cloned.1.call-done = bf16[2048,1024]{1,0:T(8,128)(2,1)} async-done(((bf16[512,1024]{1,0:T(8,128)(2,1)}), bf16[2048,1024]{1,0:T(8,128)(2,1)}) %all-gather.20.cloned.1.call-update) | async-done | bytes 4194320 | tf_op jit(solution)/shard_map/all_gather | solution.py:119
  248.3 68.8 %all-gather.16.cloned.1.call-done = bf16[2048,1024]{1,0:T(8,128)(2,1)} async-done(((bf16[512,1024]{1,0:T(8,128)(2,1)}), bf16[2048,1024]{1,0:T(8,128)(2,1)}) %all-gather.16.cloned.1.call-update) | async-done | bytes 4194320 | tf_op jit(solution)/shard_map/all_gather | solution.py:120
  328.8 47.1 %all-gather.22.cloned.1.call-done = bf16[4096,1024]{0,1:T(8,128)(2,1)} async-done(((bf16[1024,1024]{0,1:T(8,128)(2,1)}), bf16[4096,1024]{0,1:T(8,128)(2,1)}) %all-gather.22.cloned.1.call-update) | async-done | bytes 8388624 | tf_op jit(solution)/shard_map/all_gather | solution.py:138
  400.2 197.2 %while.50 = (s32[]{:T(128)}, f32[16,1024,1]{1,0,2:T(8,128)S(1)}, f32[16,1024,1]{1,0,2:T(8,128)S(1)}, s32[4,1024]{1,0:T(4,128)S(1)}, s32[1024]{0:T(1024)S(1)}, /*...) while((s32[]{:T(128)}, f32[16,1024,1]{1,0,2:T(8,128)S(1)}, ...), condition=%wide.region_10.11_spmd.clone, body=%wide.region_7.10_spmd.clone.sunk | while | flops 2271299584 | bytes 142452880 | solution.py:171
  637.9 109.1 %while.51 = (s32[]{:T(128)}, f32[1024,16,64]{0,2,1:T(8,128)}, bf16[4,1024,16,64]{1,3,2,0:T(8,128)(2,1)}, s32[4,1024]{1,0:T(4,128)S(1)}, s32[1024]{0:T(1024)S(1)}...) while((s32[]{:T(128)}, f32[1024,16,64]{0,2,1:T(8,128)}, ...), condition=%wide.region_12.13_spmd.clone, body=%wide.region_11.12_spmd.clone.sunk | while | flops 4370466816 | bytes 16887448 | solution.py:188
  763.2 98.6 %reduce-scatter.16.cloned.1.call-done = f32[512,2048]{1,0:T(8,128)} async-done(((f32[1024,2048]{1,0:T(8,128)}), f32[512,2048]{1,0:T(8,128)}) %reduce-scatter.16.cloned.1.call-update) | async-done | bytes 4194320 | tf_op jit(solution)/shard_map/reduce_scatter | solution.py:74
  870.4 279.8 %all-gather.32.cloned.1.call-done = bf16[2048,4096]{1,0:T(8,128)(2,1)} async-done(((bf16[512,4096]{1,0:T(8,128)(2,1)}), bf16[2048,4096]{1,0:T(8,128)(2,1)}) %all-gather.32.cloned.1.call-update) | async-done | bytes 16777232 | tf_op jit(solution)/shard_map/all_gather | solution.py:125
  1150.2 57.0 %all-gather.28.cloned.1.call-done = bf16[1024,2048]{1,0:T(8,128)(2,1)} async-done(((bf16[512,2048]{1,0:T(8,128)(2,1)}), bf16[1024,2048]{1,0:T(8,128)(2,1)}) %all-gather.28.cloned.1.call-update) | async-done | bytes 4194320 | tf_op jit(solution)/shard_map/all_gather | solution.py:70
  1230.6 265.0 %all-gather.30.cloned.1.call-done = bf16[2048,4096]{1,0:T(8,128)(2,1)} async-done(((bf16[512,4096]{1,0:T(8,128)(2,1)}), bf16[2048,4096]{1,0:T(8,128)(2,1)}) %all-gather.30.cloned.1.call-update) | async-done | bytes 16777232 | tf_op jit(solution)/shard_map/all_gather | solution.py:124
  1519.1 33.0 all-gather.36.cloned.1.call-done
  1552.1 288.5 %all-gather.34.cloned.1.call-done = bf16[2048,4096]{1,0:T(8,128)(2,1)} async-done(((bf16[512,4096]{1,0:T(8,128)(2,1)}), bf16[2048,4096]{1,0:T(8,128)(2,1)}) %all-gather.34.cloned.1.call-update) | async-done | bytes 16777232 | tf_op jit(solution)/shard_map/all_gather | solution.py:126
  1840.6 34.7 multiply_convert_fusion
  1919.1 97.5 %reduce-scatter.20.cloned.1.call-done = f32[512,2048]{1,0:T(8,128)} async-done(((f32[1024,2048]{1,0:T(8,128)}), f32[512,2048]{1,0:T(8,128)}) %reduce-scatter.20.cloned.1.call-update) | async-done | bytes 4194320 | tf_op jit(solution)/shard_map/reduce_scatter | solution.py:74
  2025.7 56.3 %all-gather.38.cloned.1.call-done = bf16[1024,2048]{1,0:T(8,128)(2,1)} async-done(((bf16[512,2048]{1,0:T(8,128)(2,1)}), bf16[1024,2048]{1,0:T(8,128)(2,1)}) %all-gather.38.cloned.1.call-update) | async-done | bytes 4194320 | tf_op jit(solution)/shard_map/all_gather | solution.py:70
  2091.4 223.1 %while.52 = (s32[]{:T(128)}, f32[16,1024,1]{1,2,0:T(1,128)S(1)}, s32[4,1024]{1,0:T(4,128)S(1)}, s32[1024]{0:T(1024)S(1)}, s32[1024]{0:T(1024)S(1)}, /*index=5*/s...) while((s32[]{:T(128)}, f32[16,1024,1]{1,2,0:T(1,128)S(1)}, ...), condition=%wide.region_20.21_spmd.clone, body=%wide.region_18.20_spmd.clone.sunk | while | flops 4385163264 | bytes 145074336 | solution.py:231
  2314.5 522.7 %while.53 = (s32[]{:T(128)}, f32[1024,16,64]{0,2,1:T(8,128)}, bf16[4,1024,16,64]{1,3,2,0:T(8,128)(2,1)}, bf16[4,1024,16,64]{1,3,2,0:T(8,128)(2,1)}, bf16[4,1024,...) while((s32[]{:T(128)}, f32[1024,16,64]{0,2,1:T(8,128)}, ...), condition=%wide.region_22.23_spmd.clone, body=%wide.region_21.22_spmd.clone.sunk | while | flops 10915678208 | bytes 336832672 | solution.py:257
  2367.5 41.2 %fusion.197 = bf16[16,1024,1024]{1,2,0:T(8,128)(2,1)} fusion(f32[16,1024,1024]{2,1,0:T(8,128)} %fusion.196, f32[16,1024]{1,0:T(8,128)S(1)} %bitcast.308, f32[16,1024]{1,0:T(8,128)S(1)} %bitcast.307, pred[1024,1024]{0,1:T(8,128)(4,1)S(1)} %compare_and_fusion.11, bf16[1024,16,64]{0,2,1:T(8,128)(2,1)} %get-tuple-element.1279, ...), kind=kOutput, calls=%fused_computation.59.clone.2 | convolution fusion | flops 2248146944 | bytes 106037248 | tf_op jit(solution)/shard_map/while/body/eval_jaxpr/qhd,khd->hqk/dot_general | solution.py:236
  2497.1 41.2 %fusion.197 = bf16[16,1024,1024]{1,2,0:T(8,128)(2,1)} fusion(f32[16,1024,1024]{2,1,0:T(8,128)} %fusion.196, f32[16,1024]{1,0:T(8,128)S(1)} %bitcast.308, f32[16,1024]{1,0:T(8,128)S(1)} %bitcast.307, pred[1024,1024]{0,1:T(8,128)(4,1)S(1)} %compare_and_fusion.11, bf16[1024,16,64]{0,2,1:T(8,128)(2,1)} %get-tuple-element.1279, ...), kind=kOutput, calls=%fused_computation.59.clone.2 | convolution fusion | flops 2248146944 | bytes 106037248 | tf_op jit(solution)/shard_map/while/body/eval_jaxpr/qhd,khd->hqk/dot_general | solution.py:236
  2628.0 41.2 %fusion.197 = bf16[16,1024,1024]{1,2,0:T(8,128)(2,1)} fusion(f32[16,1024,1024]{2,1,0:T(8,128)} %fusion.196, f32[16,1024]{1,0:T(8,128)S(1)} %bitcast.308, f32[16,1024]{1,0:T(8,128)S(1)} %bitcast.307, pred[1024,1024]{0,1:T(8,128)(4,1)S(1)} %compare_and_fusion.11, bf16[1024,16,64]{0,2,1:T(8,128)(2,1)} %get-tuple-element.1279, ...), kind=kOutput, calls=%fused_computation.59.clone.2 | convolution fusion | flops 2248146944 | bytes 106037248 | tf_op jit(solution)/shard_map/while/body/eval_jaxpr/qhd,khd->hqk/dot_general | solution.py:236
  2758.8 41.2 %fusion.197 = bf16[16,1024,1024]{1,2,0:T(8,128)(2,1)} fusion(f32[16,1024,1024]{2,1,0:T(8,128)} %fusion.196, f32[16,1024]{1,0:T(8,128)S(1)} %bitcast.308, f32[16,1024]{1,0:T(8,128)S(1)} %bitcast.307, pred[1024,1024]{0,1:T(8,128)(4,1)S(1)} %compare_and_fusion.11, bf16[1024,16,64]{0,2,1:T(8,128)(2,1)} %get-tuple-element.1279, ...), kind=kOutput, calls=%fused_computation.59.clone.2 | convolution fusion | flops 2248146944 | bytes 106037248 | tf_op jit(solution)/shard_map/while/body/eval_jaxpr/qhd,khd->hqk/dot_general | solution.py:236
  3084.9 104.4 %reduce-scatter.40.cloned.1.call-done = bf16[128,4096]{1,0:T(8,128)(2,1)} async-done(((bf16[2048,4096]{1,0:T(8,128)(2,1)}), bf16[128,4096]{1,0:T(8,128)(2,1)}) %reduce-scatter.40.cloned.1.call-update) | async-done | bytes 1048592
  3192.5 178.4 %reduce-scatter.38.cloned.1.call-done = bf16[128,4096]{1,0:T(8,128)(2,1)} async-done(((bf16[2048,4096]{1,0:T(8,128)(2,1)}), bf16[128,4096]{1,0:T(8,128)(2,1)}) %reduce-scatter.38.cloned.1.call-update) | async-done | bytes 1048592 | tf_op jit(solution)/shard_map/reduce_scatter | solution.py:309
  3373.7 178.8 %reduce-scatter.36.cloned.1.call-done = bf16[128,4096]{1,0:T(8,128)(2,1)} async-done(((bf16[2048,4096]{1,0:T(8,128)(2,1)}), bf16[128,4096]{1,0:T(8,128)(2,1)}) %reduce-scatter.36.cloned.1.call-update) | async-done | bytes 1048592 | tf_op jit(solution)/shard_map/reduce_scatter | solution.py:306
  3555.2 72.5 %reduce-scatter.34.cloned.1.call-done = bf16[128,1024]{1,0:T(8,128)(2,1)} async-done(((bf16[2048,1024]{1,0:T(8,128)(2,1)}), bf16[128,1024]{1,0:T(8,128)(2,1)}) %reduce-scatter.34.cloned.1.call-update) | async-done | bytes 262160 | tf_op jit(solution)/shard_map/reduce_scatter | solution.py:303
  3629.5 74.1 %reduce-scatter.32.cloned.1.call-done = bf16[128,1024]{1,0:T(8,128)(2,1)} async-done(((bf16[2048,1024]{1,0:T(8,128)(2,1)}), bf16[128,1024]{1,0:T(8,128)(2,1)}) %reduce-scatter.32.cloned.1.call-update) | async-done | bytes 262160 | tf_op jit(solution)/shard_map/reduce_scatter | solution.py:300
  3705.4 73.8 %reduce-scatter.28.cloned.1.call-done = bf16[128,1024]{1,0:T(8,128)(2,1)} async-done(((bf16[2048,1024]{1,0:T(8,128)(2,1)}), bf16[128,1024]{1,0:T(8,128)(2,1)}) %reduce-scatter.28.cloned.1.call-update) | async-done | bytes 262160 | tf_op jit(solution)/shard_map/reduce_scatter | solution.py:294
  3780.9 73.8 %reduce-scatter.30.cloned.1.call-done = bf16[128,1024]{1,0:T(8,128)(2,1)} async-done(((bf16[2048,1024]{1,0:T(8,128)(2,1)}), bf16[128,1024]{1,0:T(8,128)(2,1)}) %reduce-scatter.30.cloned.1.call-update) | async-done | bytes 262160 | tf_op jit(solution)/shard_map/reduce_scatter | solution.py:297
  3856.6 98.9 %reduce-scatter.26.cloned.1.call-done = f32[512,2048]{1,0:T(8,128)} async-done(((f32[1024,2048]{1,0:T(8,128)}), f32[512,2048]{1,0:T(8,128)}) %reduce-scatter.26.cloned.1.call-update) | async-done | bytes 4194320 | tf_op jit(solution)/shard_map/reduce_scatter | solution.py:74
  3958.8 40.0 all-reduce.2
  4000.0 58.3 %reduce-scatter.18.cloned.1.call-done = f32[512,2048]{1,0:T(8,128)} async-done(((f32[1024,2048]{1,0:T(8,128)}), f32[512,2048]{1,0:T(8,128)}) %reduce-scatter.18.cloned.1.call-update) | async-done | bytes 4194320 | tf_op jit(solution)/shard_map/reduce_scatter | solution.py:74
  (359 shorter events, 1405.6 us)
Async XLA Ops:
  7.2 65.8 %all-gather.14.cloned.1.call-start = ((), (), s32[]{:S(2)}) async-start(), calls=%async_computation.13 | async-start | bytes 6291456 | tf_op jit(solution)/shard_map/all_gather | solution.py:70
  13.4 142.0 %all-gather.24.cloned.1.call-start = ((), (), s32[]{:S(2)}) async-start(), calls=%async_computation.18 | async-start | bytes 5242880 | tf_op jit(solution)/shard_map/all_gather | solution.py:118
  14.2 222.1 %all-gather.20.cloned.1.call-start = ((), (), s32[]{:S(2)}) async-start(), calls=%async_computation.16 | async-start | bytes 5242880 | tf_op jit(solution)/shard_map/all_gather | solution.py:119
  14.9 302.1 %all-gather.16.cloned.1.call-start = ((), (), s32[]{:S(2)}) async-start(), calls=%async_computation.14 | async-start | bytes 5242880 | tf_op jit(solution)/shard_map/all_gather | solution.py:120
  15.5 360.4 %all-gather.22.cloned.1.call-start = ((), (), s32[]{:S(2)}) async-start(), calls=%async_computation.17 | async-start | bytes 10485760 | tf_op jit(solution)/shard_map/all_gather | solution.py:138
  248.0 349.4 %all-gather.18.cloned.1.call-start = ((), (), s32[]{:S(2)}) async-start(), calls=%async_computation.15 | async-start | bytes 10485760 | tf_op jit(solution)/shard_map/all_gather | solution.py:139
  326.3 425.3 %all-gather.26.cloned.1.call-start = ((), (), s32[]{:S(2)}) async-start(), calls=%async_computation.19 | async-start | bytes 5242880 | tf_op jit(solution)/shard_map/all_gather | solution.py:121
  327.1 534.6 %reduce-scatter.16.cloned.1.call-start = ((), (), s32[]{:S(2)}) async-start(), calls=%async_computation.20 | async-start | bytes 12582912 | tf_op jit(solution)/shard_map/reduce_scatter | solution.py:74
  762.4 387.8 %all-gather.32.cloned.1.call-start = ((), (), s32[]{:S(2)}) async-start(), calls=%async_computation.23 | async-start | bytes 20971520 | tf_op jit(solution)/shard_map/all_gather | solution.py:125
  763.1 444.1 %all-gather.28.cloned.1.call-start = ((), (), s32[]{:S(2)}) async-start(), calls=%async_computation.21 | async-start | bytes 6291456 | tf_op jit(solution)/shard_map/all_gather | solution.py:70
  868.3 627.4 %all-gather.30.cloned.1.call-start = ((), (), s32[]{:S(2)}) async-start(), calls=%async_computation.22 | async-start | bytes 20971520 | tf_op jit(solution)/shard_map/all_gather | solution.py:124
  869.0 683.1 %all-gather.36.cloned.1.call-start = ((), (), s32[]{:S(2)}) async-start(), calls=%async_computation.26 | async-start | bytes 6291456 | tf_op jit(solution)/shard_map/all_gather | solution.py:70
  869.6 971.0 %all-gather.34.cloned.1.call-start = ((), (), s32[]{:S(2)}) async-start(), calls=%async_computation.24 | async-start | bytes 20971520 | tf_op jit(solution)/shard_map/all_gather | solution.py:126
  870.4 1146.3 %reduce-scatter.20.cloned.1.call-start = ((), (), s32[]{:S(2)}) async-start(), calls=%async_computation.27 | async-start | bytes 12582912 | tf_op jit(solution)/shard_map/reduce_scatter | solution.py:74
  1919.1 162.9 %all-gather.38.cloned.1.call-start = ((), (), s32[]{:S(2)}) async-start(), calls=%async_computation.28 | async-start | bytes 6291456 | tf_op jit(solution)/shard_map/all_gather | solution.py:70
  2025.1 967.3 %reduce-scatter.24.cloned.1.call-start = ((), (), s32[]{:S(2)}) async-start(), calls=%async_computation.30 | async-start | bytes 10485760 | tf_op jit(solution)/shard_map/reduce_scatter | solution.py:267
  2860.4 146.2 %reduce-scatter.22.cloned.1.call-start = ((), (), s32[]{:S(2)}) async-start(), calls=%async_computation.29 | async-start | bytes 10485760 | tf_op jit(solution)/shard_map/reduce_scatter | solution.py:261
  2885.5 303.8 %reduce-scatter.40.cloned.1.call-start = ((), (), s32[]{:S(2)}) async-start(), calls=%async_computation.38 | async-start | bytes 17825792
  2931.0 439.9 %reduce-scatter.38.cloned.1.call-start = ((), (), s32[]{:S(2)}) async-start(), calls=%async_computation.37 | async-start | bytes 17825792 | tf_op jit(solution)/shard_map/reduce_scatter | solution.py:309
  2956.0 596.4 %reduce-scatter.36.cloned.1.call-start = ((), (), s32[]{:S(2)}) async-start(), calls=%async_computation.36 | async-start | bytes 17825792 | tf_op jit(solution)/shard_map/reduce_scatter | solution.py:306
  2981.9 645.8 %reduce-scatter.34.cloned.1.call-start = ((), (), s32[]{:S(2)}) async-start(), calls=%async_computation.35 | async-start | bytes 4456448 | tf_op jit(solution)/shard_map/reduce_scatter | solution.py:303
  2992.1 711.5 %reduce-scatter.32.cloned.1.call-start = ((), (), s32[]{:S(2)}) async-start(), calls=%async_computation.34 | async-start | bytes 4456448 | tf_op jit(solution)/shard_map/reduce_scatter | solution.py:300
  3001.8 777.3 %reduce-scatter.28.cloned.1.call-start = ((), (), s32[]{:S(2)}) async-start(), calls=%async_computation.32 | async-start | bytes 4456448 | tf_op jit(solution)/shard_map/reduce_scatter | solution.py:294
  3020.3 834.4 %reduce-scatter.30.cloned.1.call-start = ((), (), s32[]{:S(2)}) async-start(), calls=%async_computation.33 | async-start | bytes 4456448 | tf_op jit(solution)/shard_map/reduce_scatter | solution.py:297
  3030.6 924.9 %reduce-scatter.26.cloned.1.call-start = ((), (), s32[]{:S(2)}) async-start(), calls=%async_computation.31 | async-start | bytes 12582912 | tf_op jit(solution)/shard_map/reduce_scatter | solution.py:74
  3060.3 998.0 %reduce-scatter.18.cloned.1.call-start = ((), (), s32[]{:S(2)}) async-start(), calls=%async_computation.25 | async-start | bytes 12582912 | tf_op jit(solution)/shard_map/reduce_scatter | solution.py:74
  3192.5 763.0 %copy-start.6 = (bf16[512,2048]{1,0:T(8,128)(2,1)S(1)}, bf16[512,2048]{1,0:T(8,128)(2,1)}, u32[]{:S(2)}) copy-start(bf16[512,2048]{1,0:T(8,128)(2,1)} %param.21) | copy-start | bytes 6291460
  3192.5 763.0 %copy-start.29 = (f32[2048]{0:T(1024)S(1)}, f32[2048]{0:T(1024)}, u32[]{:S(2)}) copy-start(f32[2048]{0:T(1024)} %param.22) | copy-start | bytes 24580
  3192.5 763.0 %copy-start.36 = (f32[512]{0:T(512)S(1)}, f32[512]{0:T(512)}, u32[]{:S(2)}) copy-start(f32[512]{0:T(512)} %copy-done.35) | copy-start | bytes 6148
  3629.5 428.8 %copy-start.28 = (f32[2048]{0:T(1024)S(1)}, f32[2048]{0:T(1024)}, u32[]{:S(2)}) copy-start(f32[2048]{0:T(1024)} %param.27) | copy-start | bytes 24580
  3629.5 428.8 %copy-start.34 = (f32[512]{0:T(512)S(1)}, f32[512]{0:T(512)}, u32[]{:S(2)}) copy-start(f32[512]{0:T(512)} %copy-done.32) | copy-start | bytes 6148
  3629.5 428.8 %copy-start.39 = (f32[512]{0:T(512)S(1)}, f32[512]{0:T(512)}, u32[]{:S(2)}) copy-start(f32[512]{0:T(512)} %copy-done.38) | copy-start | bytes 6148
  (43 other events, 1987.5 us)
Sparse Core Ops, SparseCore 0:
  13.5 59.4 all-gather.13
  74.6 80.7 all-gather.23
  157.0 79.2 all-gather.19
  237.7 79.2 all-gather.15
  319.0 56.8 all-gather.21
  377.9 58.2 all-gather.17
  437.7 80.7 all-gather.25
  762.5 99.2 reduce-scatter.15
  863.4 286.7 all-gather.31
  1152.2 54.9 all-gather.27
  1208.9 286.7 all-gather.29
  1497.1 54.9 all-gather.35
  1553.8 286.7 all-gather.33
  1919.2 97.4 reduce-scatter.19
  2025.2 56.7 all-gather.37
  2860.6 71.7 reduce-scatter.23
  2934.9 71.6 reduce-scatter.21
  3010.6 178.5 reduce-scatter.39
  3193.3 177.5 reduce-scatter.37
  3374.9 177.5 reduce-scatter.35
  3556.3 71.3 reduce-scatter.33
  3632.0 71.5 reduce-scatter.31
  3707.4 71.6 reduce-scatter.27
  3783.3 71.3 reduce-scatter.29
  3857.1 98.3 reduce-scatter.25
  3957.7 100.4 reduce-scatter.17
where the time goes:
time: 4090 us; the launch traced here: 4070 us
  waiting for transfers between devices  2420 us (59%)
  matrix products  1260 us (31%)
  other arithmetic  179 us (4%)
  local copies, waits for them, and re-layouts  150 us (4%)
    reduce_scatter x4, waiting for transfers between devices, reduce_rows(): return lax.psum_scatter(rows, 'tensor', scatter_dimension=0, tiled=True)  353 us
    dot_general x12, matrix products, block_scores(): jnp.einsum('qhd,khd->hqk', query_heads, key_block, preferred_element_type...  300 us
    all_gather x1, waiting for transfers between devices, body(): lax.all_gather(down_weight, 'fsdp', axis=0, tiled=True)  288 us
    all_gather x1, waiting for transfers between devices, body(): lax.all_gather(up_weight, 'fsdp', axis=0, tiled=True)  280 us
    all_gather x1, waiting for transfers between devices, body(): lax.all_gather(gate_weight, 'fsdp', axis=0, tiled=True)  265 us
    all_gather x4, waiting for transfers between devices, spread_rows(): return lax.all_gather(rows, 'tensor', axis=0, tiled=True)  202 us
    reduce_scatter x1, waiting for transfers between devices, body(): lax.psum_scatter(gate_grad.astype(jnp.bfloat16), ('fsdp', 'ctx'), scatter...  179 us
    reduce_scatter x1, waiting for transfers between devices, body(): lax.psum_scatter(up_grad.astype(jnp.bfloat16), ('fsdp', 'ctx'), scatter_d...  178 us
  transfers between devices with their start and end apart: 26, of which 23 were waited for; matrix products, arithmetic and copies ran while one was open for 17% of the time, Pallas kernels for 0%

commit v1 on v0

v1 whole, which is shorter than its diff:
```python
import functools

import jax
import jax.numpy as jnp
from jax import lax
from jax.experimental import pallas as pl
from jax.experimental.pallas import tpu as pltpu
from jax.sharding import PartitionSpec as P

HEAD_DIM = 64
TRUNK = 2176
MOST_SEG = 128
ROPE_BASE = 130000.0
EPSILON = 1e-05
NEG_LARGE = -1e30
SCALE = HEAD_DIM ** (-0.5)

BQ = 256
BK = 512
GROUP = ("ctx", "tensor")

F32 = jnp.float32
BF16 = jnp.bfloat16


def pick_table(onehot, table):
    return jnp.sum(jnp.where(onehot, table[None, :], 0), axis=1)


def tree_tables(lengths_row, parent_row, tree_len):
    branches = lengths_row.shape[0] - parent_row.shape[0]
    ends = TRUNK + jnp.cumsum(lengths_row)
    starts = ends - lengths_row
    matches = parent_row[:, None] - 1 == jnp.arange(branches, dtype=jnp.int32)[None, :]
    parent_len = jnp.sum(jnp.where(matches, lengths_row[None, :branches], 0), axis=1)
    zero_one = jnp.zeros((1,), jnp.int32)
    seg_start = jnp.concatenate([zero_one, starts])
    seg_base = jnp.concatenate(
        [zero_one, jnp.full((branches,), TRUNK, jnp.int32), TRUNK + parent_len]
    )
    seg_parent = jnp.concatenate([zero_one, jnp.zeros((branches,), jnp.int32), parent_row])
    positions = jnp.arange(tree_len, dtype=jnp.int32)
    above = jnp.sum((ends[None, :] <= positions[:, None]).astype(jnp.int32), axis=1)
    segment = (positions >= TRUNK).astype(jnp.int32) + above
    onehot = segment[:, None] == jnp.arange(seg_start.shape[0], dtype=jnp.int32)[None, :]
    depth = positions - pick_table(onehot, seg_start) + pick_table(onehot, seg_base)
    parent = pick_table(onehot, seg_parent)
    return (segment, parent, depth)


def rope_tables(depth, width):
    half = HEAD_DIM // 2
    lane = jnp.arange(width, dtype=jnp.int32)
    freqs = jnp.power(ROPE_BASE, -(2.0 * (lane % half).astype(F32)) / HEAD_DIM)
    angles = depth.astype(F32)[:, None] * freqs[None, :]
    sign = jnp.where(lane % HEAD_DIM < half, -1.0, 1.0)
    return jnp.cos(angles), jnp.sin(angles) * sign[None, :]


def partner(x):
    half = HEAD_DIM // 2
    width = x.shape[1]
    if width == HEAD_DIM:
        return jnp.concatenate([x[:, half:], x[:, :half]], axis=1)
    lane = lax.broadcasted_iota(jnp.int32, x.shape, 1)
    ahead = pltpu.roll(x, width - half, 1)
    behind = pltpu.roll(x, half, 1)
    return jnp.where(lane % HEAD_DIM < half, ahead, behind)


def head_mask(shape, head):
    lane = lax.broadcasted_iota(jnp.int32, shape, 1)
    return lane // HEAD_DIM == head


def dot_t(a, b):
    return lax.dot_general(a, b, (((1,), (1,)), ((), ())), preferred_element_type=F32)


def dot_n(a, b):
    return lax.dot_general(a, b, (((1,), (0,)), ((), ())), preferred_element_type=F32)


def dot_tn(a, b):
    return lax.dot_general(a, b, (((0,), (0,)), ((), ())), preferred_element_type=F32)


def block_plan(i, tile):
    last_trunk = TRUNK // BK * BK // BQ
    branch_end = TRUNK + 4 * MOST_SEG
    mixed_end = -(-(branch_end + MOST_SEG) // BQ)
    base = TRUNK // BK * BK

    @pl.when(i < last_trunk)
    def _():
        count = (i * BQ) // BK

        @pl.loop(0, count)
        def _(j):
            tile(pl.multiple_of(j * BK, BK), BK, 0)

        tile(pl.multiple_of(count * BK, BK), BK, 1)

    @pl.when(i >= last_trunk)
    def _():
        @pl.loop(0, base // BK)
        def _(j):
            tile(pl.multiple_of(j * BK, BK), BK, 0)

    @pl.when((i >= last_trunk) & (i < mixed_end))
    def _():
        tile(base, mixed_end * BQ - base, 2)

    @pl.when(i >= mixed_end)
    def _():
        tile(base, branch_end - base, 3)
        tile(pl.multiple_of(i * BQ - MOST_SEG, MOST_SEG), BQ + MOST_SEG, 4)


def seen_mask(kind, i, start, width, seg_k, par_seg_q):
    shape = (BQ, width)
    seg_q = par_seg_q[:, 0:1]
    par_q = par_seg_q[:, 1:2]
    if kind == 3:
        return (seg_k == 0) | (seg_k == par_q)
    rows = lax.broadcasted_iota(jnp.int32, shape, 0) + i * BQ
    cols = lax.broadcasted_iota(jnp.int32, shape, 1) + start
    causal = cols <= rows
    if kind == 1:
        return causal
    if kind == 4:
        return causal & (seg_k == seg_q)
    return causal & ((seg_k == 0) | (seg_k == seg_q) | (seg_k == par_q))


def fwd_kernel(
    heads, q_ref, k_ref, v_ref, cos_ref, sin_ref, segk_ref, segq_ref,
    o_ref, lse_ref, qr_ref, kr_ref, vr_ref, m_ref, l_ref, acc_ref,
):
    i = pl.program_id(1)

    @pl.when(i == 0)
    def _():
        @pl.loop(0, k_ref.shape[0] // BK)
        def _(j):
            rows = pl.ds(pl.multiple_of(j * BK, BK), BK)
            k = k_ref[rows, :]
            kr_ref[rows, :] = (k * cos_ref[rows, :] + partner(k) * sin_ref[rows, :]).astype(BF16)
            vr_ref[rows, :] = v_ref[rows, :].astype(BF16)

    rows = pl.ds(pl.multiple_of(i * BQ, BQ), BQ)
    q = q_ref[...]
    q = (q * cos_ref[rows, :] + partner(q) * sin_ref[rows, :]).astype(BF16)
    qr_ref[...] = q
    q = q * jnp.asarray(SCALE, BF16)
    q_heads = [jnp.where(head_mask(q.shape, h), q, jnp.zeros_like(q)) for h in range(heads)]
    m_ref[...] = jnp.full_like(m_ref, NEG_LARGE)
    l_ref[...] = jnp.zeros_like(l_ref)
    acc_ref[...] = jnp.zeros_like(acc_ref)

    def tile(start, width, kind):
        keys = pl.ds(start, width)
        k = kr_ref[keys, :]
        v = vr_ref[keys, :]
        seen = None
        if kind != 0:
            seen = seen_mask(kind, i, start, width, segk_ref[:, keys], segq_ref[...])
        for h in range(heads):
            s = dot_t(q_heads[h], k)
            if seen is not None:
                s = jnp.where(seen, s, NEG_LARGE)
            old = m_ref[h]
            new = jnp.maximum(old, jnp.max(s, axis=1, keepdims=True))
            p = jnp.exp(s - new)
            fade = jnp.exp(old - new)
            l_ref[h] = l_ref[h] * fade + jnp.sum(p, axis=1, keepdims=True)
            acc_ref[h] = acc_ref[h] * fade + dot_n(p.astype(BF16), v)
            m_ref[h] = new

    block_plan(i, tile)
    out = None
    for h in range(heads):
        total = l_ref[h]
        part = acc_ref[h] / total
        out = part if h == 0 else jnp.where(head_mask(part.shape, h), part, out)
        lse_ref[0, :, h : h + 1] = m_ref[h] + jnp.log(total)
    o_ref[...] = out.astype(BF16)


def bwd_kernel(
    heads, q_ref, k_ref, v_ref, o_ref, do_ref, lse_ref, cos_ref, sin_ref, segk_ref, segq_ref,
    dq_ref, dk_ref, dv_ref, dq_acc, dk_acc, dv_acc,
):
    i = pl.program_id(1)

    @pl.when(i == 0)
    def _():
        dk_acc[...] = jnp.zeros_like(dk_acc)
        dv_acc[...] = jnp.zeros_like(dv_acc)

    q = q_ref[...]
    scaled = q * jnp.asarray(SCALE, BF16)
    do = do_ref[...]
    product = do.astype(F32) * o_ref[...].astype(F32)
    zero = jnp.zeros_like(q)
    masks = [head_mask(q.shape, h) for h in range(heads)]
    q_heads = [jnp.where(m, scaled, zero) for m in masks]
    do_heads = [jnp.where(m, do, zero) for m in masks]
    deltas = [jnp.sum(jnp.where(m, product, 0.0), axis=1, keepdims=True) for m in masks]
    lses = [lse_ref[0, :, h : h + 1] for h in range(heads)]
    dq_acc[...] = jnp.zeros_like(dq_acc)

    def tile(start, width, kind):
        keys = pl.ds(start, width)
        k = k_ref[keys, :]
        v = v_ref[keys, :]
        seen = None
        if kind != 0:
            seen = seen_mask(kind, i, start, width, segk_ref[:, keys], segq_ref[...])
        for h in range(heads):
            s = dot_t(q_heads[h], k)
            p = jnp.exp(s - lses[h])
            if seen is not None:
                p = jnp.where(seen, p, 0.0)
            dp = dot_t(do_heads[h], v)
            ds = (p * (dp - deltas[h])).astype(BF16)
            dv_acc[keys, :] += dot_tn(p.astype(BF16), do_heads[h])
            dk_acc[keys, :] += dot_tn(ds, q_heads[h])
            dq_acc[h] += dot_n(ds, k)

    block_plan(i, tile)
    dq = dq_acc[0]
    for h in range(1, heads):
        dq = jnp.where(masks[h], dq_acc[h], dq)
    dq = dq * SCALE
    rows = pl.ds(pl.multiple_of(i * BQ, BQ), BQ)
    dq_ref[...] = (dq * cos_ref[rows, :] - partner(dq) * sin_ref[rows, :]).astype(BF16)

    @pl.when(i == pl.num_programs(1) - 1)
    def _():
        @pl.loop(0, dk_acc.shape[0] // BK)
        def _(j):
            rows = pl.ds(pl.multiple_of(j * BK, BK), BK)
            dk = dk_acc[rows, :]
            dk_ref[rows, :] = (dk * cos_ref[rows, :] - partner(dk) * sin_ref[rows, :]).astype(BF16)
            dv_ref[rows, :] = dv_acc[rows, :].astype(BF16)


def attention_cost(tree_len, width, products):
    pairs = tree_len * tree_len // 2
    heads = width // HEAD_DIM
    return pl.CostEstimate(
        flops=products * 2 * pairs * 128 * heads * 2,
        bytes_accessed=tree_len * width * 24,
        transcendentals=pairs * heads,
    )


def attention_forward(qkv, cosine, sine, seg_keys, seg_queries, width):
    tree_len = qkv.shape[0]
    gw = min(2 * HEAD_DIM, width)
    groups, heads = width // gw, gw // HEAD_DIM
    row_block = pl.BlockSpec((BQ, gw), lambda g, i: (i, g))
    table = pl.BlockSpec((tree_len, gw), lambda g, i: (0, 0))
    full = pl.BlockSpec((tree_len, gw), lambda g, i: (0, g))
    act = jax.ShapeDtypeStruct((tree_len, width), BF16)
    if width % 128 == 0:
        queries, keys, values, step = qkv, qkv, qkv, groups
    else:
        queries, keys, values = jnp.split(qkv, 3, axis=1)
        step = 0
    return pl.pallas_call(
        functools.partial(fwd_kernel, heads),
        grid=(groups, tree_len // BQ),
        in_specs=[
            row_block,
            pl.BlockSpec((tree_len, gw), lambda g, i: (0, step + g)),
            pl.BlockSpec((tree_len, gw), lambda g, i: (0, 2 * step + g)),
            table,
            table,
            pl.BlockSpec((1, tree_len), lambda g, i: (0, 0)),
            pl.BlockSpec((BQ, 2), lambda g, i: (i, 0)),
        ],
        out_specs=[row_block, pl.BlockSpec((1, BQ, heads), lambda g, i: (g, i, 0)), row_block, full, full],
        out_shape=[act, jax.ShapeDtypeStruct((groups, tree_len, heads), F32), act, act, act],
        scratch_shapes=[
            pltpu.VMEM((heads, BQ, 1), F32),
            pltpu.VMEM((heads, BQ, 1), F32),
            pltpu.VMEM((heads, BQ, gw), F32),
        ],
        compiler_params=pltpu.CompilerParams(vmem_limit_bytes=56 << 20),
        cost_estimate=attention_cost(tree_len, width, 2),
        name="tree_attention_forward",
    )(queries, keys, values, cosine, sine, seg_keys, seg_queries)


def attention_backward(q, k, v, out, grad, lse, cosine, sine, seg_keys, seg_queries):
    tree_len, width = q.shape
    gw = min(2 * HEAD_DIM, width)
    groups, heads = width // gw, gw // HEAD_DIM
    row_block = pl.BlockSpec((BQ, gw), lambda g, i: (i, g))
    table = pl.BlockSpec((tree_len, gw), lambda g, i: (0, 0))
    full = pl.BlockSpec((tree_len, gw), lambda g, i: (0, g))
    act = jax.ShapeDtypeStruct((tree_len, width), BF16)
    return pl.pallas_call(
        functools.partial(bwd_kernel, heads),
        grid=(groups, tree_len // BQ),
        in_specs=[
            row_block, full, full, row_block, row_block,
            pl.BlockSpec((1, BQ, heads), lambda g, i: (g, i, 0)),
            table, table,
            pl.BlockSpec((1, tree_len), lambda g, i: (0, 0)),
            pl.BlockSpec((BQ, 2), lambda g, i: (i, 0)),
        ],
        out_specs=[row_block, full, full],
        out_shape=[act, act, act],
        scratch_shapes=[
            pltpu.VMEM((heads, BQ, gw), F32),
            pltpu.VMEM((tree_len, gw), F32),
            pltpu.VMEM((tree_len, gw), F32),
        ],
        compiler_params=pltpu.CompilerParams(vmem_limit_bytes=56 << 20),
        cost_estimate=attention_cost(tree_len, width, 5),
        name="tree_attention_backward",
    )(q, k, v, out, grad, lse, cosine, sine, seg_keys, seg_queries)


def gather_rows(rows):
    return lax.all_gather(rows, GROUP, axis=0, tiled=True)


def scatter_rows(rows):
    return lax.psum_scatter(rows.astype(BF16), GROUP, scatter_dimension=0, tiled=True)


def line_gather(own):
    size = lax.axis_size("fsdp")
    me = lax.axis_index("fsdp")
    ups = [(i, i + 1) for i in range(size - 1)]
    downs = [(i + 1, i) for i in range(size - 1)]
    rows = own.shape[0]
    from_below, from_above = [own], [own]
    for _ in range(size - 1):
        from_below.append(lax.ppermute(from_below[-1], "fsdp", ups))
        from_above.append(lax.ppermute(from_above[-1], "fsdp", downs))
    whole = jnp.zeros((size * rows,) + own.shape[1:], own.dtype)
    whole = lax.dynamic_update_slice_in_dim(whole, own, me * rows, 0)
    for k in range(1, size):
        piece = jnp.where(me >= k, from_below[k], from_above[size - k])
        whole = lax.dynamic_update_slice_in_dim(whole, piece, ((me - k) % size) * rows, 0)
    return whole


def line_scatter(blocks):
    size = lax.axis_size("fsdp")
    me = lax.axis_index("fsdp")
    ups = [(i, i + 1) for i in range(size - 1)]
    downs = [(i + 1, i) for i in range(size - 1)]
    rows = blocks.shape[0] // size

    def block(offset):
        return lax.dynamic_slice_in_dim(blocks, ((me + offset) % size) * rows, rows, 0)

    up, down = block(size - 1), block(-(size - 1))
    for k in range(size - 2, 0, -1):
        up = lax.ppermute(up, "fsdp", ups)
        down = lax.ppermute(down, "fsdp", downs)
        up = (block(k).astype(F32) + up.astype(F32)).astype(BF16)
        down = (block(-k).astype(F32) + down.astype(F32)).astype(BF16)
    up = lax.ppermute(up, "fsdp", ups)
    down = lax.ppermute(down, "fsdp", downs)
    return (block(0).astype(F32) + up.astype(F32) + down.astype(F32)).astype(BF16)


def swap_columns(part, count):
    size = lax.axis_size("ctx")
    rows, columns = part.shape[0] // size, part.shape[1] // count
    got = lax.all_to_all(part.reshape(size, rows, count, columns), "ctx", split_axis=0, concat_axis=0)
    got = got.reshape(size, rows, count, columns)
    return [got[:, :, c].transpose(1, 0, 2).reshape(rows, size * columns).astype(F32) for c in range(count)]


def normalize(rows):
    norm_inv = lax.rsqrt(jnp.mean(rows * rows, axis=1, keepdims=True) + EPSILON)
    return (rows * norm_inv, norm_inv)


def norm_backward(grad_rows, scaled, norm_inv, gain):
    weighted = grad_rows * gain[None, :]
    inner = jnp.mean(weighted * scaled, axis=1, keepdims=True)
    return norm_inv * (weighted - scaled * inner)


def body(
    tokens_in,
    attn_gain,
    query_weight,
    key_weight,
    value_weight,
    output_weight,
    mlp_gain,
    gate_weight,
    up_weight,
    down_weight,
    seg_lengths,
    leaf_parent,
    cotangent,
):
    ctx = lax.axis_index("ctx")
    parts = lax.axis_size("ctx")
    tree_len = tokens_in.shape[0] * parts * lax.axis_size("tensor")
    width = query_weight.shape[1] // parts
    units = gate_weight.shape[1] // parts

    def mine(weight, columns):
        return lax.dynamic_slice_in_dim(weight, ctx * columns, columns, 1)

    x_rows = tokens_in.astype(F32)
    attn_scaled, attn_inv = normalize(x_rows)
    attn_in = gather_rows((attn_scaled * attn_gain[None, :]).astype(BF16))
    w_attn = line_gather(
        jnp.concatenate([mine(w, width) for w in (query_weight, key_weight, value_weight, output_weight)], axis=1)
    )
    w_gate = line_gather(mine(gate_weight, units))
    w_up = line_gather(mine(up_weight, units))
    w_down = line_gather(mine(down_weight, units))
    w_qkv, w_out = w_attn[:, : 3 * width], w_attn[:, 3 * width :]

    segment, parent, depth = tree_tables(seg_lengths[0], leaf_parent[0], tree_len)
    cosine, sine = rope_tables(depth, min(2 * HEAD_DIM, width))
    seg_keys = segment[None, :]
    seg_queries = jnp.stack([segment, parent], axis=1)

    qkv = jnp.dot(attn_in, w_qkv, preferred_element_type=F32)
    attn_out, lse, query_rows, key_rows, value_rows = attention_forward(
        qkv, cosine, sine, seg_keys, seg_queries, width
    )
    mid_rows = x_rows + scatter_rows(dot_t(attn_out, w_out)).astype(F32)
    mlp_scaled, mlp_inv = normalize(mid_rows)
    mlp_in = gather_rows((mlp_scaled * mlp_gain[None, :]).astype(BF16))
    cot_all = gather_rows(cotangent)

    gate = jnp.dot(mlp_in, w_gate, preferred_element_type=F32)
    up_proj = jnp.dot(mlp_in, w_up, preferred_element_type=F32)
    sigmoid_gate = jax.nn.sigmoid(gate)
    hidden = (gate * sigmoid_gate * up_proj).astype(BF16)
    hidden_grad = jnp.dot(cot_all, w_down, preferred_element_type=F32)
    gate_rows_grad = (
        hidden_grad * up_proj * sigmoid_gate * (1.0 + gate * (1.0 - sigmoid_gate))
    ).astype(BF16)
    up_rows_grad = (hidden_grad * gate * sigmoid_gate).astype(BF16)

    mlp_in_grad = scatter_rows(dot_t(gate_rows_grad, w_gate) + dot_t(up_rows_grad, w_up)).astype(F32)
    mlp_back = norm_backward(mlp_in_grad, mlp_scaled, mlp_inv, mlp_gain)
    mlp_gain_part = jnp.sum(mlp_in_grad * mlp_scaled, axis=0)
    mid_grad = cotangent.astype(F32) + mlp_back
    mid_all = gather_rows(mid_grad.astype(BF16))

    gate_grad = line_scatter(dot_tn(mlp_in, gate_rows_grad).astype(BF16))
    up_grad = line_scatter(dot_tn(mlp_in, up_rows_grad).astype(BF16))
    down_grad = line_scatter(dot_tn(cot_all, hidden).astype(BF16))
    block_out = (mid_rows + scatter_rows(dot_t(hidden, w_down)).astype(F32)).astype(BF16)

    out_heads_grad = jnp.dot(mid_all, w_out, preferred_element_type=F32).astype(BF16)
    output_grad = dot_tn(mid_all, attn_out)
    query_pre_grad, key_pre_grad, value_pre_grad = attention_backward(
        query_rows, key_rows, value_rows, attn_out, out_heads_grad, lse, cosine, sine, seg_keys, seg_queries
    )
    pre_grad = jnp.concatenate([query_pre_grad, key_pre_grad, value_pre_grad], axis=1)
    attn_in_grad = scatter_rows(dot_t(pre_grad, w_qkv)).astype(F32)
    qkv_grad = dot_tn(attn_in, pre_grad)
    attn_gain_part = jnp.sum(qkv_grad * w_qkv.astype(F32), axis=1) / attn_gain
    gain_grads = lax.psum_scatter(
        jnp.stack([attn_gain_part, mlp_gain_part]), ("fsdp", "ctx", "tensor"), scatter_dimension=1, tiled=True
    )
    attn_grad = line_scatter(jnp.concatenate([qkv_grad, output_grad], axis=1).astype(BF16))
    query_out, key_out, value_out, output_out = swap_columns(attn_grad, 4)
    (gate_out,) = swap_columns(gate_grad, 1)
    (up_out,) = swap_columns(up_grad, 1)
    (down_out,) = swap_columns(down_grad, 1)

    attn_back = norm_backward(attn_in_grad, attn_scaled, attn_inv, attn_gain)
    input_grad = (mid_grad + attn_back).astype(BF16)
    return (
        block_out,
        input_grad,
        gain_grads[0],
        query_out,
        key_out,
        value_out,
        output_out,
        gain_grads[1],
        gate_out,
        up_out,
        down_out,
    )


def solution(mesh):
    rows = P(("fsdp", "ctx", "tensor"), None)
    weight = P("fsdp", "tensor")
    gain = P(("fsdp", "ctx", "tensor"))
    grad = P(("fsdp", "ctx"), "tensor")
    in_specs = (
        rows, P(), weight, weight, weight, weight, P(), weight, weight, weight, P("fsdp", None), P("fsdp", None), rows,
    )
    out_specs = (rows, rows, gain, grad, grad, grad, grad, gain, grad, grad, grad)
    return jax.shard_map(body, mesh=mesh, in_specs=in_specs, out_specs=out_specs, check_vma=False)
```

time: 4090 us -> 1660 us (0.41)
  waiting for transfers between devices: 2420 us -> 653 us
  matrix products: 1260 us -> 322 us
  Pallas kernels: 0 us -> 328 us
  starting transfers between devices: 2.54 us -> 153 us
  local copies, waits for them, and re-layouts: 150 us -> 69.5 us
  other arithmetic: 179 us -> 118 us
    all_gather x13 -> x4, waiting for transfers between devices: 1300 us -> 89.8 us  [gather_rows(): return lax.all_gather(rows, GROUP, axis=0, tiled=True)]
    dot_general x57 -> x15, matrix products: 1260 us -> 322 us  [the longest x5 110 us: dot_t(): lax.dot_general(a, b, (((1,), (1,)), ((), ())), preferred_element_type=F32)]
    reduce_scatter x12 -> x4, waiting for transfers between devices: 1010 us -> 233 us  [scatter_rows(): lax.psum_scatter(rows.astype(BF16), GROUP, scatter_dimension=0, tiled=True)]
    pallas_call x0 -> x2, Pallas kernels: none -> 328 us  [the longest x1 171 us: attention_backward(): pl.pallas_call(functools.partial(bwd_kernel, heads), grid=(groups, tree_l...]
    ppermute x0 -> x48, waiting for transfers between devices: none -> 325 us  [the longest x12 174 us: line_gather(): from_above.append(lax.ppermute(from_above[-1], 'fsdp', downs))]
    ppermute x0 -> x48, starting transfers between devices: none -> 136 us  [the longest x12 52.9 us: line_gather(): from_below.append(lax.ppermute(from_below[-1], 'fsdp', ups))]
    unnamed x27 -> x10, waiting for transfers between devices: 110 us -> 0.83 us
    reduce_sum x6 -> x2, other arithmetic: 96.2 us -> 6.44 us  [the longest x1 3.92 us: body(): mlp_gain_part = jnp.sum(mlp_in_grad * mlp_scaled, axis=0)]
  transfers between devices with their start and end apart: 26 -> 61, of which waited for: 23 -> 32; matrix products, arithmetic and copies ran while one was open for 17% -> 18% of each run, Pallas kernels for 0% -> 0%
where the time goes in v1:
time: 1660 us
  waiting for transfers between devices  653 us (39%)
  Pallas kernels  328 us (20%)
  matrix products  322 us (19%)
  starting transfers between devices  153 us (9%)
  other arithmetic  118 us (7%)
  local copies, waits for them, and re-layouts  69.5 us (4%)
    reduce_scatter x4, waiting for transfers between devices, scatter_rows(): lax.psum_scatter(rows.astype(BF16), GROUP, scatter_dimension=0, tiled=True)  233 us
    ppermute x12, waiting for transfers between devices, line_gather(): from_above.append(lax.ppermute(from_above[-1], 'fsdp', downs))  174 us
    pallas_call x1, Pallas kernels, attention_backward(): pl.pallas_call(functools.partial(bwd_kernel, heads), grid=(groups, tree_l...  171 us
    pallas_call x1, Pallas kernels, attention_forward(): pl.pallas_call(functools.partial(fwd_kernel, heads), grid=(groups, tree_l...  157 us
    dot_general x5, matrix products, dot_t(): lax.dot_general(a, b, (((1,), (1,)), ((), ())), preferred_element_type=F32)  110 us
    ppermute x12, waiting for transfers between devices, line_scatter(): down = lax.ppermute(down, 'fsdp', downs)  102 us
    dot_general x5, matrix products, dot_tn(): lax.dot_general(a, b, (((0,), (0,)), ((), ())), preferred_element_type=F32)  97.3 us
    all_gather x4, waiting for transfers between devices, gather_rows(): return lax.all_gather(rows, GROUP, axis=0, tiled=True)  89.8 us
  transfers between devices with their start and end apart: 61, of which 32 were waited for; matrix products, arithmetic and copies ran while one was open for 18% of the time, Pallas kernels for 0%

profile of v1, /device:TPU:0, one launch (start us, length us, event | category | flops | bytes accessed | tf_op | source)
XLA Modules:
  0.0 1657.8 jit_solution(8971261357326658584)
XLA Ops:
  28.1 20.4 %collective-permute-done.1 = bf16[512,1024]{0,1:T(8,128)(2,1)S(1)} collective-permute-done((bf16[512,1024]{0,1:T(8,128)(2,1)}, bf16[512,1024]{0,1:T(8,128)(2,1)S(1)}, u32[]{:S(2)}, u32[]{:S(2)}) %collective-permute-start.1) | collective-permute-done | bytes 1048608 | tf_op jit(solution)/shard_map/ppermute | solution.py:345
  112.2 19.4 %fusion.23.q_ref.k_ref.v_ref = f32[4096,768]{1,0:T(8,128)} fusion(bf16[4096,2048]{1,0:T(8,128)(2,1)} %all-gather.5.cloned.1.call-done, bf16[2048,1024]{0,1:T(8,128)(2,1)} %select_dynamic-update-slice_fusion.9), kind=kOutput, calls=%fused_computation.62 | convolution fusion | flops 12884901888 | bytes 32505856 | tf_op jit(solution)/shard_map/dot_general | solution.py:434
  131.6 157.3 %tree_attention_forward.1 = (bf16[4096,256]{1,0:T(8,128)(2,1)}, f32[2,4096,2]{2,1,0:T(8,128)}, bf16[4096,256]{1,0:T(8,128)(2,1)}, bf16[4096,256]{1,0:T(8,128)(2,1)}, bf16[4096,256]{1,0:T(8,128)(2,1)}) custom-call(f32[4096,768]{1,0:T(8,128)} %fusion.23.q_ref.k_ref.v_ref, f32[4096,768]{1,0:T(8,128)} %fusion.23.q_ref.k_ref.v_ref, ...), custom_call_target="tpu_custom_call" | custom-call | flops 34359738368 | bytes 25165824 | tf_op jit(solution)/shard_map/tree_attention_forward/pallas_call | solution.py:272
  301.9 118.3 %reduce-scatter.8.cloned.1.call-done = bf16[512,2048]{1,0:T(8,128)(2,1)} async-done(((bf16[4096,2048]{1,0:T(8,128)(2,1)}), bf16[512,2048]{1,0:T(8,128)(2,1)}) %reduce-scatter.8.cloned.1.call-update) | async-done | bytes 2097168 | tf_op jit(solution)/shard_map/reduce_scatter | solution.py:333
  460.3 17.7 %collective-permute-done.19 = bf16[512,1024]{0,1:T(8,128)(2,1)} collective-permute-done((bf16[512,1024]{0,1:T(8,128)(2,1)S(1)}, bf16[512,1024]{0,1:T(8,128)(2,1)}, u32[]{:S(2)}, u32[]{:S(2)}) %collective-permute-start.19) | collective-permute-done | bytes 1048608 | tf_op jit(solution)/shard_map/ppermute | solution.py:345
  482.8 17.6 %collective-permute-done.13 = bf16[512,1024]{0,1:T(8,128)(2,1)S(1)} collective-permute-done((bf16[512,1024]{0,1:T(8,128)(2,1)S(1)}, bf16[512,1024]{0,1:T(8,128)(2,1)S(1)}, u32[]{:S(2)}, u32[]{:S(2)}) %collective-permute-start.13) | collective-permute-done | bytes 1048608 | tf_op jit(solution)/shard_map/ppermute | solution.py:345
  505.1 17.7 %collective-permute-done.8 = bf16[512,1024]{0,1:T(8,128)(2,1)S(1)} collective-permute-done((bf16[512,1024]{0,1:T(8,128)(2,1)}, bf16[512,1024]{0,1:T(8,128)(2,1)S(1)}, u32[]{:S(2)}, u32[]{:S(2)}) %collective-permute-start.8) | collective-permute-done | bytes 1048608 | tf_op jit(solution)/shard_map/ppermute | solution.py:345
  527.6 17.7 %collective-permute-done.20 = bf16[512,1024]{0,1:T(8,128)(2,1)S(1)} collective-permute-done((bf16[512,1024]{0,1:T(8,128)(2,1)}, bf16[512,1024]{0,1:T(8,128)(2,1)S(1)}, u32[]{:S(2)}, u32[]{:S(2)}) %collective-permute-start.20) | collective-permute-done | bytes 1048608 | tf_op jit(solution)/shard_map/ppermute | solution.py:345
  572.5 17.7 %collective-permute-done.9 = bf16[512,1024]{0,1:T(8,128)(2,1)S(1)} collective-permute-done((bf16[512,1024]{0,1:T(8,128)(2,1)S(1)}, bf16[512,1024]{0,1:T(8,128)(2,1)S(1)}, u32[]{:S(2)}, u32[]{:S(2)}) %collective-permute-start.9) | collective-permute-done | bytes 1048608 | tf_op jit(solution)/shard_map/ppermute | solution.py:345
  596.5 16.2 collective-permute-done.21
  615.4 18.6 %collective-permute-done.15 = bf16[512,1024]{0,1:T(8,128)(2,1)S(1)} collective-permute-done((bf16[512,1024]{0,1:T(8,128)(2,1)S(1)}, bf16[512,1024]{0,1:T(8,128)(2,1)S(1)}, u32[]{:S(2)}, u32[]{:S(2)}) %collective-permute-start.15) | collective-permute-done | bytes 1048608 | tf_op jit(solution)/shard_map/ppermute | solution.py:345
  643.2 23.6 %fusion.58 = f32[1024,4096]{0,1:T(8,128)} fusion(bf16[2048,1024]{0,1:T(8,128)(2,1)} %select_dynamic-update-slice_fusion, bf16[4096,2048]{1,0:T(8,128)(2,1)} %all-gather.9.cloned.1.call-done), kind=kOutput, calls=%fused_computation.187 | convolution fusion | flops 17179869184 | bytes 37748736 | tf_op jit(solution)/shard_map/dot_general | solution.py:447
  666.8 23.5 %fusion.57 = f32[4096,1024]{1,0:T(8,128)} fusion(bf16[4096,2048]{1,0:T(8,128)(2,1)} %all-gather.7.cloned.1.call-done, bf16[2048,1024]{0,1:T(8,128)(2,1)} %select_dynamic-update-slice_fusion.6), kind=kOutput, calls=%fused_computation.186 | convolution fusion | flops 17179869184 | bytes 37748736 | tf_op jit(solution)/shard_map/dot_general | solution.py:443
  690.4 36.2 %fusion.2 = (bf16[4096,1024]{1,0:T(8,128)(2,1)}, bf16[4096,1024]{1,0:T(8,128)(2,1)}, bf16[4096,1024]{1,0:T(8,128)(2,1)}) fusion(f32[1024,4096]{0,1:T(8,128)} %fusion.58, f32[4096,1024]{1,0:T(8,128)} %fusion.57, bf16[4096,2048]{1,0:T(8,128)(2,1)} %all-gather.7.cloned.1.call-done, bf16[2048,1024]{0,1:T(8,128)(2,1)} %select_dynamic-update-slice_fusion.3), kind=kOutput, calls=%fused_computation.5 | convolution fusion | flops 17246978048 | bytes 79691776 | tf_op jit(solution)/shard_map/dot_general | solution.py:444
  726.6 25.2 %fusion.59 = f32[4096,2048]{1,0:T(8,128)} fusion(bf16[4096,1024]{1,0:T(8,128)(2,1)} %get-tuple-element.66, bf16[2048,1024]{0,1:T(8,128)(2,1)} %select_dynamic-update-slice_fusion.3), kind=kOutput, calls=%fused_computation.188 | convolution fusion | flops 17179869184 | bytes 46137344 | tf_op jit(solution)/shard_map/dot_general | solution.py:77
  751.7 28.1 %add_convert_fusion = bf16[4096,2048]{1,0:T(8,128)(2,1)} fusion(f32[4096,2048]{1,0:T(8,128)} %fusion.59, bf16[4096,1024]{1,0:T(8,128)(2,1)} %get-tuple-element.65, bf16[2048,1024]{0,1:T(8,128)(2,1)} %select_dynamic-update-slice_fusion.6), kind=kOutput, calls=%fused_computation | convolution fusion | flops 17196646400 | bytes 62914560 | tf_op jit(solution)/shard_map/dot_general | solution.py:77
  779.9 115.1 %reduce-scatter.12.cloned.1.call-done = bf16[512,2048]{1,0:T(8,128)(2,1)} async-done(((bf16[4096,2048]{1,0:T(8,128)(2,1)}), bf16[512,2048]{1,0:T(8,128)(2,1)}) %reduce-scatter.12.cloned.1.call-update) | async-done | bytes 2097168 | tf_op jit(solution)/shard_map/reduce_scatter | solution.py:333
  903.2 89.8 %all-gather.11.cloned.1.call-done = bf16[4096,2048]{1,0:T(8,128)(2,1)} async-done(((bf16[512,2048]{1,0:T(8,128)(2,1)}), bf16[4096,2048]{1,0:T(8,128)(2,1)}) %all-gather.11.cloned.1.call-update) | async-done | bytes 16777232 | tf_op jit(solution)/shard_map/all_gather | solution.py:329
  1005.0 170.6 %tree_attention_backward.1 = (bf16[4096,256]{1,0:T(8,128)(2,1)}, bf16[4096,256]{1,0:T(8,128)(2,1)}, bf16[4096,256]{1,0:T(8,128)(2,1)}) custom-call(bf16[4096,256]{1,0:T(8,128)(2,1)} %get-tuple-element.20.q_ref, bf16[4096,256]{1,0:T(8,128)(2,1)} %get-tuple-element.21.k_ref, bf16[4096,256]{1,0:T(8,128)(2,1)} %get-tuple-element.22.v_ref, ...), custom_call_target="tpu_custom_call" | custom-call | flops 85899345920 | bytes 25165824 | tf_op jit(solution)/shard_map/tree_attention_backward/pallas_call | solution.py:305
  1178.6 20.0 %fusion.55 = (bf16[2048,768]{0,1:T(8,128)(2,1)S(1)}, f32[2048]{0:T(1024)S(1)}) fusion(bf16[2048,1024]{0,1:T(8,128)(2,1)} %select_dynamic-update-slice_fusion.9, bf16[4096,2048]{1,0:T(8,128)(2,1)} %all-gather.5.cloned.1.call-done, bf16[4096,768]{1,0:T(8,128)(2,1)S(1)} %constant_dynamic-update-slice_fusion.4), kind=kOutput, calls=%fused_computation.184 | convolution fusion | flops 12891191296 | bytes 29368320 | tf_op jit(solution)/shard_map/dot_general | solution.py:85
  1200.2 20.4 %convolution_convert_fusion = bf16[4096,2048]{1,0:T(8,128)(2,1)} fusion(bf16[4096,768]{1,0:T(8,128)(2,1)} %copy-done.16, bf16[2048,1024]{0,1:T(8,128)(2,1)} %select_dynamic-update-slice_fusion.9), kind=kOutput, calls=%fused_computation.10 | convolution fusion | flops 12893290496 | bytes 26214400 | tf_op jit(solution)/shard_map/dot_general | solution.py:77
  1220.7 23.7 %convolution_convert_fusion.1 = bf16[4096,2048]{1,0:T(8,128)(2,1)} fusion(bf16[4096,1024]{1,0:T(8,128)(2,1)} %get-tuple-element.67, bf16[2048,1024]{0,1:T(8,128)(2,1)} %select_dynamic-update-slice_fusion), kind=kOutput, calls=%fused_computation.11 | convolution fusion | flops 17188257792 | bytes 29360128 | tf_op jit(solution)/shard_map/dot_general | solution.py:77
  1244.5 23.0 %convolution_convert_fusion.4 = bf16[1024,2048]{1,0:T(8,128)(2,1)S(1)} fusion(bf16[4096,1024]{1,0:T(8,128)(2,1)} %get-tuple-element.67, bf16[4096,2048]{1,0:T(8,128)(2,1)} %all-gather.9.cloned.1.call-done), kind=kOutput, calls=%fused_computation.54 | convolution fusion | flops 17181966336 | bytes 29360128 | tf_op jit(solution)/shard_map/dot_general | solution.py:85
  1274.9 22.8 %convolution_convert_fusion.5 = bf16[2048,1024]{1,0:T(8,128)(2,1)S(1)} fusion(bf16[4096,2048]{1,0:T(8,128)(2,1)} %all-gather.7.cloned.1.call-done, bf16[4096,1024]{1,0:T(8,128)(2,1)} %get-tuple-element.66), kind=kOutput, calls=%fused_computation.55 | convolution fusion | flops 17181966336 | bytes 29360128 | tf_op jit(solution)/shard_map/dot_general | solution.py:85
  1303.9 22.6 %convolution_convert_fusion.6 = bf16[2048,1024]{1,0:T(8,128)(2,1)S(1)} fusion(bf16[4096,2048]{1,0:T(8,128)(2,1)S(1)} %bitcast.162, bf16[4096,1024]{1,0:T(8,128)(2,1)} %get-tuple-element.65), kind=kOutput, calls=%fused_computation.56 | convolution fusion | flops 17181966336 | bytes 29360128 | tf_op jit(solution)/shard_map/dot_general | solution.py:85
  1365.4 13.4 collective-permute-done.43
  1384.1 17.1 %collective-permute-done.37 = bf16[512,1024]{1,0:T(8,128)(2,1)} collective-permute-done((bf16[512,1024]{1,0:T(8,128)(2,1)}, bf16[512,1024]{1,0:T(8,128)(2,1)}, u32[]{:S(2)}, u32[]{:S(2)}) %collective-permute-start.37) | collective-permute-done | bytes 1048608 | tf_op jit(solution)/shard_map/ppermute | solution.py:366
  1438.1 13.5 collective-permute-done.40
  1461.3 12.7 collective-permute-done.27
  1525.8 15.7 collective-permute-done.41
  1549.2 14.7 collective-permute-done.28
  1572.2 14.2 collective-permute-done.35
  (298 shorter events, 458.0 us)
Async XLA Ops:
  7.2 105.0 %all-gather.5.cloned.1.call-start = ((), (), s32[]{:S(2)}) async-start(), calls=%async_computation.9 | async-start | bytes 18874368 | tf_op jit(solution)/shard_map/all_gather | solution.py:329
  13.4 406.8 %reduce-scatter.8.cloned.1.call-start = ((), (), s32[]{:S(2)}) async-start(), calls=%async_computation.10 | async-start | bytes 18874368 | tf_op jit(solution)/shard_map/reduce_scatter | solution.py:333
  301.1 342.1 %all-gather.9.cloned.1.call-start = ((), (), s32[]{:S(2)}) async-start(), calls=%async_computation.13 | async-start | bytes 18874368 | tf_op jit(solution)/shard_map/all_gather | solution.py:329
  301.8 365.0 %all-gather.7.cloned.1.call-start = ((), (), s32[]{:S(2)}) async-start(), calls=%async_computation.11 | async-start | bytes 18874368 | tf_op jit(solution)/shard_map/all_gather | solution.py:329
  425.6 469.4 %reduce-scatter.12.cloned.1.call-start = ((), (), s32[]{:S(2)}) async-start(), calls=%async_computation.14 | async-start | bytes 18874368 | tf_op jit(solution)/shard_map/reduce_scatter | solution.py:333
  446.7 53.6 %collective-permute-start.13 = (bf16[512,1024]{0,1:T(8,128)(2,1)S(1)}, bf16[512,1024]{0,1:T(8,128)(2,1)S(1)}, u32[]{:S(2)}, u32[]{:S(2)}) collective-permute-start(bf16[512,1024]{0,1:T(8,128)(2,1)S(1)} %copy.134), channel_id=1, source_target_pairs={{8,0},{16,8},{24,16},{9,1},{17,9},{25,17},{10,2},{18,10},{26,18},{... | collective-permute-start | bytes 3145736 | tf_op jit(solution)/shard_map/ppermute | solution.py:345
  459.0 63.9 %collective-permute-start.8 = (bf16[512,1024]{0,1:T(8,128)(2,1)}, bf16[512,1024]{0,1:T(8,128)(2,1)S(1)}, u32[]{:S(2)}, u32[]{:S(2)}) collective-permute-start(bf16[512,1024]{0,1:T(8,128)(2,1)} %collective-permute-done.7), channel_id=1, source_target_pairs={{8,0},{16,8},{24,16},{9,1},{17,9},{25,17},{10,2},{18,10},{26,18},{... | collective-permute-start | bytes 3145736 | tf_op jit(solution)/shard_map/ppermute | solution.py:345
  481.5 63.9 %collective-permute-start.20 = (bf16[512,1024]{0,1:T(8,128)(2,1)}, bf16[512,1024]{0,1:T(8,128)(2,1)S(1)}, u32[]{:S(2)}, u32[]{:S(2)}) collective-permute-start(bf16[512,1024]{0,1:T(8,128)(2,1)} %collective-permute-done.19), channel_id=1, source_target_pairs={{8,0},{16,8},{24,16},{9,1},{17,9},{25,17},{10,2},{18,10},{26,18},{... | collective-permute-start | bytes 3145736 | tf_op jit(solution)/shard_map/ppermute | solution.py:345
  500.4 58.0 %collective-permute-start.22 = (bf16[512,1024]{0,1:T(8,128)(2,1)}, bf16[512,1024]{0,1:T(8,128)(2,1)S(1)}, u32[]{:S(2)}, u32[]{:S(2)}) collective-permute-start(bf16[512,1024]{0,1:T(8,128)(2,1)} %collective-permute-done.18), channel_id=1, source_target_pairs={{0,8},{8,16},{16,24},{1,9},{9,17},{17,25},{2,10},{10,18},{18,26},{... | collective-permute-start | bytes 3145736 | tf_op jit(solution)/shard_map/ppermute | solution.py:344
  503.8 64.0 %collective-permute-start.14 = (bf16[512,1024]{0,1:T(8,128)(2,1)S(1)}, bf16[512,1024]{0,1:T(8,128)(2,1)S(1)}, u32[]{:S(2)}, u32[]{:S(2)}) collective-permute-start(bf16[512,1024]{0,1:T(8,128)(2,1)S(1)} %collective-permute-done.13), channel_id=1, source_target_pairs={{8,0},{16,8},{24,16},{9,1},{17,9},{25,17},{10,2},{18,10},{26,18},{... | collective-permute-start | bytes 3145736 | tf_op jit(solution)/shard_map/ppermute | solution.py:345
  526.3 64.0 %collective-permute-start.9 = (bf16[512,1024]{0,1:T(8,128)(2,1)S(1)}, bf16[512,1024]{0,1:T(8,128)(2,1)S(1)}, u32[]{:S(2)}, u32[]{:S(2)}) collective-permute-start(bf16[512,1024]{0,1:T(8,128)(2,1)S(1)} %collective-permute-done.8), channel_id=1, source_target_pairs={{8,0},{16,8},{24,16},{9,1},{17,9},{25,17},{10,2},{18,10},{26,18},{... | collective-permute-start | bytes 3145736 | tf_op jit(solution)/shard_map/ppermute | solution.py:345
  545.3 67.4 %collective-permute-start.21 = (bf16[512,1024]{0,1:T(8,128)(2,1)S(1)}, bf16[512,1024]{0,1:T(8,128)(2,1)S(1)}, u32[]{:S(2)}, u32[]{:S(2)}) collective-permute-start(bf16[512,1024]{0,1:T(8,128)(2,1)S(1)} %collective-permute-done.20), channel_id=1, source_target_pairs={{8,0},{16,8},{24,16},{9,1},{17,9},{25,17},{10,2},{18,10},{26,18},{... | collective-permute-start | bytes 3145736 | tf_op jit(solution)/shard_map/ppermute | solution.py:345
  558.3 78.4 %collective-permute-start.11 = (bf16[512,1024]{0,1:T(8,128)(2,1)S(1)}, bf16[512,1024]{0,1:T(8,128)(2,1)S(1)}, u32[]{:S(2)}, u32[]{:S(2)}) collective-permute-start(bf16[512,1024]{0,1:T(8,128)(2,1)S(1)} %collective-permute-done.10), channel_id=1, source_target_pairs={{0,8},{8,16},{16,24},{1,9},{9,17},{17,25},{2,10},{10,18},{18,26},{... | collective-permute-start | bytes 3145736 | tf_op jit(solution)/shard_map/ppermute | solution.py:344
  567.8 71.5 %collective-permute-start.23 = (bf16[512,1024]{0,1:T(8,128)(2,1)S(1)}, bf16[512,1024]{0,1:T(8,128)(2,1)S(1)}, u32[]{:S(2)}, u32[]{:S(2)}) collective-permute-start(bf16[512,1024]{0,1:T(8,128)(2,1)S(1)} %collective-permute-done.22), channel_id=1, source_target_pairs={{0,8},{8,16},{16,24},{1,9},{9,17},{17,25},{2,10},{10,18},{18,26},{... | collective-permute-start | bytes 3145736 | tf_op jit(solution)/shard_map/ppermute | solution.py:344
  571.2 62.8 %collective-permute-start.15 = (bf16[512,1024]{0,1:T(8,128)(2,1)S(1)}, bf16[512,1024]{0,1:T(8,128)(2,1)S(1)}, u32[]{:S(2)}, u32[]{:S(2)}) collective-permute-start(bf16[512,1024]{0,1:T(8,128)(2,1)S(1)} %collective-permute-done.14), channel_id=1, source_target_pairs={{8,0},{16,8},{24,16},{9,1},{17,9},{25,17},{10,2},{18,10},{26,18},{... | collective-permute-start | bytes 3145736 | tf_op jit(solution)/shard_map/ppermute | solution.py:345
  590.3 51.6 %collective-permute-start.17 = (bf16[512,1024]{0,1:T(8,128)(2,1)S(1)}, bf16[512,1024]{0,1:T(8,128)(2,1)S(1)}, u32[]{:S(2)}, u32[]{:S(2)}) collective-permute-start(bf16[512,1024]{0,1:T(8,128)(2,1)S(1)} %collective-permute-done.16), channel_id=1, source_target_pairs={{0,8},{8,16},{16,24},{1,9},{9,17},{17,25},{2,10},{10,18},{18,26},{... | collective-permute-start | bytes 3145736 | tf_op jit(solution)/shard_map/ppermute | solution.py:344
  779.9 213.1 %all-gather.11.cloned.1.call-start = ((), (), s32[]{:S(2)}) async-start(), calls=%async_computation.15 | async-start | bytes 18874368 | tf_op jit(solution)/shard_map/all_gather | solution.py:329
  903.0 722.2 %reduce-scatter.16.cloned.1.call-start = ((), (), s32[]{:S(2)}) async-start(), calls=%async_computation.17 | async-start | bytes 1081344
  1200.1 440.3 %reduce-scatter.14.cloned.1.call-start = ((), (), s32[]{:S(2)}) async-start(), calls=%async_computation.16 | async-start | bytes 18874368 | tf_op jit(solution)/shard_map/reduce_scatter | solution.py:333
  1220.6 422.4 %reduce-scatter.10.cloned.1.call-start = ((), (), s32[]{:S(2)}) async-start(), calls=%async_computation.12 | async-start | bytes 18874368 | tf_op jit(solution)/shard_map/reduce_scatter | solution.py:333
  1270.3 64.4 %collective-permute-start.42 = (bf16[512,1024]{0,1:T(8,128)(2,1)}, bf16[512,1024]{0,1:T(8,128)(2,1)}, u32[]{:S(2)}, u32[]{:S(2)}) collective-permute-start(bf16[512,1024]{0,1:T(8,128)(2,1)} %get-tuple-element.72), channel_id=1, source_target_pairs={{0,8},{8,16},{16,24},{1,9},{9,17},{17,25},{2,10},{10,18},{18,26},{... | collective-permute-start | bytes 3145736 | tf_op jit(solution)/shard_map/ppermute | solution.py:366
  1347.7 53.5 %collective-permute-start.37 = (bf16[512,1024]{1,0:T(8,128)(2,1)}, bf16[512,1024]{1,0:T(8,128)(2,1)}, u32[]{:S(2)}, u32[]{:S(2)}) collective-permute-start(bf16[512,1024]{1,0:T(8,128)(2,1)} %add_convert_fusion.6), channel_id=1, source_target_pairs={{0,8},{8,16},{16,24},{1,9},{9,17},{17,25},{2,10},{10,18},{18,26},{... | collective-permute-start | bytes 3145736 | tf_op jit(solution)/shard_map/ppermute | solution.py:366
  1356.3 66.3 %collective-permute-start.33 = (bf16[512,1024]{1,0:T(8,128)(2,1)}, bf16[512,1024]{1,0:T(8,128)(2,1)S(1)}, u32[]{:S(2)}, u32[]{:S(2)}) collective-permute-start(bf16[512,1024]{1,0:T(8,128)(2,1)} %get-tuple-element.81), channel_id=1, source_target_pairs={{8,0},{16,8},{24,16},{9,1},{17,9},{25,17},{10,2},{18,10},{26,18},{... | collective-permute-start | bytes 3145736 | tf_op jit(solution)/shard_map/ppermute | solution.py:367
  1361.7 72.8 %collective-permute-start.31 = (bf16[512,1024]{1,0:T(8,128)(2,1)S(1)}, bf16[512,1024]{1,0:T(8,128)(2,1)S(1)}, u32[]{:S(2)}, u32[]{:S(2)}) collective-permute-start(bf16[512,1024]{1,0:T(8,128)(2,1)S(1)} %add_convert_fusion.11), channel_id=1, source_target_pairs={{0,8},{8,16},{16,24},{1,9},{9,17},{17,25},{2,10},{10,18},{18,26},{... | collective-permute-start | bytes 3145736 | tf_op jit(solution)/shard_map/ppermute | solution.py:366
  1434.5 62.0 %collective-permute-start.47 = (bf16[512,1024]{0,1:T(8,128)(2,1)}, bf16[512,1024]{0,1:T(8,128)(2,1)}, u32[]{:S(2)}, u32[]{:S(2)}) collective-permute-start(bf16[512,1024]{0,1:T(8,128)(2,1)} %fusion.27), channel_id=1, source_target_pairs={{8,0},{16,8},{24,16},{9,1},{17,9},{25,17},{10,2},{18,10},{26,18},{... | collective-permute-start | bytes 3145736 | tf_op jit(solution)/shard_map/ppermute | solution.py:371
  1451.6 67.4 %collective-permute-start.34 = (bf16[512,1024]{1,0:T(8,128)(2,1)}, bf16[512,1024]{1,0:T(8,128)(2,1)}, u32[]{:S(2)}, u32[]{:S(2)}) collective-permute-start(bf16[512,1024]{1,0:T(8,128)(2,1)} %get-tuple-element.79), channel_id=1, source_target_pairs={{8,0},{16,8},{24,16},{9,1},{17,9},{25,17},{10,2},{18,10},{26,18},{... | collective-permute-start | bytes 3145736 | tf_op jit(solution)/shard_map/ppermute | solution.py:367
  1452.9 71.6 %collective-permute-start.38 = (bf16[512,1024]{1,0:T(8,128)(2,1)}, bf16[512,1024]{1,0:T(8,128)(2,1)}, u32[]{:S(2)}, u32[]{:S(2)}) collective-permute-start(bf16[512,1024]{1,0:T(8,128)(2,1)} %get-tuple-element.74), channel_id=1, source_target_pairs={{0,8},{8,16},{16,24},{1,9},{9,17},{17,25},{2,10},{10,18},{18,26},{... | collective-permute-start | bytes 3145736 | tf_op jit(solution)/shard_map/ppermute | solution.py:370
  1474.0 67.4 %collective-permute-start.41 = (bf16[512,1024]{1,0:T(8,128)(2,1)}, bf16[512,1024]{1,0:T(8,128)(2,1)}, u32[]{:S(2)}, u32[]{:S(2)}) collective-permute-start(bf16[512,1024]{1,0:T(8,128)(2,1)} %add_convert_fusion.3), channel_id=1, source_target_pairs={{8,0},{16,8},{24,16},{9,1},{17,9},{25,17},{10,2},{18,10},{26,18},{... | collective-permute-start | bytes 3145736 | tf_op jit(solution)/shard_map/ppermute | solution.py:371
  1479.6 69.6 %collective-permute-start.25 = (bf16[512,1024]{0,1:T(8,128)(2,1)}, bf16[512,1024]{0,1:T(8,128)(2,1)}, u32[]{:S(2)}, u32[]{:S(2)}) collective-permute-start(bf16[512,1024]{0,1:T(8,128)(2,1)} %get-tuple-element.84), channel_id=1, source_target_pairs={{0,8},{8,16},{16,24},{1,9},{9,17},{17,25},{2,10},{10,18},{18,26},{... | collective-permute-start | bytes 3145736 | tf_op jit(solution)/shard_map/ppermute | solution.py:366
  1496.5 67.4 %collective-permute-start.28 = (bf16[512,1024]{0,1:T(8,128)(2,1)}, bf16[512,1024]{0,1:T(8,128)(2,1)}, u32[]{:S(2)}, u32[]{:S(2)}) collective-permute-start(bf16[512,1024]{0,1:T(8,128)(2,1)} %get-tuple-element.85), channel_id=1, source_target_pairs={{8,0},{16,8},{24,16},{9,1},{17,9},{25,17},{10,2},{18,10},{26,18},{... | collective-permute-start | bytes 3145736 | tf_op jit(solution)/shard_map/ppermute | solution.py:367
  1519.0 53.2 %collective-permute-start.32 = (bf16[512,1024]{1,0:T(8,128)(2,1)}, bf16[512,1024]{1,0:T(8,128)(2,1)}, u32[]{:S(2)}, u32[]{:S(2)}) collective-permute-start(bf16[512,1024]{1,0:T(8,128)(2,1)} %get-tuple-element.78), channel_id=1, source_target_pairs={{0,8},{8,16},{16,24},{1,9},{9,17},{17,25},{2,10},{10,18},{18,26},{... | collective-permute-start | bytes 3145736 | tf_op jit(solution)/shard_map/ppermute | solution.py:370
  1524.5 61.9 %collective-permute-start.35 = (bf16[512,1024]{1,0:T(8,128)(2,1)}, bf16[512,1024]{1,0:T(8,128)(2,1)}, u32[]{:S(2)}, u32[]{:S(2)}) collective-permute-start(bf16[512,1024]{1,0:T(8,128)(2,1)} %add_convert_fusion.8), channel_id=1, source_target_pairs={{8,0},{16,8},{24,16},{9,1},{17,9},{25,17},{10,2},{18,10},{26,18},{... | collective-permute-start | bytes 3145736 | tf_op jit(solution)/shard_map/ppermute | solution.py:371
  (64 other events, 2121.1 us)
Sparse Core Ops, SparseCore 0:
  13.5 92.5 all-gather.4
  301.2 118.9 reduce-scatter.7
  422.1 89.8 all-gather.8
  513.7 89.8 all-gather.6
  780.0 114.9 reduce-scatter.11
  903.1 89.8 all-gather.10
  1200.2 136.0 reduce-scatter.15
  1340.3 112.1 reduce-scatter.13
  1456.5 132.1 reduce-scatter.9

commit v2 on v1

v2 whole, which is shorter than its diff:
```python
import functools

import jax
import jax.numpy as jnp
from jax import lax
from jax.experimental import pallas as pl
from jax.experimental.pallas import tpu as pltpu
from jax.sharding import PartitionSpec as P

HEAD_DIM = 64
TRUNK = 2176
MOST_SEG = 128
ROPE_BASE = 130000.0
EPSILON = 1e-05
NEG_LARGE = -1e30
SCALE = HEAD_DIM ** (-0.5)

BQ = 512
BK = 512
GROUP = ("ctx", "tensor")

F32 = jnp.float32
BF16 = jnp.bfloat16


def pick_table(onehot, table):
    return jnp.sum(jnp.where(onehot, table[None, :], 0), axis=1)


def tree_tables(lengths_row, parent_row, tree_len):
    branches = lengths_row.shape[0] - parent_row.shape[0]
    ends = TRUNK + jnp.cumsum(lengths_row)
    starts = ends - lengths_row
    matches = parent_row[:, None] - 1 == jnp.arange(branches, dtype=jnp.int32)[None, :]
    parent_len = jnp.sum(jnp.where(matches, lengths_row[None, :branches], 0), axis=1)
    zero_one = jnp.zeros((1,), jnp.int32)
    seg_start = jnp.concatenate([zero_one, starts])
    seg_base = jnp.concatenate(
        [zero_one, jnp.full((branches,), TRUNK, jnp.int32), TRUNK + parent_len]
    )
    seg_parent = jnp.concatenate([zero_one, jnp.zeros((branches,), jnp.int32), parent_row])
    positions = jnp.arange(tree_len, dtype=jnp.int32)
    above = jnp.sum((ends[None, :] <= positions[:, None]).astype(jnp.int32), axis=1)
    segment = (positions >= TRUNK).astype(jnp.int32) + above
    onehot = segment[:, None] == jnp.arange(seg_start.shape[0], dtype=jnp.int32)[None, :]
    depth = positions - pick_table(onehot, seg_start) + pick_table(onehot, seg_base)
    parent = pick_table(onehot, seg_parent)
    return (segment, parent, depth)


def rope_tables(depth, width):
    half = HEAD_DIM // 2
    lane = jnp.arange(width, dtype=jnp.int32)
    freqs = jnp.power(ROPE_BASE, -(2.0 * (lane % half).astype(F32)) / HEAD_DIM)
    angles = depth.astype(F32)[:, None] * freqs[None, :]
    sign = jnp.where(lane % HEAD_DIM < half, -1.0, 1.0)
    return jnp.cos(angles), jnp.sin(angles) * sign[None, :]


def partner(x):
    half = HEAD_DIM // 2
    width = x.shape[1]
    if width == HEAD_DIM:
        return jnp.concatenate([x[:, half:], x[:, :half]], axis=1)
    lane = lax.broadcasted_iota(jnp.int32, x.shape, 1)
    ahead = pltpu.roll(x, width - half, 1)
    behind = pltpu.roll(x, half, 1)
    return jnp.where(lane % HEAD_DIM < half, ahead, behind)


def head_mask(shape, head):
    lane = lax.broadcasted_iota(jnp.int32, shape, 1)
    return lane // HEAD_DIM == head


def dot_t(a, b):
    return lax.dot_general(a, b, (((1,), (1,)), ((), ())), preferred_element_type=F32)


def dot_n(a, b):
    return lax.dot_general(a, b, (((1,), (0,)), ((), ())), preferred_element_type=F32)


def dot_tn(a, b):
    return lax.dot_general(a, b, (((0,), (0,)), ((), ())), preferred_element_type=F32)


def key_plan(i, tile):
    base = TRUNK // BK * BK
    branch_end = TRUNK + 4 * MOST_SEG
    first_tree = base // BQ
    mixed_end = -(-(branch_end + MOST_SEG) // BQ)
    chunks = jnp.minimum(i * BQ, base) // BK

    @pl.when(i < first_tree)
    def _():
        @pl.loop(0, chunks)
        def _(j):
            start = pl.multiple_of(j * BK, BK)
            tile(start, BK, 0, start)

    @pl.when(i >= first_tree)
    def _():
        tile(0, base, 0, 0)

    @pl.when(i < first_tree)
    def _():
        start = pl.multiple_of(chunks * BK, BK)
        tile(start, BK, 1, start)

    for block in range(first_tree, mixed_end):

        @pl.when(i == block)
        def _(block=block):
            tile(base, (block + 1) * BQ - base, 2, base)

    @pl.when(i >= mixed_end)
    def _():
        tile(base, branch_end - base, 3, base)
        tile(pl.multiple_of(i * BQ - MOST_SEG, MOST_SEG), BQ + MOST_SEG, 4, branch_end)


def most_keys():
    return TRUNK + 4 * MOST_SEG + BQ + MOST_SEG


def seen_mask(kind, q_at, k_at, seg_q, par_q, seg_k):
    if kind == 3:
        return (seg_k == 0) | (seg_k == par_q)
    causal = k_at <= q_at
    if kind == 1:
        return causal
    if kind == 4:
        return causal & (seg_k == seg_q)
    return causal & ((seg_k == 0) | (seg_k == seg_q) | (seg_k == par_q))


def fwd_kernel(
    heads, q_ref, k_ref, v_ref, cos_ref, sin_ref, segk_ref, segq_ref,
    o_ref, lse_ref, qr_ref, kr_ref, vr_ref, kt_ref, va_ref, s_ref, m_ref, acc_ref,
):
    i = pl.program_id(1)
    wide = 2 * HEAD_DIM

    @pl.when(i == 0)
    def _():
        @pl.loop(0, k_ref.shape[0] // BK)
        def _(j):
            rows = pl.ds(pl.multiple_of(j * BK, BK), BK)
            k = k_ref[rows, :]
            k = (k * cos_ref[rows, :] + partner(k) * sin_ref[rows, :]).astype(BF16)
            kr_ref[rows, :] = k
            kt_ref[:, rows] = jnp.transpose(k)
            v = v_ref[rows, :].astype(BF16)
            vr_ref[rows, :] = v
            if heads == 1:
                va_ref[0, rows, :] = jnp.concatenate([v, jnp.ones_like(v)], axis=1)
            else:
                for h in range(heads):
                    va_ref[h, rows, :] = jnp.where(head_mask(v.shape, h), v, jnp.ones_like(v))

    rows = pl.ds(pl.multiple_of(i * BQ, BQ), BQ)
    q = q_ref[...]
    q = (q * cos_ref[rows, :] + partner(q) * sin_ref[rows, :]).astype(BF16)
    qr_ref[...] = q
    q = q * jnp.asarray(SCALE, BF16)
    q_heads = [jnp.where(head_mask(q.shape, h), q, jnp.zeros_like(q)) for h in range(heads)]
    m_ref[...] = jnp.full_like(m_ref, NEG_LARGE)
    acc_ref[...] = jnp.zeros_like(acc_ref)

    def score_tile(start, width, kind, place):
        keys = pl.ds(start, width)
        k = kt_ref[:, keys]
        seen = None
        if kind != 0:
            shape = (BQ, width)
            seen = seen_mask(
                kind,
                lax.broadcasted_iota(jnp.int32, shape, 0) + i * BQ,
                lax.broadcasted_iota(jnp.int32, shape, 1) + start,
                segq_ref[:, 0:1], segq_ref[:, 1:2], segk_ref[:, keys],
            )
        for h in range(heads):
            s = dot_n(q_heads[h], k)
            if seen is not None:
                s = jnp.where(seen, s, NEG_LARGE)
            s_ref[h, :, pl.ds(place, width)] = s
            largest = m_ref[h]
            for c in range(width // 128):
                largest = jnp.maximum(largest, s[:, c * 128 : (c + 1) * 128])
            m_ref[h] = largest

    key_plan(i, score_tile)
    for h in range(heads):
        m_ref[h] = jnp.broadcast_to(jnp.max(m_ref[h], axis=1, keepdims=True), (BQ, 128))

    def value_tile(start, width, kind, place):
        keys = pl.ds(start, width)
        for h in range(heads):
            m = m_ref[h]
            parts = [
                jnp.exp(s_ref[h, :, pl.ds(place + c * 128, 128)] - m).astype(BF16) for c in range(width // 128)
            ]
            acc_ref[h] += dot_n(jnp.concatenate(parts, axis=1), va_ref[h, keys, :])

    key_plan(i, value_tile)
    out, lse = None, None
    for h in range(heads):
        acc = acc_ref[h]
        part = acc / pltpu.roll(acc, HEAD_DIM, 1)
        stat = m_ref[h] + jnp.log(jnp.broadcast_to(acc[:, (1 - h) * HEAD_DIM : (1 - h) * HEAD_DIM + 1], (BQ, wide)))
        mask = head_mask((BQ, wide), h)
        out = part if h == 0 else jnp.where(mask, part, out)
        lse = stat if h == 0 else jnp.where(mask, stat, lse)
    o_ref[...] = out[:, : heads * HEAD_DIM].astype(BF16)
    turned = jnp.transpose(lse)
    for h in range(heads):
        lse_ref[0, h : h + 1, :] = turned[h * HEAD_DIM : h * HEAD_DIM + 1, :]


def bwd_kernel(
    heads, q_ref, k_ref, v_ref, o_ref, do_ref, lse_ref, cos_ref, sin_ref, segk_ref, segq_ref,
    dq_ref, dk_ref, dv_ref, dq_acc, dk_acc, dv_acc,
):
    i = pl.program_id(1)

    @pl.when(i == 0)
    def _():
        dk_acc[...] = jnp.zeros_like(dk_acc)
        dv_acc[...] = jnp.zeros_like(dv_acc)

    q = q_ref[...]
    scaled = q * jnp.asarray(SCALE, BF16)
    do = do_ref[...]
    product = jnp.transpose(do.astype(F32) * o_ref[...].astype(F32))
    zero = jnp.zeros_like(q)
    masks = [head_mask(q.shape, h) for h in range(heads)]
    q_heads = [jnp.where(m, scaled, zero) for m in masks]
    do_heads = [jnp.where(m, do, zero) for m in masks]
    deltas = [
        jnp.sum(product[h * HEAD_DIM : (h + 1) * HEAD_DIM, :], axis=0, keepdims=True) for h in range(heads)
    ]
    lses = [lse_ref[0, h : h + 1, :] for h in range(heads)]
    q_turned = [jnp.transpose(x) for x in q_heads]
    do_turned = [jnp.transpose(x) for x in do_heads]
    q_stack = jnp.concatenate(q_heads, axis=0)
    do_stack = jnp.concatenate(do_heads, axis=0)
    dq_acc[...] = jnp.zeros_like(dq_acc)

    def tile(start, width, kind, place):
        keys = pl.ds(start, width)
        k = k_ref[keys, :]
        v = v_ref[keys, :]
        seen = None
        if kind != 0:
            shape = (width, BQ)
            seen = seen_mask(
                kind,
                lax.broadcasted_iota(jnp.int32, shape, 1) + i * BQ,
                lax.broadcasted_iota(jnp.int32, shape, 0) + start,
                segq_ref[0:1, :], segq_ref[1:2, :], segk_ref[keys, :],
            )
        probs, grads, k_heads = [], [], []
        for h in range(heads):
            s = dot_n(k, q_turned[h])
            p = jnp.exp(s - lses[h])
            if seen is not None:
                p = jnp.where(seen, p, 0.0)
            dp = dot_n(v, do_turned[h])
            probs.append(p.astype(BF16))
            grads.append((p * (dp - deltas[h])).astype(BF16))
            k_heads.append(jnp.where(head_mask(k.shape, h), k, jnp.zeros_like(k)))
        grad_row = jnp.concatenate(grads, axis=1)
        dv_acc[keys, :] += dot_n(jnp.concatenate(probs, axis=1), do_stack)
        dk_acc[keys, :] += dot_n(grad_row, q_stack)
        dq_acc[...] += dot_tn(jnp.concatenate(grads, axis=0), jnp.concatenate(k_heads, axis=0))

    key_plan(i, tile)
    dq = dq_acc[...] * SCALE
    rows = pl.ds(pl.multiple_of(i * BQ, BQ), BQ)
    dq_ref[...] = (dq * cos_ref[rows, :] - partner(dq) * sin_ref[rows, :]).astype(BF16)

    @pl.when(i == pl.num_programs(1) - 1)
    def _():
        @pl.loop(0, dk_acc.shape[0] // BK)
        def _(j):
            rows = pl.ds(pl.multiple_of(j * BK, BK), BK)
            dk = dk_acc[rows, :]
            dk_ref[rows, :] = (dk * cos_ref[rows, :] - partner(dk) * sin_ref[rows, :]).astype(BF16)
            dv_ref[rows, :] = dv_acc[rows, :].astype(BF16)


def small_cost():
    return pl.CostEstimate(flops=1 << 20, bytes_accessed=1 << 20, transcendentals=0)


def attention_forward(qkv, cosine, sine, seg_keys, seg_queries, width):
    tree_len = qkv.shape[0]
    gw = min(2 * HEAD_DIM, width)
    groups, heads = width // gw, gw // HEAD_DIM
    row_block = pl.BlockSpec((BQ, gw), lambda g, i: (i, g))
    table = pl.BlockSpec((tree_len, gw), lambda g, i: (0, 0))
    full = pl.BlockSpec((tree_len, gw), lambda g, i: (0, g))
    act = jax.ShapeDtypeStruct((tree_len, width), BF16)
    if width % 128 == 0:
        queries, keys, values, step = qkv, qkv, qkv, groups
    else:
        queries, keys, values = jnp.split(qkv, 3, axis=1)
        step = 0
    return pl.pallas_call(
        functools.partial(fwd_kernel, heads),
        grid=(groups, tree_len // BQ),
        in_specs=[
            row_block,
            pl.BlockSpec((tree_len, gw), lambda g, i: (0, step + g)),
            pl.BlockSpec((tree_len, gw), lambda g, i: (0, 2 * step + g)),
            table,
            table,
            pl.BlockSpec((1, tree_len), lambda g, i: (0, 0)),
            pl.BlockSpec((BQ, 2), lambda g, i: (i, 0)),
        ],
        out_specs=[row_block, pl.BlockSpec((1, heads, BQ), lambda g, i: (g, 0, i)), row_block, full, full],
        out_shape=[act, jax.ShapeDtypeStruct((groups, heads, tree_len), F32), act, act, act],
        scratch_shapes=[
            pltpu.VMEM((gw, tree_len), BF16),
            pltpu.VMEM((heads, tree_len, 128), BF16),
            pltpu.VMEM((heads, BQ, most_keys()), F32),
            pltpu.VMEM((heads, BQ, 128), F32),
            pltpu.VMEM((heads, BQ, 128), F32),
        ],
        compiler_params=pltpu.CompilerParams(vmem_limit_bytes=56 << 20),
        cost_estimate=small_cost(),
        name="tree_attention_forward",
    )(queries, keys, values, cosine, sine, seg_keys, seg_queries)


def attention_backward(q, k, v, out, grad, lse, cosine, sine, seg_keys, seg_queries):
    tree_len, width = q.shape
    gw = min(2 * HEAD_DIM, width)
    groups, heads = width // gw, gw // HEAD_DIM
    row_block = pl.BlockSpec((BQ, gw), lambda g, i: (i, g))
    table = pl.BlockSpec((tree_len, gw), lambda g, i: (0, 0))
    full = pl.BlockSpec((tree_len, gw), lambda g, i: (0, g))
    act = jax.ShapeDtypeStruct((tree_len, width), BF16)
    return pl.pallas_call(
        functools.partial(bwd_kernel, heads),
        grid=(groups, tree_len // BQ),
        in_specs=[
            row_block, full, full, row_block, row_block,
            pl.BlockSpec((1, heads, BQ), lambda g, i: (g, 0, i)),
            table, table,
            pl.BlockSpec((tree_len, 1), lambda g, i: (0, 0)),
            pl.BlockSpec((2, BQ), lambda g, i: (0, i)),
        ],
        out_specs=[row_block, full, full],
        out_shape=[act, act, act],
        scratch_shapes=[
            pltpu.VMEM((BQ, gw), F32),
            pltpu.VMEM((tree_len, gw), F32),
            pltpu.VMEM((tree_len, gw), F32),
        ],
        compiler_params=pltpu.CompilerParams(vmem_limit_bytes=56 << 20),
        cost_estimate=small_cost(),
        name="tree_attention_backward",
    )(q, k, v, out, grad, lse, cosine, sine, seg_keys.T, seg_queries.T)


MESH = pl.DeviceIdType.MESH


def plane_place():
    ctx, row = lax.axis_index("ctx"), lax.axis_index("tensor")
    x, core = ctx // 2, ctx % 2
    return x, core, row


def plane_neighbours(x, core, row):
    over_x = {"ctx": (1 - x) * 2 + core}
    over_core = {"ctx": x * 2 + 1 - core}
    over_row = {"tensor": 1 - row}
    return over_x, over_row, over_core


def enter_plane(neighbours):
    barrier = pltpu.get_barrier_semaphore()
    for device in neighbours:
        pl.semaphore_signal(barrier, inc=1, device_id=device, device_id_type=MESH)
    pl.semaphore_wait(barrier, 3)


def gather_kernel(own_ref, all_ref, local_sem, send_sem, recv_sem):
    x, core, row = plane_place()
    over_x, over_row, over_core = plane_neighbours(x, core, row)
    rows = own_ref.shape[0]
    half = rows // 2

    def place(far_x, far_row, part):
        bx = x + far_x - 2 * far_x * x
        by = row + far_row - 2 * far_row * row
        return pl.ds(pl.multiple_of(((bx * 2 + core) * 2 + by) * rows + part * half, half), half)

    enter_plane((over_x, over_row, over_core))
    copies = {}

    def send(slot, source, target, device):
        copies[slot] = pltpu.make_async_remote_copy(
            src_ref=source, dst_ref=all_ref.at[target], send_sem=send_sem.at[slot], recv_sem=recv_sem.at[slot],
            device_id=device, device_id_type=MESH,
        )
        copies[slot].start()

    mine = [own_ref.at[pl.ds(part * half, half)] for part in range(2)]
    own = [place(0, 0, part) for part in range(2)]
    send(0, mine[0], own[0], over_row)
    send(3, mine[1], own[1], over_x)
    send(1, mine[1], own[1], over_row)
    send(4, mine[0], own[0], over_x)
    send(6, mine[0], own[0], over_core)
    send(7, mine[1], own[1], over_core)
    local = [pltpu.make_async_copy(mine[part], all_ref.at[own[part]], local_sem.at[part]) for part in range(2)]
    for copy in local:
        copy.start()

    def forward(got, target, hops):
        copies[got].wait_recv()
        for slot, device in hops:
            send(slot, all_ref.at[target], target, device)

    forward(0, place(0, 1, 0), ((5, over_x), (8, over_core)))
    forward(3, place(1, 0, 1), ((2, over_row), (9, over_core)))
    forward(1, place(0, 1, 1), ((10, over_core),))
    forward(4, place(1, 0, 0), ((11, over_core),))
    forward(5, place(1, 1, 0), ((12, over_core),))
    forward(2, place(1, 1, 1), ((13, over_core),))
    for slot in range(6, 14):
        copies[slot].wait_recv()
    for slot in range(14):
        copies[slot].wait_send()
    for copy in local:
        copy.wait()


def plane_gather(rows):
    count, width = rows.shape
    return pl.pallas_call(
        gather_kernel,
        in_specs=[pl.BlockSpec(memory_space=pl.ANY)],
        out_specs=pl.BlockSpec(memory_space=pl.ANY),
        out_shape=jax.ShapeDtypeStruct((8 * count, width), rows.dtype),
        scratch_shapes=[
            pltpu.SemaphoreType.DMA((2,)),
            pltpu.SemaphoreType.DMA((14,)),
            pltpu.SemaphoreType.DMA((14,)),
        ],
        compiler_params=pltpu.CompilerParams(collective_id=0, has_side_effects=True),
        cost_estimate=small_cost(),
        name="plane_gather",
    )(rows)


PIECES = ((1, 1, 0), (1, 1, 1), (1, 0, 0), (0, 1, 1), (0, 1, 0), (1, 0, 1), (0, 0, 0), (0, 0, 1))
COLS = 512


def scatter_kernel(rows, parts, *refs):
    a_refs, (w_ref, out_ref, core_out, core_in, sums, first_in, next_out, next_in, sems) = refs[:parts], refs[parts:]
    x, core, row = plane_place()
    over_x, over_row, over_core = plane_neighbours(x, core, row)
    half = rows // 2
    width = out_ref.shape[1]
    chunks = width // COLS

    def place(piece, on_core):
        far_x, far_row, part = PIECES[piece]
        bx = x + far_x - 2 * far_x * x
        by = row + far_row - 2 * far_row * row
        return pl.ds(pl.multiple_of(((bx * 2 + on_core) * 2 + by) * rows + part * half, half), half)

    enter_plane((over_x, over_row, over_core))

    def columns(j):
        return pl.ds(pl.multiple_of(j * COLS, COLS), COLS)

    def partial(piece, on_core, j):
        taken, total = place(piece, on_core), None
        for p, a_ref in enumerate(a_refs):
            depth = a_ref.shape[1]
            term = dot_t(a_ref[taken, :], w_ref[columns(j), p * depth : (p + 1) * depth])
            total = term if p == 0 else total + term
        return total

    def remote(source, target, slot, device):
        return pltpu.make_async_remote_copy(
            src_ref=source, dst_ref=target, send_sem=sems.at[0, slot], recv_sem=sems.at[1, slot],
            device_id=device, device_id_type=MESH,
        )

    core_copies, first_copies, next_copies = [], [], []

    def for_partner(piece):
        @pl.loop(0, chunks)
        def _(j):
            core_out[piece, :, columns(j)] = partial(piece, 1 - core, j).astype(BF16)

        copy = remote(core_out.at[piece], core_in.at[piece], piece, over_core)
        copy.start()
        core_copies.append(copy)

    def for_self(piece):
        core_copies[piece].wait_recv()

        @pl.loop(0, chunks)
        def _(j):
            total = partial(piece, core, j) + core_in[piece, :, columns(j)].astype(F32)
            sums[piece, :, columns(j)] = total.astype(BF16)

        if piece < 4:
            copy = remote(sums.at[piece], first_in.at[piece], 8 + piece, over_x if piece % 2 == 0 else over_row)
            copy.start()
            first_copies.append(copy)

    for_partner(0)
    for piece in range(8):
        if piece < 7:
            for_partner(piece + 1)
        for_self(piece)
    for part in range(2):
        first_copies[part].wait_recv()

        @pl.loop(0, chunks)
        def _(j):
            total = sums[4 + part, :, columns(j)].astype(F32) + first_in[part, :, columns(j)].astype(F32)
            next_out[part, :, columns(j)] = total.astype(BF16)

        copy = remote(next_out.at[part], next_in.at[part], 12 + part, over_row if part == 0 else over_x)
        copy.start()
        next_copies.append(copy)
    for part in range(2):
        first_copies[2 + part].wait_recv()
        next_copies[part].wait_recv()

        @pl.loop(0, chunks)
        def _(j):
            total = sums[6 + part, :, columns(j)].astype(F32) + first_in[2 + part, :, columns(j)].astype(F32)
            out_ref[pl.ds(part * half, half), columns(j)] = total + next_in[part, :, columns(j)].astype(F32)

    for copy in core_copies + first_copies + next_copies:
        copy.wait_send()


def plane_scatter(parts, w, collective_id):
    count = parts[0].shape[0]
    width = w.shape[0]
    rows = count // 8
    half = rows // 2
    return pl.pallas_call(
        functools.partial(scatter_kernel, rows, len(parts)),
        in_specs=[pl.BlockSpec(memory_space=pltpu.VMEM)] * (len(parts) + 1),
        out_specs=pl.BlockSpec(memory_space=pltpu.VMEM),
        out_shape=jax.ShapeDtypeStruct((rows, width), F32),
        scratch_shapes=[
            pltpu.VMEM((8, half, width), BF16),
            pltpu.VMEM((8, half, width), BF16),
            pltpu.VMEM((8, half, width), BF16),
            pltpu.VMEM((4, half, width), BF16),
            pltpu.VMEM((2, half, width), BF16),
            pltpu.VMEM((2, half, width), BF16),
            pltpu.SemaphoreType.DMA((2, 14)),
        ],
        compiler_params=pltpu.CompilerParams(
            collective_id=collective_id, has_side_effects=True, vmem_limit_bytes=60 << 20
        ),
        cost_estimate=small_cost(),
        name="plane_scatter",
    )(*parts, w)


def is_plane():
    return lax.axis_size("ctx") == 4 and lax.axis_size("tensor") == 2


def gather_rows(rows):
    return lax.all_gather(rows, GROUP, axis=0, tiled=True)


def scatter_rows(rows):
    return lax.psum_scatter(rows.astype(BF16), GROUP, scatter_dimension=0, tiled=True).astype(F32)


def gather_now(rows):
    return plane_gather(rows) if is_plane() else gather_rows(rows)


def product_scatter(parts, w, collective_id):
    if is_plane():
        return plane_scatter(parts, w, collective_id)
    return scatter_rows(dot_t(jnp.concatenate(parts, axis=1), w))


def gather_weight(own):
    return lax.all_gather(own, "fsdp", axis=0, tiled=True)


def scatter_weight(grad):
    return lax.psum_scatter(grad.astype(BF16), "fsdp", scatter_dimension=0, tiled=True)


def swap_columns(part, count):
    size = lax.axis_size("ctx")
    rows, columns = part.shape[0] // size, part.shape[1] // count
    got = lax.all_to_all(part.reshape(size, rows, count * columns), "ctx", split_axis=0, concat_axis=0)
    return [
        jnp.concatenate([got[j, :, c * columns : (c + 1) * columns] for j in range(size)], axis=1).astype(F32)
        for c in range(count)
    ]


def normalize(rows):
    norm_inv = lax.rsqrt(jnp.mean(rows * rows, axis=1, keepdims=True) + EPSILON)
    return (rows * norm_inv, norm_inv)


def norm_backward(grad_rows, scaled, norm_inv, gain):
    weighted = grad_rows * gain[None, :]
    inner = jnp.mean(weighted * scaled, axis=1, keepdims=True)
    return norm_inv * (weighted - scaled * inner)


def body(
    tokens_in,
    attn_gain,
    query_weight,
    key_weight,
    value_weight,
    output_weight,
    mlp_gain,
    gate_weight,
    up_weight,
    down_weight,
    seg_lengths,
    leaf_parent,
    cotangent,
):
    ctx = lax.axis_index("ctx")
    parts = lax.axis_size("ctx")
    tree_len = tokens_in.shape[0] * parts * lax.axis_size("tensor")
    width = query_weight.shape[1] // parts
    units = gate_weight.shape[1] // parts

    def mine(weight, columns):
        return lax.dynamic_slice_in_dim(weight, ctx * columns, columns, 1)

    x_rows = tokens_in.astype(F32)
    attn_scaled, attn_inv = normalize(x_rows)
    w_attn = gather_weight(
        jnp.concatenate([mine(w, width) for w in (query_weight, key_weight, value_weight, output_weight)], axis=1)
    )
    w_gate = gather_weight(mine(gate_weight, units))
    w_up = gather_weight(mine(up_weight, units))
    cot_all = gather_rows(cotangent)
    w_down = gather_weight(mine(down_weight, units))
    attn_in = gather_now((attn_scaled * attn_gain[None, :]).astype(BF16))
    w_qkv, w_out = w_attn[:, : 3 * width], w_attn[:, 3 * width :]

    segment, parent, depth = tree_tables(seg_lengths[0], leaf_parent[0], tree_len)
    cosine, sine = rope_tables(depth, min(2 * HEAD_DIM, width))
    seg_keys = segment[None, :]
    seg_queries = jnp.stack([segment, parent], axis=1)

    qkv = jnp.dot(attn_in, w_qkv, preferred_element_type=F32)
    attn_out, lse, query_rows, key_rows, value_rows = attention_forward(
        qkv, cosine, sine, seg_keys, seg_queries, width
    )
    mid_rows = x_rows + product_scatter([attn_out], w_out, 1)
    mlp_scaled, mlp_inv = normalize(mid_rows)
    mlp_in = gather_now((mlp_scaled * mlp_gain[None, :]).astype(BF16))

    gate = jnp.dot(mlp_in, w_gate, preferred_element_type=F32)
    up_proj = jnp.dot(mlp_in, w_up, preferred_element_type=F32)
    sigmoid_gate = jax.nn.sigmoid(gate)
    hidden = (gate * sigmoid_gate * up_proj).astype(BF16)
    down_rows, cot_all = lax.optimization_barrier((dot_t(hidden, w_down).astype(BF16), cot_all))
    down_rows = scatter_rows(down_rows)
    hidden_grad = jnp.dot(cot_all, w_down, preferred_element_type=F32)
    gate_rows_grad = (
        hidden_grad * up_proj * sigmoid_gate * (1.0 + gate * (1.0 - sigmoid_gate))
    ).astype(BF16)
    up_rows_grad = (hidden_grad * gate * sigmoid_gate).astype(BF16)

    mlp_in_grad = scatter_rows(dot_t(gate_rows_grad, w_gate) + dot_t(up_rows_grad, w_up))
    gate_part = dot_tn(mlp_in, gate_rows_grad).astype(BF16)
    up_part = dot_tn(mlp_in, up_rows_grad).astype(BF16)
    down_part = dot_tn(cot_all, hidden).astype(BF16)
    mlp_in_grad, gate_part, up_part, down_part, down_rows = lax.optimization_barrier(
        (mlp_in_grad, gate_part, up_part, down_part, down_rows)
    )
    block_out = (mid_rows + down_rows).astype(BF16)
    mlp_back = norm_backward(mlp_in_grad, mlp_scaled, mlp_inv, mlp_gain)
    mlp_gain_part = jnp.sum(mlp_in_grad * mlp_scaled, axis=0)
    mid_grad = cotangent.astype(F32) + mlp_back
    mid_all = gather_now(mid_grad.astype(BF16))

    gate_grad = scatter_weight(gate_part)
    up_grad = scatter_weight(up_part)
    down_grad = scatter_weight(down_part)

    out_heads_grad = jnp.dot(mid_all, w_out, preferred_element_type=F32).astype(BF16)
    output_grad = dot_tn(mid_all, attn_out)
    pre_grads = attention_backward(
        query_rows, key_rows, value_rows, attn_out, out_heads_grad, lse, cosine, sine, seg_keys, seg_queries
    )
    pre_grads, gate_grad, up_grad, down_grad = lax.optimization_barrier((pre_grads, gate_grad, up_grad, down_grad))
    qkv_grad = jnp.concatenate([dot_tn(attn_in, grad) for grad in pre_grads], axis=1)
    attn_gain_part = jnp.sum(qkv_grad * w_qkv.astype(F32), axis=1) / attn_gain
    attn_part = jnp.concatenate([qkv_grad, output_grad], axis=1).astype(BF16)
    pre_grads, attn_part = lax.optimization_barrier((pre_grads, attn_part))
    attn_in_grad = product_scatter(pre_grads, w_qkv, 2)
    gain_grads = lax.psum_scatter(
        jnp.stack([attn_gain_part, mlp_gain_part]), ("fsdp", "ctx", "tensor"), scatter_dimension=1, tiled=True
    )
    attn_grad = scatter_weight(attn_part)
    (gate_out,) = swap_columns(gate_grad, 1)
    (up_out,) = swap_columns(up_grad, 1)
    (down_out,) = swap_columns(down_grad, 1)
    query_out, key_out, value_out, output_out = swap_columns(attn_grad, 4)

    attn_back = norm_backward(attn_in_grad, attn_scaled, attn_inv, attn_gain)
    input_grad = (mid_grad + attn_back).astype(BF16)
    return (
        block_out,
        input_grad,
        gain_grads[0],
        query_out,
        key_out,
        value_out,
        output_out,
        gain_grads[1],
        gate_out,
        up_out,
        down_out,
    )


def solution(mesh):
    rows = P(("fsdp", "ctx", "tensor"), None)
    weight = P("fsdp", "tensor")
    gain = P(("fsdp", "ctx", "tensor"))
    grad = P(("fsdp", "ctx"), "tensor")
    in_specs = (
        rows, P(), weight, weight, weight, weight, P(), weight, weight, weight, P("fsdp", None), P("fsdp", None), rows,
    )
    out_specs = (rows, rows, gain, grad, grad, grad, grad, gain, grad, grad, grad)
    return jax.shard_map(body, mesh=mesh, in_specs=in_specs, out_specs=out_specs, check_vma=False)
```

time: 1660 us -> 1330 us (0.80)
  waiting for transfers between devices: 653 us -> 250 us
  Pallas kernels: 328 us -> 636 us
  starting transfers between devices: 153 us -> 15.8 us
  other arithmetic: 118 us -> 63.8 us
  local copies, waits for them, and re-layouts: 69.5 us -> 38.1 us
  matrix products: 322 us -> 303 us
    pallas_call x0 -> x5, Pallas kernels: none -> 432 us  [the longest x3 249 us: plane_gather(): pl.pallas_call(gather_kernel, in_specs=[pl.BlockSpec(memory_space=pl.ANY)...]
    ppermute x48 -> x0, waiting for transfers between devices: 325 us -> none  [the longest x12 174 us: line_gather(): from_above.append(lax.ppermute(from_above[-1], 'fsdp', downs))]
    ppermute x48 -> x0, starting transfers between devices: 136 us -> none  [the longest x12 52.9 us: line_gather(): from_below.append(lax.ppermute(from_below[-1], 'fsdp', ups))]
    all_gather x4 -> x1, waiting for transfers between devices: 89.8 us -> 0.01 us  [gather_rows(): return lax.all_gather(rows, GROUP, axis=0, tiled=True)]
    pallas_call x1, Pallas kernels: 157 us -> 79.9 us  [attention_forward(): pl.pallas_call(functools.partial(fwd_kernel, heads), grid=(groups, tree_l...]
    reduce_scatter x4 -> x2, waiting for transfers between devices: 233 us -> 158 us  [scatter_rows(): lax.psum_scatter(rows.astype(BF16), GROUP, scatter_dimension=0, tiled=True)]
    reduce_scatter x0 -> x4, waiting for transfers between devices: none -> 70 us  [scatter_weight(): lax.psum_scatter(grad.astype(BF16), 'fsdp', scatter_dimension=0, tiled=True)]
    pallas_call x1, Pallas kernels: 171 us -> 124 us  [attention_backward(): pl.pallas_call(functools.partial(bwd_kernel, heads), grid=(groups, tree_l...]
  transfers between devices with their start and end apart: 61 -> 16, of which waited for: 32 -> 6; matrix products, arithmetic and copies ran while one was open for 18% -> 20% of each run, Pallas kernels for 0% -> 48%
where the time goes in v2:
time: 1330 us; the launch traced here: 1320 us
  Pallas kernels  636 us (48%)
  matrix products  303 us (23%)
  waiting for transfers between devices  250 us (19%)
  other arithmetic  63.8 us (5%)
  local copies, waits for them, and re-layouts  38.1 us (3%)
  starting transfers between devices  15.8 us (1%)
  between operations  14.9 us (1%)
    pallas_call x3, Pallas kernels, plane_gather(): pl.pallas_call(gather_kernel, in_specs=[pl.BlockSpec(memory_space=pl.ANY)...  249 us
    pallas_call x2, Pallas kernels, plane_scatter(): pl.pallas_call(functools.partial(scatter_kernel, rows, len(parts)), in_sp...  183 us
    reduce_scatter x2, waiting for transfers between devices, scatter_rows(): lax.psum_scatter(rows.astype(BF16), GROUP, scatter_dimension=0, tiled=True)  158 us
    pallas_call x1, Pallas kernels, attention_backward(): pl.pallas_call(functools.partial(bwd_kernel, heads), grid=(groups, tree_l...  124 us
    dot_general x7, matrix products, dot_tn(): lax.dot_general(a, b, (((0,), (0,)), ((), ())), preferred_element_type=F32)  108 us
    pallas_call x1, Pallas kernels, attention_forward(): pl.pallas_call(functools.partial(fwd_kernel, heads), grid=(groups, tree_l...  79.9 us
    dot_general x3, matrix products, dot_t(): lax.dot_general(a, b, (((1,), (1,)), ((), ())), preferred_element_type=F32)  76.2 us
    reduce_scatter x4, waiting for transfers between devices, scatter_weight(): lax.psum_scatter(grad.astype(BF16), 'fsdp', scatter_dimension=0, tiled=True)  70 us
  transfers between devices with their start and end apart: 16, of which 6 were waited for; matrix products, arithmetic and copies ran while one was open for 20% of the time, Pallas kernels for 48%

profile of v2, /device:TPU:0, one launch (start us, length us, event | category | flops | bytes accessed | tf_op | source)
XLA Modules:
  0.0 1322.2 jit_solution(17411635166981219930)
XLA Ops:
  25.0 77.0 %plane_gather.3 = bf16[4096,2048]{1,0:T(8,128)(2,1)} custom-call(bf16[512,2048]{1,0:T(8,128)(2,1)} %fusion.4.own_ref), custom_call_target="tpu_custom_call" | custom-call | flops 1048576 | bytes 1048576 | tf_op jit(solution)/shard_map/plane_gather/pallas_call | solution.py:445
  102.7 9.3 fusion.11
  114.3 19.3 %fusion.23.q_ref.k_ref.v_ref = f32[4096,768]{1,0:T(8,128)} fusion(bf16[4096,2048]{1,0:T(8,128)(2,1)} %plane_gather.3, bf16[2048,1024]{1,0:T(8,128)(2,1)} %all-gather.6.cloned.1.call-done), kind=kOutput, calls=%fused_computation.120 | convolution fusion | flops 12884901888 | bytes 32505856 | tf_op jit(solution)/shard_map/dot_general | solution.py:670
  133.6 79.9 %tree_attention_forward.1 = (bf16[4096,256]{1,0:T(8,128)(2,1)}, f32[2,2,4096]{2,1,0:T(2,128)}, bf16[4096,256]{1,0:T(8,128)(2,1)}, bf16[4096,256]{1,0:T(8,128)(2,1)}, bf16[4096,256]{1,0:T(8,128)(2,1)}) custom-call(f32[4096,768]{1,0:T(8,128)} %fusion.23.q_ref.k_ref.v_ref, f32[4096,768]{1,0:T(8,128)} %fusion.23.q_ref.k_ref.v_ref, ...), custom_call_target="tpu_custom_call" | custom-call | flops 1048576 | bytes 1048576 | tf_op jit(solution)/shard_map/tree_attention_forward/pallas_call | solution.py:310
  213.6 82.0 %plane_scatter.2 = f32[512,2048]{1,0:T(8,128)} custom-call(bf16[4096,256]{1,0:T(8,128)(2,1)} %get-tuple-element.36.refs_0_.o_ref, bf16[2048,256]{1,0:T(8,128)(2,1)} %slice.134.refs_1_), custom_call_target="tpu_custom_call" | custom-call | flops 1048576 | bytes 1048576 | tf_op jit(solution)/shard_map/plane_scatter/pallas_call | solution.py:556
  302.1 97.2 %plane_gather.4 = bf16[4096,2048]{1,0:T(8,128)(2,1)} custom-call(bf16[512,2048]{1,0:T(8,128)(2,1)} %multiply_convert_fusion.3.own_ref), custom_call_target="tpu_custom_call" | custom-call | flops 1048576 | bytes 1048576 | tf_op jit(solution)/shard_map/plane_gather/pallas_call | solution.py:445
  399.3 25.7 %fusion.30 = f32[4096,1024]{1,0:T(8,128)} fusion(bf16[4096,2048]{1,0:T(8,128)(2,1)} %plane_gather.4, bf16[2048,1024]{1,0:T(8,128)(2,1)} %all-gather.8.cloned.1.call-done), kind=kOutput, calls=%fused_computation.127 | convolution fusion | flops 17179869184 | bytes 37748736 | tf_op jit(solution)/shard_map/dot_general | solution.py:678
  425.0 29.3 %multiply_convert_fusion.2 = (bf16[4096,1024]{1,0:T(8,128)(2,1)}, f32[4096,1024]{1,0:T(8,128)}) fusion(f32[4096,1024]{1,0:T(8,128)} %fusion.30, bf16[4096,2048]{1,0:T(8,128)(2,1)} %plane_gather.4, bf16[2048,1024]{1,0:T(8,128)(2,1)} %all-gather.10.cloned.1.call-done), kind=kOutput, calls=%fused_computation.3 | convolution fusion | flops 17205035008 | bytes 62914560 | tf_op jit(solution)/shard_map/dot_general | solution.py:679
  454.3 23.8 %convolution_convert_fusion = bf16[4096,2048]{1,0:T(8,128)(2,1)} fusion(bf16[4096,1024]{1,0:T(8,128)(2,1)} %get-tuple-element.106, bf16[2048,1024]{1,0:T(8,128)(2,1)} %all-gather.12.cloned.1.call-done), kind=kOutput, calls=%fused_computation.5 | convolution fusion | flops 17188257792 | bytes 29360128 | tf_op jit(solution)/shard_map/dot_general | solution.py:77
  478.1 32.8 %multiply_convert_fusion = (bf16[4096,1024]{1,0:T(8,128)(2,1)}, bf16[4096,1024]{1,0:T(8,128)(2,1)}) fusion(f32[4096,1024]{1,0:T(8,128)} %fusion.30, f32[4096,1024]{1,0:T(8,128)} %get-tuple-element.107, bf16[4096,2048]{1,0:T(8,128)(2,1)} %all-gather.14.cloned.1.call-done, bf16[2048,1024]{1,0:T(8,128)(2,1)} %all-gather.12.cloned.1.call-done), kind=kOutput, calls=%fused_computation.1 | convolution fusion | flops 17234395136 | bytes 71303168 | tf_op jit(solution)/shard_map/dot_general | solution.py:684
  510.9 25.8 %fusion.31 = f32[4096,2048]{1,0:T(8,128)} fusion(bf16[4096,1024]{1,0:T(8,128)(2,1)} %get-tuple-element.69, bf16[2048,1024]{1,0:T(8,128)(2,1)} %all-gather.8.cloned.1.call-done), kind=kOutput, calls=%fused_computation.128 | convolution fusion | flops 17179869184 | bytes 46137344 | tf_op jit(solution)/shard_map/dot_general | solution.py:77
  536.7 26.5 %add_convert_fusion = bf16[4096,2048]{1,0:T(8,128)(2,1)} fusion(f32[4096,2048]{1,0:T(8,128)} %fusion.31, bf16[4096,1024]{1,0:T(8,128)(2,1)} %get-tuple-element.68, bf16[2048,1024]{1,0:T(8,128)(2,1)S(1)} %copy-done.22), kind=kOutput, calls=%fused_computation | convolution fusion | flops 17196646400 | bytes 62914560 | tf_op jit(solution)/shard_map/dot_general | solution.py:77
  564.1 24.2 %convolution_convert_fusion.2 = bf16[2048,1024]{1,0:T(8,128)(2,1)} fusion(bf16[4096,2048]{1,0:T(8,128)(2,1)} %all-gather.14.cloned.1.call-done, bf16[4096,1024]{1,0:T(8,128)(2,1)} %get-tuple-element.106), kind=kOutput, calls=%fused_computation.29 | convolution fusion | flops 17181966336 | bytes 29360128 | tf_op jit(solution)/shard_map/dot_general | solution.py:85
  588.3 24.3 %convolution_convert_fusion.3 = bf16[2048,1024]{1,0:T(8,128)(2,1)} fusion(bf16[4096,2048]{1,0:T(8,128)(2,1)} %plane_gather.4, bf16[4096,1024]{1,0:T(8,128)(2,1)} %get-tuple-element.68), kind=kOutput, calls=%fused_computation.30 | convolution fusion | flops 17181966336 | bytes 29360128 | tf_op jit(solution)/shard_map/dot_general | solution.py:85
  612.7 24.1 %convolution_convert_fusion.4 = bf16[2048,1024]{1,0:T(8,128)(2,1)} fusion(bf16[4096,2048]{1,0:T(8,128)(2,1)} %plane_gather.4, bf16[4096,1024]{1,0:T(8,128)(2,1)} %get-tuple-element.69), kind=kOutput, calls=%fused_computation.31 | convolution fusion | flops 17181966336 | bytes 29360128 | tf_op jit(solution)/shard_map/dot_general | solution.py:85
  636.8 42.4 %reduce-scatter.10.cloned.1.call-done = bf16[512,2048]{1,0:T(8,128)(2,1)} async-done(((bf16[4096,2048]{1,0:T(8,128)(2,1)}), bf16[512,2048]{1,0:T(8,128)(2,1)}) %reduce-scatter.10.cloned.1.call-update) | async-done | bytes 2097168 | tf_op jit(solution)/shard_map/reduce_scatter | solution.py:587
  683.3 115.4 %reduce-scatter.12.cloned.1.call-done = bf16[512,2048]{1,0:T(8,128)(2,1)} async-done(((bf16[4096,2048]{1,0:T(8,128)(2,1)}), bf16[512,2048]{1,0:T(8,128)(2,1)}) %reduce-scatter.12.cloned.1.call-update) | async-done | bytes 2097168 | tf_op jit(solution)/shard_map/reduce_scatter | solution.py:587
  798.8 4.1 convert_element_type.136
  806.8 5.4 multiply_reduce_fusion
  816.0 74.9 %plane_gather.5 = bf16[4096,2048]{1,0:T(8,128)(2,1)} custom-call(bf16[512,2048]{1,0:T(8,128)(2,1)} %fusion.25.own_ref), custom_call_target="tpu_custom_call" | custom-call | flops 1048576 | bytes 1048576 | tf_op jit(solution)/shard_map/plane_gather/pallas_call | solution.py:445
  890.9 11.9 convolution_convert_fusion.1.do_ref
  902.8 124.2 %tree_attention_backward.1 = (bf16[4096,256]{1,0:T(8,128)(2,1)}, bf16[4096,256]{1,0:T(8,128)(2,1)}, bf16[4096,256]{1,0:T(8,128)(2,1)}) custom-call(bf16[4096,256]{1,0:T(8,128)(2,1)} %get-tuple-element.41.q_ref, bf16[4096,256]{1,0:T(8,128)(2,1)} %get-tuple-element.42.k_ref, bf16[4096,256]{1,0:T(8,128)(2,1)} %get-tuple-element.43.v_ref, ...), custom_call_target="tpu_custom_call" | custom-call | flops 1048576 | bytes 1048576 | tf_op jit(solution)/shard_map/tree_attention_backward/pallas_call | solution.py:345
  1026.9 8.6 convolution_convert_fusion.5
  1039.0 10.1 fusion.29
  1049.2 10.2 fusion.28
  1059.4 6.2 fusion.27
  1089.3 101.2 %plane_scatter.3 = f32[512,2048]{1,0:T(8,128)} custom-call(bf16[4096,256]{1,0:T(8,128)(2,1)} %get-tuple-element.54.refs_0_, bf16[4096,256]{1,0:T(8,128)(2,1)} %get-tuple-element.55.refs_1_, bf16[4096,256]{1,0:T(8,128)(2,1)} %get-tuple-element.56.refs_2_, bf16[2048,768]{1,0:T(8,128)(2,1)} %slice.133.refs_3_), custom_call_target="tpu_custom_call" | custom-call | flops 1048576 | bytes 1048576 | tf_op jit(solution)/shard_map/plane_scatter/pallas_call | solution.py:556
  1193.6 4.3 all-to-all-start.2
  1197.9 9.8 fusion.9
  1207.7 8.6 reduce-scatter.22.cloned.1.call-done
  1224.8 66.6 %reduce-scatter.20.cloned.1.call-done = bf16[512,1024]{0,1:T(8,128)(2,1)} async-done(((bf16[2048,1024]{0,1:T(8,128)(2,1)}), bf16[512,1024]{0,1:T(8,128)(2,1)}) %reduce-scatter.20.cloned.1.call-update) | async-done | bytes 1048592 | tf_op jit(solution)/shard_map/reduce_scatter | solution.py:605
  1300.4 11.3 all-to-all-done
  (157 shorter events, 90.7 us)
Async XLA Ops:
  7.2 104.9 %all-gather.6.cloned.1.call-start = ((), (), s32[]{:S(2)}) async-start(), calls=%async_computation.11 | async-start | bytes 5242880 | tf_op jit(solution)/shard_map/all_gather | solution.py:601
  10.5 388.7 %all-gather.8.cloned.1.call-start = ((), (), s32[]{:S(2)}) async-start(), calls=%async_computation.12 | async-start | bytes 5242880 | tf_op jit(solution)/shard_map/all_gather | solution.py:601
  12.9 5.7 copy-start.21
  12.9 412.1 %all-gather.10.cloned.1.call-start = ((), (), s32[]{:S(2)}) async-start(), calls=%async_computation.13 | async-start | bytes 5242880 | tf_op jit(solution)/shard_map/all_gather | solution.py:601
  15.3 7.4 copy-start.3
  15.3 438.9 %all-gather.12.cloned.1.call-start = ((), (), s32[]{:S(2)}) async-start(), calls=%async_computation.14 | async-start | bytes 5242880 | tf_op jit(solution)/shard_map/all_gather | solution.py:601
  17.8 460.3 %all-gather.14.cloned.1.call-start = ((), (), s32[]{:S(2)}) async-start(), calls=%async_computation.15 | async-start | bytes 18874368 | tf_op jit(solution)/shard_map/all_gather | solution.py:583
  18.4 660.8 %reduce-scatter.10.cloned.1.call-start = ((), (), s32[]{:S(2)}) async-start(), calls=%async_computation.16 | async-start | bytes 18874368 | tf_op jit(solution)/shard_map/reduce_scatter | solution.py:587
  23.2 78.9 %copy-start.18 = (f32[512]{0:T(512)}, f32[512]{0:T(512)S(1)}, u32[]{:S(2)}) copy-start(f32[512]{0:T(512)S(1)} %add_rsqrt_fusion.1) | copy-start | bytes 6148
  510.9 25.8 %copy-start.22 = (bf16[2048,1024]{1,0:T(8,128)(2,1)S(1)}, bf16[2048,1024]{1,0:T(8,128)(2,1)}, u32[]{:S(2)}) copy-start(bf16[2048,1024]{1,0:T(8,128)(2,1)} %all-gather.10.cloned.1.call-done) | copy-start | bytes 12582916
  563.3 235.5 %reduce-scatter.12.cloned.1.call-start = ((), (), s32[]{:S(2)}) async-start(), calls=%async_computation.17 | async-start | bytes 18874368 | tf_op jit(solution)/shard_map/reduce_scatter | solution.py:587
  564.0 471.5 %reduce-scatter.14.cloned.1.call-start = ((), (), s32[]{:S(2)}) async-start(), calls=%async_computation.18 | async-start | bytes 5242880 | tf_op jit(solution)/shard_map/reduce_scatter | solution.py:605
  803.0 232.6 %reduce-scatter.16.cloned.1.call-start = ((), (), s32[]{:S(2)}) async-start(), calls=%async_computation.19 | async-start | bytes 5242880 | tf_op jit(solution)/shard_map/reduce_scatter | solution.py:605
  803.7 235.3 %reduce-scatter.18.cloned.1.call-start = ((), (), s32[]{:S(2)}) async-start(), calls=%async_computation.20 | async-start | bytes 5242880 | tf_op jit(solution)/shard_map/reduce_scatter | solution.py:605
  803.8 8.4 copy-start.5
  804.3 412.0 %reduce-scatter.22.cloned.1.call-start = ((), (), s32[]{:S(2)}) async-start(), calls=%async_computation.22 | async-start | bytes 1081344
  806.8 6.7 copy-start.2
  902.8 124.2 %copy-start.6 = (bf16[4096,256]{1,0:T(8,128)(2,1)S(1)}, bf16[4096,256]{1,0:T(8,128)(2,1)}, u32[]{:S(2)}) copy-start(bf16[4096,256]{1,0:T(8,128)(2,1)} %get-tuple-element.36.refs_0_.o_ref) | copy-start | bytes 6291460
  1026.9 12.1 copy-start.7
  1039.0 10.1 copy-start.8
  1039.0 20.3 %slice-start = ((s8[16777216]{0:T(1024)(128)(4,1)}), s8[4194304]{0:T(1024)(128)(4,1)S(1)}, s32[]{:S(2)}) async-start(s8[16777216]{0:T(1024)(128)(4,1)} %bitcast.106), calls=%async_computation.23 | async-start | bytes 8388608
  1039.0 20.3 %slice-start.1 = ((s8[16777216]{0:T(1024)(128)(4,1)}), s8[4194304]{0:T(1024)(128)(4,1)S(1)}, s32[]{:S(2)}) async-start(s8[16777216]{0:T(1024)(128)(4,1)} %bitcast.106), calls=%async_computation.24 | async-start | bytes 8388608
  1049.2 10.2 slice-start.2
  1049.2 10.2 slice-start.3
  1049.2 10.2 copy-start.9
  1078.4 213.0 %reduce-scatter.20.cloned.1.call-start = ((), (), s32[]{:S(2)}) async-start(), calls=%async_computation.21 | async-start | bytes 5242880 | tf_op jit(solution)/shard_map/reduce_scatter | solution.py:605
  1082.1 111.6 %all-to-all-start.3 = ((bf16[4,128,1024]{2,1,0:T(8,128)(2,1)}), bf16[4,128,1024]{2,1,0:T(8,128)(2,1)S(1)}, u32[]{:S(2)}, u32[]{:S(2)}) async-start(bf16[4,128,1024]{2,1,0:T(8,128)(2,1)} %bitcast.39), calls=%async_computation.9 | async-start | bytes 2097152 | tf_op jit(solution)/shard_map/all_to_all | solution.py:611
  1089.3 101.2 %copy-start.4 = (bf16[512,2048]{1,0:T(8,128)(2,1)S(1)}, bf16[512,2048]{1,0:T(8,128)(2,1)}, u32[]{:S(2)}) copy-start(bf16[512,2048]{1,0:T(8,128)(2,1)} %param.13) | copy-start | bytes 6291460
  1089.3 101.2 %copy-start.19 = (f32[512]{0:T(512)S(1)}, f32[512]{0:T(512)}, u32[]{:S(2)}) copy-start(f32[512]{0:T(512)} %copy-done.18) | copy-start | bytes 6148
  1193.6 24.7 %all-to-all-start.2 = ((bf16[4,128,1024]{2,1,0:T(8,128)(2,1)}), bf16[4,128,1024]{2,1,0:T(8,128)(2,1)}, u32[]{:S(2)}, u32[]{:S(2)}) async-start(bf16[4,128,1024]{2,1,0:T(8,128)(2,1)} %bitcast.110), calls=%async_computation.8 | async-start | bytes 2097152 | tf_op jit(solution)/shard_map/all_to_all | solution.py:611
  1218.4 75.3 %all-to-all-start.1 = ((bf16[4,128,1024]{2,1,0:T(8,128)(2,1)}), bf16[4,128,1024]{2,1,0:T(8,128)(2,1)S(1)}, u32[]{:S(2)}, u32[]{:S(2)}) async-start(bf16[4,128,1024]{2,1,0:T(8,128)(2,1)} %bitcast.109), calls=%async_computation.7 | async-start | bytes 2097152 | tf_op jit(solution)/shard_map/all_to_all | solution.py:611
  1293.7 18.0 %all-to-all-start = ((bf16[4,128,1024]{2,1,0:T(8,128)(2,1)}), bf16[4,128,1024]{2,1,0:T(8,128)(2,1)S(1)}, u32[]{:S(2)}, u32[]{:S(2)}) async-start(bf16[4,128,1024]{2,1,0:T(8,128)(2,1)} %bitcast.11), calls=%async_computation.6 | async-start | bytes 2097152 | tf_op jit(solution)/shard_map/all_to_all | solution.py:611
  (11 other events, 37.3 us)
Sparse Core Ops, SparseCore 0:
  10.6 83.5 all-gather.5
  95.8 79.2 all-gather.7
  176.7 79.2 all-gather.9
  257.4 79.2 all-gather.11
  338.5 110.7 all-gather.13
  563.4 115.7 reduce-scatter.9
  682.8 115.9 reduce-scatter.11
  803.1 76.7 reduce-scatter.13
  882.3 77.2 reduce-scatter.15
  961.7 77.2 reduce-scatter.17
  1078.5 137.7 reduce-scatter.21
  1218.4 72.9 reduce-scatter.19

commit v3 on v2

--- a/solution.py
+++ b/solution.py
@@ -463,7 +463,9 @@
 
 
 def scatter_kernel(rows, parts, *refs):
-    a_refs, (w_ref, out_ref, core_out, core_in, sums, first_in, next_out, next_in, sems) = refs[:parts], refs[parts:]
+    a_refs, w_refs = refs[:parts], refs[parts : 2 * parts]
+    (out_ref, core_out, core_in, first_in, next_in, sems), rest = refs[2 * parts : 2 * parts + 6], refs[2 * parts + 6 :]
+    a_bufs, a_sems = rest[:parts], rest[parts]
     x, core, row = plane_place()
     over_x, over_row, over_core = plane_neighbours(x, core, row)
     half = rows // 2
@@ -476,17 +478,31 @@
         by = row + far_row - 2 * far_row * row
         return pl.ds(pl.multiple_of(((bx * 2 + on_core) * 2 + by) * rows + part * half, half), half)
 
-    enter_plane((over_x, over_row, over_core))
-
     def columns(j):
         return pl.ds(pl.multiple_of(j * COLS, COLS), COLS)
 
-    def partial(piece, on_core, j):
-        taken, total = place(piece, on_core), None
-        for p, a_ref in enumerate(a_refs):
-            depth = a_ref.shape[1]
-            term = dot_t(a_ref[taken, :], w_ref[columns(j), p * depth : (p + 1) * depth])
-            total = term if p == 0 else total + term
+    steps = [(0, True)]
+    for piece in range(8):
+        steps += [(piece + 1, True)] * (piece < 7) + [(piece, False)]
+
+    def load(step):
+        piece, partner_half = steps[step]
+        taken = place(piece, 1 - core if partner_half else core)
+        return [
+            pltpu.make_async_copy(a_ref.at[taken], a_buf.at[step % 2], a_sems.at[step % 2, p])
+            for p, (a_ref, a_buf) in enumerate(zip(a_refs, a_bufs))
+        ]
+
+    loads = {0: load(0)}
+    for copy in loads[0]:
+        copy.start()
+    enter_plane((over_x, over_row, over_core))
+
+    def partial(slot, j):
+        total = None
+        for a_buf, w_ref in zip(a_bufs, w_refs):
+            term = dot_t(a_buf[slot], w_ref[columns(j), :])
+            total = term if total is None else total + term
         return total
 
     def remote(source, target, slot, device):
@@ -496,83 +512,83 @@
         )
 
     core_copies, first_copies, next_copies = [], [], []
-
-    def for_partner(piece):
+    for step, (piece, partner_half) in enumerate(steps):
+        for copy in loads[step]:
+            copy.wait()
+        if step + 1 < len(steps):
+            loads[step + 1] = load(step + 1)
+            for copy in loads[step + 1]:
+                copy.start()
+        if partner_half:
+
+            @pl.loop(0, chunks)
+            def _(j, step=step, piece=piece):
+                core_out[piece, :, columns(j)] = partial(step % 2, j).astype(BF16)
+
+            core_copies.append(remote(core_out.at[piece], core_in.at[piece], piece, over_core))
+            core_copies[-1].start()
+            continue
+        core_copies[piece].wait_recv()
+
         @pl.loop(0, chunks)
-        def _(j):
-            core_out[piece, :, columns(j)] = partial(piece, 1 - core, j).astype(BF16)
-
-        copy = remote(core_out.at[piece], core_in.at[piece], piece, over_core)
-        copy.start()
-        core_copies.append(copy)
-
-    def for_self(piece):
-        core_copies[piece].wait_recv()
-
-        @pl.loop(0, chunks)
-        def _(j):
-            total = partial(piece, core, j) + core_in[piece, :, columns(j)].astype(F32)
-            sums[piece, :, columns(j)] = total.astype(BF16)
+        def _(j, step=step, piece=piece):
+            total = partial(step % 2, j) + core_in[piece, :, columns(j)].astype(F32)
+            core_in[piece, :, columns(j)] = total.astype(BF16)
 
         if piece < 4:
-            copy = remote(sums.at[piece], first_in.at[piece], 8 + piece, over_x if piece % 2 == 0 else over_row)
-            copy.start()
-            first_copies.append(copy)
-
-    for_partner(0)
-    for piece in range(8):
-        if piece < 7:
-            for_partner(piece + 1)
-        for_self(piece)
+            first_copies.append(
+                remote(core_in.at[piece], first_in.at[piece], 8 + piece, over_x if piece % 2 == 0 else over_row)
+            )
+            first_copies[-1].start()
     for part in range(2):
         first_copies[part].wait_recv()
 
         @pl.loop(0, chunks)
-        def _(j):
-            total = sums[4 + part, :, columns(j)].astype(F32) + first_in[part, :, columns(j)].astype(F32)
-            next_out[part, :, columns(j)] = total.astype(BF16)
-
-        copy = remote(next_out.at[part], next_in.at[part], 12 + part, over_row if part == 0 else over_x)
-        copy.start()
-        next_copies.append(copy)
+        def _(j, part=part):
+            total = core_in[4 + part, :, columns(j)].astype(F32) + first_in[part, :, columns(j)].astype(F32)
+            core_in[4 + part, :, columns(j)] = total.astype(BF16)
+
+        next_copies.append(remote(core_in.at[4 + part], next_in.at[part], 12 + part, over_row if part == 0 else over_x))
+        next_copies[-1].start()
     for part in range(2):
         first_copies[2 + part].wait_recv()
         next_copies[part].wait_recv()
 
         @pl.loop(0, chunks)
-        def _(j):
-            total = sums[6 + part, :, columns(j)].astype(F32) + first_in[2 + part, :, columns(j)].astype(F32)
+        def _(j, part=part):
+            total = core_in[6 + part, :, columns(j)].astype(F32) + first_in[2 + part, :, columns(j)].astype(F32)
             out_ref[pl.ds(part * half, half), columns(j)] = total + next_in[part, :, columns(j)].astype(F32)
 
     for copy in core_copies + first_copies + next_copies:
         copy.wait_send()
 
 
-def plane_scatter(parts, w, collective_id):
+def plane_scatter(parts, weights, collective_id):
     count = parts[0].shape[0]
-    width = w.shape[0]
+    width = weights[0].shape[0]
     rows = count // 8
     half = rows // 2
+    vmem = pl.BlockSpec(memory_space=pltpu.VMEM)
     return pl.pallas_call(
         functools.partial(scatter_kernel, rows, len(parts)),
-        in_specs=[pl.BlockSpec(memory_space=pltpu.VMEM)] * (len(parts) + 1),
-        out_specs=pl.BlockSpec(memory_space=pltpu.VMEM),
+        in_specs=[pl.BlockSpec(memory_space=pl.ANY)] * len(parts) + [vmem] * len(parts),
+        out_specs=vmem,
         out_shape=jax.ShapeDtypeStruct((rows, width), F32),
         scratch_shapes=[
             pltpu.VMEM((8, half, width), BF16),
             pltpu.VMEM((8, half, width), BF16),
-            pltpu.VMEM((8, half, width), BF16),
             pltpu.VMEM((4, half, width), BF16),
             pltpu.VMEM((2, half, width), BF16),
-            pltpu.VMEM((2, half, width), BF16),
             pltpu.SemaphoreType.DMA((2, 14)),
-        ],
+        ]
+        + [pltpu.VMEM((2, half, a.shape[1]), BF16) for a in parts]
+        + [pltpu.SemaphoreType.DMA((2, len(parts)))],
         compiler_params=pltpu.CompilerParams(
-            collective_id=collective_id, has_side_effects=True, vmem_limit_bytes=60 << 20
+            collective_id=collective_id, has_side_effects=True, vmem_limit_bytes=52 << 20
         ),
         cost_estimate=small_cost(),
         name="plane_scatter",
-    )(*parts, w)
+    )(*parts, *weights)
 
 
 def is_plane():
@@ -591,10 +607,10 @@
     return plane_gather(rows) if is_plane() else gather_rows(rows)
 
 
-def product_scatter(parts, w, collective_id):
+def product_scatter(parts, weights, collective_id):
     if is_plane():
-        return plane_scatter(parts, w, collective_id)
-    return scatter_rows(dot_t(jnp.concatenate(parts, axis=1), w))
+        return plane_scatter(parts, weights, collective_id)
+    return scatter_rows(dot_t(jnp.concatenate(parts, axis=1), jnp.concatenate(weights, axis=1)))
 
 
 def gather_weight(own):
@@ -655,14 +671,15 @@
     w_attn = gather_weight(
         jnp.concatenate([mine(w, width) for w in (query_weight, key_weight, value_weight, output_weight)], axis=1)
     )
+    cot_all = gather_rows(cotangent)
     w_gate = gather_weight(mine(gate_weight, units))
     w_up = gather_weight(mine(up_weight, units))
-    cot_all = gather_rows(cotangent)
     w_down = gather_weight(mine(down_weight, units))
     attn_in = gather_now((attn_scaled * attn_gain[None, :]).astype(BF16))
     w_qkv, w_out = w_attn[:, : 3 * width], w_attn[:, 3 * width :]
 
-    segment, parent, depth = tree_tables(seg_lengths[0], leaf_parent[0], tree_len)
+    attn_in, lengths_row, parent_row = lax.optimization_barrier((attn_in, seg_lengths[0], leaf_parent[0]))
+    segment, parent, depth = tree_tables(lengths_row, parent_row, tree_len)
     cosine, sine = rope_tables(depth, min(2 * HEAD_DIM, width))
     seg_keys = segment[None, :]
     seg_queries = jnp.stack([segment, parent], axis=1)
@@ -671,9 +688,10 @@
     attn_out, lse, query_rows, key_rows, value_rows = attention_forward(
         qkv, cosine, sine, seg_keys, seg_queries, width
     )
-    mid_rows = x_rows + product_scatter([attn_out], w_out, 1)
+    mid_rows = x_rows + product_scatter([attn_out], [w_out], 1)
     mlp_scaled, mlp_inv = normalize(mid_rows)
-    mlp_in = gather_now((mlp_scaled * mlp_gain[None, :]).astype(BF16))
+    mlp_own, cot_all = lax.optimization_barrier(((mlp_scaled * mlp_gain[None, :]).astype(BF16), cot_all))
+    mlp_in = gather_now(mlp_own)
 
     gate = jnp.dot(mlp_in, w_gate, preferred_element_type=F32)
     up_proj = jnp.dot(mlp_in, w_up, preferred_element_type=F32)
@@ -687,19 +705,19 @@
     ).astype(BF16)
     up_rows_grad = (hidden_grad * gate * sigmoid_gate).astype(BF16)
 
-    mlp_in_grad = scatter_rows(dot_t(gate_rows_grad, w_gate) + dot_t(up_rows_grad, w_up))
+    mlp_in_grad = product_scatter([gate_rows_grad, up_rows_grad], [w_gate, w_up], 3)
+    mlp_back = norm_backward(mlp_in_grad, mlp_scaled, mlp_inv, mlp_gain)
+    mlp_gain_part = jnp.sum(mlp_in_grad * mlp_scaled, axis=0)
+    mid_grad = cotangent.astype(F32) + mlp_back
+    mid_low, mlp_in, cot_all, down_rows = lax.optimization_barrier(
+        (mid_grad.astype(BF16), mlp_in, cot_all, down_rows)
+    )
+    block_out = (mid_rows + down_rows).astype(BF16)
+    mid_all = gather_rows(mid_low)
     gate_part = dot_tn(mlp_in, gate_rows_grad).astype(BF16)
     up_part = dot_tn(mlp_in, up_rows_grad).astype(BF16)
     down_part = dot_tn(cot_all, hidden).astype(BF16)
-    mlp_in_grad, gate_part, up_part, down_part, down_rows = lax.optimization_barrier(
-        (mlp_in_grad, gate_part, up_part, down_part, down_rows)
-    )
-    block_out = (mid_rows + down_rows).astype(BF16)
-    mlp_back = norm_backward(mlp_in_grad, mlp_scaled, mlp_inv, mlp_gain)
-    mlp_gain_part = jnp.sum(mlp_in_grad * mlp_scaled, axis=0)
-    mid_grad = cotangent.astype(F32) + mlp_back
-    mid_all = gather_now(mid_grad.astype(BF16))
-
+    mid_all, gate_part, up_part, down_part = lax.optimization_barrier((mid_all, gate_part, up_part, down_part))
     gate_grad = scatter_weight(gate_part)
     up_grad = scatter_weight(up_part)
     down_grad = scatter_weight(down_part)
@@ -709,19 +727,21 @@
     pre_grads = attention_backward(
         query_rows, key_rows, value_rows, attn_out, out_heads_grad, lse, cosine, sine, seg_keys, seg_queries
     )
-    pre_grads, gate_grad, up_grad, down_grad = lax.optimization_barrier((pre_grads, gate_grad, up_grad, down_grad))
+    pre_grads, gate_grad, up_grad = lax.optimization_barrier((pre_grads, gate_grad, up_grad))
     qkv_grad = jnp.concatenate([dot_tn(attn_in, grad) for grad in pre_grads], axis=1)
     attn_gain_part = jnp.sum(qkv_grad * w_qkv.astype(F32), axis=1) / attn_gain
     attn_part = jnp.concatenate([qkv_grad, output_grad], axis=1).astype(BF16)
     pre_grads, attn_part = lax.optimization_barrier((pre_grads, attn_part))
-    attn_in_grad = product_scatter(pre_grads, w_qkv, 2)
+    attn_in_grad = product_scatter(
+        pre_grads, [w_attn[:, j * width : (j + 1) * width] for j in range(3)], 2
+    )
+    devices = lax.axis_size(("fsdp", "ctx", "tensor"))
+    gain_parts = [part.reshape(devices, -1) for part in (attn_gain_part, mlp_gain_part)]
     gain_grads = lax.psum_scatter(
-        jnp.stack([attn_gain_part, mlp_gain_part]), ("fsdp", "ctx", "tensor"), scatter_dimension=1, tiled=True
-    )
+        jnp.concatenate(gain_parts, axis=1), ("fsdp", "ctx", "tensor"), scatter_dimension=0, tiled=True
+    ).reshape(2, -1)
     attn_grad = scatter_weight(attn_part)
-    (gate_out,) = swap_columns(gate_grad, 1)
-    (up_out,) = swap_columns(up_grad, 1)
-    (down_out,) = swap_columns(down_grad, 1)
+    gate_out, up_out, down_out = swap_columns(jnp.concatenate([gate_grad, up_grad, down_grad], axis=1), 3)
     query_out, key_out, value_out, output_out = swap_columns(attn_grad, 4)
 
     attn_back = norm_backward(attn_in_grad, attn_scaled, attn_inv, attn_gain)

time: 1330 us -> 1170 us (0.88)
  waiting for transfers between devices: 250 us -> 94.1 us
  matrix products: 303 us -> 254 us
  blocking collectives: 0 us -> 39.9 us
  Pallas kernels: 636 us -> 667 us
    reduce_scatter x2 -> x1, waiting for transfers between devices: 158 us -> 0.01 us  [scatter_rows(): lax.psum_scatter(rows.astype(BF16), GROUP, scatter_dimension=0, tiled=True)]
    pallas_call x2 -> x3, Pallas kernels: 183 us -> 311 us  [plane_scatter(): pl.pallas_call(functools.partial(scatter_kernel, rows, len(parts)), in_sp...]
    pallas_call x3 -> x2, Pallas kernels: 249 us -> 152 us  [plane_gather(): pl.pallas_call(gather_kernel, in_specs=[pl.BlockSpec(memory_space=pl.ANY)...]
    dot_general x3 -> x1, matrix products: 76.2 us -> 23.8 us  [dot_t(): lax.dot_general(a, b, (((1,), (1,)), ((), ())), preferred_element_type=F32)]
    unnamed x0 -> x1, blocking collectives: none -> 39.9 us
    all_gather x1 -> x2, waiting for transfers between devices: 0.01 us -> 18.5 us  [gather_rows(): return lax.all_gather(rows, GROUP, axis=0, tiled=True)]
  transfers between devices with their start and end apart: 16 -> 13, of which waited for: 6 -> 5; matrix products, arithmetic and copies ran while one was open for 20% -> 26% of each run, Pallas kernels for 48% -> 57%
where the time goes in v3:
time: 1170 us
  Pallas kernels  667 us (57%)
  matrix products  254 us (22%)
  waiting for transfers between devices  94.1 us (8%)
  other arithmetic  56.8 us (5%)
  blocking collectives  39.9 us (3%)
  local copies, waits for them, and re-layouts  31.2 us (3%)
  between operations  14.6 us (1%)
    pallas_call x3, Pallas kernels, plane_scatter(): pl.pallas_call(functools.partial(scatter_kernel, rows, len(parts)), in_sp...  311 us
    pallas_call x2, Pallas kernels, plane_gather(): pl.pallas_call(gather_kernel, in_specs=[pl.BlockSpec(memory_space=pl.ANY)...  152 us
    pallas_call x1, Pallas kernels, attention_backward(): pl.pallas_call(functools.partial(bwd_kernel, heads), grid=(groups, tree_l...  124 us
    dot_general x7, matrix products, dot_tn(): lax.dot_general(a, b, (((0,), (0,)), ((), ())), preferred_element_type=F32)  107 us
    pallas_call x1, Pallas kernels, attention_forward(): pl.pallas_call(functools.partial(fwd_kernel, heads), grid=(groups, tree_l...  79.8 us
    reduce_scatter x4, waiting for transfers between devices, scatter_weight(): lax.psum_scatter(grad.astype(BF16), 'fsdp', scatter_dimension=0, tiled=True)  60 us
    unnamed x1, blocking collectives  39.9 us
    dot_general x1, matrix products, body(): hidden_grad = jnp.dot(cot_all, w_down, preferred_element_type=F32)  38.7 us
  transfers between devices with their start and end apart: 13, of which 5 were waited for; matrix products, arithmetic and copies ran while one was open for 26% of the time, Pallas kernels for 57%

profile of v3, /device:TPU:0, one launch (start us, length us, event | category | flops | bytes accessed | tf_op | source)
XLA Modules:
  0.0 1166.2 jit_solution(506045357909973458)
XLA Ops:
  20.9 77.0 %plane_gather.2 = bf16[4096,2048]{1,0:T(8,128)(2,1)} custom-call(bf16[512,2048]{1,0:T(8,128)(2,1)} %fusion.4.own_ref), custom_call_target="tpu_custom_call" | custom-call | flops 1048576 | bytes 1048576 | tf_op jit(solution)/shard_map/plane_gather/pallas_call | solution.py:445
  102.2 9.4 fusion.13
  111.6 19.2 %fusion.11.q_ref.k_ref.v_ref = f32[4096,768]{1,0:T(8,128)} fusion(bf16[4096,2048]{1,0:T(8,128)(2,1)} %plane_gather.2, bf16[2048,1024]{1,0:T(8,128)(2,1)} %all-gather.7.cloned.1.call-done), kind=kOutput, calls=%fused_computation.34 | convolution fusion | flops 12884901888 | bytes 32505856 | tf_op jit(solution)/shard_map/dot_general | solution.py:687
  130.8 79.8 %tree_attention_forward.1 = (bf16[4096,256]{1,0:T(8,128)(2,1)}, f32[2,2,4096]{2,1,0:T(2,128)}, bf16[4096,256]{1,0:T(8,128)(2,1)}, bf16[4096,256]{1,0:T(8,128)(2,1)}, bf16[4096,256]{1,0:T(8,128)(2,1)}) custom-call(f32[4096,768]{1,0:T(8,128)} %fusion.11.q_ref.k_ref.v_ref, f32[4096,768]{1,0:T(8,128)} %fusion.11.q_ref.k_ref.v_ref, ...), custom_call_target="tpu_custom_call" | custom-call | flops 1048576 | bytes 1048576 | tf_op jit(solution)/shard_map/tree_attention_forward/pallas_call | solution.py:310
  212.2 80.1 %plane_scatter.3 = f32[512,2048]{1,0:T(8,128)} custom-call(bf16[4096,256]{1,0:T(8,128)(2,1)} %get-tuple-element.46.refs_0_.o_ref, bf16[2048,256]{1,0:T(8,128)(2,1)S(1)} %get-tuple-element.89.refs_1_), custom_call_target="tpu_custom_call" | custom-call | flops 1048576 | bytes 1048576 | tf_op jit(solution)/shard_map/plane_scatter/pallas_call | solution.py:572
  298.9 74.6 %plane_gather.3 = bf16[4096,2048]{1,0:T(8,128)(2,1)} custom-call(bf16[512,2048]{1,0:T(8,128)(2,1)} %multiply_convert_fusion.3.own_ref), custom_call_target="tpu_custom_call" | custom-call | flops 1048576 | bytes 1048576 | tf_op jit(solution)/shard_map/plane_gather/pallas_call | solution.py:445
  373.5 23.5 %fusion.30 = f32[4096,1024]{1,0:T(8,128)} fusion(bf16[4096,2048]{1,0:T(8,128)(2,1)} %plane_gather.3, bf16[2048,1024]{1,0:T(8,128)(2,1)} %all-gather.11.cloned.1.call-done.refs_2_), kind=kOutput, calls=%fused_computation.128 | convolution fusion | flops 17179869184 | bytes 37748736 | tf_op jit(solution)/shard_map/dot_general | solution.py:696
  397.0 29.1 %multiply_convert_fusion.2 = (bf16[4096,1024]{1,0:T(8,128)(2,1)}, f32[4096,1024]{1,0:T(8,128)}) fusion(f32[4096,1024]{1,0:T(8,128)} %fusion.30, bf16[4096,2048]{1,0:T(8,128)(2,1)} %plane_gather.3, bf16[2048,1024]{1,0:T(8,128)(2,1)} %all-gather.13.cloned.1.call-done.refs_3_), kind=kOutput, calls=%fused_computation.2 | convolution fusion | flops 17205035008 | bytes 62914560 | tf_op jit(solution)/shard_map/dot_general | solution.py:697
  428.3 23.8 %convolution_convert_fusion = bf16[4096,2048]{1,0:T(8,128)(2,1)} fusion(bf16[4096,1024]{1,0:T(8,128)(2,1)} %get-tuple-element.124, bf16[2048,1024]{1,0:T(8,128)(2,1)} %all-gather.15.cloned.1.call-done), kind=kOutput, calls=%fused_computation.4 | convolution fusion | flops 17188257792 | bytes 29360128 | tf_op jit(solution)/shard_map/dot_general | solution.py:77
  452.2 38.7 %multiply_convert_fusion = (bf16[4096,1024]{1,0:T(8,128)(2,1)}, bf16[4096,1024]{1,0:T(8,128)(2,1)}) fusion(f32[4096,1024]{1,0:T(8,128)} %fusion.30, f32[4096,1024]{1,0:T(8,128)} %get-tuple-element.125, bf16[4096,2048]{1,0:T(8,128)(2,1)} %all-gather.9.cloned.1.call-done, bf16[2048,1024]{1,0:T(8,128)(2,1)} %all-gather.15.cloned.1.call-done), kind=kOutput, calls=%fused_computation | convolution fusion | flops 17234395136 | bytes 71303168 | tf_op jit(solution)/shard_map/dot_general | solution.py:702
  490.9 135.8 %plane_scatter.4 = f32[512,2048]{1,0:T(8,128)} custom-call(bf16[4096,1024]{1,0:T(8,128)(2,1)} %get-tuple-element.83.refs_0_, bf16[4096,1024]{1,0:T(8,128)(2,1)} %get-tuple-element.82.refs_1_, bf16[2048,1024]{1,0:T(8,128)(2,1)} %all-gather.11.cloned.1.call-done.refs_2_, bf16[2048,1024]{1,0:T(8,128)(2,1)} %all-gather.13.cloned.1.call-done.refs_3_), custom_call_target="tpu_custom_call" | custom-call | flops 1048576 | bytes 1048576 | tf_op jit(solution)/shard_map/plane_scatter/pallas_call | solution.py:572
  626.8 3.3 multiply_reduce_fusion
  633.4 4.1 convert_element_type.127
  637.6 23.9 %convolution_convert_fusion.3 = bf16[2048,1024]{1,0:T(8,128)(2,1)} fusion(bf16[4096,2048]{1,0:T(8,128)(2,1)} %plane_gather.3, bf16[4096,1024]{1,0:T(8,128)(2,1)} %get-tuple-element.82.refs_1_), kind=kOutput, calls=%fused_computation.29 | convolution fusion | flops 17181966336 | bytes 29360128 | tf_op jit(solution)/shard_map/dot_general | solution.py:85
  661.6 23.7 %convolution_convert_fusion.4 = bf16[2048,1024]{1,0:T(8,128)(2,1)} fusion(bf16[4096,2048]{1,0:T(8,128)(2,1)} %plane_gather.3, bf16[4096,1024]{1,0:T(8,128)(2,1)} %get-tuple-element.83.refs_0_), kind=kOutput, calls=%fused_computation.30 | convolution fusion | flops 17181966336 | bytes 29360128 | tf_op jit(solution)/shard_map/dot_general | solution.py:85
  685.3 23.8 %convolution_convert_fusion.2 = bf16[2048,1024]{1,0:T(8,128)(2,1)} fusion(bf16[4096,2048]{1,0:T(8,128)(2,1)} %all-gather.9.cloned.1.call-done, bf16[4096,1024]{1,0:T(8,128)(2,1)} %get-tuple-element.124), kind=kOutput, calls=%fused_computation.28 | convolution fusion | flops 17181966336 | bytes 29360128 | tf_op jit(solution)/shard_map/dot_general | solution.py:85
  709.1 18.5 %all-gather.17.cloned.1.call-done = bf16[4096,2048]{1,0:T(8,128)(2,1)} async-done(((bf16[512,2048]{1,0:T(8,128)(2,1)}), bf16[4096,2048]{1,0:T(8,128)(2,1)}) %all-gather.17.cloned.1.call-update) | async-done | bytes 16777232 | tf_op jit(solution)/shard_map/all_gather | solution.py:599
  731.0 12.6 %convolution_convert_fusion.1.do_ref = bf16[4096,256]{1,0:T(8,128)(2,1)} fusion(bf16[4096,2048]{1,0:T(8,128)(2,1)} %all-gather.17.cloned.1.call-done, bf16[2048,1024]{1,0:T(8,128)(2,1)} %all-gather.7.cloned.1.call-done), kind=kOutput, calls=%fused_computation.13 | convolution fusion | flops 4296015872 | bytes 19922944 | tf_op jit(solution)/shard_map/dot_general | solution.py:725
  743.6 124.4 %tree_attention_backward.1 = (bf16[4096,256]{1,0:T(8,128)(2,1)}, bf16[4096,256]{1,0:T(8,128)(2,1)}, bf16[4096,256]{1,0:T(8,128)(2,1)}) custom-call(bf16[4096,256]{1,0:T(8,128)(2,1)} %get-tuple-element.52.q_ref, bf16[4096,256]{1,0:T(8,128)(2,1)} %get-tuple-element.53.k_ref, bf16[4096,256]{1,0:T(8,128)(2,1)} %get-tuple-element.54.v_ref, ...), custom_call_target="tpu_custom_call" | custom-call | flops 1048576 | bytes 1048576 | tf_op jit(solution)/shard_map/tree_attention_backward/pallas_call | solution.py:345
  868.0 9.5 convolution_convert_fusion.5
  877.6 8.8 reduce-scatter.8.cloned.1.call-done
  886.4 10.1 fusion.29
  896.6 9.8 fusion.28
  906.4 5.8 fusion.27
  914.6 51.2 %reduce-scatter.14.cloned.1.call-done = bf16[512,1024]{1,0:T(8,128)(2,1)} async-done(((bf16[2048,1024]{1,0:T(8,128)(2,1)}), bf16[512,1024]{1,0:T(8,128)(2,1)}) %reduce-scatter.14.cloned.1.call-update) | async-done | bytes 1048592 | tf_op jit(solution)/shard_map/reduce_scatter | solution.py:621
  968.6 4.8 all-to-all-start.1
  981.4 3.6 fusion
  985.1 95.2 %plane_scatter.5 = f32[512,2048]{1,0:T(8,128)} custom-call(bf16[4096,256]{1,0:T(8,128)(2,1)} %get-tuple-element.68.refs_0_, bf16[4096,256]{1,0:T(8,128)(2,1)} %get-tuple-element.69.refs_1_, bf16[4096,256]{1,0:T(8,128)(2,1)} %get-tuple-element.70.refs_2_, bf16[2048,256]{1,0:T(8,128)(2,1)S(1)} %get-tuple-element.88.refs_3_, ...), custom_call_target="tpu_custom_call" | custom-call | flops 1048576 | bytes 1048576 | tf_op jit(solution)/shard_map/plane_scatter/pallas_call | solution.py:572
  1080.4 39.9 %all-reduce = f32[32,128]{1,0:T(8,128)S(1)} all-reduce(f32[32,128]{1,0:T(8,128)S(1)} %pad_maximum_fusion.3), channel_id=5, replica_groups=mesh['fsdp'=4,'ctx'=4,'tensor'=2] {'fsdp','ctx','tensor'}, use_global_device_ids=true, to_apply=%region_15.16.clone | all-reduce | flops 4096 | bytes 32768
  1124.5 7.3 fusion.9
  1137.9 3.5 all-to-all-start
  1144.5 11.4 all-to-all-done
  (157 shorter events, 65.0 us)
Async XLA Ops:
  7.2 104.4 %all-gather.7.cloned.1.call-start = ((), (), s32[]{:S(2)}) async-start(), calls=%async_computation.7 | async-start | bytes 5242880 | tf_op jit(solution)/shard_map/all_gather | solution.py:617
  10.5 288.4 %all-gather.9.cloned.1.call-start = ((), (), s32[]{:S(2)}) async-start(), calls=%async_computation.8 | async-start | bytes 18874368 | tf_op jit(solution)/shard_map/all_gather | solution.py:599
  11.3 362.3 %all-gather.11.cloned.1.call-start = ((), (), s32[]{:S(2)}) async-start(), calls=%async_computation.9 | async-start | bytes 5242880 | tf_op jit(solution)/shard_map/all_gather | solution.py:617
  13.6 383.4 %all-gather.13.cloned.1.call-start = ((), (), s32[]{:S(2)}) async-start(), calls=%async_computation.10 | async-start | bytes 5242880 | tf_op jit(solution)/shard_map/all_gather | solution.py:617
  16.2 412.2 %all-gather.15.cloned.1.call-start = ((), (), s32[]{:S(2)}) async-start(), calls=%async_computation.11 | async-start | bytes 5242880 | tf_op jit(solution)/shard_map/all_gather | solution.py:617
  18.5 614.9 %reduce-scatter.6.cloned.1.call-start = ((), (), s32[]{:S(2)}) async-start(), calls=%async_computation.12 | async-start | bytes 18874368 | tf_op jit(solution)/shard_map/reduce_scatter | solution.py:603
  19.1 78.9 %copy-start.25 = (f32[512]{0:T(512)}, f32[512]{0:T(512)S(1)}, u32[]{:S(2)}) copy-start(f32[512]{0:T(512)S(1)} %add_rsqrt_fusion.1) | copy-start | bytes 6148
  20.9 77.0 %copy-start.27 = (s32[1,20]{1,0:T(1,128)S(1)}, s32[1,20]{1,0:T(1,128)}, u32[]{:S(2)}) copy-start(s32[1,20]{1,0:T(1,128)} %param.23) | copy-start | bytes 244
  20.9 77.4 %copy-start.28 = (s32[1,16]{1,0:T(1,128)S(1)}, s32[1,16]{1,0:T(1,128)}, u32[]{:S(2)}) copy-start(s32[1,16]{1,0:T(1,128)} %param.24) | copy-start | bytes 196
  98.5 32.3 %copy-start.17 = (s32[4096,1]{0,1:T(1,128)}, s32[4096,1]{0,1:T(1,128)S(1)}, u32[]{:S(2)}) copy-start(s32[4096,1]{0,1:T(1,128)S(1)} %fusion.15) | copy-start | bytes 49156
  130.8 79.8 %copy-start.8 = (bf16[2048,1024]{1,0:T(8,128)(2,1)S(1)}, bf16[2048,1024]{1,0:T(8,128)(2,1)}, u32[]{:S(2)}) copy-start(bf16[2048,1024]{1,0:T(8,128)(2,1)} %all-gather.7.cloned.1.call-done) | copy-start | bytes 12582916
  452.1 275.4 %all-gather.17.cloned.1.call-start = ((), (), s32[]{:S(2)}) async-start(), calls=%async_computation.13 | async-start | bytes 18874368 | tf_op jit(solution)/shard_map/all_gather | solution.py:599
  490.9 135.9 %copy-start.1 = (f32[512,2048]{1,0:T(8,128)S(1)}, f32[512,2048]{1,0:T(8,128)}, u32[]{:S(2)}) copy-start(f32[512,2048]{1,0:T(8,128)} %copy-done) | copy-start | bytes 12582916
  490.9 135.9 %copy-start.22 = (f32[2048]{0:T(1024)S(1)}, f32[2048]{0:T(1024)}, u32[]{:S(2)}) copy-start(f32[2048]{0:T(1024)} %param.19) | copy-start | bytes 24580
  490.9 135.9 %copy-start.24 = (f32[512]{0:T(512)S(1)}, f32[512]{0:T(512)}, u32[]{:S(2)}) copy-start(f32[512]{0:T(512)} %copy-done.23) | copy-start | bytes 6148
  637.6 240.0 %reduce-scatter.10.cloned.1.call-start = ((), (), s32[]{:S(2)}) async-start(), calls=%async_computation.15 | async-start | bytes 5242880 | tf_op jit(solution)/shard_map/reduce_scatter | solution.py:621
  727.6 158.8 %reduce-scatter.8.cloned.1.call-start = ((), (), s32[]{:S(2)}) async-start(), calls=%async_computation.14 | async-start | bytes 5242880 | tf_op jit(solution)/shard_map/reduce_scatter | solution.py:621
  728.4 237.4 %reduce-scatter.14.cloned.1.call-start = ((), (), s32[]{:S(2)}) async-start(), calls=%async_computation.17 | async-start | bytes 5242880 | tf_op jit(solution)/shard_map/reduce_scatter | solution.py:621
  728.9 406.7 %reduce-scatter.12.cloned.1.call-start = ((), (), s32[]{:S(2)}) async-start(), calls=%async_computation.16 | async-start | bytes 5242880 | tf_op jit(solution)/shard_map/reduce_scatter | solution.py:621
  743.6 124.4 %copy-start.9 = (bf16[4096,256]{1,0:T(8,128)(2,1)S(1)}, bf16[4096,256]{1,0:T(8,128)(2,1)}, u32[]{:S(2)}) copy-start(bf16[4096,256]{1,0:T(8,128)(2,1)} %get-tuple-element.46.refs_0_.o_ref) | copy-start | bytes 6291460
  868.0 18.4 %copy-start.10 = (bf16[4096,256]{1,0:T(8,128)(2,1)S(1)}, bf16[4096,256]{1,0:T(8,128)(2,1)}, u32[]{:S(2)}) copy-start(bf16[4096,256]{1,0:T(8,128)(2,1)} %get-tuple-element.68.refs_0_) | copy-start | bytes 6291460
  886.4 10.2 copy-start.11
  886.4 20.0 %slice-start = ((s8[16777216]{0:T(1024)(128)(4,1)}), s8[4194304]{0:T(1024)(128)(4,1)S(1)}, s32[]{:S(2)}) async-start(s8[16777216]{0:T(1024)(128)(4,1)} %bitcast.95), calls=%async_computation.18 | async-start | bytes 8388608
  886.4 20.0 %slice-start.1 = ((s8[16777216]{0:T(1024)(128)(4,1)}), s8[4194304]{0:T(1024)(128)(4,1)S(1)}, s32[]{:S(2)}) async-start(s8[16777216]{0:T(1024)(128)(4,1)} %bitcast.95), calls=%async_computation.19 | async-start | bytes 8388608
  896.5 9.8 slice-start.3
  896.5 9.8 copy-start.12
  914.5 51.3 %copy-start.13 = (bf16[512,1024]{1,0:T(8,128)(2,1)S(1)}, bf16[512,1024]{1,0:T(8,128)(2,1)}, u32[]{:S(2)}) copy-start(bf16[512,1024]{1,0:T(8,128)(2,1)} %reduce-scatter.10.cloned.1.call-done) | copy-start | bytes 3145732
  914.5 51.3 %copy-start.14 = (bf16[512,1024]{1,0:T(8,128)(2,1)S(1)}, bf16[512,1024]{1,0:T(8,128)(2,1)}, u32[]{:S(2)}) copy-start(bf16[512,1024]{1,0:T(8,128)(2,1)} %reduce-scatter.8.cloned.1.call-done) | copy-start | bytes 3145732
  968.6 163.2 %all-to-all-start.1 = ((bf16[4,128,3072]{2,1,0:T(8,128)(2,1)}), bf16[4,128,3072]{2,1,0:T(8,128)(2,1)}, u32[]{:S(2)}, u32[]{:S(2)}) async-start(bf16[4,128,3072]{2,1,0:T(8,128)(2,1)} %bitcast.97), calls=%async_computation.6 | async-start | bytes 6291456 | tf_op jit(solution)/shard_map/all_to_all | solution.py:627
  985.1 135.8 %copy-start.5 = (bf16[512,2048]{1,0:T(8,128)(2,1)S(1)}, bf16[512,2048]{1,0:T(8,128)(2,1)}, u32[]{:S(2)}) copy-start(bf16[512,2048]{1,0:T(8,128)(2,1)} %param.13) | copy-start | bytes 6291460
  985.1 135.8 %copy-start.26 = (f32[512]{0:T(512)S(1)}, f32[512]{0:T(512)}, u32[]{:S(2)}) copy-start(f32[512]{0:T(512)} %copy-done.25) | copy-start | bytes 6148
  1137.9 18.0 %all-to-all-start = ((bf16[4,128,1024]{2,1,0:T(8,128)(2,1)}), bf16[4,128,1024]{2,1,0:T(8,128)(2,1)S(1)}, u32[]{:S(2)}, u32[]{:S(2)}) async-start(bf16[4,128,1024]{2,1,0:T(8,128)(2,1)} %bitcast.8), calls=%async_computation.4 | async-start | bytes 2097152 | tf_op jit(solution)/shard_map/all_to_all | solution.py:627
  (14 other events, 61.4 us)
Sparse Core Ops, SparseCore 0:
  10.6 83.4 all-gather.6
  96.0 88.3 all-gather.8
  186.0 80.7 all-gather.10
  268.2 79.2 all-gather.12
  349.0 79.2 all-gather.14
  452.3 166.7 reduce-scatter.5
  637.7 89.8 all-gather.16
  729.9 76.7 reduce-scatter.9
  809.1 77.2 reduce-scatter.7
  888.5 77.2 reduce-scatter.13
  968.2 77.2 reduce-scatter.11

commit v4 on v3

--- a/solution.py
+++ b/solution.py
@@ -388,7 +388,74 @@
     pl.semaphore_wait(barrier, 3)
 
 
-def gather_kernel(own_ref, all_ref, local_sem, send_sem, recv_sem):
+TOKENS_AT_ONCE = 2048
+LEFT_AT_ONCE = 512
+STEP = 512
+
+
+def product_buffers(columns):
+    return [
+        pltpu.VMEM((2, TOKENS_AT_ONCE, LEFT_AT_ONCE), BF16),
+        pltpu.VMEM((2 * TOKENS_AT_ONCE, columns), BF16),
+        pltpu.VMEM((LEFT_AT_ONCE, columns), F32),
+        pltpu.VMEM((LEFT_AT_ONCE, columns), BF16),
+        pltpu.SemaphoreType.DMA((4,)),
+    ]
+
+
+def token_product(left_ref, right_ref, out_ref, left_buf, right_buf, total, out_buf, sems):
+    tokens = left_ref.shape[0]
+    parts, groups = tokens // TOKENS_AT_ONCE, left_ref.shape[1] // LEFT_AT_ONCE
+
+    def load(step):
+        group, part = step // parts, step % parts
+        source = left_ref.at[
+            pl.ds(part * TOKENS_AT_ONCE, TOKENS_AT_ONCE), pl.ds(group * LEFT_AT_ONCE, LEFT_AT_ONCE)
+        ]
+        return pltpu.make_async_copy(source, left_buf.at[step % 2], sems.at[step % 2])
+
+    def store(group):
+        return pltpu.make_async_copy(out_buf, out_ref.at[pl.ds(group * LEFT_AT_ONCE, LEFT_AT_ONCE)], sems.at[3])
+
+    whole = pltpu.make_async_copy(right_ref, right_buf, sems.at[2])
+    whole.start()
+    load(0).start()
+    whole.wait()
+    for group in range(groups):
+        for part in range(parts):
+            step = group * parts + part
+            load(step).wait()
+            if step + 1 < groups * parts:
+                load(step + 1).start()
+            if part == 0:
+                total[...] = jnp.zeros_like(total)
+
+            @pl.loop(0, TOKENS_AT_ONCE // STEP)
+            def _(j, step=step, part=part):
+                left = left_buf[step % 2, pl.ds(pl.multiple_of(j * STEP, STEP), STEP), :]
+                right = right_buf[pl.ds(pl.multiple_of(part * TOKENS_AT_ONCE + j * STEP, STEP), STEP), :]
+                total[...] += dot_tn(left, right)
+
+        if group > 0:
+            store(group - 1).wait()
+        out_buf[...] = total[...].astype(BF16)
+        store(group).start()
+        yield
+    store(groups - 1).wait()
+
+
+def finish(product):
+    for _ in product:
+        pass
+
+
+def gather_kernel(*refs):
+    if len(refs) == 5:
+        own_ref, all_ref, local_sem, send_sem, recv_sem = refs
+        product = iter(())
+    else:
+        own_ref, left_ref, right_ref, all_ref, out_ref, local_sem, send_sem, recv_sem = refs[:8]
+        product = token_product(left_ref, right_ref, out_ref, *refs[8:])
     x, core, row = plane_place()
     over_x, over_row, over_core = plane_neighbours(x, core, row)
     rows = own_ref.shape[0]
@@ -426,8 +493,11 @@
         for slot, device in hops:
             send(slot, all_ref.at[target], target, device)
 
+    for _ in range(3):
+        next(product, None)
     forward(0, place(0, 1, 0), ((5, over_x), (8, over_core)))
     forward(3, place(1, 0, 1), ((2, over_row), (9, over_core)))
+    finish(product)
     forward(1, place(0, 1, 1), ((10, over_core),))
     forward(4, place(1, 0, 0), ((11, over_core),))
     forward(5, place(1, 1, 0), ((12, over_core),))
@@ -440,32 +510,51 @@
         copy.wait()
 
 
-def plane_gather(rows):
+def plane_gather(rows, left=None, right=None):
     count, width = rows.shape
-    return pl.pallas_call(
+    hbm = pl.BlockSpec(memory_space=pl.ANY)
+    scratch = [pltpu.SemaphoreType.DMA((2,)), pltpu.SemaphoreType.DMA((14,)), pltpu.SemaphoreType.DMA((14,))]
+    inputs, outputs = [rows], [jax.ShapeDtypeStruct((8 * count, width), rows.dtype)]
+    if left is not None:
+        inputs += [left, right]
+        outputs += [jax.ShapeDtypeStruct((left.shape[1], right.shape[1]), BF16)]
+        scratch += product_buffers(right.shape[1])
+    result = pl.pallas_call(
         gather_kernel,
-        in_specs=[pl.BlockSpec(memory_space=pl.ANY)],
-        out_specs=pl.BlockSpec(memory_space=pl.ANY),
-        out_shape=jax.ShapeDtypeStruct((8 * count, width), rows.dtype),
-        scratch_shapes=[
-            pltpu.SemaphoreType.DMA((2,)),
-            pltpu.SemaphoreType.DMA((14,)),
-            pltpu.SemaphoreType.DMA((14,)),
-        ],
-        compiler_params=pltpu.CompilerParams(collective_id=0, has_side_effects=True),
+        in_specs=[hbm] * len(inputs),
+        out_specs=[hbm] * len(outputs),
+        out_shape=outputs,
+        scratch_shapes=scratch,
+        compiler_params=pltpu.CompilerParams(
+            collective_id=0 if left is None else 4,
+            has_side_effects=True,
+            vmem_limit_bytes=None if left is None else 48 << 20,
+        ),
         cost_estimate=small_cost(),
         name="plane_gather",
-    )(rows)
+    )(*inputs)
+    return result[0] if left is None else result
 
 
 PIECES = ((1, 1, 0), (1, 1, 1), (1, 0, 0), (0, 1, 1), (0, 1, 0), (1, 0, 1), (0, 0, 0), (0, 0, 1))
 COLS = 512
 
 
-def scatter_kernel(rows, parts, *refs):
-    a_refs, w_refs = refs[:parts], refs[parts : 2 * parts]
-    (out_ref, core_out, core_in, first_in, next_in, sems), rest = refs[2 * parts : 2 * parts + 6], refs[2 * parts + 6 :]
-    a_bufs, a_sems = rest[:parts], rest[parts]
+def scatter_kernel(rows, parts, jobs, *refs):
+    def take(count):
+        nonlocal refs
+        taken, refs = refs[:count], refs[count:]
+        return taken
+
+    a_refs, w_refs, lefts, rights = take(parts), take(parts), take(jobs), take(jobs)
+    (out_ref,), products = take(1), take(jobs)
+    core_out, core_in, first_in, next_in, sems = take(5)
+    a_bufs, (a_sems,), buffers = take(parts), take(1), refs
+
+    def work(job):
+        if job < jobs:
+            finish(token_product(lefts[job], rights[job], products[job], *buffers))
+
     x, core, row = plane_place()
     over_x, over_row, over_core = plane_neighbours(x, core, row)
     half = rows // 2
@@ -540,6 +629,7 @@
                 remote(core_in.at[piece], first_in.at[piece], 8 + piece, over_x if piece % 2 == 0 else over_row)
             )
             first_copies[-1].start()
+    work(0)
     for part in range(2):
         first_copies[part].wait_recv()
 
@@ -550,6 +640,7 @@
 
         next_copies.append(remote(core_in.at[4 + part], next_in.at[part], 12 + part, over_row if part == 0 else over_x))
         next_copies[-1].start()
+    work(1)
     for part in range(2):
         first_copies[2 + part].wait_recv()
         next_copies[part].wait_recv()
@@ -563,17 +654,19 @@
         copy.wait_send()
 
 
-def plane_scatter(parts, weights, collective_id):
+def plane_scatter(parts, weights, collective_id, jobs=()):
     count = parts[0].shape[0]
     width = weights[0].shape[0]
     rows = count // 8
     half = rows // 2
-    vmem = pl.BlockSpec(memory_space=pltpu.VMEM)
+    vmem, hbm = pl.BlockSpec(memory_space=pltpu.VMEM), pl.BlockSpec(memory_space=pl.ANY)
+    lefts, rights = [left for left, _ in jobs], [right for _, right in jobs]
     return pl.pallas_call(
-        functools.partial(scatter_kernel, rows, len(parts)),
-        in_specs=[pl.BlockSpec(memory_space=pl.ANY)] * len(parts) + [vmem] * len(parts),
-        out_specs=vmem,
-        out_shape=jax.ShapeDtypeStruct((rows, width), F32),
+        functools.partial(scatter_kernel, rows, len(parts), len(jobs)),
+        in_specs=[hbm] * len(parts) + [vmem] * len(parts) + [hbm] * (2 * len(jobs)),
+        out_specs=[vmem] + [hbm] * len(jobs),
+        out_shape=[jax.ShapeDtypeStruct((rows, width), F32)]
+        + [jax.ShapeDtypeStruct((left.shape[1], right.shape[1]), BF16) for left, right in jobs],
         scratch_shapes=[
             pltpu.VMEM((8, half, width), BF16),
             pltpu.VMEM((8, half, width), BF16),
@@ -582,13 +675,14 @@
             pltpu.SemaphoreType.DMA((2, 14)),
         ]
         + [pltpu.VMEM((2, half, a.shape[1]), BF16) for a in parts]
-        + [pltpu.SemaphoreType.DMA((2, len(parts)))],
+        + [pltpu.SemaphoreType.DMA((2, len(parts)))]
+        + (product_buffers(rights[0].shape[1]) if jobs else []),
         compiler_params=pltpu.CompilerParams(
-            collective_id=collective_id, has_side_effects=True, vmem_limit_bytes=52 << 20
+            collective_id=collective_id, has_side_effects=True, vmem_limit_bytes=(58 if jobs else 52) << 20
         ),
         cost_estimate=small_cost(),
         name="plane_scatter",
-    )(*parts, *weights)
+    )(*parts, *weights, *lefts, *rights)
 
 
 def is_plane():
@@ -607,10 +701,17 @@
     return plane_gather(rows) if is_plane() else gather_rows(rows)
 
 
-def product_scatter(parts, weights, collective_id):
+def gather_with_product(rows, left, right):
     if is_plane():
-        return plane_scatter(parts, weights, collective_id)
-    return scatter_rows(dot_t(jnp.concatenate(parts, axis=1), jnp.concatenate(weights, axis=1)))
+        return plane_gather(rows, left, right)
+    return gather_rows(rows), dot_tn(left, right).astype(BF16)
+
+
+def product_scatter(parts, weights, collective_id, jobs=()):
+    if is_plane():
+        return plane_scatter(parts, weights, collective_id, jobs)
+    rows = scatter_rows(dot_t(jnp.concatenate(parts, axis=1), jnp.concatenate(weights, axis=1)))
+    return [rows] + [dot_tn(left, right).astype(BF16) for left, right in jobs]
 
 
 def gather_weight(own):
@@ -688,7 +789,7 @@
     attn_out, lse, query_rows, key_rows, value_rows = attention_forward(
         qkv, cosine, sine, seg_keys, seg_queries, width
     )
-    mid_rows = x_rows + product_scatter([attn_out], [w_out], 1)
+    mid_rows = x_rows + product_scatter([attn_out], [w_out], 1)[0]
     mlp_scaled, mlp_inv = normalize(mid_rows)
     mlp_own, cot_all = lax.optimization_barrier(((mlp_scaled * mlp_gain[None, :]).astype(BF16), cot_all))
     mlp_in = gather_now(mlp_own)
@@ -705,44 +806,53 @@
     ).astype(BF16)
     up_rows_grad = (hidden_grad * gate * sigmoid_gate).astype(BF16)
 
-    mlp_in_grad = product_scatter([gate_rows_grad, up_rows_grad], [w_gate, w_up], 3)
-    mlp_back = norm_backward(mlp_in_grad, mlp_scaled, mlp_inv, mlp_gain)
-    mlp_gain_part = jnp.sum(mlp_in_grad * mlp_scaled, axis=0)
-    mid_grad = cotangent.astype(F32) + mlp_back
-    mid_low, mlp_in, cot_all, down_rows = lax.optimization_barrier(
-        (mid_grad.astype(BF16), mlp_in, cot_all, down_rows)
+    mlp_in_grad, down_part, up_part = product_scatter(
+        [gate_rows_grad, up_rows_grad], [w_gate, w_up], 3, [(cot_all, hidden), (mlp_in, up_rows_grad)]
     )
+    down_grad = scatter_weight(down_part)
+    up_grad = scatter_weight(up_part)
+    mid_grad = cotangent.astype(F32) + norm_backward(mlp_in_grad, mlp_scaled, mlp_inv, mlp_gain)
+    mid_low, down_rows = lax.optimization_barrier((mid_grad.astype(BF16), down_rows))
     block_out = (mid_rows + down_rows).astype(BF16)
-    mid_all = gather_rows(mid_low)
-    gate_part = dot_tn(mlp_in, gate_rows_grad).astype(BF16)
-    up_part = dot_tn(mlp_in, up_rows_grad).astype(BF16)
-    down_part = dot_tn(cot_all, hidden).astype(BF16)
-    mid_all, gate_part, up_part, down_part = lax.optimization_barrier((mid_all, gate_part, up_part, down_part))
+    mid_all, gate_part = gather_with_product(mid_low, mlp_in, gate_rows_grad)
     gate_grad = scatter_weight(gate_part)
-    up_grad = scatter_weight(up_part)
-    down_grad = scatter_weight(down_part)
 
     out_heads_grad = jnp.dot(mid_all, w_out, preferred_element_type=F32).astype(BF16)
-    output_grad = dot_tn(mid_all, attn_out)
+    output_grad = dot_tn(mid_all, attn_out).astype(BF16)
     pre_grads = attention_backward(
         query_rows, key_rows, value_rows, attn_out, out_heads_grad, lse, cosine, sine, seg_keys, seg_queries
     )
-    pre_grads, gate_grad, up_grad = lax.optimization_barrier((pre_grads, gate_grad, up_grad))
-    qkv_grad = jnp.concatenate([dot_tn(attn_in, grad) for grad in pre_grads], axis=1)
-    attn_gain_part = jnp.sum(qkv_grad * w_qkv.astype(F32), axis=1) / attn_gain
-    attn_part = jnp.concatenate([qkv_grad, output_grad], axis=1).astype(BF16)
+    pre_grads, gate_grad, up_grad, down_grad = lax.optimization_barrier((pre_grads, gate_grad, up_grad, down_grad))
+    attn_part = jnp.concatenate([dot_tn(attn_in, grad).astype(BF16) for grad in pre_grads] + [output_grad], axis=1)
+    attn_grad = scatter_weight(attn_part)
     pre_grads, attn_part = lax.optimization_barrier((pre_grads, attn_part))
-    attn_in_grad = product_scatter(
-        pre_grads, [w_attn[:, j * width : (j + 1) * width] for j in range(3)], 2
-    )
-    devices = lax.axis_size(("fsdp", "ctx", "tensor"))
-    gain_parts = [part.reshape(devices, -1) for part in (attn_gain_part, mlp_gain_part)]
-    gain_grads = lax.psum_scatter(
-        jnp.concatenate(gain_parts, axis=1), ("fsdp", "ctx", "tensor"), scatter_dimension=0, tiled=True
-    ).reshape(2, -1)
-    attn_grad = scatter_weight(attn_part)
+    (attn_in_grad,) = product_scatter(pre_grads, [w_attn[:, j * width : (j + 1) * width] for j in range(3)], 2)
+    attn_in_grad, attn_grad = lax.optimization_barrier((attn_in_grad, attn_grad))
     gate_out, up_out, down_out = swap_columns(jnp.concatenate([gate_grad, up_grad, down_grad], axis=1), 3)
     query_out, key_out, value_out, output_out = swap_columns(attn_grad, 4)
+
+    def gain_part(pairs, gain):
+        held = query_out.shape[0]
+        total = sum(
+            jnp.sum(lax.dynamic_slice_in_dim(weight, ctx * held, held, 0).astype(F32) * grad, axis=1)
+            for weight, grad in pairs
+        )
+        first = (lax.axis_index("fsdp") * parts + ctx) * held
+        return total / lax.dynamic_slice_in_dim(gain, first, held, 0)
+
+    sums = jnp.stack(
+        [
+            gain_part([(query_weight, query_out), (key_weight, key_out), (value_weight, value_out)], attn_gain),
+            gain_part([(gate_weight, gate_out), (up_weight, up_out)], mlp_gain),
+        ]
+    )
+    row, others = lax.axis_index("tensor"), lax.axis_size("tensor")
+    kept = sums.shape[1] // others
+    if others == 2:
+        got = lax.ppermute(lax.dynamic_slice_in_dim(sums, (1 - row) * kept, kept, 1), "tensor", [(0, 1), (1, 0)])
+        gain_grads = lax.dynamic_slice_in_dim(sums, row * kept, kept, 1) + got
+    else:
+        gain_grads = lax.dynamic_slice_in_dim(lax.psum(sums, "tensor"), row * kept, kept, 1)
 
     attn_back = norm_backward(attn_in_grad, attn_scaled, attn_inv, attn_gain)
     input_grad = (mid_grad + attn_back).astype(BF16)

time: 1170 us -> 1060 us (0.906)
  Pallas kernels: 667 us -> 754 us
  waiting for transfers between devices: 94.1 us -> 8.39 us
  matrix products: 254 us -> 178 us
  blocking collectives: 39.9 us -> 0 us
    pallas_call x5 -> x6, Pallas kernels: 463 us -> 549 us  [the longest x3 323 us: plane_scatter(): pl.pallas_call(functools.partial(scatter_kernel, rows, len(parts), len(jo...]
    dot_general x7 -> x4, matrix products: 107 us -> 31 us  [dot_tn(): lax.dot_general(a, b, (((0,), (0,)), ((), ())), preferred_element_type=F32)]
    reduce_scatter x4, waiting for transfers between devices: 60 us -> 0.01 us  [scatter_weight(): lax.psum_scatter(grad.astype(BF16), 'fsdp', scatter_dimension=0, tiled=True)]
    unnamed x1 -> x0, blocking collectives: 39.9 us -> none
    all_gather x2 -> x1, waiting for transfers between devices: 18.5 us -> 0.01 us  [gather_rows(): return lax.all_gather(rows, GROUP, axis=0, tiled=True)]
  transfers between devices with their start and end apart: 13 -> 13, of which waited for: 5 -> 3; matrix products, arithmetic and copies ran while one was open for 26% -> 19% of each run, Pallas kernels for 57% -> 72%
where the time goes in v4:
time: 1060 us; the launch traced here: 1050 us
  Pallas kernels  754 us (71%)
  matrix products  178 us (17%)
  other arithmetic  61.8 us (6%)
  local copies, waits for them, and re-layouts  26.9 us (3%)
  between operations  14.9 us (1%)
    pallas_call x3, Pallas kernels, plane_scatter(): pl.pallas_call(functools.partial(scatter_kernel, rows, len(parts), len(jo...  323 us
    pallas_call x3, Pallas kernels, plane_gather(): pl.pallas_call(gather_kernel, in_specs=[hbm] * len(inputs), out_specs=[hb...  226 us
    pallas_call x1, Pallas kernels, attention_backward(): pl.pallas_call(functools.partial(bwd_kernel, heads), grid=(groups, tree_l...  124 us
    pallas_call x1, Pallas kernels, attention_forward(): pl.pallas_call(functools.partial(fwd_kernel, heads), grid=(groups, tree_l...  80.2 us
    dot_general x1, matrix products, body(): hidden_grad = jnp.dot(cot_all, w_down, preferred_element_type=F32)  38.9 us
    dot_general x4, matrix products, dot_tn(): lax.dot_general(a, b, (((0,), (0,)), ((), ())), preferred_element_type=F32)  31 us
    dot_general x1, matrix products, body(): up_proj = jnp.dot(mlp_in, w_up, preferred_element_type=F32)  29 us
    dot_general x1, matrix products, dot_t(): lax.dot_general(a, b, (((1,), (1,)), ((), ())), preferred_element_type=F32)  23.9 us
  transfers between devices with their start and end apart: 13, of which 3 were waited for; matrix products, arithmetic and copies ran while one was open for 19% of the time, Pallas kernels for 72%

profile of v4, /device:TPU:0, one launch (start us, length us, event | category | flops | bytes accessed | tf_op | source)
XLA Modules:
  0.0 1053.6 jit_solution(1805916042409818938)
XLA Ops:
  20.9 77.0 %plane_gather.3 = bf16[4096,2048]{1,0:T(8,128)(2,1)} custom-call(bf16[512,2048]{1,0:T(8,128)(2,1)} %fusion.3.refs_0_), custom_call_target="tpu_custom_call" | custom-call | flops 1048576 | bytes 1048576 | tf_op jit(solution)/shard_map/plane_gather/pallas_call | solution.py:522
  102.2 9.4 fusion.12
  111.5 19.2 %fusion.10.q_ref.k_ref.v_ref = f32[4096,768]{1,0:T(8,128)} fusion(bf16[4096,2048]{1,0:T(8,128)(2,1)} %plane_gather.3, bf16[2048,1024]{1,0:T(8,128)(2,1)} %all-gather.6.cloned.1.call-done), kind=kOutput, calls=%fused_computation.25 | convolution fusion | flops 12884901888 | bytes 32505856 | tf_op jit(solution)/shard_map/dot_general | solution.py:788
  130.8 80.2 %tree_attention_forward.1 = (bf16[4096,256]{1,0:T(8,128)(2,1)}, f32[2,2,4096]{2,1,0:T(2,128)}, bf16[4096,256]{1,0:T(8,128)(2,1)}, bf16[4096,256]{1,0:T(8,128)(2,1)}, bf16[4096,256]{1,0:T(8,128)(2,1)}) custom-call(f32[4096,768]{1,0:T(8,128)} %fusion.10.q_ref.k_ref.v_ref, f32[4096,768]{1,0:T(8,128)} %fusion.10.q_ref.k_ref.v_ref, ...), custom_call_target="tpu_custom_call" | custom-call | flops 1048576 | bytes 1048576 | tf_op jit(solution)/shard_map/tree_attention_forward/pallas_call | solution.py:310
  212.6 80.1 %plane_scatter.3 = f32[512,2048]{1,0:T(8,128)} custom-call(bf16[4096,256]{1,0:T(8,128)(2,1)} %get-tuple-element.47.refs_0_.o_ref, bf16[2048,256]{1,0:T(8,128)(2,1)S(1)} %get-tuple-element.97.refs_1_), custom_call_target="tpu_custom_call" | custom-call | flops 1048576 | bytes 1048576 | tf_op jit(solution)/shard_map/plane_scatter/pallas_call | solution.py:664
  292.7 3.0 multiply_reduce_fusion.1
  298.3 74.7 %plane_gather.4.refs_5_.refs_1_ = bf16[4096,2048]{1,0:T(8,128)(2,1)} custom-call(bf16[512,2048]{1,0:T(8,128)(2,1)} %multiply_convert_fusion.3.refs_0_), custom_call_target="tpu_custom_call" | custom-call | flops 1048576 | bytes 1048576 | tf_op jit(solution)/shard_map/plane_gather/pallas_call | solution.py:522
  373.0 23.5 %fusion.29 = f32[4096,1024]{1,0:T(8,128)} fusion(bf16[4096,2048]{1,0:T(8,128)(2,1)} %plane_gather.4.refs_5_.refs_1_, bf16[2048,1024]{1,0:T(8,128)(2,1)} %all-gather.10.cloned.1.call-done.refs_2_), kind=kOutput, calls=%fused_computation.133 | convolution fusion | flops 17179869184 | bytes 37748736 | tf_op jit(solution)/shard_map/dot_general | solution.py:797
  396.6 29.0 %multiply_convert_fusion.2 = (bf16[4096,1024]{1,0:T(8,128)(2,1)}, f32[4096,1024]{1,0:T(8,128)}) fusion(f32[4096,1024]{1,0:T(8,128)} %fusion.29, bf16[4096,2048]{1,0:T(8,128)(2,1)} %plane_gather.4.refs_5_.refs_1_, bf16[2048,1024]{1,0:T(8,128)(2,1)} %all-gather.12.cloned.1.call-done.refs_3_), kind=kOutput, calls=%fused_computation.2 | convolution fusion | flops 17205035008 | bytes 62914560 | tf_op jit(solution)/shard_map/dot_general | solution.py:798
  425.6 2.7 all-gather.14.cloned.1.call-done
  428.3 23.9 %convolution_convert_fusion = bf16[4096,2048]{1,0:T(8,128)(2,1)} fusion(bf16[4096,1024]{1,0:T(8,128)(2,1)} %get-tuple-element.132.refs_6_, bf16[2048,1024]{1,0:T(8,128)(2,1)} %all-gather.14.cloned.1.call-done), kind=kOutput, calls=%fused_computation.4 | convolution fusion | flops 17188257792 | bytes 29360128 | tf_op jit(solution)/shard_map/dot_general | solution.py:77
  452.3 38.9 %multiply_convert_fusion = (bf16[4096,1024]{1,0:T(8,128)(2,1)}, bf16[4096,1024]{1,0:T(8,128)(2,1)}) fusion(f32[4096,1024]{1,0:T(8,128)} %fusion.29, f32[4096,1024]{1,0:T(8,128)} %get-tuple-element.133, bf16[4096,2048]{1,0:T(8,128)(2,1)} %all-gather.8.cloned.1.call-done.refs_4_, bf16[2048,1024]{1,0:T(8,128)(2,1)} %all-gather.14.cloned.1.call-done), kind=kOutput, calls=%fused_computation | convolution fusion | flops 17234395136 | bytes 71303168 | tf_op jit(solution)/shard_map/dot_general | solution.py:803
  491.2 135.8 %plane_scatter.4 = (f32[512,2048]{1,0:T(8,128)}, bf16[2048,1024]{1,0:T(8,128)(2,1)}, bf16[2048,1024]{1,0:T(8,128)(2,1)}) custom-call(bf16[4096,1024]{1,0:T(8,128)(2,1)} %get-tuple-element.91.refs_0_.refs_2_, bf16[4096,1024]{1,0:T(8,128)(2,1)} %get-tuple-element.90.refs_1_.refs_7_, bf16[2048,1024]{1,0:T(8,128)(2,1)} %all-gather.10.cloned.1.call-done.refs_2_, ...), custom_call_target="tpu_custom_call" | custom-call | flops 1048576 | bytes 1048576 | tf_op jit(solution)/shard_map/plane_scatter/pallas_call | solution.py:664
  628.5 4.5 multiply_reduce_fusion
  635.8 3.2 fusion.27.refs_0_
  639.1 4.2 convert_element_type.141
  643.3 74.8 %plane_gather.5 = (bf16[4096,2048]{1,0:T(8,128)(2,1)}, bf16[2048,1024]{1,0:T(8,128)(2,1)}) custom-call(bf16[512,2048]{1,0:T(8,128)(2,1)S(1)} %fusion.27.refs_0_, bf16[4096,2048]{1,0:T(8,128)(2,1)} %plane_gather.4.refs_5_.refs_1_, bf16[4096,1024]{1,0:T(8,128)(2,1)} %get-tuple-element.91.refs_0_.refs_2_), custom_call_target="tpu_custom_call" | custom-call | flops 1048576 | bytes 1048576 | tf_op jit(solution)/shard_map/plane_gather/pallas_call | solution.py:522
  720.8 11.9 %convolution_convert_fusion.1.do_ref = bf16[4096,256]{1,0:T(8,128)(2,1)} fusion(bf16[4096,2048]{1,0:T(8,128)(2,1)} %get-tuple-element.58, bf16[2048,1024]{1,0:T(8,128)(2,1)} %all-gather.6.cloned.1.call-done), kind=kOutput, calls=%fused_computation.11 | convolution fusion | flops 4296015872 | bytes 19922944 | tf_op jit(solution)/shard_map/dot_general | solution.py:820
  732.8 124.2 %tree_attention_backward.1 = (bf16[4096,256]{1,0:T(8,128)(2,1)}, bf16[4096,256]{1,0:T(8,128)(2,1)}, bf16[4096,256]{1,0:T(8,128)(2,1)}) custom-call(bf16[4096,256]{1,0:T(8,128)(2,1)} %get-tuple-element.54.q_ref, bf16[4096,256]{1,0:T(8,128)(2,1)} %get-tuple-element.55.k_ref, bf16[4096,256]{1,0:T(8,128)(2,1)} %get-tuple-element.56.v_ref, ...), custom_call_target="tpu_custom_call" | custom-call | flops 1048576 | bytes 1048576 | tf_op jit(solution)/shard_map/tree_attention_backward/pallas_call | solution.py:345
  857.0 9.5 convolution_convert_fusion.2
  866.5 8.5 convolution_convert_fusion.5
  875.1 8.5 convolution_convert_fusion.4
  883.9 4.5 convolution_convert_fusion.3
  892.2 2.8 pad_maximum_fusion.1
  895.0 4.9 all-to-all-start.1
  899.9 106.9 %plane_scatter.5 = f32[512,2048]{1,0:T(8,128)} custom-call(bf16[4096,256]{1,0:T(8,128)(2,1)} %get-tuple-element.69.refs_0_, bf16[4096,256]{1,0:T(8,128)(2,1)} %get-tuple-element.70.refs_1_, bf16[4096,256]{1,0:T(8,128)(2,1)} %get-tuple-element.71.refs_2_, bf16[2048,256]{1,0:T(8,128)(2,1)S(1)} %get-tuple-element.96.refs_3_, ...), custom_call_target="tpu_custom_call" | custom-call | flops 1048576 | bytes 1048576 | tf_op jit(solution)/shard_map/plane_scatter/pallas_call | solution.py:664
  1009.1 2.9 multiply_reduce_fusion.2
  1012.0 2.9 multiply_reduce_fusion.3
  1018.8 3.5 all-to-all-start
  1022.3 3.2 fusion.4
  1026.5 7.7 fusion.8
  1034.2 2.5 all-to-all-done
  (149 shorter events, 50.1 us)
Async XLA Ops:
  7.2 104.4 %all-gather.6.cloned.1.call-start = ((), (), s32[]{:S(2)}) async-start(), calls=%async_computation.7 | async-start | bytes 5242880 | tf_op jit(solution)/shard_map/all_gather | solution.py:718
  10.5 287.8 %all-gather.8.cloned.1.call-start = ((), (), s32[]{:S(2)}) async-start(), calls=%async_computation.8 | async-start | bytes 18874368 | tf_op jit(solution)/shard_map/all_gather | solution.py:693
  11.3 361.8 %all-gather.10.cloned.1.call-start = ((), (), s32[]{:S(2)}) async-start(), calls=%async_computation.9 | async-start | bytes 5242880 | tf_op jit(solution)/shard_map/all_gather | solution.py:718
  13.6 5.4 copy-start.21
  13.6 382.9 %all-gather.12.cloned.1.call-start = ((), (), s32[]{:S(2)}) async-start(), calls=%async_computation.10 | async-start | bytes 5242880 | tf_op jit(solution)/shard_map/all_gather | solution.py:718
  16.1 412.2 %all-gather.14.cloned.1.call-start = ((), (), s32[]{:S(2)}) async-start(), calls=%async_computation.11 | async-start | bytes 5242880 | tf_op jit(solution)/shard_map/all_gather | solution.py:718
  18.5 620.7 %reduce-scatter.6.cloned.1.call-start = ((), (), s32[]{:S(2)}) async-start(), calls=%async_computation.12 | async-start | bytes 18874368 | tf_op jit(solution)/shard_map/reduce_scatter | solution.py:697
  19.0 78.9 %copy-start.25 = (f32[512]{0:T(512)}, f32[512]{0:T(512)S(1)}, u32[]{:S(2)}) copy-start(f32[512]{0:T(512)S(1)} %add_rsqrt_fusion.1) | copy-start | bytes 6148
  20.9 77.0 %copy-start.27 = (s32[1,20]{1,0:T(1,128)S(1)}, s32[1,20]{1,0:T(1,128)}, u32[]{:S(2)}) copy-start(s32[1,20]{1,0:T(1,128)} %param.23) | copy-start | bytes 244
  20.9 77.4 %copy-start.28 = (s32[1,16]{1,0:T(1,128)S(1)}, s32[1,16]{1,0:T(1,128)}, u32[]{:S(2)}) copy-start(s32[1,16]{1,0:T(1,128)} %param.24) | copy-start | bytes 196
  98.5 32.3 %copy-start.17 = (s32[4096,1]{0,1:T(1,128)}, s32[4096,1]{0,1:T(1,128)S(1)}, u32[]{:S(2)}) copy-start(s32[4096,1]{0,1:T(1,128)S(1)} %fusion.14) | copy-start | bytes 49156
  130.8 80.2 %copy-start.10 = (bf16[2048,1024]{1,0:T(8,128)(2,1)S(1)}, bf16[2048,1024]{1,0:T(8,128)(2,1)}, u32[]{:S(2)}) copy-start(bf16[2048,1024]{1,0:T(8,128)(2,1)} %all-gather.6.cloned.1.call-done) | copy-start | bytes 12582916
  452.3 414.2 %reduce-scatter.10.cloned.1.call-start = ((), (), s32[]{:S(2)}) async-start(), calls=%async_computation.14 | async-start | bytes 5242880 | tf_op jit(solution)/shard_map/reduce_scatter | solution.py:722
  627.0 239.5 %reduce-scatter.12.cloned.1.call-start = ((), (), s32[]{:S(2)}) async-start(), calls=%async_computation.15 | async-start | bytes 5242880 | tf_op jit(solution)/shard_map/reduce_scatter | solution.py:722
  627.7 238.7 %reduce-scatter.8.cloned.1.call-start = ((), (), s32[]{:S(2)}) async-start(), calls=%async_computation.13 | async-start | bytes 5242880 | tf_op jit(solution)/shard_map/reduce_scatter | solution.py:722
  628.5 6.0 copy-start.5
  628.5 7.3 copy-start.7
  718.1 298.4 %reduce-scatter.14.cloned.1.call-start = ((), (), s32[]{:S(2)}) async-start(), calls=%async_computation.16 | async-start | bytes 5242880 | tf_op jit(solution)/shard_map/reduce_scatter | solution.py:722
  732.8 124.2 %copy-start.9 = (bf16[4096,256]{1,0:T(8,128)(2,1)S(1)}, bf16[4096,256]{1,0:T(8,128)(2,1)}, u32[]{:S(2)}) copy-start(bf16[4096,256]{1,0:T(8,128)(2,1)} %get-tuple-element.47.refs_0_.o_ref) | copy-start | bytes 6291460
  857.0 9.5 copy-start.11
  866.5 8.5 copy-start.12
  866.5 17.1 %slice-start = ((s8[16777216]{0:T(1024)(128)(4,1)}), s8[4194304]{0:T(1024)(128)(4,1)S(1)}, s32[]{:S(2)}) async-start(s8[16777216]{0:T(1024)(128)(4,1)} %bitcast.93), calls=%async_computation.17 | async-start | bytes 8388608
  866.5 17.1 %slice-start.1 = ((s8[16777216]{0:T(1024)(128)(4,1)}), s8[4194304]{0:T(1024)(128)(4,1)S(1)}, s32[]{:S(2)}) async-start(s8[16777216]{0:T(1024)(128)(4,1)} %bitcast.93), calls=%async_computation.18 | async-start | bytes 8388608
  875.0 8.6 slice-start.2
  875.0 8.6 slice-start.3
  875.1 8.8 copy-start.13
  895.0 111.9 %all-to-all-start.1 = ((bf16[4,128,3072]{2,1,0:T(8,128)(2,1)}), bf16[4,128,3072]{2,1,0:T(8,128)(2,1)}, u32[]{:S(2)}, u32[]{:S(2)}) async-start(bf16[4,128,3072]{2,1,0:T(8,128)(2,1)} %bitcast.95), calls=%async_computation.6 | async-start | bytes 6291456 | tf_op jit(solution)/shard_map/all_to_all | solution.py:728
  1014.9 7.4 copy-start.6
  1014.9 7.4 copy-start.22
  1014.9 7.4 copy-start.26
  1018.8 18.0 %all-to-all-start = ((bf16[4,128,1024]{2,1,0:T(8,128)(2,1)}), bf16[4,128,1024]{2,1,0:T(8,128)(2,1)S(1)}, u32[]{:S(2)}, u32[]{:S(2)}) async-start(bf16[4,128,1024]{2,1,0:T(8,128)(2,1)} %bitcast.96), calls=%async_computation.5 | async-start | bytes 2097152 | tf_op jit(solution)/shard_map/all_to_all | solution.py:728
  1042.4 3.6 collective-permute-start
  (14 other events, 37.9 us)
Sparse Core Ops, SparseCore 0:
  10.6 83.4 all-gather.5
  96.0 88.3 all-gather.7
  186.0 80.7 all-gather.9
  268.2 79.2 all-gather.11
  349.0 79.2 all-gather.13
  452.4 167.2 reduce-scatter.5
  627.1 76.7 reduce-scatter.9
  706.3 77.2 reduce-scatter.11
  785.9 77.2 reduce-scatter.7
  890.8 76.4 reduce-scatter.13

commit v5 on v4

--- a/solution.py
+++ b/solution.py
@@ -57,6 +57,209 @@
     return jnp.cos(angles), jnp.sin(angles) * sign[None, :]
 
 
+MESH = pl.DeviceIdType.MESH
+
+
+def plane_place():
+    ctx, row = lax.axis_index("ctx"), lax.axis_index("tensor")
+    x, core = ctx // 2, ctx % 2
+    return x, core, row
+
+
+def plane_neighbours(x, core, row):
+    over_x = {"ctx": (1 - x) * 2 + core}
+    over_core = {"ctx": x * 2 + 1 - core}
+    over_row = {"tensor": 1 - row}
+    return over_x, over_row, over_core
+
+
+def enter_plane(neighbours):
+    barrier = pltpu.get_barrier_semaphore()
+    for device in neighbours:
+        pl.semaphore_signal(barrier, inc=1, device_id=device, device_id_type=MESH)
+    pl.semaphore_wait(barrier, 3)
+
+
+PIECES = ((1, 1, 0), (1, 1, 1), (1, 0, 0), (0, 1, 1), (0, 1, 0), (1, 0, 1), (0, 0, 0), (0, 0, 1))
+COLS = 512
+
+
+class PlaneGather:
+    def __init__(self, own_ref, all_ref, local_sem, send_sem, recv_sem):
+        self.own_ref, self.all_ref, self.sems = own_ref, all_ref, (local_sem, send_sem, recv_sem)
+        self.x, self.core, self.row = plane_place()
+        self.devices = plane_neighbours(self.x, self.core, self.row)
+        self.rows = own_ref.shape[0]
+
+    def place(self, far_x, far_row, part):
+        bx = self.x + far_x - 2 * far_x * self.x
+        by = self.row + far_row - 2 * far_row * self.row
+        half = self.rows // 2
+        return pl.ds(pl.multiple_of(((bx * 2 + self.core) * 2 + by) * self.rows + part * half, half), half)
+
+    def copy(self, slot):
+        far_x, far_row, part, device = (
+            (0, 0, 0, 1), (0, 0, 1, 1), (1, 0, 1, 1), (0, 0, 1, 0), (0, 0, 0, 0), (0, 1, 0, 0), (0, 0, 0, 2),
+            (0, 0, 1, 2), (0, 1, 0, 2), (1, 0, 1, 2), (0, 1, 1, 2), (1, 0, 0, 2), (1, 1, 0, 2), (1, 1, 1, 2),
+        )[slot]
+        half = self.rows // 2
+        target = self.place(far_x, far_row, part)
+        own = far_x == 0 and far_row == 0
+        source = self.own_ref.at[pl.ds(part * half, half)] if own else self.all_ref.at[target]
+        return pltpu.make_async_remote_copy(
+            src_ref=source, dst_ref=self.all_ref.at[target], send_sem=self.sems[1].at[slot],
+            recv_sem=self.sems[2].at[slot], device_id=self.devices[device], device_id_type=MESH,
+        )
+
+    def local(self, part):
+        half = self.rows // 2
+        return pltpu.make_async_copy(
+            self.own_ref.at[pl.ds(part * half, half)], self.all_ref.at[self.place(0, 0, part)], self.sems[0].at[part]
+        )
+
+    def start(self):
+        enter_plane(self.devices)
+        for slot in (0, 3, 1, 4, 6, 7):
+            self.copy(slot).start()
+        for part in range(2):
+            self.local(part).start()
+
+    def forward(self, got, slots):
+        self.copy(got).wait_recv()
+        for slot in slots:
+            self.copy(slot).start()
+
+    def first(self):
+        self.forward(0, (5, 8))
+        self.forward(3, (2, 9))
+
+    def second(self):
+        self.forward(1, (10,))
+        self.forward(4, (11,))
+
+    def finish(self):
+        self.forward(5, (12,))
+        self.forward(2, (13,))
+        for slot in range(6, 14):
+            self.copy(slot).wait_recv()
+        for slot in range(14):
+            self.copy(slot).wait_send()
+        for part in range(2):
+            self.local(part).wait()
+
+
+def gather_sems():
+    return [pltpu.SemaphoreType.DMA((2,)), pltpu.SemaphoreType.DMA((14,)), pltpu.SemaphoreType.DMA((14,))]
+
+
+class PlaneScatter:
+    def __init__(self, part_ref, out_ref, core_in, first_in, next_in, own, total, sems, own_sems):
+        self.part_ref, self.out_ref, self.core_in, self.first_in, self.next_in = part_ref, out_ref, core_in, first_in, next_in
+        self.own, self.total, self.sems, self.own_sems = own, total, sems, own_sems
+        self.x, self.core, self.row = plane_place()
+        self.devices = plane_neighbours(self.x, self.core, self.row)
+        self.rows = part_ref.shape[0] // 8
+
+    def place(self, piece, on_core):
+        far_x, far_row, part = PIECES[piece]
+        bx = self.x + far_x - 2 * far_x * self.x
+        by = self.row + far_row - 2 * far_row * self.row
+        half = self.rows // 2
+        return pl.ds(pl.multiple_of(((bx * 2 + on_core) * 2 + by) * self.rows + part * half, half), half)
+
+    def copy(self, slot):
+        if slot < 8:
+            source, target, device = self.part_ref.at[self.place(slot, 1 - self.core)], self.core_in.at[slot], 2
+        elif slot < 12:
+            source, target, device = self.core_in.at[slot - 8], self.first_in.at[slot - 8], slot % 2
+        else:
+            source, target, device = self.core_in.at[slot - 8], self.next_in.at[slot - 12], 1 - slot % 2
+        return pltpu.make_async_remote_copy(
+            src_ref=source, dst_ref=target, send_sem=self.sems.at[0, slot], recv_sem=self.sems.at[1, slot],
+            device_id=self.devices[device], device_id_type=MESH,
+        )
+
+    def load(self, piece):
+        return pltpu.make_async_copy(
+            self.part_ref.at[self.place(piece, self.core)], self.own.at[piece % 4], self.own_sems.at[piece % 4]
+        )
+
+    def add(self, target, where, *others):
+        @pl.loop(0, target.shape[-1] // COLS)
+        def _(j):
+            columns = pl.ds(pl.multiple_of(j * COLS, COLS), COLS)
+            total = sum(ref[slot, :, columns].astype(F32) for ref, slot in others)
+            target[where, :, columns] = total.astype(target.dtype)
+
+    def start(self):
+        enter_plane(self.devices)
+        for slot in range(8):
+            self.copy(slot).start()
+        for piece in range(4):
+            self.load(piece).start()
+
+    def first(self):
+        for piece in range(4):
+            self.load(piece).wait()
+            self.copy(piece).wait_recv()
+            self.add(self.core_in, piece, (self.own, piece), (self.core_in, piece))
+            self.copy(8 + piece).start()
+        for piece in range(4, 8):
+            self.load(piece).start()
+
+    def second(self):
+        for piece in range(4, 8):
+            self.load(piece).wait()
+            self.copy(piece).wait_recv()
+            self.add(self.core_in, piece, (self.own, piece - 4), (self.core_in, piece))
+
+    def third(self):
+        for part in range(2):
+            self.copy(8 + part).wait_recv()
+            self.add(self.core_in, 4 + part, (self.core_in, 4 + part), (self.first_in, part))
+            self.copy(12 + part).start()
+
+    def finish(self):
+        half = self.rows // 2
+        for part in range(2):
+            self.copy(10 + part).wait_recv()
+            self.copy(12 + part).wait_recv()
+            self.add(self.total, part, (self.core_in, 6 + part), (self.first_in, 2 + part), (self.next_in, part))
+        stores = [
+            pltpu.make_async_copy(
+                self.total.at[part], self.out_ref.at[pl.ds(part * half, half)], self.own_sems.at[part]
+            )
+            for part in range(2)
+        ]
+        for store in stores:
+            store.start()
+        for slot in range(14):
+            self.copy(slot).wait_send()
+        for store in stores:
+            store.wait()
+
+
+def scatter_scratch(rows, width):
+    half = rows // 2
+    return [
+        pltpu.VMEM((8, half, width), BF16),
+        pltpu.VMEM((4, half, width), BF16),
+        pltpu.VMEM((2, half, width), BF16),
+        pltpu.VMEM((4, half, width), BF16),
+        pltpu.VMEM((2, half, width), BF16),
+        pltpu.SemaphoreType.DMA((2, 14)),
+        pltpu.SemaphoreType.DMA((4,)),
+    ]
+
+
+def at_step(step, total, places):
+    for place, phase in places:
+
+        @pl.when(step == place)
+        def _(phase=phase):
+            phase()
+
+
 def partner(x):
     half = HEAD_DIM // 2
     width = x.shape[1]
@@ -135,7 +338,17 @@
     return causal & ((seg_k == 0) | (seg_k == seg_q) | (seg_k == par_q))
 
 
-def fwd_kernel(
+def fwd_kernel(heads, hosts, *refs):
+    if not hosts:
+        return fwd_work(heads, *refs)
+    gather = PlaneGather(refs[7], refs[13], *refs[-3:])
+    step, total = pl.program_id(0) * pl.num_programs(1) + pl.program_id(1), 16
+    at_step(step, total, ((0, gather.start), (6, gather.first), (12, gather.second)))
+    fwd_work(heads, *refs[:7], *refs[8:13], *refs[14:-3])
+    at_step(step, total, ((total - 1, gather.finish),))
+
+
+def fwd_work(
     heads, q_ref, k_ref, v_ref, cos_ref, sin_ref, segk_ref, segq_ref,
     o_ref, lse_ref, qr_ref, kr_ref, vr_ref, kt_ref, va_ref, s_ref, m_ref, acc_ref,
 ):
@@ -218,7 +431,19 @@
         lse_ref[0, h : h + 1, :] = turned[h * HEAD_DIM : h * HEAD_DIM + 1, :]
 
 
-def bwd_kernel(
+def bwd_kernel(heads, hosts, *refs):
+    if not hosts:
+        return bwd_work(heads, *refs)
+    scatter = PlaneScatter(refs[10], refs[14], *refs[-7:])
+    step, total = pl.program_id(0) * pl.num_programs(1) + pl.program_id(1), 16
+    at_step(
+        step, total, ((0, scatter.start), (3, scatter.first), (5, scatter.second), (7, scatter.third))
+    )
+    bwd_work(heads, *refs[:10], *refs[11:14], *refs[15:-7])
+    at_step(step, total, ((total - 1, scatter.finish),))
+
+
+def bwd_work(
     heads, q_ref, k_ref, v_ref, o_ref, do_ref, lse_ref, cos_ref, sin_ref, segk_ref, segq_ref,
     dq_ref, dk_ref, dv_ref, dq_acc, dk_acc, dv_acc,
 ):
@@ -294,7 +519,7 @@
     return pl.CostEstimate(flops=1 << 20, bytes_accessed=1 << 20, transcendentals=0)
 
 
-def attention_forward(qkv, cosine, sine, seg_keys, seg_queries, width):
+def attention_forward(qkv, cosine, sine, seg_keys, seg_queries, width, hosted=None):
     tree_len = qkv.shape[0]
     gw = min(2 * HEAD_DIM, width)
     groups, heads = width // gw, gw // HEAD_DIM
@@ -307,8 +532,10 @@
     else:
         queries, keys, values = jnp.split(qkv, 3, axis=1)
         step = 0
+    hosts = hosted is not None
+    hbm = pl.BlockSpec(memory_space=pl.ANY)
     return pl.pallas_call(
-        functools.partial(fwd_kernel, heads),
+        functools.partial(fwd_kernel, heads, hosts),
         grid=(groups, tree_len // BQ),
         in_specs=[
             row_block,
@@ -318,23 +545,28 @@
             table,
             pl.BlockSpec((1, tree_len), lambda g, i: (0, 0)),
             pl.BlockSpec((BQ, 2), lambda g, i: (i, 0)),
-        ],
-        out_specs=[row_block, pl.BlockSpec((1, heads, BQ), lambda g, i: (g, 0, i)), row_block, full, full],
-        out_shape=[act, jax.ShapeDtypeStruct((groups, heads, tree_len), F32), act, act, act],
+        ]
+        + [hbm] * hosts,
+        out_specs=[row_block, pl.BlockSpec((1, heads, BQ), lambda g, i: (g, 0, i)), row_block, full, full] + [hbm] * hosts,
+        out_shape=[act, jax.ShapeDtypeStruct((groups, heads, tree_len), F32), act, act, act]
+        + ([jax.ShapeDtypeStruct((8 * hosted.shape[0], hosted.shape[1]), BF16)] if hosts else []),
         scratch_shapes=[
             pltpu.VMEM((gw, tree_len), BF16),
             pltpu.VMEM((heads, tree_len, 128), BF16),
             pltpu.VMEM((heads, BQ, most_keys()), F32),
             pltpu.VMEM((heads, BQ, 128), F32),
             pltpu.VMEM((heads, BQ, 128), F32),
-        ],
-        compiler_params=pltpu.CompilerParams(vmem_limit_bytes=56 << 20),
+        ]
+        + (gather_sems() if hosts else []),
+        compiler_params=pltpu.CompilerParams(
+            vmem_limit_bytes=56 << 20, collective_id=6 if hosts else None, has_side_effects=hosts
+        ),
         cost_estimate=small_cost(),
         name="tree_attention_forward",
-    )(queries, keys, values, cosine, sine, seg_keys, seg_queries)
-
-
-def attention_backward(q, k, v, out, grad, lse, cosine, sine, seg_keys, seg_queries):
+    )(queries, keys, values, cosine, sine, seg_keys, seg_queries, *([hosted] if hosts else []))
+
+
+def attention_backward(q, k, v, out, grad, lse, cosine, sine, seg_keys, seg_queries, hosted=None):
     tree_len, width = q.shape
     gw = min(2 * HEAD_DIM, width)
     groups, heads = width // gw, gw // HEAD_DIM
@@ -342,8 +574,10 @@
     table = pl.BlockSpec((tree_len, gw), lambda g, i: (0, 0))
     full = pl.BlockSpec((tree_len, gw), lambda g, i: (0, g))
     act = jax.ShapeDtypeStruct((tree_len, width), BF16)
+    hosts = hosted is not None
+    hbm = pl.BlockSpec(memory_space=pl.ANY)
     return pl.pallas_call(
-        functools.partial(bwd_kernel, heads),
+        functools.partial(bwd_kernel, heads, hosts),
         grid=(groups, tree_len // BQ),
         in_specs=[
             row_block, full, full, row_block, row_block,
@@ -351,41 +585,23 @@
             table, table,
             pl.BlockSpec((tree_len, 1), lambda g, i: (0, 0)),
             pl.BlockSpec((2, BQ), lambda g, i: (0, i)),
-        ],
-        out_specs=[row_block, full, full],
-        out_shape=[act, act, act],
+        ]
+        + [hbm] * hosts,
+        out_specs=[row_block, full, full] + [hbm] * hosts,
+        out_shape=[act, act, act]
+        + ([jax.ShapeDtypeStruct((hosted.shape[0] // 8, hosted.shape[1]), BF16)] if hosts else []),
         scratch_shapes=[
             pltpu.VMEM((BQ, gw), F32),
             pltpu.VMEM((tree_len, gw), F32),
             pltpu.VMEM((tree_len, gw), F32),
-        ],
-        compiler_params=pltpu.CompilerParams(vmem_limit_bytes=56 << 20),
+        ]
+        + (scatter_scratch(hosted.shape[0] // 8, hosted.shape[1]) if hosts else []),
+        compiler_params=pltpu.CompilerParams(
+            vmem_limit_bytes=60 << 20, collective_id=7 if hosts else None, has_side_effects=hosts
+        ),
         cost_estimate=small_cost(),
         name="tree_attention_backward",
-    )(q, k, v, out, grad, lse, cosine, sine, seg_keys.T, seg_queries.T)
-
-
-MESH = pl.DeviceIdType.MESH
-
-
-def plane_place():
-    ctx, row = lax.axis_index("ctx"), lax.axis_index("tensor")
-    x, core = ctx // 2, ctx % 2
-    return x, core, row
-
-
-def plane_neighbours(x, core, row):
-    over_x = {"ctx": (1 - x) * 2 + core}
-    over_core = {"ctx": x * 2 + 1 - core}
-    over_row = {"tensor": 1 - row}
-    return over_x, over_row, over_core
-
-
-def enter_plane(neighbours):
-    barrier = pltpu.get_barrier_semaphore()
-    for device in neighbours:
-        pl.semaphore_signal(barrier, inc=1, device_id=device, device_id_type=MESH)
-    pl.semaphore_wait(barrier, 3)
+    )(q, k, v, out, grad, lse, cosine, sine, seg_keys.T, seg_queries.T, *([hosted] if hosts else []))
 
 
 TOKENS_AT_ONCE = 2048
@@ -449,95 +665,91 @@
         pass
 
 
-def gather_kernel(*refs):
-    if len(refs) == 5:
-        own_ref, all_ref, local_sem, send_sem, recv_sem = refs
-        product = iter(())
-    else:
-        own_ref, left_ref, right_ref, all_ref, out_ref, local_sem, send_sem, recv_sem = refs[:8]
-        product = token_product(left_ref, right_ref, out_ref, *refs[8:])
-    x, core, row = plane_place()
-    over_x, over_row, over_core = plane_neighbours(x, core, row)
-    rows = own_ref.shape[0]
-    half = rows // 2
-
-    def place(far_x, far_row, part):
-        bx = x + far_x - 2 * far_x * x
-        by = row + far_row - 2 * far_row * row
-        return pl.ds(pl.multiple_of(((bx * 2 + core) * 2 + by) * rows + part * half, half), half)
-
-    enter_plane((over_x, over_row, over_core))
-    copies = {}
-
-    def send(slot, source, target, device):
-        copies[slot] = pltpu.make_async_remote_copy(
-            src_ref=source, dst_ref=all_ref.at[target], send_sem=send_sem.at[slot], recv_sem=recv_sem.at[slot],
-            device_id=device, device_id_type=MESH,
-        )
-        copies[slot].start()
-
-    mine = [own_ref.at[pl.ds(part * half, half)] for part in range(2)]
-    own = [place(0, 0, part) for part in range(2)]
-    send(0, mine[0], own[0], over_row)
-    send(3, mine[1], own[1], over_x)
-    send(1, mine[1], own[1], over_row)
-    send(4, mine[0], own[0], over_x)
-    send(6, mine[0], own[0], over_core)
-    send(7, mine[1], own[1], over_core)
-    local = [pltpu.make_async_copy(mine[part], all_ref.at[own[part]], local_sem.at[part]) for part in range(2)]
-    for copy in local:
-        copy.start()
-
-    def forward(got, target, hops):
-        copies[got].wait_recv()
-        for slot, device in hops:
-            send(slot, all_ref.at[target], target, device)
-
-    for _ in range(3):
-        next(product, None)
-    forward(0, place(0, 1, 0), ((5, over_x), (8, over_core)))
-    forward(3, place(1, 0, 1), ((2, over_row), (9, over_core)))
-    finish(product)
-    forward(1, place(0, 1, 1), ((10, over_core),))
-    forward(4, place(1, 0, 0), ((11, over_core),))
-    forward(5, place(1, 1, 0), ((12, over_core),))
-    forward(2, place(1, 1, 1), ((13, over_core),))
-    for slot in range(6, 14):
-        copies[slot].wait_recv()
-    for slot in range(14):
-        copies[slot].wait_send()
-    for copy in local:
-        copy.wait()
-
-
-def plane_gather(rows, left=None, right=None):
+def row_product(left_ref, right_ref, out_ref, left_buf, right_buf, out_buf, sems):
+    groups = left_ref.shape[0] // LEFT_AT_ONCE
+
+    def rows(group):
+        return pl.ds(group * LEFT_AT_ONCE, LEFT_AT_ONCE)
+
+    def load(group):
+        return pltpu.make_async_copy(left_ref.at[rows(group)], left_buf.at[group % 2], sems.at[group % 2])
+
+    def store(group):
+        return pltpu.make_async_copy(out_buf.at[group % 2], out_ref.at[rows(group)], sems.at[3 + group % 2])
+
+    whole = pltpu.make_async_copy(right_ref, right_buf, sems.at[2])
+    whole.start()
+    load(0).start()
+    whole.wait()
+    for group in range(groups):
+        load(group).wait()
+        if group + 1 < groups:
+            load(group + 1).start()
+        if group > 1:
+            store(group - 2).wait()
+
+        @pl.loop(0, right_ref.shape[1] // STEP)
+        def _(j, group=group):
+            columns = pl.ds(pl.multiple_of(j * STEP, STEP), STEP)
+            out_buf[group % 2, :, columns] = dot_n(left_buf[group % 2], right_buf[:, columns]).astype(BF16)
+
+        store(group).start()
+        yield
+    for group in range(max(0, groups - 2), groups):
+        store(group).wait()
+
+
+def row_product_buffers(depth, columns):
+    return [
+        pltpu.VMEM((2, LEFT_AT_ONCE, depth), BF16),
+        pltpu.VMEM((depth, columns), BF16),
+        pltpu.VMEM((2, LEFT_AT_ONCE, columns), BF16),
+        pltpu.SemaphoreType.DMA((5,)),
+    ]
+
+
+def gather_kernel(kind, jobs, *refs):
+    own_ref, lefts, rights = refs[0], refs[1 : 1 + jobs], refs[1 + jobs : 1 + 2 * jobs]
+    all_ref, outs, refs = refs[1 + 2 * jobs], refs[2 + 2 * jobs : 2 + 3 * jobs], refs[2 + 3 * jobs :]
+    gather, buffers = PlaneGather(own_ref, all_ref, *refs[:3]), refs[3:]
+
+    def work():
+        for job in range(jobs):
+            yield from kind(lefts[job], rights[job], outs[job], *buffers)
+
+    work = work()
+
+    def some(count):
+        for _ in range(count):
+            next(work, None)
+
+    gather.start()
+    some(4)
+    gather.first()
+    some(4)
+    gather.second()
+    finish(work)
+    gather.finish()
+
+
+def plane_gather(rows, kind=None, jobs=(), buffers=(), shape=()):
     count, width = rows.shape
     hbm = pl.BlockSpec(memory_space=pl.ANY)
-    scratch = [pltpu.SemaphoreType.DMA((2,)), pltpu.SemaphoreType.DMA((14,)), pltpu.SemaphoreType.DMA((14,))]
-    inputs, outputs = [rows], [jax.ShapeDtypeStruct((8 * count, width), rows.dtype)]
-    if left is not None:
-        inputs += [left, right]
-        outputs += [jax.ShapeDtypeStruct((left.shape[1], right.shape[1]), BF16)]
-        scratch += product_buffers(right.shape[1])
-    result = pl.pallas_call(
-        gather_kernel,
-        in_specs=[hbm] * len(inputs),
+    outputs = [jax.ShapeDtypeStruct((8 * count, width), rows.dtype)] + [jax.ShapeDtypeStruct(shape, BF16)] * len(jobs)
+    return pl.pallas_call(
+        functools.partial(gather_kernel, kind, len(jobs)),
+        in_specs=[hbm] * (1 + 2 * len(jobs)),
         out_specs=[hbm] * len(outputs),
         out_shape=outputs,
-        scratch_shapes=scratch,
+        scratch_shapes=gather_sems() + list(buffers),
         compiler_params=pltpu.CompilerParams(
-            collective_id=0 if left is None else 4,
+            collective_id=0 if kind is None else 4 if kind is token_product else 5,
             has_side_effects=True,
-            vmem_limit_bytes=None if left is None else 48 << 20,
+            vmem_limit_bytes=None if kind is None else 48 << 20,
         ),
         cost_estimate=small_cost(),
         name="plane_gather",
-    )(*inputs)
-    return result[0] if left is None else result
-
-
-PIECES = ((1, 1, 0), (1, 1, 1), (1, 0, 0), (0, 1, 1), (0, 1, 0), (1, 0, 1), (0, 0, 0), (0, 0, 1))
-COLS = 512
+    )(rows, *[left for left, _ in jobs], *[right for _, right in jobs])
 
 
 def scatter_kernel(rows, parts, jobs, *refs):
@@ -698,13 +910,21 @@
 
 
 def gather_now(rows):
-    return plane_gather(rows) if is_plane() else gather_rows(rows)
-
-
-def gather_with_product(rows, left, right):
+    return plane_gather(rows)[0] if is_plane() else gather_rows(rows)
+
+
+def gather_with_token_products(rows, jobs):
     if is_plane():
-        return plane_gather(rows, left, right)
-    return gather_rows(rows), dot_tn(left, right).astype(BF16)
+        columns = jobs[0][1].shape[1]
+        return plane_gather(rows, token_product, jobs, product_buffers(columns), (jobs[0][0].shape[1], columns))
+    return [gather_rows(rows)] + [dot_tn(left, right).astype(BF16) for left, right in jobs]
+
+
+def gather_with_row_product(rows, left, right):
+    if is_plane():
+        shape = (left.shape[0], right.shape[1])
+        return plane_gather(rows, row_product, [(left, right)], row_product_buffers(*right.shape), shape)
+    return gather_rows(rows), dot_n(left, right).astype(BF16)
 
 
 def product_scatter(parts, weights, collective_id, jobs=()):
@@ -772,10 +992,9 @@
     w_attn = gather_weight(
         jnp.concatenate([mine(w, width) for w in (query_weight, key_weight, value_weight, output_weight)], axis=1)
     )
-    cot_all = gather_rows(cotangent)
     w_gate = gather_weight(mine(gate_weight, units))
+    w_down = gather_weight(mine(down_weight, units))
     w_up = gather_weight(mine(up_weight, units))
-    w_down = gather_weight(mine(down_weight, units))
     attn_in = gather_now((attn_scaled * attn_gain[None, :]).astype(BF16))
     w_qkv, w_out = w_attn[:, : 3 * width], w_attn[:, 3 * width :]
 
@@ -786,46 +1005,59 @@
     seg_queries = jnp.stack([segment, parent], axis=1)
 
     qkv = jnp.dot(attn_in, w_qkv, preferred_element_type=F32)
-    attn_out, lse, query_rows, key_rows, value_rows = attention_forward(
-        qkv, cosine, sine, seg_keys, seg_queries, width
-    )
+    if is_plane():
+        attn_out, lse, query_rows, key_rows, value_rows, cot_all = attention_forward(
+            qkv, cosine, sine, seg_keys, seg_queries, width, cotangent
+        )
+    else:
+        attn_out, lse, query_rows, key_rows, value_rows = attention_forward(
+            qkv, cosine, sine, seg_keys, seg_queries, width
+        )
+        cot_all = gather_rows(cotangent)
     mid_rows = x_rows + product_scatter([attn_out], [w_out], 1)[0]
     mlp_scaled, mlp_inv = normalize(mid_rows)
-    mlp_own, cot_all = lax.optimization_barrier(((mlp_scaled * mlp_gain[None, :]).astype(BF16), cot_all))
-    mlp_in = gather_now(mlp_own)
+    mlp_own = (mlp_scaled * mlp_gain[None, :]).astype(BF16)
+    mlp_in, hidden_grad = gather_with_row_product(mlp_own, cot_all, w_down)
 
     gate = jnp.dot(mlp_in, w_gate, preferred_element_type=F32)
     up_proj = jnp.dot(mlp_in, w_up, preferred_element_type=F32)
     sigmoid_gate = jax.nn.sigmoid(gate)
     hidden = (gate * sigmoid_gate * up_proj).astype(BF16)
-    down_rows, cot_all = lax.optimization_barrier((dot_t(hidden, w_down).astype(BF16), cot_all))
-    down_rows = scatter_rows(down_rows)
-    hidden_grad = jnp.dot(cot_all, w_down, preferred_element_type=F32)
+    hidden_grad = hidden_grad.astype(F32)
     gate_rows_grad = (
         hidden_grad * up_proj * sigmoid_gate * (1.0 + gate * (1.0 - sigmoid_gate))
     ).astype(BF16)
     up_rows_grad = (hidden_grad * gate * sigmoid_gate).astype(BF16)
 
-    mlp_in_grad, down_part, up_part = product_scatter(
-        [gate_rows_grad, up_rows_grad], [w_gate, w_up], 3, [(cot_all, hidden), (mlp_in, up_rows_grad)]
+    mlp_in_grad, down_part = product_scatter(
+        [gate_rows_grad, up_rows_grad], [w_gate, w_up], 3, [(cot_all, hidden)]
     )
     down_grad = scatter_weight(down_part)
+    mid_grad = cotangent.astype(F32) + norm_backward(mlp_in_grad, mlp_scaled, mlp_inv, mlp_gain)
+    mid_all, up_part, gate_part = gather_with_token_products(
+        mid_grad.astype(BF16), [(mlp_in, up_rows_grad), (mlp_in, gate_rows_grad)]
+    )
     up_grad = scatter_weight(up_part)
-    mid_grad = cotangent.astype(F32) + norm_backward(mlp_in_grad, mlp_scaled, mlp_inv, mlp_gain)
-    mid_low, down_rows = lax.optimization_barrier((mid_grad.astype(BF16), down_rows))
-    block_out = (mid_rows + down_rows).astype(BF16)
-    mid_all, gate_part = gather_with_product(mid_low, mlp_in, gate_rows_grad)
     gate_grad = scatter_weight(gate_part)
 
     out_heads_grad = jnp.dot(mid_all, w_out, preferred_element_type=F32).astype(BF16)
     output_grad = dot_tn(mid_all, attn_out).astype(BF16)
-    pre_grads = attention_backward(
-        query_rows, key_rows, value_rows, attn_out, out_heads_grad, lse, cosine, sine, seg_keys, seg_queries
-    )
-    pre_grads, gate_grad, up_grad, down_grad = lax.optimization_barrier((pre_grads, gate_grad, up_grad, down_grad))
+    out_heads_grad, down_grad = lax.optimization_barrier((out_heads_grad, down_grad))
+    down_rows = dot_t(hidden, w_down).astype(BF16)
+    if is_plane():
+        *pre_grads, down_rows = attention_backward(
+            query_rows, key_rows, value_rows, attn_out, out_heads_grad, lse, cosine, sine, seg_keys, seg_queries, down_rows
+        )
+    else:
+        pre_grads = attention_backward(
+            query_rows, key_rows, value_rows, attn_out, out_heads_grad, lse, cosine, sine, seg_keys, seg_queries
+        )
+        down_rows = scatter_rows(down_rows)
+    block_out = (mid_rows + down_rows.astype(F32)).astype(BF16)
+    pre_grads, up_grad = lax.optimization_barrier((pre_grads, up_grad))
     attn_part = jnp.concatenate([dot_tn(attn_in, grad).astype(BF16) for grad in pre_grads] + [output_grad], axis=1)
+    pre_grads, attn_part, gate_grad = lax.optimization_barrier((pre_grads, attn_part, gate_grad))
     attn_grad = scatter_weight(attn_part)
-    pre_grads, attn_part = lax.optimization_barrier((pre_grads, attn_part))
     (attn_in_grad,) = product_scatter(pre_grads, [w_attn[:, j * width : (j + 1) * width] for j in range(3)], 2)
     attn_in_grad, attn_grad = lax.optimization_barrier((attn_in_grad, attn_grad))
     gate_out, up_out, down_out = swap_columns(jnp.concatenate([gate_grad, up_grad, down_grad], axis=1), 3)

time: 1060 us -> 1020 us (0.962)
  matrix products: 178 us -> 150 us
  Pallas kernels: 754 us -> 742 us
    dot_general x1 -> x0, matrix products: 38.9 us -> none  [body(): hidden_grad = jnp.dot(cot_all, w_down, preferred_element_type=F32)]
    pallas_call x3, Pallas kernels: 323 us -> 297 us  [plane_scatter(): pl.pallas_call(functools.partial(scatter_kernel, rows, len(parts), len(jo...]
    pallas_call x5, Pallas kernels: 431 us -> 445 us  [the longest x3 226 us: plane_gather(): pl.pallas_call(functools.partial(gather_kernel, kind, len(jobs)), in_spec...]
  transfers between devices with their start and end apart: 13 -> 11, of which waited for: 3 -> 2; matrix products, arithmetic and copies ran while one was open for 19% -> 18% of each run, Pallas kernels for 72% -> 63%
where the time goes in v5:
time: 1020 us; the launch traced here: 1010 us
  Pallas kernels  742 us (73%)
  matrix products  150 us (15%)
  other arithmetic  60 us (6%)
  local copies, waits for them, and re-layouts  27.8 us (3%)
  between operations  14.8 us (1%)
  starting transfers between devices  10.3 us (1%)
    pallas_call x3, Pallas kernels, plane_scatter(): pl.pallas_call(functools.partial(scatter_kernel, rows, len(parts), len(jo...  297 us
    pallas_call x3, Pallas kernels, plane_gather(): pl.pallas_call(functools.partial(gather_kernel, kind, len(jobs)), in_spec...  226 us
    pallas_call x1, Pallas kernels, attention_backward(): pl.pallas_call(functools.partial(bwd_kernel, heads, hosts), grid=(groups,...  131 us
    pallas_call x1, Pallas kernels, attention_forward(): pl.pallas_call(functools.partial(fwd_kernel, heads, hosts), grid=(groups,...  88.6 us
    dot_general x4, matrix products, dot_tn(): lax.dot_general(a, b, (((0,), (0,)), ((), ())), preferred_element_type=F32)  36.4 us
    dot_general x1, matrix products, body(): up_proj = jnp.dot(mlp_in, w_up, preferred_element_type=F32)  35.2 us
    dot_general x1, matrix products, body(): gate = jnp.dot(mlp_in, w_gate, preferred_element_type=F32)  23.4 us
    dot_general x1, matrix products, dot_t(): lax.dot_general(a, b, (((1,), (1,)), ((), ())), preferred_element_type=F32)  22.5 us
  transfers between devices with their start and end apart: 11, of which 2 were waited for; matrix products, arithmetic and copies ran while one was open for 18% of the time, Pallas kernels for 63%

profile of v5, /device:TPU:0, one launch (start us, length us, event | category | flops | bytes accessed | tf_op | source)
XLA Modules:
  0.0 1009.1 jit_solution(7798465065131067380)
XLA Ops:
  10.6 2.3 constant_dynamic-slice_fusion.4
  12.9 2.4 constant_dynamic-slice_fusion.2
  15.4 2.3 constant_dynamic-slice_fusion.3
  20.8 77.0 %plane_gather.3 = bf16[4096,2048]{1,0:T(8,128)(2,1)} custom-call(bf16[512,2048]{1,0:T(8,128)(2,1)} %fusion.8.refs_0_), custom_call_target="tpu_custom_call" | custom-call | flops 1048576 | bytes 1048576 | tf_op jit(solution)/shard_map/plane_gather/pallas_call | solution.py:739
  102.2 9.4 fusion.17
  111.6 19.2 %fusion.15.refs_0_.refs_1_.refs_2_ = f32[4096,768]{1,0:T(8,128)} fusion(bf16[4096,2048]{1,0:T(8,128)(2,1)} %plane_gather.3, bf16[2048,1024]{1,0:T(8,128)(2,1)} %all-gather.5.cloned.1.call-done), kind=kOutput, calls=%fused_computation.30 | convolution fusion | flops 12884901888 | bytes 32505856 | tf_op jit(solution)/shard_map/dot_general | solution.py:1007
  130.8 88.6 %tree_attention_forward.1 = (bf16[4096,256]{1,0:T(8,128)(2,1)}, f32[2,2,4096]{2,1,0:T(2,128)}, bf16[4096,256]{1,0:T(8,128)(2,1)}, bf16[4096,256]{1,0:T(8,128)(2,...) custom-call(f32[4096,768]{1,0:T(8,128)} %fusion.15.refs_0_.refs_1_.refs_2_, ...), custom_call_target="tpu_custom_call" | custom-call | flops 1048576 | bytes 1048576 | tf_op jit(solution)/shard_map/tree_attention_forward/pallas_call | solution.py:537
  221.0 80.2 %plane_scatter.3 = f32[512,2048]{1,0:T(8,128)} custom-call(bf16[4096,256]{1,0:T(8,128)(2,1)} %get-tuple-element.47.refs_0_.refs_3_, bf16[2048,256]{1,0:T(8,128)(2,1)S(1)} %get-tuple-element.98.refs_1_), custom_call_target="tpu_custom_call" | custom-call | flops 1048576 | bytes 1048576 | tf_op jit(solution)/shard_map/plane_scatter/pallas_call | solution.py:876
  301.2 3.0 multiply_reduce_fusion.1
  306.0 74.5 %plane_gather.4 = (bf16[4096,2048]{1,0:T(8,128)(2,1)}, bf16[4096,1024]{1,0:T(8,128)(2,1)}) custom-call(bf16[512,2048]{1,0:T(8,128)(2,1)S(1)} %multiply_convert_fusion.1.refs_0_, bf16[4096,2048]{1,0:T(8,128)(2,1)} %get-tuple-element.51.refs_1_.refs_4_, bf16[2048,1024]{1,0:T(8,128)(2,1)} %all-gather.7.cloned.1.call-done.refs_2_), custom_call_target="tpu_custom_call" | custom-call | flops 1048576 | bytes 1048576 | tf_op jit(solution)/shard_map/plane_gather/pallas_call | solution.py:739
  380.5 23.4 %fusion.34 = f32[4096,1024]{1,0:T(8,128)} fusion(bf16[4096,2048]{1,0:T(8,128)(2,1)} %get-tuple-element.53.refs_1_.refs_2_, bf16[2048,1024]{1,0:T(8,128)(2,1)} %all-gather.11.cloned.1.call-done.refs_2_), kind=kOutput, calls=%fused_computation.138 | convolution fusion | flops 17179869184 | bytes 37748736 | tf_op jit(solution)/shard_map/dot_general | solution.py:1022
  403.9 35.2 %multiply_convert_fusion = (bf16[4096,1024]{1,0:T(8,128)(2,1)}, bf16[4096,1024]{1,0:T(8,128)(2,1)}, bf16[4096,1024]{1,0:T(8,128)(2,1)}) fusion(f32[4096,1024]{1,0:T(8,128)} %fusion.34, bf16[4096,1024]{1,0:T(8,128)(2,1)} %get-tuple-element.52, bf16[4096,2048]{1,0:T(8,128)(2,1)} %get-tuple-element.53.refs_1_.refs_2_, ...), kind=kOutput, calls=%fused_computation.7 | convolution fusion | flops 17251172352 | bytes 71303168 | tf_op jit(solution)/shard_map/dot_general | solution.py:1023
  439.2 109.5 %plane_scatter.4 = (f32[512,2048]{1,0:T(8,128)}, bf16[2048,1024]{1,0:T(8,128)(2,1)}) custom-call(bf16[4096,1024]{1,0:T(8,128)(2,1)} %get-tuple-element.91.refs_0_.refs_4_, bf16[4096,1024]{1,0:T(8,128)(2,1)} %get-tuple-element.92.refs_1_.refs_3_, bf16[2048,1024]{1,0:T(8,128)(2,1)} %all-gather.11.cloned.1.call-done.refs_2_, ...), custom_call_target="tpu_custom_call" | custom-call | flops 1048576 | bytes 1048576 | tf_op jit(solution)/shard_map/plane_scatter/pallas_call | solution.py:876
  550.3 4.5 multiply_reduce_fusion
  559.2 74.4 %plane_gather.5 = (bf16[4096,2048]{1,0:T(8,128)(2,1)}, bf16[2048,1024]{1,0:T(8,128)(2,1)}, bf16[2048,1024]{1,0:T(8,128)(2,1)}) custom-call(bf16[512,2048]{1,0:T(8,128)(2,1)S(1)} %fusion.32.refs_0_, bf16[4096,2048]{1,0:T(8,128)(2,1)} %get-tuple-element.53.refs_1_.refs_2_, bf16[4096,2048]{1,0:T(8,128)(2,1)} %get-tuple-element.53.refs_1_.refs_2_, ...), custom_call_target="tpu_custom_call" | custom-call | flops 1048576 | bytes 1048576 | tf_op jit(solution)/shard_map/plane_gather/pallas_call | solution.py:739
  636.8 12.8 %convolution_convert_fusion.1.refs_4_ = bf16[4096,256]{1,0:T(8,128)(2,1)} fusion(bf16[4096,2048]{1,0:T(8,128)(2,1)} %get-tuple-element.55, bf16[2048,1024]{1,0:T(8,128)(2,1)} %all-gather.5.cloned.1.call-done), kind=kOutput, calls=%fused_computation.16 | convolution fusion | flops 4296015872 | bytes 19922944 | tf_op jit(solution)/shard_map/dot_general | solution.py:1043
  649.6 9.5 convolution_convert_fusion.2
  659.1 22.5 %convolution_convert_fusion.refs_10_ = bf16[4096,2048]{1,0:T(8,128)(2,1)} fusion(bf16[4096,1024]{1,0:T(8,128)(2,1)S(1)} %bitcast.95, bf16[2048,1024]{1,0:T(8,128)(2,1)} %all-gather.7.cloned.1.call-done.refs_2_), kind=kOutput, calls=%fused_computation.9 | convolution fusion | flops 17188257792 | bytes 29360128 | tf_op jit(solution)/shard_map/dot_general | solution.py:280
  681.6 130.9 %tree_attention_backward.1 = (bf16[4096,256]{1,0:T(8,128)(2,1)}, bf16[4096,256]{1,0:T(8,128)(2,1)}, bf16[4096,256]{1,0:T(8,128)(2,1)}, bf16[512,2048]{1,0:T(8,128)(2,1)}) custom-call(bf16[4096,256]{1,0:T(8,128)(2,1)} %get-tuple-element.48.refs_0_, bf16[4096,256]{1,0:T(8,128)(2,1)} %get-tuple-element.49.refs_1_, bf16[4096,256]{1,0:T(8,128)(2,1)} %get-tuple-element.50.refs_2_, ...), custom_call_target="tpu_custom_call" | custom-call | flops 1048576 | bytes 1048576 | tf_op jit(solution)/shard_map/tree_attention_backward/pallas_call | solution.py:579
  812.6 12.0 %convolution_convert_fusion.5 = bf16[2048,256]{0,1:T(8,128)(2,1)} fusion(bf16[4096,2048]{1,0:T(8,128)(2,1)} %plane_gather.3, bf16[4096,256]{1,0:T(8,128)(2,1)} %get-tuple-element.68.refs_0_), kind=kOutput, calls=%fused_computation.38 | convolution fusion | flops 4295491584 | bytes 19922944 | tf_op jit(solution)/shard_map/dot_general | solution.py:288
  824.6 9.5 convolution_convert_fusion.4
  834.1 5.5 convolution_convert_fusion.3
  839.6 7.7 pad_maximum_fusion
  847.4 3.2 pad_maximum_fusion.1
  850.5 4.7 all-to-all-start.1
  855.2 106.9 %plane_scatter.5 = f32[512,2048]{1,0:T(8,128)} custom-call(bf16[4096,256]{1,0:T(8,128)(2,1)} %get-tuple-element.68.refs_0_, bf16[4096,256]{1,0:T(8,128)(2,1)} %get-tuple-element.69.refs_1_, bf16[4096,256]{1,0:T(8,128)(2,1)} %get-tuple-element.70.refs_2_, bf16[2048,256]{1,0:T(8,128)(2,1)S(1)} %get-tuple-element.97.refs_3_, ...), custom_call_target="tpu_custom_call" | custom-call | flops 1048576 | bytes 1048576 | tf_op jit(solution)/shard_map/plane_scatter/pallas_call | solution.py:876
  964.3 2.9 multiply_reduce_fusion.2
  967.2 2.9 multiply_reduce_fusion.3
  974.0 3.7 all-to-all-start
  977.8 3.2 fusion.9
  981.9 7.4 fusion.13
  989.4 2.8 all-to-all-done
  (138 shorter events, 40.4 us)
Async XLA Ops:
  7.2 104.4 %all-gather.5.cloned.1.call-start = ((), (), s32[]{:S(2)}) async-start(), calls=%async_computation.6 | async-start | bytes 5242880 | tf_op jit(solution)/shard_map/all_gather | solution.py:938
  10.5 295.5 %all-gather.7.cloned.1.call-start = ((), (), s32[]{:S(2)}) async-start(), calls=%async_computation.7 | async-start | bytes 5242880 | tf_op jit(solution)/shard_map/all_gather | solution.py:938
  12.9 6.0 copy-start.19
  12.9 367.6 %all-gather.11.cloned.1.call-start = ((), (), s32[]{:S(2)}) async-start(), calls=%async_computation.9 | async-start | bytes 5242880 | tf_op jit(solution)/shard_map/all_gather | solution.py:938
  15.4 388.6 %all-gather.9.cloned.1.call-start = ((), (), s32[]{:S(2)}) async-start(), calls=%async_computation.8 | async-start | bytes 5242880 | tf_op jit(solution)/shard_map/all_gather | solution.py:938
  17.8 663.8 %reduce-scatter.5.cloned.1.call-start = ((), (), s32[]{:S(2)}) async-start(), calls=%async_computation.10 | async-start | bytes 5242880 | tf_op jit(solution)/shard_map/reduce_scatter | solution.py:942
  20.8 77.0 %copy-start.23 = (s32[1,20]{1,0:T(1,128)S(1)}, s32[1,20]{1,0:T(1,128)}, u32[]{:S(2)}) copy-start(s32[1,20]{1,0:T(1,128)} %param.23) | copy-start | bytes 244
  20.8 77.4 %copy-start.24 = (s32[1,16]{1,0:T(1,128)S(1)}, s32[1,16]{1,0:T(1,128)}, u32[]{:S(2)}) copy-start(s32[1,16]{1,0:T(1,128)} %param.24) | copy-start | bytes 196
  130.8 88.6 %copy-start.10 = (bf16[2048,1024]{1,0:T(8,128)(2,1)S(1)}, bf16[2048,1024]{1,0:T(8,128)(2,1)}, u32[]{:S(2)}) copy-start(bf16[2048,1024]{1,0:T(8,128)(2,1)} %all-gather.5.cloned.1.call-done) | copy-start | bytes 12582916
  221.0 83.2 %copy-start.18 = (f32[2048]{0:T(1024)S(1)}, f32[2048]{0:T(1024)}, u32[]{:S(2)}) copy-start(f32[2048]{0:T(1024)} %param.19) | copy-start | bytes 24580
  548.7 263.8 %reduce-scatter.7.cloned.1.call-start = ((), (), s32[]{:S(2)}) async-start(), calls=%async_computation.11 | async-start | bytes 5242880 | tf_op jit(solution)/shard_map/reduce_scatter | solution.py:942
  550.3 6.7 copy-start.6
  550.3 7.3 copy-start.7
  633.6 213.7 %reduce-scatter.9.cloned.1.call-start = ((), (), s32[]{:S(2)}) async-start(), calls=%async_computation.12 | async-start | bytes 5242880 | tf_op jit(solution)/shard_map/reduce_scatter | solution.py:942
  636.3 335.5 %reduce-scatter.11.cloned.1.call-start = ((), (), s32[]{:S(2)}) async-start(), calls=%async_computation.13 | async-start | bytes 5242880 | tf_op jit(solution)/shard_map/reduce_scatter | solution.py:942
  636.8 12.8 %copy-start.9 = (bf16[4096,256]{1,0:T(8,128)(2,1)S(1)}, bf16[4096,256]{1,0:T(8,128)(2,1)}, u32[]{:S(2)}) copy-start(bf16[4096,256]{1,0:T(8,128)(2,1)} %get-tuple-element.47.refs_0_.refs_3_) | copy-start | bytes 6291460
  636.8 22.3 %slice-start.4 = ((s8[8388608]{0:T(1024)(128)(4,1)}), s8[4194304]{0:T(1024)(128)(4,1)S(1)}, s32[]{:S(2)}) async-start(s8[8388608]{0:T(1024)(128)(4,1)} %bitcast.94), calls=%async_computation.18 | async-start | bytes 8388608
  649.6 9.5 slice-start.5
  812.5 12.0 %copy-start.11 = (bf16[4096,256]{1,0:T(8,128)(2,1)S(1)}, bf16[4096,256]{1,0:T(8,128)(2,1)}, u32[]{:S(2)}) copy-start(bf16[4096,256]{1,0:T(8,128)(2,1)} %get-tuple-element.69.refs_1_) | copy-start | bytes 6291460
  812.5 21.5 %slice-start = ((s8[16777216]{0:T(1024)(128)(4,1)}), s8[4194304]{0:T(1024)(128)(4,1)S(1)}, s32[]{:S(2)}) async-start(s8[16777216]{0:T(1024)(128)(4,1)} %bitcast.91), calls=%async_computation.14 | async-start | bytes 8388608
  812.6 21.5 %slice-start.1 = ((s8[16777216]{0:T(1024)(128)(4,1)}), s8[4194304]{0:T(1024)(128)(4,1)S(1)}, s32[]{:S(2)}) async-start(s8[16777216]{0:T(1024)(128)(4,1)} %bitcast.91), calls=%async_computation.15 | async-start | bytes 8388608
  824.6 9.5 slice-start.2
  824.6 9.5 slice-start.3
  824.6 9.5 copy-start.12
  834.1 5.5 copy-start.13
  834.1 5.5 copy-start.14
  834.1 5.5 copy-start.15
  850.5 111.7 %all-to-all-start.1 = ((bf16[4,128,3072]{2,1,0:T(8,128)(2,1)}), bf16[4,128,3072]{2,1,0:T(8,128)(2,1)}, u32[]{:S(2)}, u32[]{:S(2)}) async-start(bf16[4,128,3072]{2,1,0:T(8,128)(2,1)} %bitcast.93), calls=%async_computation.5 | async-start | bytes 6291456 | tf_op jit(solution)/shard_map/all_to_all | solution.py:948
  970.1 7.6 copy-start.20
  970.2 7.6 copy-start.22
  974.0 18.1 %all-to-all-start = ((bf16[4,128,1024]{2,1,0:T(8,128)(2,1)}), bf16[4,128,1024]{2,1,0:T(8,128)(2,1)S(1)}, u32[]{:S(2)}, u32[]{:S(2)}) async-start(bf16[4,128,1024]{2,1,0:T(8,128)(2,1)} %bitcast.96), calls=%async_computation.4 | async-start | bytes 2097152 | tf_op jit(solution)/shard_map/all_to_all | solution.py:948
  997.9 3.6 collective-permute-start
  (10 other events, 28.3 us)
Sparse Core Ops, SparseCore 0:
  10.6 83.4 all-gather.4
  95.7 79.2 all-gather.6
  176.6 79.2 all-gather.10
  257.4 79.2 all-gather.8
  548.9 77.0 reduce-scatter.4
  633.7 77.1 reduce-scatter.6
  713.2 77.2 reduce-scatter.8
  847.5 77.1 reduce-scatter.10

commit v6 on v5

--- a/solution.py
+++ b/solution.py
@@ -2,6 +2,7 @@
 
 import jax
 import jax.numpy as jnp
+import numpy as np
 from jax import lax
 from jax.experimental import pallas as pl
 from jax.experimental.pallas import tpu as pltpu
@@ -48,13 +49,93 @@
     return (segment, parent, depth)
 
 
+def rope_freqs(width):
+    half = HEAD_DIM // 2
+    powers = -2.0 * (np.arange(width) % half) / HEAD_DIM
+    return np.power(ROPE_BASE, powers).astype(np.float32)[None, :]
+
+
 def rope_tables(depth, width):
-    half = HEAD_DIM // 2
-    lane = jnp.arange(width, dtype=jnp.int32)
-    freqs = jnp.power(ROPE_BASE, -(2.0 * (lane % half).astype(F32)) / HEAD_DIM)
-    angles = depth.astype(F32)[:, None] * freqs[None, :]
-    sign = jnp.where(lane % HEAD_DIM < half, -1.0, 1.0)
+    angles = depth.astype(F32)[:, None] * rope_freqs(width)
+    sign = np.where(np.arange(width) % HEAD_DIM < HEAD_DIM // 2, -1.0, 1.0).astype(np.float32)
     return jnp.cos(angles), jnp.sin(angles) * sign[None, :]
+
+
+def lay_out(segment, parent):
+    both = jnp.stack([segment, parent])
+    return jnp.pad(both, ((0, 6), (0, 0))), jnp.pad(both.T, ((0, 0), (0, 126)))
+
+
+TABLE_ROWS = 512
+TABLE_STEP = 64
+
+
+def tables_at(positions, lengths, parents):
+    leaves = parents.shape[1]
+    branches = lengths.shape[1] - leaves
+    zero = jnp.zeros_like(positions)
+    segment = jnp.where(positions >= TRUNK, 1, 0)
+    parent, depth = zero, positions
+    end = jnp.full((1, 1), TRUNK, jnp.int32)
+    starts = []
+    for s in range(branches + leaves):
+        start, end = end, end + lengths[:, s : s + 1]
+        inside = (positions >= start) & (positions < end)
+        base, above = jnp.full((1, 1), TRUNK, jnp.int32), jnp.zeros((1, 1), jnp.int32)
+        if s >= branches:
+            above = parents[:, s - branches : s - branches + 1]
+            for b in range(branches):
+                base = base + jnp.where(above == b + 1, lengths[:, b : b + 1], 0)
+        segment = segment + jnp.where(positions >= end, 1, 0)
+        parent = jnp.where(inside, above, parent)
+        depth = jnp.where(inside, positions - start + base, depth)
+    return segment, parent, depth
+
+
+def sine_cosine(x):
+    turns = jnp.floor(x * np.float32(2.0 / np.pi) + 0.5)
+    r = x - turns * np.float32(1.5703125)
+    r = r - turns * np.float32(4.837512969970703125e-4)
+    r = r - turns * np.float32(7.549789954891882e-8)
+    z = r * r
+    sine = ((np.float32(-1.9515295891e-4) * z + np.float32(8.3321608736e-3)) * z - np.float32(1.6666654611e-1)) * z * r + r
+    cosine = (
+        (np.float32(2.443315711809948e-5) * z - np.float32(1.388731625493765e-3)) * z + np.float32(4.166664568298827e-2)
+    ) * z * z - np.float32(0.5) * z + np.float32(1.0)
+    quarter = turns.astype(jnp.int32) & 3
+    odd = (quarter & 1) == 1
+    first, second = jnp.where(odd, cosine, sine), jnp.where(odd, sine, cosine)
+    return jnp.where(quarter >= 2, -first, first), jnp.where((quarter == 1) | (quarter == 2), -second, second)
+
+
+def table_work(lengths, parents, freqs, rows_ref, cols_ref, cos_ref, sin_ref, cols_buf, cos_buf, sin_buf, sems):
+    tokens = cos_ref.shape[0]
+    shape = (8, tokens)
+    segment, parent, _ = tables_at(lax.broadcasted_iota(jnp.int32, shape, 1), lengths, parents)
+    line = lax.broadcasted_iota(jnp.int32, shape, 0)
+    rows_ref[...] = jnp.where(line == 0, segment, jnp.where(line == 1, parent, 0))
+    copies = []
+    for chunk in range(tokens // TABLE_ROWS):
+        rows = pl.ds(chunk * TABLE_ROWS, TABLE_ROWS)
+
+        @pl.loop(0, TABLE_ROWS // TABLE_STEP)
+        def _(j, chunk=chunk):
+            first = pl.multiple_of(chunk * TABLE_ROWS + j * TABLE_STEP, TABLE_STEP)
+            taken = pl.ds(first, TABLE_STEP)
+            shape = (TABLE_STEP, 128)
+            lane = lax.broadcasted_iota(jnp.int32, shape, 1)
+            segment, parent, depth = tables_at(lax.broadcasted_iota(jnp.int32, shape, 0) + first, lengths, parents)
+            cols_buf[taken, :] = jnp.where(lane == 0, segment, jnp.where(lane == 1, parent, 0))
+            sine, cosine = sine_cosine(depth.astype(F32) * freqs[...])
+            cos_buf[taken, :] = cosine
+            sin_buf[taken, :] = jnp.where(lane % HEAD_DIM < HEAD_DIM // 2, -sine, sine)
+
+        for kind, (source, target) in enumerate(((cols_buf, cols_ref), (cos_buf, cos_ref), (sin_buf, sin_ref))):
+            copies.append(pltpu.make_async_copy(source.at[rows], target.at[rows], sems.at[kind, chunk]))
+            copies[-1].start()
+        yield
+    for copy in copies:
+        copy.wait()
 
 
 MESH = pl.DeviceIdType.MESH
@@ -349,7 +430,7 @@
 
 
 def fwd_work(
-    heads, q_ref, k_ref, v_ref, cos_ref, sin_ref, segk_ref, segq_ref,
+    heads, q_ref, k_ref, v_ref, cos_ref, sin_ref, rows_ref, cols_ref,
     o_ref, lse_ref, qr_ref, kr_ref, vr_ref, kt_ref, va_ref, s_ref, m_ref, acc_ref,
 ):
     i = pl.program_id(1)
@@ -391,7 +472,7 @@
                 kind,
                 lax.broadcasted_iota(jnp.int32, shape, 0) + i * BQ,
                 lax.broadcasted_iota(jnp.int32, shape, 1) + start,
-                segq_ref[:, 0:1], segq_ref[:, 1:2], segk_ref[:, keys],
+                cols_ref[:, 0:1], cols_ref[:, 1:2], rows_ref[0:1, keys],
             )
         for h in range(heads):
             s = dot_n(q_heads[h], k)
@@ -444,7 +525,7 @@
 
 
 def bwd_work(
-    heads, q_ref, k_ref, v_ref, o_ref, do_ref, lse_ref, cos_ref, sin_ref, segk_ref, segq_ref,
+    heads, q_ref, k_ref, v_ref, o_ref, do_ref, lse_ref, cos_ref, sin_ref, rows_ref, cols_ref,
     dq_ref, dk_ref, dv_ref, dq_acc, dk_acc, dv_acc,
 ):
     i = pl.program_id(1)
@@ -483,7 +564,7 @@
                 kind,
                 lax.broadcasted_iota(jnp.int32, shape, 1) + i * BQ,
                 lax.broadcasted_iota(jnp.int32, shape, 0) + start,
-                segq_ref[0:1, :], segq_ref[1:2, :], segk_ref[keys, :],
+                rows_ref[0:1, :], rows_ref[1:2, :], cols_ref[keys, 0:1],
             )
         probs, grads, k_heads = [], [], []
         for h in range(heads):
@@ -519,7 +600,7 @@
     return pl.CostEstimate(flops=1 << 20, bytes_accessed=1 << 20, transcendentals=0)
 
 
-def attention_forward(qkv, cosine, sine, seg_keys, seg_queries, width, hosted=None):
+def attention_forward(qkv, cosine, sine, rows_table, cols_table, width, hosted=None):
     tree_len = qkv.shape[0]
     gw = min(2 * HEAD_DIM, width)
     groups, heads = width // gw, gw // HEAD_DIM
@@ -543,8 +624,8 @@
             pl.BlockSpec((tree_len, gw), lambda g, i: (0, 2 * step + g)),
             table,
             table,
-            pl.BlockSpec((1, tree_len), lambda g, i: (0, 0)),
-            pl.BlockSpec((BQ, 2), lambda g, i: (i, 0)),
+            pl.BlockSpec((8, tree_len), lambda g, i: (0, 0)),
+            pl.BlockSpec((BQ, 128), lambda g, i: (i, 0)),
         ]
         + [hbm] * hosts,
         out_specs=[row_block, pl.BlockSpec((1, heads, BQ), lambda g, i: (g, 0, i)), row_block, full, full] + [hbm] * hosts,
@@ -563,10 +644,10 @@
         ),
         cost_estimate=small_cost(),
         name="tree_attention_forward",
-    )(queries, keys, values, cosine, sine, seg_keys, seg_queries, *([hosted] if hosts else []))
-
-
-def attention_backward(q, k, v, out, grad, lse, cosine, sine, seg_keys, seg_queries, hosted=None):
+    )(queries, keys, values, cosine, sine, rows_table, cols_table, *([hosted] if hosts else []))
+
+
+def attention_backward(q, k, v, out, grad, lse, cosine, sine, rows_table, cols_table, hosted=None):
     tree_len, width = q.shape
     gw = min(2 * HEAD_DIM, width)
     groups, heads = width // gw, gw // HEAD_DIM
@@ -583,8 +664,8 @@
             row_block, full, full, row_block, row_block,
             pl.BlockSpec((1, heads, BQ), lambda g, i: (g, 0, i)),
             table, table,
-            pl.BlockSpec((tree_len, 1), lambda g, i: (0, 0)),
-            pl.BlockSpec((2, BQ), lambda g, i: (0, i)),
+            pl.BlockSpec((8, BQ), lambda g, i: (0, i)),
+            pl.BlockSpec((tree_len, 128), lambda g, i: (0, 0)),
         ]
         + [hbm] * hosts,
         out_specs=[row_block, full, full] + [hbm] * hosts,
@@ -601,7 +682,7 @@
         ),
         cost_estimate=small_cost(),
         name="tree_attention_backward",
-    )(q, k, v, out, grad, lse, cosine, sine, seg_keys.T, seg_queries.T, *([hosted] if hosts else []))
+    )(q, k, v, out, grad, lse, cosine, sine, rows_table, cols_table, *([hosted] if hosts else []))
 
 
 TOKENS_AT_ONCE = 2048
@@ -665,7 +746,7 @@
         pass
 
 
-def row_product(left_ref, right_ref, out_ref, left_buf, right_buf, out_buf, sems):
+def row_product(turned, left_ref, right_ref, out_ref, left_buf, right_buf, out_buf, sems):
     groups = left_ref.shape[0] // LEFT_AT_ONCE
 
     def rows(group):
@@ -688,10 +769,14 @@
         if group > 1:
             store(group - 2).wait()
 
-        @pl.loop(0, right_ref.shape[1] // STEP)
+        @pl.loop(0, out_ref.shape[1] // STEP)
         def _(j, group=group):
             columns = pl.ds(pl.multiple_of(j * STEP, STEP), STEP)
-            out_buf[group % 2, :, columns] = dot_n(left_buf[group % 2], right_buf[:, columns]).astype(BF16)
+            if turned:
+                part = dot_t(left_buf[group % 2], right_buf[columns, :])
+            else:
+                part = dot_n(left_buf[group % 2], right_buf[:, columns])
+            out_buf[group % 2, :, columns] = part.astype(BF16)
 
         store(group).start()
         yield
@@ -699,57 +784,101 @@
         store(group).wait()
 
 
-def row_product_buffers(depth, columns):
+def row_product_buffers(right, turned):
     return [
-        pltpu.VMEM((2, LEFT_AT_ONCE, depth), BF16),
-        pltpu.VMEM((depth, columns), BF16),
-        pltpu.VMEM((2, LEFT_AT_ONCE, columns), BF16),
+        pltpu.VMEM((2, LEFT_AT_ONCE, right.shape[1 if turned else 0]), BF16),
+        pltpu.VMEM(right.shape, BF16),
+        pltpu.VMEM((2, LEFT_AT_ONCE, right.shape[0 if turned else 1]), BF16),
         pltpu.SemaphoreType.DMA((5,)),
     ]
 
 
-def gather_kernel(kind, jobs, *refs):
-    own_ref, lefts, rights = refs[0], refs[1 : 1 + jobs], refs[1 + jobs : 1 + 2 * jobs]
-    all_ref, outs, refs = refs[1 + 2 * jobs], refs[2 + 2 * jobs : 2 + 3 * jobs], refs[2 + 3 * jobs :]
-    gather, buffers = PlaneGather(own_ref, all_ref, *refs[:3]), refs[3:]
-
-    def work():
-        for job in range(jobs):
-            yield from kind(lefts[job], rights[job], outs[job], *buffers)
-
-    work = work()
+def gather_kernel(works, counts, paces, *refs):
+    def take(count):
+        nonlocal refs
+        taken, refs = refs[:count], refs[count:]
+        return taken
+
+    (own_ref,) = take(1)
+    inputs = [take(count[0]) for count in counts]
+    (all_ref,) = take(1)
+    outputs = [take(count[1]) for count in counts]
+    gather = PlaneGather(own_ref, all_ref, *take(3))
+    buffers, held = [], {}
+    for work, count in zip(works, counts):
+        if work not in held:
+            held[work] = take(count[2])
+        buffers.append(held[work])
+
+    def all_work():
+        for work, given, wanted, room in zip(works, inputs, outputs, buffers):
+            yield from work(*given, *wanted, *room)
+
+    going = all_work()
 
     def some(count):
         for _ in range(count):
-            next(work, None)
+            next(going, None)
 
     gather.start()
-    some(4)
+    some(paces[0])
     gather.first()
-    some(4)
+    some(paces[1])
     gather.second()
-    finish(work)
+    finish(going)
     gather.finish()
 
 
-def plane_gather(rows, kind=None, jobs=(), buffers=(), shape=()):
+def plane_gather(rows, collective_id=0, jobs=(), paces=(0, 0)):
     count, width = rows.shape
     hbm = pl.BlockSpec(memory_space=pl.ANY)
-    outputs = [jax.ShapeDtypeStruct((8 * count, width), rows.dtype)] + [jax.ShapeDtypeStruct(shape, BF16)] * len(jobs)
+    scratch, held = gather_sems(), set()
+    for work, _, _, _, _, buffers in jobs:
+        if work not in held:
+            held.add(work)
+            scratch += buffers
     return pl.pallas_call(
-        functools.partial(gather_kernel, kind, len(jobs)),
-        in_specs=[hbm] * (1 + 2 * len(jobs)),
-        out_specs=[hbm] * len(outputs),
-        out_shape=outputs,
-        scratch_shapes=gather_sems() + list(buffers),
+        functools.partial(
+            gather_kernel,
+            [job[0] for job in jobs],
+            [(len(job[1]), len(job[3]), len(job[5])) for job in jobs],
+            paces,
+        ),
+        in_specs=[hbm] + [spec for job in jobs for spec in job[2]],
+        out_specs=[hbm] + [spec for job in jobs for spec in job[4]],
+        out_shape=[jax.ShapeDtypeStruct((8 * count, width), rows.dtype)] + [out for job in jobs for out in job[3]],
+        scratch_shapes=scratch,
         compiler_params=pltpu.CompilerParams(
-            collective_id=0 if kind is None else 4 if kind is token_product else 5,
-            has_side_effects=True,
-            vmem_limit_bytes=None if kind is None else 48 << 20,
+            collective_id=collective_id, has_side_effects=True, vmem_limit_bytes=(48 << 20) if jobs else None
         ),
         cost_estimate=small_cost(),
         name="plane_gather",
-    )(rows, *[left for left, _ in jobs], *[right for _, right in jobs])
+    )(rows, *[value for job in jobs for value in job[1]])
+
+
+HBM = pl.BlockSpec(memory_space=pl.ANY)
+VMEM = pl.BlockSpec(memory_space=pltpu.VMEM)
+ROWS_TURNED = functools.partial(row_product, True)
+ROWS_STRAIGHT = functools.partial(row_product, False)
+
+
+def token_job(left, right):
+    out = jax.ShapeDtypeStruct((left.shape[1], right.shape[1]), BF16)
+    return token_product, [left, right], [HBM] * 2, [out], [HBM], product_buffers(right.shape[1])
+
+
+def row_job(left, right, turned):
+    out = jax.ShapeDtypeStruct((left.shape[0], right.shape[0 if turned else 1]), BF16)
+    work = ROWS_TURNED if turned else ROWS_STRAIGHT
+    return work, [left, right], [HBM] * 2, [out], [HBM], row_product_buffers(right, turned)
+
+
+def table_job(lengths, parents, tokens):
+    outs = [jax.ShapeDtypeStruct((8, tokens), jnp.int32), jax.ShapeDtypeStruct((tokens, 128), jnp.int32)]
+    outs += [jax.ShapeDtypeStruct((tokens, 128), F32)] * 2
+    room = [pltpu.VMEM(out.shape, out.dtype) for out in outs[1:]]
+    room += [pltpu.SemaphoreType.DMA((3, tokens // TABLE_ROWS))]
+    return table_work, [lengths, parents, rope_freqs(128)], [VMEM] * 3, outs, [VMEM, HBM, HBM, HBM], room
 
 
 def scatter_kernel(rows, parts, jobs, *refs):
@@ -841,7 +970,6 @@
                 remote(core_in.at[piece], first_in.at[piece], 8 + piece, over_x if piece % 2 == 0 else over_row)
             )
             first_copies[-1].start()
-    work(0)
     for part in range(2):
         first_copies[part].wait_recv()
 
@@ -852,7 +980,8 @@
 
         next_copies.append(remote(core_in.at[4 + part], next_in.at[part], 12 + part, over_row if part == 0 else over_x))
         next_copies[-1].start()
-    work(1)
+    for job in range(jobs):
+        work(job)
     for part in range(2):
         first_copies[2 + part].wait_recv()
         next_copies[part].wait_recv()
@@ -913,18 +1042,22 @@
     return plane_gather(rows)[0] if is_plane() else gather_rows(rows)
 
 
-def gather_with_token_products(rows, jobs):
+def gather_with_tables(rows, lengths, parents, tokens, width):
     if is_plane():
-        columns = jobs[0][1].shape[1]
-        return plane_gather(rows, token_product, jobs, product_buffers(columns), (jobs[0][0].shape[1], columns))
-    return [gather_rows(rows)] + [dot_tn(left, right).astype(BF16) for left, right in jobs]
-
-
-def gather_with_row_product(rows, left, right):
+        return plane_gather(rows, 8, [table_job(lengths, parents, tokens)], (4, 4))
+    segment, parent, depth = tree_tables(lengths[0], parents[0], tokens)
+    return [gather_rows(rows), *lay_out(segment, parent), *rope_tables(depth, width)]
+
+
+def gather_with_products(rows, collective_id, token_pairs, row_pairs):
     if is_plane():
-        shape = (left.shape[0], right.shape[1])
-        return plane_gather(rows, row_product, [(left, right)], row_product_buffers(*right.shape), shape)
-    return gather_rows(rows), dot_n(left, right).astype(BF16)
+        jobs = [token_job(*pair) for pair in token_pairs] + [row_job(*pair) for pair in row_pairs]
+        return plane_gather(rows, collective_id, jobs, (4, 4))
+    return (
+        [gather_rows(rows)]
+        + [dot_tn(left, right).astype(BF16) for left, right in token_pairs]
+        + [(dot_t if turned else dot_n)(left, right).astype(BF16) for left, right, turned in row_pairs]
+    )
 
 
 def product_scatter(parts, weights, collective_id, jobs=()):
@@ -942,12 +1075,15 @@
     return lax.psum_scatter(grad.astype(BF16), "fsdp", scatter_dimension=0, tiled=True)
 
 
-def swap_columns(part, count):
+def swap_rows(part):
     size = lax.axis_size("ctx")
-    rows, columns = part.shape[0] // size, part.shape[1] // count
-    got = lax.all_to_all(part.reshape(size, rows, count * columns), "ctx", split_axis=0, concat_axis=0)
+    return lax.all_to_all(part.reshape(size, part.shape[0] // size, -1), "ctx", split_axis=0, concat_axis=0)
+
+
+def lay_side_by_side(got, count):
+    columns = got.shape[2] // count
     return [
-        jnp.concatenate([got[j, :, c * columns : (c + 1) * columns] for j in range(size)], axis=1).astype(F32)
+        jnp.concatenate([got[j, :, c * columns : (c + 1) * columns] for j in range(got.shape[0])], axis=1).astype(F32)
         for c in range(count)
     ]
 
@@ -995,29 +1131,25 @@
     w_gate = gather_weight(mine(gate_weight, units))
     w_down = gather_weight(mine(down_weight, units))
     w_up = gather_weight(mine(up_weight, units))
-    attn_in = gather_now((attn_scaled * attn_gain[None, :]).astype(BF16))
+    attn_in, rows_table, cols_table, cosine, sine = gather_with_tables(
+        (attn_scaled * attn_gain[None, :]).astype(BF16), seg_lengths, leaf_parent, tree_len, min(2 * HEAD_DIM, width)
+    )
     w_qkv, w_out = w_attn[:, : 3 * width], w_attn[:, 3 * width :]
-
-    attn_in, lengths_row, parent_row = lax.optimization_barrier((attn_in, seg_lengths[0], leaf_parent[0]))
-    segment, parent, depth = tree_tables(lengths_row, parent_row, tree_len)
-    cosine, sine = rope_tables(depth, min(2 * HEAD_DIM, width))
-    seg_keys = segment[None, :]
-    seg_queries = jnp.stack([segment, parent], axis=1)
 
     qkv = jnp.dot(attn_in, w_qkv, preferred_element_type=F32)
     if is_plane():
         attn_out, lse, query_rows, key_rows, value_rows, cot_all = attention_forward(
-            qkv, cosine, sine, seg_keys, seg_queries, width, cotangent
+            qkv, cosine, sine, rows_table, cols_table, width, cotangent
         )
     else:
         attn_out, lse, query_rows, key_rows, value_rows = attention_forward(
-            qkv, cosine, sine, seg_keys, seg_queries, width
+            qkv, cosine, sine, rows_table, cols_table, width
         )
         cot_all = gather_rows(cotangent)
     mid_rows = x_rows + product_scatter([attn_out], [w_out], 1)[0]
     mlp_scaled, mlp_inv = normalize(mid_rows)
     mlp_own = (mlp_scaled * mlp_gain[None, :]).astype(BF16)
-    mlp_in, hidden_grad = gather_with_row_product(mlp_own, cot_all, w_down)
+    mlp_in, hidden_grad = gather_with_products(mlp_own, 5, [], [(cot_all, w_down, False)])
 
     gate = jnp.dot(mlp_in, w_gate, preferred_element_type=F32)
     up_proj = jnp.dot(mlp_in, w_up, preferred_element_type=F32)
@@ -1034,8 +1166,8 @@
     )
     down_grad = scatter_weight(down_part)
     mid_grad = cotangent.astype(F32) + norm_backward(mlp_in_grad, mlp_scaled, mlp_inv, mlp_gain)
-    mid_all, up_part, gate_part = gather_with_token_products(
-        mid_grad.astype(BF16), [(mlp_in, up_rows_grad), (mlp_in, gate_rows_grad)]
+    mid_all, up_part, gate_part, down_rows = gather_with_products(
+        mid_grad.astype(BF16), 4, [(mlp_in, up_rows_grad), (mlp_in, gate_rows_grad)], [(hidden, w_down, True)]
     )
     up_grad = scatter_weight(up_part)
     gate_grad = scatter_weight(gate_part)
@@ -1043,25 +1175,25 @@
     out_heads_grad = jnp.dot(mid_all, w_out, preferred_element_type=F32).astype(BF16)
     output_grad = dot_tn(mid_all, attn_out).astype(BF16)
     out_heads_grad, down_grad = lax.optimization_barrier((out_heads_grad, down_grad))
-    down_rows = dot_t(hidden, w_down).astype(BF16)
     if is_plane():
         *pre_grads, down_rows = attention_backward(
-            query_rows, key_rows, value_rows, attn_out, out_heads_grad, lse, cosine, sine, seg_keys, seg_queries, down_rows
+            query_rows, key_rows, value_rows, attn_out, out_heads_grad, lse, cosine, sine, rows_table, cols_table, down_rows
         )
     else:
         pre_grads = attention_backward(
-            query_rows, key_rows, value_rows, attn_out, out_heads_grad, lse, cosine, sine, seg_keys, seg_queries
+            query_rows, key_rows, value_rows, attn_out, out_heads_grad, lse, cosine, sine, rows_table, cols_table
         )
         down_rows = scatter_rows(down_rows)
     block_out = (mid_rows + down_rows.astype(F32)).astype(BF16)
-    pre_grads, up_grad = lax.optimization_barrier((pre_grads, up_grad))
+    pre_grads, up_grad, gate_grad = lax.optimization_barrier((pre_grads, up_grad, gate_grad))
+    swapped = swap_rows(jnp.concatenate([gate_grad, up_grad, down_grad], axis=1))
     attn_part = jnp.concatenate([dot_tn(attn_in, grad).astype(BF16) for grad in pre_grads] + [output_grad], axis=1)
-    pre_grads, attn_part, gate_grad = lax.optimization_barrier((pre_grads, attn_part, gate_grad))
+    pre_grads, attn_part, swapped = lax.optimization_barrier((pre_grads, attn_part, swapped))
     attn_grad = scatter_weight(attn_part)
     (attn_in_grad,) = product_scatter(pre_grads, [w_attn[:, j * width : (j + 1) * width] for j in range(3)], 2)
     attn_in_grad, attn_grad = lax.optimization_barrier((attn_in_grad, attn_grad))
-    gate_out, up_out, down_out = swap_columns(jnp.concatenate([gate_grad, up_grad, down_grad], axis=1), 3)
-    query_out, key_out, value_out, output_out = swap_columns(attn_grad, 4)
+    gate_out, up_out, down_out = lay_side_by_side(swapped, 3)
+    query_out, key_out, value_out, output_out = lay_side_by_side(swap_rows(attn_grad), 4)
 
     def gain_part(pairs, gain):
         held = query_out.shape[0]

time: 1020 us -> 970 us (0.951)
  Pallas kernels: 742 us -> 721 us
  matrix products: 150 us -> 131 us
  other arithmetic: 60 us -> 44.5 us
  waiting for transfers between devices: 4.66 us -> 15.7 us
    pallas_call x3, Pallas kernels: 297 us -> 257 us  [plane_scatter(): pl.pallas_call(functools.partial(scatter_kernel, rows, len(parts), len(jo...]
    dot_general x1 -> x0, matrix products: 22.5 us -> none  [dot_t(): lax.dot_general(a, b, (((1,), (1,)), ((), ())), preferred_element_type=F32)]
    pallas_call x3, Pallas kernels: 226 us -> 245 us  [plane_gather(): pl.pallas_call(functools.partial(gather_kernel, [job[0] for job in jobs],...]
  transfers between devices with their start and end apart: 11 -> 11, of which waited for: 2 -> 4; matrix products, arithmetic and copies ran while one was open for 18% -> 14% of each run, Pallas kernels for 63% -> 65%
where the time goes in v6:
time: 970 us; the launch traced here: 962 us
  Pallas kernels  721 us (74%)
  matrix products  131 us (14%)
  other arithmetic  44.5 us (5%)
  local copies, waits for them, and re-layouts  25.2 us (3%)
  waiting for transfers between devices  15.7 us (2%)
  between operations  14.7 us (2%)
    pallas_call x3, Pallas kernels, plane_scatter(): pl.pallas_call(functools.partial(scatter_kernel, rows, len(parts), len(jo...  257 us
    pallas_call x3, Pallas kernels, plane_gather(): pl.pallas_call(functools.partial(gather_kernel, [job[0] for job in jobs],...  245 us
    pallas_call x1, Pallas kernels, attention_backward(): pl.pallas_call(functools.partial(bwd_kernel, heads, hosts), grid=(groups,...  131 us
    pallas_call x1, Pallas kernels, attention_forward(): pl.pallas_call(functools.partial(fwd_kernel, heads, hosts), grid=(groups,...  88.1 us
    dot_general x4, matrix products, dot_tn(): lax.dot_general(a, b, (((0,), (0,)), ((), ())), preferred_element_type=F32)  40.7 us
    dot_general x1, matrix products, body(): up_proj = jnp.dot(mlp_in, w_up, preferred_element_type=F32)  35.3 us
    dot_general x1, matrix products, body(): gate = jnp.dot(mlp_in, w_gate, preferred_element_type=F32)  23.4 us
    dot_general x1, matrix products, body(): qkv = jnp.dot(attn_in, w_qkv, preferred_element_type=F32)  19.9 us
  transfers between devices with their start and end apart: 11, of which 4 were waited for; matrix products, arithmetic and copies ran while one was open for 14% of the time, Pallas kernels for 65%

profile of v6, /device:TPU:0, one launch (start us, length us, event | category | flops | bytes accessed | tf_op | source)
XLA Modules:
  0.0 961.7 jit_solution(8334765070957423561)
XLA Ops:
  10.6 2.3 constant_dynamic-slice_fusion.4
  12.9 2.4 constant_dynamic-slice_fusion.2
  15.4 2.3 constant_dynamic-slice_fusion.3
  20.8 77.3 %plane_gather.3 = (bf16[4096,2048]{1,0:T(8,128)(2,1)}, s32[8,4096]{1,0:T(8,128)S(1)}, s32[4096,128]{1,0:T(8,128)S(1)}, f32[4096,128]{1,0:T(8,128)S(1)}, f32[4096,128]{1,0:T(8,128)}) custom-call(bf16[512,2048]{1,0:T(8,128)(2,1)} %fusion.8.refs_0_, s32[1,20]{1,0:T(1,128)S(1)} %copy-done.3, s32[1,16]{1,0:T(1,128)S(1)} %copy-done.4, f32[1,128]{1,0:T(1,128)S(1)} %copy-done.5), custom_call_target="tpu_custom_call" | custom-call | flops 1048576 | bytes 1048576 | tf_op jit(solution)/shard_map/plane_gather/pallas_call | solution.py:840
  101.3 19.9 %fusion.15.refs_0_.refs_1_.refs_2_ = f32[4096,768]{1,0:T(8,128)} fusion(bf16[4096,2048]{1,0:T(8,128)(2,1)} %get-tuple-element.48, bf16[2048,1024]{1,0:T(8,128)(2,1)} %all-gather.5.cloned.1.call-done), kind=kOutput, calls=%fused_computation.29 | convolution fusion | flops 12884901888 | bytes 32505856 | tf_op jit(solution)/shard_map/dot_general | solution.py:1139
  121.2 88.1 %tree_attention_forward.1 = (bf16[4096,256]{1,0:T(8,128)(2,1)}, f32[2,2,4096]{2,1,0:T(2,128)}, bf16[4096,256]{1,0:T(8,128)(2,1)}, bf16[4096,256]{1,0:T(8,128)(2,...) custom-call(f32[4096,768]{1,0:T(8,128)} %fusion.15.refs_0_.refs_1_.refs_2_, ...), custom_call_target="tpu_custom_call" | custom-call | flops 1048576 | bytes 1048576 | tf_op jit(solution)/shard_map/tree_attention_forward/pallas_call | solution.py:618
  210.9 80.2 %plane_scatter.3 = f32[512,2048]{1,0:T(8,128)} custom-call(bf16[4096,256]{1,0:T(8,128)(2,1)} %get-tuple-element.53.refs_0_.refs_3_, bf16[2048,256]{1,0:T(8,128)(2,1)S(1)} %get-tuple-element.103.refs_1_), custom_call_target="tpu_custom_call" | custom-call | flops 1048576 | bytes 1048576 | tf_op jit(solution)/shard_map/plane_scatter/pallas_call | solution.py:1005
  291.1 3.0 multiply_reduce_fusion.1
  296.0 74.4 %plane_gather.4 = (bf16[4096,2048]{1,0:T(8,128)(2,1)}, bf16[4096,1024]{1,0:T(8,128)(2,1)}) custom-call(bf16[512,2048]{1,0:T(8,128)(2,1)S(1)} %multiply_convert_fusion.1.refs_0_, bf16[4096,2048]{1,0:T(8,128)(2,1)} %get-tuple-element.57.refs_1_.refs_4_, bf16[2048,1024]{1,0:T(8,128)(2,1)} %all-gather.7.cloned.1.call-done.refs_2_.refs_6_), custom_call_target="tpu_custom_call" | custom-call | flops 1048576 | bytes 1048576 | tf_op jit(solution)/shard_map/plane_gather/pallas_call | solution.py:840
  370.5 23.4 %fusion.23 = f32[4096,1024]{1,0:T(8,128)} fusion(bf16[4096,2048]{1,0:T(8,128)(2,1)} %get-tuple-element.59.refs_1_.refs_3_, bf16[2048,1024]{1,0:T(8,128)(2,1)} %all-gather.11.cloned.1.call-done.refs_2_), kind=kOutput, calls=%fused_computation.101 | convolution fusion | flops 17179869184 | bytes 37748736 | tf_op jit(solution)/shard_map/dot_general | solution.py:1154
  393.9 35.3 %multiply_convert_fusion = (bf16[4096,1024]{1,0:T(8,128)(2,1)}, bf16[4096,1024]{1,0:T(8,128)(2,1)}, bf16[4096,1024]{1,0:T(8,128)(2,1)}) fusion(f32[4096,1024]{1,0:T(8,128)} %fusion.23, bf16[4096,1024]{1,0:T(8,128)(2,1)} %get-tuple-element.58, bf16[4096,2048]{1,0:T(8,128)(2,1)} %get-tuple-element.59.refs_1_.refs_3_, ...), kind=kOutput, calls=%fused_computation.7 | convolution fusion | flops 17251172352 | bytes 71303168 | tf_op jit(solution)/shard_map/dot_general | solution.py:1155
  429.2 92.4 %plane_scatter.4 = (f32[512,2048]{1,0:T(8,128)}, bf16[2048,1024]{1,0:T(8,128)(2,1)}) custom-call(bf16[4096,1024]{1,0:T(8,128)(2,1)} %get-tuple-element.96.refs_0_.refs_4_, bf16[4096,1024]{1,0:T(8,128)(2,1)} %get-tuple-element.97.refs_1_.refs_2_, bf16[2048,1024]{1,0:T(8,128)(2,1)} %all-gather.11.cloned.1.call-done.refs_2_, ...), custom_call_target="tpu_custom_call" | custom-call | flops 1048576 | bytes 1048576 | tf_op jit(solution)/shard_map/plane_scatter/pallas_call | solution.py:1005
  523.2 4.5 multiply_reduce_fusion
  532.0 93.7 %plane_gather.5 = (bf16[4096,2048]{1,0:T(8,128)(2,1)}, bf16[2048,1024]{1,0:T(8,128)(2,1)}, bf16[2048,1024]{1,0:T(8,128)(2,1)}, bf16[4096,2048]{1,0:T(8,128)(2,1)}) custom-call(bf16[512,2048]{1,0:T(8,128)(2,1)S(1)} %fusion.21.refs_0_, bf16[4096,2048]{1,0:T(8,128)(2,1)} %get-tuple-element.59.refs_1_.refs_3_, ...), custom_call_target="tpu_custom_call" | custom-call | flops 1048576 | bytes 1048576 | tf_op jit(solution)/shard_map/plane_gather/pallas_call | solution.py:840
  626.5 12.5 %convolution_convert_fusion.1 = bf16[2048,256]{0,1:T(8,128)(2,1)} fusion(bf16[4096,2048]{1,0:T(8,128)(2,1)} %get-tuple-element.61, bf16[4096,256]{1,0:T(8,128)(2,1)} %get-tuple-element.53.refs_0_.refs_3_), kind=kOutput, calls=%fused_computation.32 | convolution fusion | flops 4295491584 | bytes 19922944 | tf_op jit(solution)/shard_map/dot_general | solution.py:369
  639.0 11.9 %convolution_convert_fusion.refs_4_ = bf16[4096,256]{1,0:T(8,128)(2,1)} fusion(bf16[4096,2048]{1,0:T(8,128)(2,1)} %get-tuple-element.61, bf16[2048,1024]{1,0:T(8,128)(2,1)} %all-gather.5.cloned.1.call-done), kind=kOutput, calls=%fused_computation.15 | convolution fusion | flops 4296015872 | bytes 19922944 | tf_op jit(solution)/shard_map/dot_general | solution.py:1175
  650.9 130.7 %tree_attention_backward.1 = (bf16[4096,256]{1,0:T(8,128)(2,1)}, bf16[4096,256]{1,0:T(8,128)(2,1)}, bf16[4096,256]{1,0:T(8,128)(2,1)}, bf16[512,2048]{1,0:T(8,128)(2,1)}) custom-call(bf16[4096,256]{1,0:T(8,128)(2,1)} %get-tuple-element.54.refs_0_, bf16[4096,256]{1,0:T(8,128)(2,1)} %get-tuple-element.55.refs_1_, bf16[4096,256]{1,0:T(8,128)(2,1)} %get-tuple-element.56.refs_2_, ...), custom_call_target="tpu_custom_call" | custom-call | flops 1048576 | bytes 1048576 | tf_op jit(solution)/shard_map/tree_attention_backward/pallas_call | solution.py:660
  782.6 3.1 pad_maximum_fusion.1
  785.7 4.7 all-to-all-start
  790.5 11.0 %convolution_convert_fusion.4 = bf16[2048,256]{0,1:T(8,128)(2,1)S(1)} fusion(bf16[4096,2048]{1,0:T(8,128)(2,1)} %get-tuple-element.48, bf16[4096,256]{1,0:T(8,128)(2,1)} %get-tuple-element.78.refs_0_), kind=kOutput, calls=%fused_computation.35 | convolution fusion | flops 4295491584 | bytes 19922944 | tf_op jit(solution)/shard_map/dot_general | solution.py:369
  801.5 8.7 convolution_convert_fusion.3
  810.2 8.4 convolution_convert_fusion.2
  818.7 2.3 pad_maximum_fusion
  821.0 6.4 all-to-all-done
  827.4 84.1 %plane_scatter.5 = f32[512,2048]{1,0:T(8,128)} custom-call(bf16[4096,256]{1,0:T(8,128)(2,1)} %get-tuple-element.78.refs_0_, bf16[4096,256]{1,0:T(8,128)(2,1)} %get-tuple-element.79.refs_1_, bf16[4096,256]{1,0:T(8,128)(2,1)} %get-tuple-element.80.refs_2_, bf16[2048,256]{1,0:T(8,128)(2,1)S(1)} %get-tuple-element.102.refs_3_, ...), custom_call_target="tpu_custom_call" | custom-call | flops 1048576 | bytes 1048576 | tf_op jit(solution)/shard_map/plane_scatter/pallas_call | solution.py:1005
  913.7 2.9 multiply_reduce_fusion.2
  916.6 2.9 multiply_reduce_fusion.3
  921.2 2.3 copy.26
  923.5 3.0 fusion.9
  926.5 3.8 all-to-all-start.1
  930.3 8.9 fusion.13
  939.2 5.5 all-to-all-done.1
  (95 shorter events, 34.5 us)
Async XLA Ops:
  7.2 94.1 %all-gather.5.cloned.1.call-start = ((), (), s32[]{:S(2)}) async-start(), calls=%async_computation.6 | async-start | bytes 5242880 | tf_op jit(solution)/shard_map/all_gather | solution.py:1071
  10.5 285.4 %all-gather.7.cloned.1.call-start = ((), (), s32[]{:S(2)}) async-start(), calls=%async_computation.7 | async-start | bytes 5242880 | tf_op jit(solution)/shard_map/all_gather | solution.py:1071
  12.9 4.9 copy-start.8
  12.9 6.0 copy-start.18
  12.9 357.6 %all-gather.11.cloned.1.call-start = ((), (), s32[]{:S(2)}) async-start(), calls=%async_computation.9 | async-start | bytes 5242880 | tf_op jit(solution)/shard_map/all_gather | solution.py:1071
  15.4 378.5 %all-gather.9.cloned.1.call-start = ((), (), s32[]{:S(2)}) async-start(), calls=%async_computation.8 | async-start | bytes 5242880 | tf_op jit(solution)/shard_map/all_gather | solution.py:1071
  17.7 3.0 copy-start.3
  17.7 3.0 copy-start.4
  17.7 3.0 copy-start.5
  17.7 633.2 %reduce-scatter.5.cloned.1.call-start = ((), (), s32[]{:S(2)}) async-start(), calls=%async_computation.10 | async-start | bytes 5242880 | tf_op jit(solution)/shard_map/reduce_scatter | solution.py:1075
  98.0 1.3 copy-start
  99.3 1.3 copy-start.1
  100.7 0.7 copy-start.2
  121.2 88.1 %copy-start.13 = (bf16[2048,1024]{1,0:T(8,128)(2,1)S(1)}, bf16[2048,1024]{1,0:T(8,128)(2,1)}, u32[]{:S(2)}) copy-start(bf16[2048,1024]{1,0:T(8,128)(2,1)} %all-gather.5.cloned.1.call-done) | copy-start | bytes 12582916
  210.9 83.2 %copy-start.17 = (f32[2048]{0:T(1024)S(1)}, f32[2048]{0:T(1024)}, u32[]{:S(2)}) copy-start(f32[2048]{0:T(1024)} %param.20) | copy-start | bytes 24580
  291.1 3.5 copy-start.6
  291.1 4.2 copy-start.9
  521.6 1.6 copy-start.10
  521.6 260.1 %reduce-scatter.7.cloned.1.call-start = ((), (), s32[]{:S(2)}) async-start(), calls=%async_computation.11 | async-start | bytes 5242880 | tf_op jit(solution)/shard_map/reduce_scatter | solution.py:1075
  523.1 4.7 copy-start.7
  523.2 6.7 copy-start.11
  523.2 7.3 copy-start.12
  625.7 156.8 %reduce-scatter.9.cloned.1.call-start = ((), (), s32[]{:S(2)}) async-start(), calls=%async_computation.12 | async-start | bytes 5242880 | tf_op jit(solution)/shard_map/reduce_scatter | solution.py:1075
  785.7 41.7 %all-to-all-start = ((bf16[4,128,3072]{2,1,0:T(8,128)(2,1)}), bf16[4,128,3072]{2,1,0:T(8,128)(2,1)}, u32[]{:S(2)}, u32[]{:S(2)}) async-start(bf16[4,128,3072]{2,1,0:T(8,128)(2,1)} %bitcast.80), calls=%async_computation.3 | async-start | bytes 6291456 | tf_op jit(solution)/shard_map/all_to_all | solution.py:1080
  790.4 130.8 %reduce-scatter.11.cloned.1.call-start = ((), (), s32[]{:S(2)}) async-start(), calls=%async_computation.13 | async-start | bytes 5242880 | tf_op jit(solution)/shard_map/reduce_scatter | solution.py:1075
  790.4 11.1 %copy-start.14 = (bf16[4096,256]{1,0:T(8,128)(2,1)S(1)}, bf16[4096,256]{1,0:T(8,128)(2,1)}, u32[]{:S(2)}) copy-start(bf16[4096,256]{1,0:T(8,128)(2,1)} %get-tuple-element.79.refs_1_) | copy-start | bytes 6291460
  801.5 8.7 copy-start.15
  810.2 8.5 copy-start.16
  916.6 6.8 copy-start.19
  916.6 6.8 copy-start.21
  926.5 18.2 %all-to-all-start.1 = ((bf16[4,128,1024]{2,1,0:T(8,128)(2,1)}), bf16[4,128,1024]{2,1,0:T(8,128)(2,1)S(1)}, u32[]{:S(2)}, u32[]{:S(2)}) async-start(bf16[4,128,1024]{2,1,0:T(8,128)(2,1)} %bitcast.81), calls=%async_computation.5 | async-start | bytes 2097152 | tf_op jit(solution)/shard_map/all_to_all | solution.py:1080
  950.4 3.6 collective-permute-start
  (1 other events, 0.6 us)
Sparse Core Ops, SparseCore 0:
  10.6 83.4 all-gather.4
  95.7 79.2 all-gather.6
  176.6 79.2 all-gather.10
  257.4 79.2 all-gather.8
  521.7 76.9 reduce-scatter.4
  625.9 77.0 reduce-scatter.6
  705.3 77.2 reduce-scatter.8
  827.5 76.3 reduce-scatter.10

commit v7 on v6

--- a/solution.py
+++ b/solution.py
@@ -109,6 +109,7 @@
 
 
 def table_work(lengths, parents, freqs, rows_ref, cols_ref, cos_ref, sin_ref, cols_buf, cos_buf, sin_buf, sems):
+    yield
     tokens = cos_ref.shape[0]
     shape = (8, tokens)
     segment, parent, _ = tables_at(lax.broadcasted_iota(jnp.int32, shape, 1), lengths, parents)
@@ -515,20 +516,29 @@
 def bwd_kernel(heads, hosts, *refs):
     if not hosts:
         return bwd_work(heads, *refs)
-    scatter = PlaneScatter(refs[10], refs[14], *refs[-7:])
+    scatter = PlaneScatter(refs[10], refs[12], *refs[-7:])
     step, total = pl.program_id(0) * pl.num_programs(1) + pl.program_id(1), 16
     at_step(
         step, total, ((0, scatter.start), (3, scatter.first), (5, scatter.second), (7, scatter.third))
     )
-    bwd_work(heads, *refs[:10], *refs[11:14], *refs[15:-7])
+    bwd_work(heads, *refs[:10], *refs[13:-7], together=refs[11])
     at_step(step, total, ((total - 1, scatter.finish),))
 
 
 def bwd_work(
     heads, q_ref, k_ref, v_ref, o_ref, do_ref, lse_ref, cos_ref, sin_ref, rows_ref, cols_ref,
-    dq_ref, dk_ref, dv_ref, dq_acc, dk_acc, dv_acc,
+    *refs, together=None,
 ):
+    if together is None:
+        dq_ref, dk_ref, dv_ref, dq_acc, dk_acc, dv_acc = refs
+    else:
+        dq_acc, dk_acc, dv_acc, dq_ref, dk_ref, dv_ref, out_sems = refs
     i = pl.program_id(1)
+
+    def store(kind, source, rows):
+        groups, width = pl.num_programs(0), source.shape[1]
+        columns = pl.ds(pl.multiple_of((kind * groups + pl.program_id(0)) * width, width), width)
+        return pltpu.make_async_copy(source, together.at[rows, columns], out_sems.at[kind])
 
     @pl.when(i == 0)
     def _():
@@ -584,7 +594,12 @@
     key_plan(i, tile)
     dq = dq_acc[...] * SCALE
     rows = pl.ds(pl.multiple_of(i * BQ, BQ), BQ)
-    dq_ref[...] = (dq * cos_ref[rows, :] - partner(dq) * sin_ref[rows, :]).astype(BF16)
+    dq = (dq * cos_ref[rows, :] - partner(dq) * sin_ref[rows, :]).astype(BF16)
+    dq_ref[...] = dq
+    if together is not None:
+        copy = store(0, dq_ref, rows)
+        copy.start()
+        copy.wait()
 
     @pl.when(i == pl.num_programs(1) - 1)
     def _():
@@ -594,6 +609,14 @@
             dk = dk_acc[rows, :]
             dk_ref[rows, :] = (dk * cos_ref[rows, :] - partner(dk) * sin_ref[rows, :]).astype(BF16)
             dv_ref[rows, :] = dv_acc[rows, :].astype(BF16)
+
+        if together is not None:
+            every = pl.ds(0, dk_acc.shape[0])
+            copies = [store(1, dk_ref, every), store(2, dv_ref, every)]
+            for copy in copies:
+                copy.start()
+            for copy in copies:
+                copy.wait()
 
 
 def small_cost():
@@ -668,15 +691,25 @@
             pl.BlockSpec((tree_len, 128), lambda g, i: (0, 0)),
         ]
         + [hbm] * hosts,
-        out_specs=[row_block, full, full] + [hbm] * hosts,
-        out_shape=[act, act, act]
-        + ([jax.ShapeDtypeStruct((hosted.shape[0] // 8, hosted.shape[1]), BF16)] if hosts else []),
+        out_specs=[hbm] * 2 if hosts else [row_block, full, full],
+        out_shape=[
+            jax.ShapeDtypeStruct((tree_len, 3 * width), BF16),
+            jax.ShapeDtypeStruct((hosted.shape[0] // 8, hosted.shape[1]), BF16),
+        ]
+        if hosts
+        else [act, act, act],
         scratch_shapes=[
             pltpu.VMEM((BQ, gw), F32),
             pltpu.VMEM((tree_len, gw), F32),
             pltpu.VMEM((tree_len, gw), F32),
         ]
-        + (scatter_scratch(hosted.shape[0] // 8, hosted.shape[1]) if hosts else []),
+        + (
+            [pltpu.VMEM((rows, gw), BF16) for rows in (BQ, tree_len, tree_len)]
+            + [pltpu.SemaphoreType.DMA((3,))]
+            + scatter_scratch(hosted.shape[0] // 8, hosted.shape[1])
+            if hosts
+            else []
+        ),
         compiler_params=pltpu.CompilerParams(
             vmem_limit_bytes=60 << 20, collective_id=7 if hosts else None, has_side_effects=hosts
         ),
@@ -717,6 +750,7 @@
     whole = pltpu.make_async_copy(right_ref, right_buf, sems.at[2])
     whole.start()
     load(0).start()
+    yield
     whole.wait()
     for group in range(groups):
         for part in range(parts):
@@ -746,6 +780,75 @@
         pass
 
 
+def pair_product(left_ref, first_ref, second_ref, out_first, out_second, left_buf, right_buf, total, out_buf, sems):
+    tokens, columns = first_ref.shape
+    parts, groups = tokens // TOKENS_AT_ONCE, left_ref.shape[1] // LEFT_AT_ONCE
+    sides = [pl.ds(0, columns), pl.ds(columns, columns)]
+
+    def load(step):
+        group, part = step // parts, step % parts
+        source = left_ref.at[
+            pl.ds(part * TOKENS_AT_ONCE, TOKENS_AT_ONCE), pl.ds(group * LEFT_AT_ONCE, LEFT_AT_ONCE)
+        ]
+        return pltpu.make_async_copy(source, left_buf.at[step % 2], sems.at[step % 2])
+
+    def stores(group):
+        rows = pl.ds(group * LEFT_AT_ONCE, LEFT_AT_ONCE)
+        return [
+            pltpu.make_async_copy(out_buf.at[:, side], out_ref.at[rows], sems.at[4 + n])
+            for n, (side, out_ref) in enumerate(zip(sides, (out_first, out_second)))
+        ]
+
+    wholes = [
+        pltpu.make_async_copy(ref, right_buf.at[:, side], sems.at[2 + n])
+        for n, (side, ref) in enumerate(zip(sides, (first_ref, second_ref)))
+    ]
+    load(0).start()
+    for copy in wholes:
+        copy.start()
+    yield
+    for copy in wholes:
+        copy.wait()
+    for group in range(groups):
+        for part in range(parts):
+            step = group * parts + part
+            load(step).wait()
+            if step + 1 < groups * parts:
+                load(step + 1).start()
+            if part == 0:
+                total[...] = jnp.zeros_like(total)
+
+            @pl.loop(0, TOKENS_AT_ONCE // STEP)
+            def _(j, step=step, part=part):
+                left = left_buf[step % 2, pl.ds(pl.multiple_of(j * STEP, STEP), STEP), :]
+                right = right_buf[pl.ds(pl.multiple_of(part * TOKENS_AT_ONCE + j * STEP, STEP), STEP), :]
+                total[...] += dot_tn(left, right)
+
+        if group > 0:
+            for copy in stores(group - 1):
+                copy.wait()
+        out_buf[...] = total[...].astype(BF16)
+        for copy in stores(group):
+            copy.start()
+        yield
+    for copy in stores(groups - 1):
+        copy.wait()
+
+
+def cut_columns(*refs):
+    count = (len(refs) - 1) // 2
+    sources, targets, sems = refs[:count], refs[count:-1], refs[-1]
+    copies = []
+    for n, (source, target) in enumerate(zip(sources, targets)):
+        columns = target.shape[1]
+        taken = pl.ds(pl.multiple_of(lax.axis_index("ctx") * columns, columns), columns)
+        copies.append(pltpu.make_async_copy(source.at[:, taken], target, sems.at[n]))
+        copies[-1].start()
+    yield
+    for copy in copies:
+        copy.wait()
+
+
 def row_product(turned, left_ref, right_ref, out_ref, left_buf, right_buf, out_buf, sems):
     groups = left_ref.shape[0] // LEFT_AT_ONCE
 
@@ -761,6 +864,7 @@
     whole = pltpu.make_async_copy(right_ref, right_buf, sems.at[2])
     whole.start()
     load(0).start()
+    yield
     whole.wait()
     for group in range(groups):
         load(group).wait()
@@ -811,8 +915,11 @@
         buffers.append(held[work])
 
     def all_work():
-        for work, given, wanted, room in zip(works, inputs, outputs, buffers):
-            yield from work(*given, *wanted, *room)
+        started = [work(*given, *wanted, *room) for work, given, wanted, room in zip(works, inputs, outputs, buffers)]
+        for one in started:
+            next(one)
+        for one in started:
+            yield from one
 
     going = all_work()
 
@@ -865,6 +972,24 @@
 def token_job(left, right):
     out = jax.ShapeDtypeStruct((left.shape[1], right.shape[1]), BF16)
     return token_product, [left, right], [HBM] * 2, [out], [HBM], product_buffers(right.shape[1])
+
+
+def pair_job(left, first, second):
+    columns = first.shape[1]
+    out = jax.ShapeDtypeStruct((left.shape[1], columns), BF16)
+    room = [
+        pltpu.VMEM((2, TOKENS_AT_ONCE, LEFT_AT_ONCE), BF16),
+        pltpu.VMEM((left.shape[0], 2 * columns), BF16),
+        pltpu.VMEM((LEFT_AT_ONCE, 2 * columns), F32),
+        pltpu.VMEM((LEFT_AT_ONCE, 2 * columns), BF16),
+        pltpu.SemaphoreType.DMA((6,)),
+    ]
+    return pair_product, [left, first, second], [HBM] * 3, [out] * 2, [HBM] * 2, room
+
+
+def cut_job(weights, parts):
+    outs = [jax.ShapeDtypeStruct((w.shape[0], w.shape[1] // parts), w.dtype) for w in weights]
+    return cut_columns, list(weights), [HBM] * len(weights), outs, [HBM] * len(weights), [pltpu.SemaphoreType.DMA((len(weights),))]
 
 
 def row_job(left, right, turned):
@@ -1026,6 +1151,44 @@
     )(*parts, *weights, *lefts, *rights)
 
 
+def gated_kernel(x_ref, grad_ref, gate_ref, up_ref, hidden_ref, gate_grad_ref, up_grad_ref):
+    columns = gate_ref.shape[1]
+    step = min(256, columns)
+    together = min(2, columns // step)
+
+    @pl.loop(0, columns // (step * together))
+    def _(j):
+        for part in range(together):
+            taken = pl.ds(pl.multiple_of((j * together + part) * step, step), step)
+            gate = dot_n(x_ref[...], gate_ref[:, taken])
+            up = dot_n(x_ref[...], up_ref[:, taken])
+            grad = grad_ref[:, taken].astype(F32)
+            sigmoid = jax.nn.sigmoid(gate)
+            silu = gate * sigmoid
+            hidden_ref[:, taken] = (silu * up).astype(BF16)
+            gate_grad_ref[:, taken] = (grad * up * sigmoid * (1.0 + gate * (1.0 - sigmoid))).astype(BF16)
+            up_grad_ref[:, taken] = (grad * silu).astype(BF16)
+
+
+def gated_rows(x, hidden_grad, w_gate, w_up):
+    tokens, depth = x.shape
+    columns = w_gate.shape[1]
+    block = 512
+    rows = pl.BlockSpec((block, columns), lambda i: (i, 0))
+    weight = pl.BlockSpec((depth, columns), lambda i: (0, 0), pipeline_mode=pl.Buffered(1))
+    out = jax.ShapeDtypeStruct((tokens, columns), BF16)
+    return pl.pallas_call(
+        gated_kernel,
+        grid=(tokens // block,),
+        in_specs=[pl.BlockSpec((block, depth), lambda i: (i, 0)), rows, weight, weight],
+        out_specs=[rows] * 3,
+        out_shape=[out] * 3,
+        compiler_params=pltpu.CompilerParams(vmem_limit_bytes=48 << 20),
+        cost_estimate=small_cost(),
+        name="gated_rows",
+    )(x, hidden_grad, w_gate, w_up)
+
+
 def is_plane():
     return lax.axis_size("ctx") == 4 and lax.axis_size("tensor") == 2
 
@@ -1042,22 +1205,31 @@
     return plane_gather(rows)[0] if is_plane() else gather_rows(rows)
 
 
-def gather_with_tables(rows, lengths, parents, tokens, width):
+def cut(weight):
+    columns = weight.shape[1] // lax.axis_size("ctx")
+    return lax.dynamic_slice_in_dim(weight, lax.axis_index("ctx") * columns, columns, 1)
+
+
+def gather_with_tables(rows, lengths, parents, tokens, width, weights):
     if is_plane():
-        return plane_gather(rows, 8, [table_job(lengths, parents, tokens)], (4, 4))
+        jobs = [cut_job(weights, lax.axis_size("ctx")), table_job(lengths, parents, tokens)]
+        got = plane_gather(rows, 8, jobs, (4, 4))
+        return got[:1] + got[1 + len(weights) :], got[1 : 1 + len(weights)]
     segment, parent, depth = tree_tables(lengths[0], parents[0], tokens)
-    return [gather_rows(rows), *lay_out(segment, parent), *rope_tables(depth, width)]
-
-
-def gather_with_products(rows, collective_id, token_pairs, row_pairs):
+    return [gather_rows(rows), *lay_out(segment, parent), *rope_tables(depth, width)], [cut(w) for w in weights]
+
+
+def gather_with_product(rows, left, right):
     if is_plane():
-        jobs = [token_job(*pair) for pair in token_pairs] + [row_job(*pair) for pair in row_pairs]
-        return plane_gather(rows, collective_id, jobs, (4, 4))
-    return (
-        [gather_rows(rows)]
-        + [dot_tn(left, right).astype(BF16) for left, right in token_pairs]
-        + [(dot_t if turned else dot_n)(left, right).astype(BF16) for left, right, turned in row_pairs]
-    )
+        return plane_gather(rows, 5, [row_job(left, right, False)], (4, 4))
+    return gather_rows(rows), dot_n(left, right).astype(BF16)
+
+
+def gather_with_three(rows, left, right, shared, first, second):
+    if is_plane():
+        return plane_gather(rows, 4, [row_job(left, right, True), pair_job(shared, first, second)], (8, 3))
+    products = dot_t(left, right), dot_tn(shared, first), dot_tn(shared, second)
+    return [gather_rows(rows)] + [product.astype(BF16) for product in products]
 
 
 def product_scatter(parts, weights, collective_id, jobs=()):
@@ -1128,12 +1300,15 @@
     w_attn = gather_weight(
         jnp.concatenate([mine(w, width) for w in (query_weight, key_weight, value_weight, output_weight)], axis=1)
     )
-    w_gate = gather_weight(mine(gate_weight, units))
-    w_down = gather_weight(mine(down_weight, units))
-    w_up = gather_weight(mine(up_weight, units))
-    attn_in, rows_table, cols_table, cosine, sine = gather_with_tables(
-        (attn_scaled * attn_gain[None, :]).astype(BF16), seg_lengths, leaf_parent, tree_len, min(2 * HEAD_DIM, width)
+    (attn_in, rows_table, cols_table, cosine, sine), cuts = gather_with_tables(
+        (attn_scaled * attn_gain[None, :]).astype(BF16),
+        seg_lengths,
+        leaf_parent,
+        tree_len,
+        min(2 * HEAD_DIM, width),
+        [gate_weight, down_weight, up_weight],
     )
+    w_gate, w_down, w_up = [gather_weight(own) for own in cuts]
     w_qkv, w_out = w_attn[:, : 3 * width], w_attn[:, 3 * width :]
 
     qkv = jnp.dot(attn_in, w_qkv, preferred_element_type=F32)
@@ -1149,25 +1324,16 @@
     mid_rows = x_rows + product_scatter([attn_out], [w_out], 1)[0]
     mlp_scaled, mlp_inv = normalize(mid_rows)
     mlp_own = (mlp_scaled * mlp_gain[None, :]).astype(BF16)
-    mlp_in, hidden_grad = gather_with_products(mlp_own, 5, [], [(cot_all, w_down, False)])
-
-    gate = jnp.dot(mlp_in, w_gate, preferred_element_type=F32)
-    up_proj = jnp.dot(mlp_in, w_up, preferred_element_type=F32)
-    sigmoid_gate = jax.nn.sigmoid(gate)
-    hidden = (gate * sigmoid_gate * up_proj).astype(BF16)
-    hidden_grad = hidden_grad.astype(F32)
-    gate_rows_grad = (
-        hidden_grad * up_proj * sigmoid_gate * (1.0 + gate * (1.0 - sigmoid_gate))
-    ).astype(BF16)
-    up_rows_grad = (hidden_grad * gate * sigmoid_gate).astype(BF16)
+    mlp_in, hidden_grad = gather_with_product(mlp_own, cot_all, w_down)
+    hidden, gate_rows_grad, up_rows_grad = gated_rows(mlp_in, hidden_grad, w_gate, w_up)
 
     mlp_in_grad, down_part = product_scatter(
         [gate_rows_grad, up_rows_grad], [w_gate, w_up], 3, [(cot_all, hidden)]
     )
     down_grad = scatter_weight(down_part)
     mid_grad = cotangent.astype(F32) + norm_backward(mlp_in_grad, mlp_scaled, mlp_inv, mlp_gain)
-    mid_all, up_part, gate_part, down_rows = gather_with_products(
-        mid_grad.astype(BF16), 4, [(mlp_in, up_rows_grad), (mlp_in, gate_rows_grad)], [(hidden, w_down, True)]
+    mid_all, down_rows, up_part, gate_part = gather_with_three(
+        mid_grad.astype(BF16), hidden, w_down, mlp_in, up_rows_grad, gate_rows_grad
     )
     up_grad = scatter_weight(up_part)
     gate_grad = scatter_weight(gate_part)
@@ -1176,21 +1342,22 @@
     output_grad = dot_tn(mid_all, attn_out).astype(BF16)
     out_heads_grad, down_grad = lax.optimization_barrier((out_heads_grad, down_grad))
     if is_plane():
-        *pre_grads, down_rows = attention_backward(
+        pre_grads, down_rows = attention_backward(
             query_rows, key_rows, value_rows, attn_out, out_heads_grad, lse, cosine, sine, rows_table, cols_table, down_rows
         )
     else:
         pre_grads = attention_backward(
             query_rows, key_rows, value_rows, attn_out, out_heads_grad, lse, cosine, sine, rows_table, cols_table
         )
+        pre_grads = jnp.concatenate(pre_grads, axis=1)
         down_rows = scatter_rows(down_rows)
     block_out = (mid_rows + down_rows.astype(F32)).astype(BF16)
     pre_grads, up_grad, gate_grad = lax.optimization_barrier((pre_grads, up_grad, gate_grad))
     swapped = swap_rows(jnp.concatenate([gate_grad, up_grad, down_grad], axis=1))
-    attn_part = jnp.concatenate([dot_tn(attn_in, grad).astype(BF16) for grad in pre_grads] + [output_grad], axis=1)
+    attn_part = jnp.concatenate([dot_tn(attn_in, pre_grads).astype(BF16), output_grad], axis=1)
     pre_grads, attn_part, swapped = lax.optimization_barrier((pre_grads, attn_part, swapped))
     attn_grad = scatter_weight(attn_part)
-    (attn_in_grad,) = product_scatter(pre_grads, [w_attn[:, j * width : (j + 1) * width] for j in range(3)], 2)
+    (attn_in_grad,) = product_scatter([pre_grads], [w_qkv], 2)
     attn_in_grad, attn_grad = lax.optimization_barrier((attn_in_grad, attn_grad))
     gate_out, up_out, down_out = lay_side_by_side(swapped, 3)
     query_out, key_out, value_out, output_out = lay_side_by_side(swap_rows(attn_grad), 4)

time: 970 us -> 1080 us (1.11)
  Pallas kernels: 721 us -> 897 us
  matrix products: 131 us -> 62.3 us
    pallas_call x3, Pallas kernels: 245 us -> 362 us  [plane_gather(): pl.pallas_call(functools.partial(gather_kernel, [job[0] for job in jobs],...]
    dot_general x2 -> x0, matrix products: 58.7 us -> none  [the longest x1 35.3 us: body(): up_proj = jnp.dot(mlp_in, w_up, preferred_element_type=F32)]
    pallas_call x0 -> x1, Pallas kernels: none -> 48.5 us  [gated_rows(): pl.pallas_call(gated_kernel, grid=(tokens // block,), in_specs=[pl.BlockS...]
    dot_general x4 -> x2, matrix products: 40.7 us -> 31.1 us  [dot_tn(): lax.dot_general(a, b, (((0,), (0,)), ((), ())), preferred_element_type=F32)]
  transfers between devices with their start and end apart: 11 -> 11, of which waited for: 4 -> 3; matrix products, arithmetic and copies ran while one was open for 14% -> 10% of each run, Pallas kernels for 65% -> 70%
where the time goes in v7:
time: 1080 us; the launch traced here: 1070 us
  Pallas kernels  897 us (83%)
  matrix products  62.3 us (6%)
  other arithmetic  43.4 us (4%)
  local copies, waits for them, and re-layouts  23.6 us (2%)
  waiting for transfers between devices  22.4 us (2%)
  between operations  14.7 us (1%)
    pallas_call x3, Pallas kernels, plane_gather(): pl.pallas_call(functools.partial(gather_kernel, [job[0] for job in jobs],...  362 us
    pallas_call x3, Pallas kernels, plane_scatter(): pl.pallas_call(functools.partial(scatter_kernel, rows, len(parts), len(jo...  257 us
    pallas_call x1, Pallas kernels, attention_backward(): pl.pallas_call(functools.partial(bwd_kernel, heads, hosts), grid=(groups,...  141 us
    pallas_call x1, Pallas kernels, attention_forward(): pl.pallas_call(functools.partial(fwd_kernel, heads, hosts), grid=(groups,...  88.2 us
    pallas_call x1, Pallas kernels, gated_rows(): pl.pallas_call(gated_kernel, grid=(tokens // block,), in_specs=[pl.BlockS...  48.5 us
    dot_general x2, matrix products, dot_tn(): lax.dot_general(a, b, (((0,), (0,)), ((), ())), preferred_element_type=F32)  31.1 us
  transfers between devices with their start and end apart: 11, of which 3 were waited for; matrix products, arithmetic and copies ran while one was open for 10% of the time, Pallas kernels for 70%

profile of v7, /device:TPU:0, one launch (start us, length us, event | category | flops | bytes accessed | tf_op | source)
XLA Modules:
  0.0 1072.8 jit_solution(27819120644172566)
XLA Ops:
  11.8 1.9 fusion.3.refs_0_
  13.7 206.4 %plane_gather.3 = (bf16[4096,2048]{1,0:T(8,128)(2,1)}, bf16[512,1024]{1,0:T(8,128)(2,1)}, bf16[512,1024]{1,0:T(8,128)(2,1)}, bf16[512,1024]{1,0:T(8,128)(2,1)}, ...) custom-call(bf16[512,2048]{1,0:T(8,128)(2,1)} %fusion.3.refs_0_, ...), custom_call_target="tpu_custom_call" | custom-call | flops 1048576 | bytes 1048576 | tf_op jit(solution)/shard_map/plane_gather/pallas_call | solution.py:947
  224.8 19.2 %fusion.14.refs_0_.refs_1_.refs_2_ = f32[4096,768]{1,0:T(8,128)} fusion(bf16[4096,2048]{1,0:T(8,128)(2,1)} %get-tuple-element.48, bf16[2048,1024]{1,0:T(8,128)(2,1)} %all-gather.5.cloned.1.call-done), kind=kOutput, calls=%fused_computation.83 | convolution fusion | flops 12884901888 | bytes 32505856 | tf_op jit(solution)/shard_map/dot_general | solution.py:1314
  244.0 88.2 %tree_attention_forward.1 = (bf16[4096,256]{1,0:T(8,128)(2,1)}, f32[2,2,4096]{2,1,0:T(2,128)}, bf16[4096,256]{1,0:T(8,128)(2,1)}, bf16[4096,256]{1,0:T(8,128)(2,...) custom-call(f32[4096,768]{1,0:T(8,128)} %fusion.14.refs_0_.refs_1_.refs_2_, ...), custom_call_target="tpu_custom_call" | custom-call | flops 1048576 | bytes 1048576 | tf_op jit(solution)/shard_map/tree_attention_forward/pallas_call | solution.py:641
  332.2 80.3 %plane_scatter.3 = f32[512,2048]{1,0:T(8,128)} custom-call(bf16[4096,256]{1,0:T(8,128)(2,1)} %get-tuple-element.53.refs_0_.refs_3_, bf16[2048,256]{1,0:T(8,128)(2,1)S(1)} %slice.129.refs_1_), custom_call_target="tpu_custom_call" | custom-call | flops 1048576 | bytes 1048576 | tf_op jit(solution)/shard_map/plane_scatter/pallas_call | solution.py:1130
  412.5 3.0 multiply_reduce_fusion.1
  417.3 74.5 %plane_gather.4 = (bf16[4096,2048]{1,0:T(8,128)(2,1)}, bf16[4096,1024]{1,0:T(8,128)(2,1)}) custom-call(bf16[512,2048]{1,0:T(8,128)(2,1)S(1)} %multiply_convert_fusion.refs_0_, bf16[4096,2048]{1,0:T(8,128)(2,1)} %get-tuple-element.57.refs_1_.refs_4_, bf16[2048,1024]{1,0:T(8,128)(2,1)} %all-gather.7.cloned.1.call-done.refs_2_), custom_call_target="tpu_custom_call" | custom-call | flops 1048576 | bytes 1048576 | tf_op jit(solution)/shard_map/plane_gather/pallas_call | solution.py:947
  491.9 2.2 copy-done
  494.1 48.5 %gated_rows.1 = (bf16[4096,1024]{1,0:T(8,128)(2,1)}, bf16[4096,1024]{1,0:T(8,128)(2,1)}, bf16[4096,1024]{1,0:T(8,128)(2,1)}) custom-call(bf16[4096,2048]{1,0:T(8,128)(2,1)} %get-tuple-element.59.x_ref.refs_3_, bf16[4096,1024]{1,0:T(8,128)(2,1)} %get-tuple-element.60.grad_ref, bf16[2048,1024]{1,0:T(8,128)(2,1)S(1)} %copy-done, ...), custom_call_target="tpu_custom_call" | custom-call | flops 1048576 | bytes 1048576 | tf_op jit(solution)/shard_map/gated_rows/pallas_call | solution.py:1180
  542.5 92.8 %plane_scatter.4 = (f32[512,2048]{1,0:T(8,128)}, bf16[2048,1024]{1,0:T(8,128)(2,1)}) custom-call(bf16[4096,1024]{1,0:T(8,128)(2,1)} %get-tuple-element.63.refs_0_.refs_5_, bf16[4096,1024]{1,0:T(8,128)(2,1)} %get-tuple-element.64.refs_1_.refs_4_, bf16[2048,1024]{1,0:T(8,128)(2,1)} %all-gather.9.cloned.1.call-done.gate_ref.refs_2_, ...), custom_call_target="tpu_custom_call" | custom-call | flops 1048576 | bytes 1048576 | tf_op jit(solution)/shard_map/plane_scatter/pallas_call | solution.py:1130
  636.9 4.5 multiply_reduce_fusion
  641.5 2.0 copy-done.12
  645.8 81.6 %plane_gather.5 = (bf16[4096,2048]{1,0:T(8,128)(2,1)}, bf16[4096,2048]{1,0:T(8,128)(2,1)}, bf16[2048,1024]{1,0:T(8,128)(2,1)}, bf16[2048,1024]{1,0:T(8,128)(2,1)}) custom-call(bf16[512,2048]{1,0:T(8,128)(2,1)S(1)} %fusion.16.refs_0_, bf16[4096,1024]{1,0:T(8,128)(2,1)} %get-tuple-element.65.refs_5_.refs_1_, ...), custom_call_target="tpu_custom_call" | custom-call | flops 1048576 | bytes 1048576 | tf_op jit(solution)/shard_map/plane_gather/pallas_call | solution.py:947
  728.2 12.3 %convolution_convert_fusion.2 = bf16[2048,256]{0,1:T(8,128)(2,1)} fusion(bf16[4096,2048]{1,0:T(8,128)(2,1)} %get-tuple-element.67, bf16[4096,256]{1,0:T(8,128)(2,1)} %get-tuple-element.53.refs_0_.refs_3_), kind=kOutput, calls=%fused_computation.22 | convolution fusion | flops 4295491584 | bytes 19922944 | tf_op jit(solution)/shard_map/dot_general | solution.py:370
  740.6 11.9 %convolution_convert_fusion.refs_4_ = bf16[4096,256]{1,0:T(8,128)(2,1)} fusion(bf16[4096,2048]{1,0:T(8,128)(2,1)} %get-tuple-element.67, bf16[2048,1024]{1,0:T(8,128)(2,1)} %all-gather.5.cloned.1.call-done), kind=kOutput, calls=%fused_computation.6 | convolution fusion | flops 4296015872 | bytes 19922944 | tf_op jit(solution)/shard_map/dot_general | solution.py:1341
  752.5 140.9 %tree_attention_backward.1 = (bf16[4096,768]{1,0:T(8,128)(2,1)}, bf16[512,2048]{1,0:T(8,128)(2,1)}) custom-call(bf16[4096,256]{1,0:T(8,128)(2,1)} %get-tuple-element.54.refs_0_, bf16[4096,256]{1,0:T(8,128)(2,1)} %get-tuple-element.55.refs_1_, bf16[4096,256]{1,0:T(8,128)(2,1)} %get-tuple-element.56.refs_2_, ...), custom_call_target="tpu_custom_call" | custom-call | flops 1048576 | bytes 1048576 | tf_op jit(solution)/shard_map/tree_attention_backward/pallas_call | solution.py:683
  893.5 3.0 pad_maximum_fusion.1
  896.5 4.7 all-to-all-start
  901.2 18.8 %convolution_convert_fusion.1 = bf16[2048,768]{0,1:T(8,128)(2,1)S(1)} fusion(bf16[4096,2048]{1,0:T(8,128)(2,1)} %get-tuple-element.48, bf16[4096,768]{1,0:T(8,128)(2,1)} %get-tuple-element.80.refs_0_), kind=kOutput, calls=%fused_computation.20 | convolution fusion | flops 12886474752 | bytes 26214400 | tf_op jit(solution)/shard_map/dot_general | solution.py:370
  920.0 2.6 pad_maximum_fusion
  922.6 15.6 %all-to-all-done = bf16[4,128,3072]{2,1,0:T(8,128)(2,1)} async-done(((bf16[4,128,3072]{2,1,0:T(8,128)(2,1)}), bf16[4,128,3072]{2,1,0:T(8,128)(2,1)}, u32[]{:S(2)}, u32[]{:S(2)}) %all-to-all-start) | async-done | bytes 3145760 | tf_op jit(solution)/shard_map/all_to_all | solution.py:1252
  938.2 3.7 slice.128.refs_1_
  942.0 84.1 %plane_scatter.5 = f32[512,2048]{1,0:T(8,128)} custom-call(bf16[4096,768]{1,0:T(8,128)(2,1)} %get-tuple-element.80.refs_0_, bf16[2048,768]{1,0:T(8,128)(2,1)} %slice.128.refs_1_), custom_call_target="tpu_custom_call" | custom-call | flops 1048576 | bytes 1048576 | tf_op jit(solution)/shard_map/plane_scatter/pallas_call | solution.py:1130
  1026.1 2.1 slice_bitcast_fusion.3
  1028.2 2.9 multiply_reduce_fusion.2
  1031.2 2.9 multiply_reduce_fusion.3
  1035.7 2.3 copy.26
  1038.0 3.5 all-to-all-start.1
  1041.5 3.2 fusion.4
  1045.6 7.5 fusion.8
  1053.1 2.8 all-to-all-done.1
  1063.3 1.9 collective-permute-done
  (90 shorter events, 26.4 us)
Async XLA Ops:
  7.2 3.6 copy-start.9
  7.2 4.6 copy-start.18
  7.2 216.2 %all-gather.5.cloned.1.call-start = ((), (), s32[]{:S(2)}) async-start(), calls=%async_computation.6 | async-start | bytes 5242880 | tf_op jit(solution)/shard_map/all_gather | solution.py:1243
  10.7 3.0 copy-start.3
  10.7 3.0 copy-start.4
  10.7 3.0 copy-start.5
  10.7 406.6 %all-gather.7.cloned.1.call-start = ((), (), s32[]{:S(2)}) async-start(), calls=%async_computation.7 | async-start | bytes 5242880 | tf_op jit(solution)/shard_map/all_gather | solution.py:1243
  220.1 1.3 copy-start.1
  221.4 0.7 copy-start.2
  222.1 269.8 %all-gather.11.cloned.1.call-start = ((), (), s32[]{:S(2)}) async-start(), calls=%async_computation.9 | async-start | bytes 5242880 | tf_op jit(solution)/shard_map/all_gather | solution.py:1243
  222.8 269.0 %all-gather.9.cloned.1.call-start = ((), (), s32[]{:S(2)}) async-start(), calls=%async_computation.8 | async-start | bytes 5242880 | tf_op jit(solution)/shard_map/all_gather | solution.py:1243
  223.4 529.1 %reduce-scatter.5.cloned.1.call-start = ((), (), s32[]{:S(2)}) async-start(), calls=%async_computation.10 | async-start | bytes 5242880 | tf_op jit(solution)/shard_map/reduce_scatter | solution.py:1247
  332.2 83.3 %copy-start.17 = (f32[2048]{0:T(1024)S(1)}, f32[2048]{0:T(1024)}, u32[]{:S(2)}) copy-start(f32[2048]{0:T(1024)} %param.20) | copy-start | bytes 24580
  412.5 3.5 copy-start.6
  412.5 4.2 copy-start.10
  491.9 2.2 copy-start
  635.3 1.6 copy-start.11
  635.3 258.1 %reduce-scatter.7.cloned.1.call-start = ((), (), s32[]{:S(2)}) async-start(), calls=%async_computation.11 | async-start | bytes 5242880 | tf_op jit(solution)/shard_map/reduce_scatter | solution.py:1247
  636.9 4.6 copy-start.7
  636.9 6.7 copy-start.12
  636.9 7.3 copy-start.13
  727.5 166.0 %reduce-scatter.9.cloned.1.call-start = ((), (), s32[]{:S(2)}) async-start(), calls=%async_computation.12 | async-start | bytes 5242880 | tf_op jit(solution)/shard_map/reduce_scatter | solution.py:1247
  752.5 141.0 %copy-start.15 = (bf16[512,1024]{1,0:T(8,128)(2,1)S(1)}, bf16[512,1024]{1,0:T(8,128)(2,1)}, u32[]{:S(2)}) copy-start(bf16[512,1024]{1,0:T(8,128)(2,1)} %reduce-scatter.5.cloned.1.call-done) | copy-start | bytes 3145732
  896.5 41.7 %all-to-all-start = ((bf16[4,128,3072]{2,1,0:T(8,128)(2,1)}), bf16[4,128,3072]{2,1,0:T(8,128)(2,1)}, u32[]{:S(2)}, u32[]{:S(2)}) async-start(bf16[4,128,3072]{2,1,0:T(8,128)(2,1)} %bitcast.72), calls=%async_computation.3 | async-start | bytes 6291456 | tf_op jit(solution)/shard_map/all_to_all | solution.py:1252
  901.2 18.8 %copy-start.16 = (bf16[2048,256]{0,1:T(8,128)(2,1)S(1)}, bf16[2048,256]{0,1:T(8,128)(2,1)}, u32[]{:S(2)}) copy-start(bf16[2048,256]{0,1:T(8,128)(2,1)} %convolution_convert_fusion.2) | copy-start | bytes 3145732
  901.2 134.5 %reduce-scatter.11.cloned.1.call-start = ((), (), s32[]{:S(2)}) async-start(), calls=%async_computation.13 | async-start | bytes 5242880 | tf_op jit(solution)/shard_map/reduce_scatter | solution.py:1247
  1034.1 7.4 copy-start.19
  1034.1 7.4 copy-start.21
  1038.0 18.0 %all-to-all-start.1 = ((bf16[4,128,1024]{2,1,0:T(8,128)(2,1)}), bf16[4,128,1024]{2,1,0:T(8,128)(2,1)S(1)}, u32[]{:S(2)}, u32[]{:S(2)}) async-start(bf16[4,128,1024]{2,1,0:T(8,128)(2,1)} %bitcast.73), calls=%async_computation.5 | async-start | bytes 2097152 | tf_op jit(solution)/shard_map/all_to_all | solution.py:1252
  1041.5 3.5 copy-start.8
  1041.5 4.1 copy-start.14
  1061.6 3.6 collective-permute-start
  (1 other events, 0.6 us)
Sparse Core Ops, SparseCore 0:
  10.8 83.4 all-gather.4
  222.2 81.0 all-gather.6
  304.9 79.2 all-gather.10
  385.6 79.2 all-gather.8
  635.4 77.0 reduce-scatter.4
  727.6 77.2 reduce-scatter.6
  807.2 77.2 reduce-scatter.8
  938.3 76.9 reduce-scatter.10

commit v8 on v7

--- a/solution.py
+++ b/solution.py
@@ -535,10 +535,10 @@
         dq_acc, dk_acc, dv_acc, dq_ref, dk_ref, dv_ref, out_sems = refs
     i = pl.program_id(1)
 
-    def store(kind, source, rows):
+    def store(kind, source, rows, sem):
         groups, width = pl.num_programs(0), source.shape[1]
         columns = pl.ds(pl.multiple_of((kind * groups + pl.program_id(0)) * width, width), width)
-        return pltpu.make_async_copy(source, together.at[rows, columns], out_sems.at[kind])
+        return pltpu.make_async_copy(source, together.at[rows, columns], out_sems.at[sem])
 
     @pl.when(i == 0)
     def _():
@@ -595,11 +595,25 @@
     dq = dq_acc[...] * SCALE
     rows = pl.ds(pl.multiple_of(i * BQ, BQ), BQ)
     dq = (dq * cos_ref[rows, :] - partner(dq) * sin_ref[rows, :]).astype(BF16)
-    dq_ref[...] = dq
-    if together is not None:
-        copy = store(0, dq_ref, rows)
-        copy.start()
-        copy.wait()
+    if together is None:
+        dq_ref[...] = dq
+    else:
+        step, last = pl.program_id(0) * pl.num_programs(1) + i, pl.num_programs(0) * pl.num_programs(1) - 1
+        for slot in range(2):
+
+            @pl.when(step % 2 == slot)
+            def _(slot=slot):
+                @pl.when(step >= 2)
+                def _():
+                    store(0, dq_ref.at[slot], rows, slot).wait()
+
+                dq_ref[slot] = dq
+                store(0, dq_ref.at[slot], rows, slot).start()
+
+        @pl.when(step == last)
+        def _():
+            for slot in range(2):
+                store(0, dq_ref.at[slot], rows, slot).wait()
 
     @pl.when(i == pl.num_programs(1) - 1)
     def _():
@@ -612,7 +626,7 @@
 
         if together is not None:
             every = pl.ds(0, dk_acc.shape[0])
-            copies = [store(1, dk_ref, every), store(2, dv_ref, every)]
+            copies = [store(1, dk_ref, every, 2), store(2, dv_ref, every, 3)]
             for copy in copies:
                 copy.start()
             for copy in copies:
@@ -704,8 +718,8 @@
             pltpu.VMEM((tree_len, gw), F32),
         ]
         + (
-            [pltpu.VMEM((rows, gw), BF16) for rows in (BQ, tree_len, tree_len)]
-            + [pltpu.SemaphoreType.DMA((3,))]
+            [pltpu.VMEM(shape, BF16) for shape in ((2, BQ, gw), (tree_len, gw), (tree_len, gw))]
+            + [pltpu.SemaphoreType.DMA((4,))]
             + scatter_scratch(hosted.shape[0] // 8, hosted.shape[1])
             if hosts
             else []
@@ -836,17 +850,26 @@
 
 
 def cut_columns(*refs):
-    count = (len(refs) - 1) // 2
-    sources, targets, sems = refs[:count], refs[count:-1], refs[-1]
-    copies = []
-    for n, (source, target) in enumerate(zip(sources, targets)):
-        columns = target.shape[1]
+    count = (len(refs) - 2) // 2
+    sources, targets, (room, sems) = refs[:count], refs[count : 2 * count], refs[2 * count :]
+
+    def inward(n):
+        columns = targets[n].shape[1]
         taken = pl.ds(pl.multiple_of(lax.axis_index("ctx") * columns, columns), columns)
-        copies.append(pltpu.make_async_copy(source.at[:, taken], target, sems.at[n]))
-        copies[-1].start()
+        return pltpu.make_async_copy(sources[n].at[:, taken], room.at[n], sems.at[0, n])
+
+    def outward(n):
+        return pltpu.make_async_copy(room.at[n], targets[n], sems.at[1, n])
+
+    for n in range(count):
+        inward(n).start()
     yield
-    for copy in copies:
-        copy.wait()
+    for n in range(count):
+        inward(n).wait()
+        outward(n).start()
+    yield
+    for n in range(count):
+        outward(n).wait()
 
 
 def row_product(turned, left_ref, right_ref, out_ref, left_buf, right_buf, out_buf, sems):
@@ -989,7 +1012,8 @@
 
 def cut_job(weights, parts):
     outs = [jax.ShapeDtypeStruct((w.shape[0], w.shape[1] // parts), w.dtype) for w in weights]
-    return cut_columns, list(weights), [HBM] * len(weights), outs, [HBM] * len(weights), [pltpu.SemaphoreType.DMA((len(weights),))]
+    room = [pltpu.VMEM((len(weights),) + outs[0].shape, BF16), pltpu.SemaphoreType.DMA((2, len(weights)))]
+    return cut_columns, list(weights), [HBM] * len(weights), outs, [HBM] * len(weights), room
 
 
 def row_job(left, right, turned):
@@ -1006,16 +1030,18 @@
     return table_work, [lengths, parents, rope_freqs(128)], [VMEM] * 3, outs, [VMEM, HBM, HBM, HBM], room
 
 
-def scatter_kernel(rows, parts, jobs, *refs):
+def scatter_kernel(rows, offsets, jobs, *refs):
+    parts = len(offsets)
+
     def take(count):
         nonlocal refs
         taken, refs = refs[:count], refs[count:]
         return taken
 
-    a_refs, w_refs, lefts, rights = take(parts), take(parts), take(jobs), take(jobs)
+    a_refs, w_homes, lefts, rights = take(parts), take(parts), take(jobs), take(jobs)
     (out_ref,), products = take(1), take(jobs)
     core_out, core_in, first_in, next_in, sems = take(5)
-    a_bufs, (a_sems,), buffers = take(parts), take(1), refs
+    a_bufs, w_refs, (a_sems, w_sems), buffers = take(parts), take(parts), take(2), refs
 
     def work(job):
         if job < jobs:
@@ -1048,10 +1074,16 @@
             for p, (a_ref, a_buf) in enumerate(zip(a_refs, a_bufs))
         ]
 
+    w_copies = [
+        pltpu.make_async_copy(home.at[:, pl.ds(offset, w_ref.shape[1])], w_ref, w_sems.at[p])
+        for p, (home, offset, w_ref) in enumerate(zip(w_homes, offsets, w_refs))
+    ]
     loads = {0: load(0)}
-    for copy in loads[0]:
+    for copy in w_copies + loads[0]:
         copy.start()
     enter_plane((over_x, over_row, over_core))
+    for copy in w_copies:
+        copy.wait()
 
     def partial(slot, j):
         total = None
@@ -1120,16 +1152,17 @@
         copy.wait_send()
 
 
-def plane_scatter(parts, weights, collective_id, jobs=()):
+def plane_scatter(parts, weights, collective_id, jobs=(), offsets=None):
     count = parts[0].shape[0]
     width = weights[0].shape[0]
     rows = count // 8
     half = rows // 2
     vmem, hbm = pl.BlockSpec(memory_space=pltpu.VMEM), pl.BlockSpec(memory_space=pl.ANY)
+    offsets = offsets or [0] * len(parts)
     lefts, rights = [left for left, _ in jobs], [right for _, right in jobs]
     return pl.pallas_call(
-        functools.partial(scatter_kernel, rows, len(parts), len(jobs)),
-        in_specs=[hbm] * len(parts) + [vmem] * len(parts) + [hbm] * (2 * len(jobs)),
+        functools.partial(scatter_kernel, rows, offsets, len(jobs)),
+        in_specs=[hbm] * (2 * len(parts) + 2 * len(jobs)),
         out_specs=[vmem] + [hbm] * len(jobs),
         out_shape=[jax.ShapeDtypeStruct((rows, width), F32)]
         + [jax.ShapeDtypeStruct((left.shape[1], right.shape[1]), BF16) for left, right in jobs],
@@ -1141,7 +1174,8 @@
             pltpu.SemaphoreType.DMA((2, 14)),
         ]
         + [pltpu.VMEM((2, half, a.shape[1]), BF16) for a in parts]
-        + [pltpu.SemaphoreType.DMA((2, len(parts)))]
+        + [pltpu.VMEM((width, a.shape[1]), BF16) for a in parts]
+        + [pltpu.SemaphoreType.DMA((2, len(parts))), pltpu.SemaphoreType.DMA((len(parts),))]
         + (product_buffers(rights[0].shape[1]) if jobs else []),
         compiler_params=pltpu.CompilerParams(
             collective_id=collective_id, has_side_effects=True, vmem_limit_bytes=(58 if jobs else 52) << 20
@@ -1232,9 +1266,11 @@
     return [gather_rows(rows)] + [product.astype(BF16) for product in products]
 
 
-def product_scatter(parts, weights, collective_id, jobs=()):
+def product_scatter(parts, weights, collective_id, jobs=(), offsets=None):
     if is_plane():
-        return plane_scatter(parts, weights, collective_id, jobs)
+        return plane_scatter(parts, weights, collective_id, jobs, offsets)
+    offsets = offsets or [0] * len(parts)
+    weights = [w[:, first : first + part.shape[1]] for part, w, first in zip(parts, weights, offsets)]
     rows = scatter_rows(dot_t(jnp.concatenate(parts, axis=1), jnp.concatenate(weights, axis=1)))
     return [rows] + [dot_tn(left, right).astype(BF16) for left, right in jobs]
 
@@ -1321,7 +1357,7 @@
             qkv, cosine, sine, rows_table, cols_table, width
         )
         cot_all = gather_rows(cotangent)
-    mid_rows = x_rows + product_scatter([attn_out], [w_out], 1)[0]
+    mid_rows = x_rows + product_scatter([attn_out], [w_attn], 1, (), [3 * width])[0]
     mlp_scaled, mlp_inv = normalize(mid_rows)
     mlp_own = (mlp_scaled * mlp_gain[None, :]).astype(BF16)
     mlp_in, hidden_grad = gather_with_product(mlp_own, cot_all, w_down)
@@ -1352,14 +1388,17 @@
         pre_grads = jnp.concatenate(pre_grads, axis=1)
         down_rows = scatter_rows(down_rows)
     block_out = (mid_rows + down_rows.astype(F32)).astype(BF16)
-    pre_grads, up_grad, gate_grad = lax.optimization_barrier((pre_grads, up_grad, gate_grad))
-    swapped = swap_rows(jnp.concatenate([gate_grad, up_grad, down_grad], axis=1))
+    pre_grads, up_grad, gate_grad, down_swapped = lax.optimization_barrier(
+        (pre_grads, up_grad, gate_grad, swap_rows(down_grad))
+    )
+    swapped = swap_rows(jnp.concatenate([gate_grad, up_grad], axis=1))
     attn_part = jnp.concatenate([dot_tn(attn_in, pre_grads).astype(BF16), output_grad], axis=1)
     pre_grads, attn_part, swapped = lax.optimization_barrier((pre_grads, attn_part, swapped))
     attn_grad = scatter_weight(attn_part)
-    (attn_in_grad,) = product_scatter([pre_grads], [w_qkv], 2)
+    (attn_in_grad,) = product_scatter([pre_grads], [w_attn], 2)
     attn_in_grad, attn_grad = lax.optimization_barrier((attn_in_grad, attn_grad))
-    gate_out, up_out, down_out = lay_side_by_side(swapped, 3)
+    gate_out, up_out = lay_side_by_side(swapped, 2)
+    (down_out,) = lay_side_by_side(down_swapped, 1)
     query_out, key_out, value_out, output_out = lay_side_by_side(swap_rows(attn_grad), 4)
 
     def gain_part(pairs, gain):

time: 1080 us -> 933 us (0.86)
  Pallas kernels: 897 us -> 760 us
    pallas_call x3, Pallas kernels: 362 us -> 234 us  [plane_gather(): pl.pallas_call(functools.partial(gather_kernel, [job[0] for job in jobs],...]
  transfers between devices with their start and end apart: 11 -> 12, of which waited for: 3 -> 3; matrix products, arithmetic and copies ran while one was open for 10% -> 10% of each run, Pallas kernels for 70% -> 67%
where the time goes in v8:
time: 933 us; the launch traced here: 925 us
  Pallas kernels  760 us (81%)
  matrix products  62.6 us (7%)
  other arithmetic  44.7 us (5%)
  local copies, waits for them, and re-layouts  17.2 us (2%)
  between operations  14.7 us (2%)
  waiting for transfers between devices  13.3 us (1%)
  starting transfers between devices  13.1 us (1%)
    pallas_call x3, Pallas kernels, plane_scatter(): pl.pallas_call(functools.partial(scatter_kernel, rows, offsets, len(jobs)...  255 us
    pallas_call x3, Pallas kernels, plane_gather(): pl.pallas_call(functools.partial(gather_kernel, [job[0] for job in jobs],...  234 us
    pallas_call x1, Pallas kernels, attention_backward(): pl.pallas_call(functools.partial(bwd_kernel, heads, hosts), grid=(groups,...  134 us
    pallas_call x1, Pallas kernels, attention_forward(): pl.pallas_call(functools.partial(fwd_kernel, heads, hosts), grid=(groups,...  88.7 us
    pallas_call x1, Pallas kernels, gated_rows(): pl.pallas_call(gated_kernel, grid=(tokens // block,), in_specs=[pl.BlockS...  48.5 us
    dot_general x2, matrix products, dot_tn(): lax.dot_general(a, b, (((0,), (0,)), ((), ())), preferred_element_type=F32)  30.7 us
    dot_general x1, matrix products, body(): qkv = jnp.dot(attn_in, w_qkv, preferred_element_type=F32)  19.2 us
  transfers between devices with their start and end apart: 12, of which 3 were waited for; matrix products, arithmetic and copies ran while one was open for 10% of the time, Pallas kernels for 67%

profile of v8, /device:TPU:0, one launch (start us, length us, event | category | flops | bytes accessed | tf_op | source)
XLA Modules:
  0.0 925.5 jit_solution(10941531654518368504)
XLA Ops:
  11.8 1.9 fusion.3.refs_0_
  13.7 77.3 %plane_gather.3 = (bf16[4096,2048]{1,0:T(8,128)(2,1)}, bf16[512,1024]{1,0:T(8,128)(2,1)}, bf16[512,1024]{1,0:T(8,128)(2,1)}, bf16[512,1024]{1,0:T(8,128)(2,1)}, ...) custom-call(bf16[512,2048]{1,0:T(8,128)(2,1)} %fusion.3.refs_0_, ...), custom_call_target="tpu_custom_call" | custom-call | flops 1048576 | bytes 1048576 | tf_op jit(solution)/shard_map/plane_gather/pallas_call | solution.py:970
  94.4 19.2 %fusion.10.refs_0_.refs_1_.refs_2_ = f32[4096,768]{1,0:T(8,128)} fusion(bf16[4096,2048]{1,0:T(8,128)(2,1)} %get-tuple-element.49, bf16[2048,1024]{1,0:T(8,128)(2,1)} %all-gather.5.cloned.1.call-done.refs_1_), kind=kOutput, calls=%fused_computation.21 | convolution fusion | flops 12884901888 | bytes 32505856 | tf_op jit(solution)/shard_map/dot_general | solution.py:1350
  113.7 88.7 %tree_attention_forward.1 = (bf16[4096,256]{1,0:T(8,128)(2,1)}, f32[2,2,4096]{2,1,0:T(2,128)}, bf16[4096,256]{1,0:T(8,128)(2,1)}, bf16[4096,256]{1,0:T(8,128)(2,...) custom-call(f32[4096,768]{1,0:T(8,128)} %fusion.10.refs_0_.refs_1_.refs_2_, ...), custom_call_target="tpu_custom_call" | custom-call | flops 1048576 | bytes 1048576 | tf_op jit(solution)/shard_map/tree_attention_forward/pallas_call | solution.py:655
  202.3 80.9 %plane_scatter.3 = f32[512,2048]{1,0:T(8,128)} custom-call(bf16[4096,256]{1,0:T(8,128)(2,1)} %get-tuple-element.54.refs_0_.refs_3_, bf16[2048,1024]{1,0:T(8,128)(2,1)} %all-gather.5.cloned.1.call-done.refs_1_), custom_call_target="tpu_custom_call" | custom-call | flops 1048576 | bytes 1048576 | tf_op jit(solution)/shard_map/plane_scatter/pallas_call | solution.py:1163
  283.3 3.0 multiply_reduce_fusion.1
  288.1 74.4 %plane_gather.4 = (bf16[4096,2048]{1,0:T(8,128)(2,1)}, bf16[4096,1024]{1,0:T(8,128)(2,1)}) custom-call(bf16[512,2048]{1,0:T(8,128)(2,1)S(1)} %multiply_convert_fusion.refs_0_, bf16[4096,2048]{1,0:T(8,128)(2,1)} %get-tuple-element.58.refs_1_.refs_4_, bf16[2048,1024]{1,0:T(8,128)(2,1)} %all-gather.7.cloned.1.call-done.refs_2_), custom_call_target="tpu_custom_call" | custom-call | flops 1048576 | bytes 1048576 | tf_op jit(solution)/shard_map/plane_gather/pallas_call | solution.py:970
  362.5 2.2 copy-done
  364.7 48.5 %gated_rows.1 = (bf16[4096,1024]{1,0:T(8,128)(2,1)}, bf16[4096,1024]{1,0:T(8,128)(2,1)}, bf16[4096,1024]{1,0:T(8,128)(2,1)}) custom-call(bf16[4096,2048]{1,0:T(8,128)(2,1)} %get-tuple-element.60.x_ref.refs_3_, bf16[4096,1024]{1,0:T(8,128)(2,1)} %get-tuple-element.61.grad_ref, bf16[2048,1024]{1,0:T(8,128)(2,1)S(1)} %copy-done, ...), custom_call_target="tpu_custom_call" | custom-call | flops 1048576 | bytes 1048576 | tf_op jit(solution)/shard_map/gated_rows/pallas_call | solution.py:1214
  413.1 91.7 %plane_scatter.4 = (f32[512,2048]{1,0:T(8,128)}, bf16[2048,1024]{1,0:T(8,128)(2,1)}) custom-call(bf16[4096,1024]{1,0:T(8,128)(2,1)} %get-tuple-element.64.refs_0_.refs_5_, bf16[4096,1024]{1,0:T(8,128)(2,1)} %get-tuple-element.65.refs_1_.refs_4_, bf16[2048,1024]{1,0:T(8,128)(2,1)} %all-gather.9.cloned.1.call-done.gate_ref.refs_2_, ...), custom_call_target="tpu_custom_call" | custom-call | flops 1048576 | bytes 1048576 | tf_op jit(solution)/shard_map/plane_scatter/pallas_call | solution.py:1163
  506.4 4.5 multiply_reduce_fusion
  515.4 81.9 %plane_gather.5 = (bf16[4096,2048]{1,0:T(8,128)(2,1)}, bf16[4096,2048]{1,0:T(8,128)(2,1)}, bf16[2048,1024]{1,0:T(8,128)(2,1)}, bf16[2048,1024]{1,0:T(8,128)(2,1)}) custom-call(bf16[512,2048]{1,0:T(8,128)(2,1)S(1)} %fusion.16.refs_0_, bf16[4096,1024]{1,0:T(8,128)(2,1)} %get-tuple-element.66.refs_5_.refs_1_, ...), custom_call_target="tpu_custom_call" | custom-call | flops 1048576 | bytes 1048576 | tf_op jit(solution)/shard_map/plane_gather/pallas_call | solution.py:970
  598.0 12.6 %convolution_convert_fusion.refs_4_ = bf16[4096,256]{1,0:T(8,128)(2,1)} fusion(bf16[4096,2048]{1,0:T(8,128)(2,1)} %get-tuple-element.68, bf16[2048,1024]{1,0:T(8,128)(2,1)} %all-gather.5.cloned.1.call-done.refs_1_), kind=kOutput, calls=%fused_computation.6 | convolution fusion | flops 4296015872 | bytes 19922944 | tf_op jit(solution)/shard_map/dot_general | solution.py:1377
  610.7 3.5 all-to-all-start
  614.2 12.0 %convolution_convert_fusion.2 = bf16[2048,256]{0,1:T(8,128)(2,1)} fusion(bf16[4096,2048]{1,0:T(8,128)(2,1)} %get-tuple-element.68, bf16[4096,256]{1,0:T(8,128)(2,1)} %get-tuple-element.54.refs_0_.refs_3_), kind=kOutput, calls=%fused_computation.23 | convolution fusion | flops 4295491584 | bytes 19922944 | tf_op jit(solution)/shard_map/dot_general | solution.py:370
  626.2 133.8 %tree_attention_backward.1 = (bf16[4096,768]{1,0:T(8,128)(2,1)}, bf16[512,2048]{1,0:T(8,128)(2,1)}) custom-call(bf16[4096,256]{1,0:T(8,128)(2,1)} %get-tuple-element.55.refs_0_, bf16[4096,256]{1,0:T(8,128)(2,1)} %get-tuple-element.56.refs_1_, bf16[4096,256]{1,0:T(8,128)(2,1)} %get-tuple-element.57.refs_2_, ...), custom_call_target="tpu_custom_call" | custom-call | flops 1048576 | bytes 1048576 | tf_op jit(solution)/shard_map/tree_attention_backward/pallas_call | solution.py:697
  760.0 3.1 pad_maximum_fusion.1
  763.1 4.5 all-to-all-start.1
  767.6 18.8 %convolution_convert_fusion.1 = bf16[2048,768]{0,1:T(8,128)(2,1)S(1)} fusion(bf16[4096,2048]{1,0:T(8,128)(2,1)} %get-tuple-element.49, bf16[4096,768]{1,0:T(8,128)(2,1)} %get-tuple-element.81.refs_0_), kind=kOutput, calls=%fused_computation.20 | convolution fusion | flops 12886474752 | bytes 26214400 | tf_op jit(solution)/shard_map/dot_general | solution.py:370
  786.4 2.6 pad_maximum_fusion
  789.0 4.3 all-to-all-done.1
  795.0 82.8 %plane_scatter.5 = f32[512,2048]{1,0:T(8,128)} custom-call(bf16[4096,768]{1,0:T(8,128)(2,1)} %get-tuple-element.81.refs_0_, bf16[2048,1024]{1,0:T(8,128)(2,1)} %all-gather.5.cloned.1.call-done.refs_1_), custom_call_target="tpu_custom_call" | custom-call | flops 1048576 | bytes 1048576 | tf_op jit(solution)/shard_map/plane_scatter/pallas_call | solution.py:1163
  879.5 2.8 multiply_reduce_fusion.2
  882.3 2.9 multiply_reduce_fusion.3
  885.3 2.3 copy.26
  887.6 3.0 fusion.4
  890.6 3.5 all-to-all-start.2
  894.1 8.9 fusion.8
  903.1 5.5 all-to-all-done.2
  908.7 1.8 multiply_reduce_fusion.4
  910.5 1.8 multiply_reduce_fusion.5
  912.3 1.8 multiply_reduce_fusion.6
  (85 shorter events, 24.4 us)
Async XLA Ops:
  7.2 3.6 copy-start.8
  7.2 4.6 copy-start.15
  7.2 87.2 %all-gather.5.cloned.1.call-start = ((), (), s32[]{:S(2)}) async-start(), calls=%async_computation.7 | async-start | bytes 5242880 | tf_op jit(solution)/shard_map/all_gather | solution.py:1279
  10.7 3.0 copy-start.3
  10.7 3.0 copy-start.4
  10.7 3.0 copy-start.5
  10.7 277.4 %all-gather.7.cloned.1.call-start = ((), (), s32[]{:S(2)}) async-start(), calls=%async_computation.8 | async-start | bytes 5242880 | tf_op jit(solution)/shard_map/all_gather | solution.py:1279
  11.2 0.6 copy-start.17
  91.0 1.3 copy-start.1
  92.4 0.7 copy-start.2
  93.0 269.4 %all-gather.9.cloned.1.call-start = ((), (), s32[]{:S(2)}) async-start(), calls=%async_computation.9 | async-start | bytes 5242880 | tf_op jit(solution)/shard_map/all_gather | solution.py:1279
  93.8 268.7 %all-gather.11.cloned.1.call-start = ((), (), s32[]{:S(2)}) async-start(), calls=%async_computation.10 | async-start | bytes 5242880 | tf_op jit(solution)/shard_map/all_gather | solution.py:1279
  94.3 516.3 %reduce-scatter.5.cloned.1.call-start = ((), (), s32[]{:S(2)}) async-start(), calls=%async_computation.11 | async-start | bytes 5242880 | tf_op jit(solution)/shard_map/reduce_scatter | solution.py:1283
  202.3 83.9 %copy-start.14 = (f32[2048]{0:T(1024)S(1)}, f32[2048]{0:T(1024)}, u32[]{:S(2)}) copy-start(f32[2048]{0:T(1024)} %param.20) | copy-start | bytes 24580
  283.2 3.5 copy-start.6
  283.2 4.1 copy-start.9
  362.5 2.2 copy-start
  504.8 1.6 copy-start.10
  504.9 255.1 %reduce-scatter.7.cloned.1.call-start = ((), (), s32[]{:S(2)}) async-start(), calls=%async_computation.12 | async-start | bytes 5242880 | tf_op jit(solution)/shard_map/reduce_scatter | solution.py:1283
  506.4 5.3 copy-start.7
  506.4 6.7 copy-start.11
  506.4 7.3 copy-start.12
  597.3 162.7 %reduce-scatter.9.cloned.1.call-start = ((), (), s32[]{:S(2)}) async-start(), calls=%async_computation.13 | async-start | bytes 5242880 | tf_op jit(solution)/shard_map/reduce_scatter | solution.py:1283
  610.7 149.3 %all-to-all-start = ((bf16[4,128,1024]{2,1,0:T(8,128)(2,1)}), bf16[4,128,1024]{2,1,0:T(8,128)(2,1)S(1)}, u32[]{:S(2)}, u32[]{:S(2)}) async-start(bf16[4,128,1024]{2,1,0:T(8,128)(2,1)} %bitcast.75), calls=%async_computation.3 | async-start | bytes 2097152 | tf_op jit(solution)/shard_map/all_to_all | solution.py:1288
  763.1 30.2 %all-to-all-start.1 = ((bf16[4,128,2048]{2,1,0:T(8,128)(2,1)}), bf16[4,128,2048]{2,1,0:T(8,128)(2,1)}, u32[]{:S(2)}, u32[]{:S(2)}) async-start(bf16[4,128,2048]{2,1,0:T(8,128)(2,1)} %bitcast.73), calls=%async_computation.4 | async-start | bytes 4194304 | tf_op jit(solution)/shard_map/all_to_all | solution.py:1288
  767.6 117.7 %reduce-scatter.11.cloned.1.call-start = ((), (), s32[]{:S(2)}) async-start(), calls=%async_computation.14 | async-start | bytes 5242880 | tf_op jit(solution)/shard_map/reduce_scatter | solution.py:1283
  767.6 18.8 %copy-start.13 = (bf16[2048,256]{0,1:T(8,128)(2,1)S(1)}, bf16[2048,256]{0,1:T(8,128)(2,1)}, u32[]{:S(2)}) copy-start(bf16[2048,256]{0,1:T(8,128)(2,1)} %convolution_convert_fusion.2) | copy-start | bytes 3145732
  882.3 5.3 copy-start.16
  882.3 5.3 copy-start.18
  890.6 18.0 %all-to-all-start.2 = ((bf16[4,128,1024]{2,1,0:T(8,128)(2,1)}), bf16[4,128,1024]{2,1,0:T(8,128)(2,1)S(1)}, u32[]{:S(2)}, u32[]{:S(2)}) async-start(bf16[4,128,1024]{2,1,0:T(8,128)(2,1)} %bitcast.74), calls=%async_computation.6 | async-start | bytes 2097152 | tf_op jit(solution)/shard_map/all_to_all | solution.py:1288
  914.3 3.6 collective-permute-start
Sparse Core Ops, SparseCore 0:
  10.8 83.4 all-gather.4
  95.9 79.2 all-gather.6
  176.8 79.2 all-gather.8
  257.5 79.2 all-gather.10
  505.0 76.2 reduce-scatter.4
  597.4 76.2 reduce-scatter.6
  676.0 77.2 reduce-scatter.8
  793.5 75.0 reduce-scatter.10

commit v9 on v8

--- a/solution.py
+++ b/solution.py
@@ -734,7 +734,8 @@
 
 TOKENS_AT_ONCE = 2048
 LEFT_AT_ONCE = 512
-STEP = 512
+TOKEN_STEP = 1024
+ROW_STEP = 1024
 
 
 def product_buffers(columns):
@@ -775,10 +776,10 @@
             if part == 0:
                 total[...] = jnp.zeros_like(total)
 
-            @pl.loop(0, TOKENS_AT_ONCE // STEP)
+            @pl.loop(0, TOKENS_AT_ONCE // TOKEN_STEP)
             def _(j, step=step, part=part):
-                left = left_buf[step % 2, pl.ds(pl.multiple_of(j * STEP, STEP), STEP), :]
-                right = right_buf[pl.ds(pl.multiple_of(part * TOKENS_AT_ONCE + j * STEP, STEP), STEP), :]
+                left = left_buf[step % 2, pl.ds(pl.multiple_of(j * TOKEN_STEP, TOKEN_STEP), TOKEN_STEP), :]
+                right = right_buf[pl.ds(pl.multiple_of(part * TOKENS_AT_ONCE + j * TOKEN_STEP, TOKEN_STEP), TOKEN_STEP), :]
                 total[...] += dot_tn(left, right)
 
         if group > 0:
@@ -832,10 +833,10 @@
             if part == 0:
                 total[...] = jnp.zeros_like(total)
 
-            @pl.loop(0, TOKENS_AT_ONCE // STEP)
+            @pl.loop(0, TOKENS_AT_ONCE // TOKEN_STEP)
             def _(j, step=step, part=part):
-                left = left_buf[step % 2, pl.ds(pl.multiple_of(j * STEP, STEP), STEP), :]
-                right = right_buf[pl.ds(pl.multiple_of(part * TOKENS_AT_ONCE + j * STEP, STEP), STEP), :]
+                left = left_buf[step % 2, pl.ds(pl.multiple_of(j * TOKEN_STEP, TOKEN_STEP), TOKEN_STEP), :]
+                right = right_buf[pl.ds(pl.multiple_of(part * TOKENS_AT_ONCE + j * TOKEN_STEP, TOKEN_STEP), TOKEN_STEP), :]
                 total[...] += dot_tn(left, right)
 
         if group > 0:
@@ -896,9 +897,9 @@
         if group > 1:
             store(group - 2).wait()
 
-        @pl.loop(0, out_ref.shape[1] // STEP)
+        @pl.loop(0, out_ref.shape[1] // ROW_STEP)
         def _(j, group=group):
-            columns = pl.ds(pl.multiple_of(j * STEP, STEP), STEP)
+            columns = pl.ds(pl.multiple_of(j * ROW_STEP, ROW_STEP), ROW_STEP)
             if turned:
                 part = dot_t(left_buf[group % 2], right_buf[columns, :])
             else:
@@ -1187,7 +1188,7 @@
 
 def gated_kernel(x_ref, grad_ref, gate_ref, up_ref, hidden_ref, gate_grad_ref, up_grad_ref):
     columns = gate_ref.shape[1]
-    step = min(256, columns)
+    step = min(512, columns)
     together = min(2, columns // step)
 
     @pl.loop(0, columns // (step * together))
@@ -1200,14 +1201,14 @@
             sigmoid = jax.nn.sigmoid(gate)
             silu = gate * sigmoid
             hidden_ref[:, taken] = (silu * up).astype(BF16)
-            gate_grad_ref[:, taken] = (grad * up * sigmoid * (1.0 + gate * (1.0 - sigmoid))).astype(BF16)
+            gate_grad_ref[:, taken] = (grad * up * (sigmoid + silu * (1.0 - sigmoid))).astype(BF16)
             up_grad_ref[:, taken] = (grad * silu).astype(BF16)
 
 
 def gated_rows(x, hidden_grad, w_gate, w_up):
     tokens, depth = x.shape
     columns = w_gate.shape[1]
-    block = 512
+    block = 256
     rows = pl.BlockSpec((block, columns), lambda i: (i, 0))
     weight = pl.BlockSpec((depth, columns), lambda i: (0, 0), pipeline_mode=pl.Buffered(1))
     out = jax.ShapeDtypeStruct((tokens, columns), BF16)
@@ -1221,6 +1222,80 @@
         cost_estimate=small_cost(),
         name="gated_rows",
     )(x, hidden_grad, w_gate, w_up)
+
+
+def heads_kernel(x_ref, w_ref, out_ref, heads_ref, grad_ref, total):
+    i = pl.program_id(0)
+
+    @pl.when(i == 0)
+    def _():
+        total[...] = jnp.zeros_like(total)
+
+    heads_ref[...] = dot_n(x_ref[...], w_ref[...]).astype(BF16)
+    total[...] += dot_tn(out_ref[...], x_ref[...])
+
+    @pl.when(i == pl.num_programs(0) - 1)
+    def _():
+        grad_ref[...] = jnp.transpose(total[...]).astype(BF16)
+
+
+def heads_and_output_grad(mid, w_attn, attn_out):
+    tokens, depth = mid.shape
+    width = attn_out.shape[1]
+    if width % 128:
+        return dot_n(mid, w_attn[:, 3 * width :]).astype(BF16), dot_tn(mid, attn_out).astype(BF16)
+    block = 1024
+    rows = pl.BlockSpec((block, width), lambda i: (i, 0))
+    return pl.pallas_call(
+        heads_kernel,
+        grid=(tokens // block,),
+        in_specs=[pl.BlockSpec((block, depth), lambda i: (i, 0)), pl.BlockSpec((depth, width), lambda i: (0, 3)), rows],
+        out_specs=[rows, pl.BlockSpec((depth, width), lambda i: (0, 0))],
+        out_shape=[jax.ShapeDtypeStruct((tokens, width), BF16), jax.ShapeDtypeStruct((depth, width), BF16)],
+        scratch_shapes=[pltpu.VMEM((width, depth), F32)],
+        compiler_params=pltpu.CompilerParams(vmem_limit_bytes=40 << 20),
+        cost_estimate=small_cost(),
+        name="heads_and_output_grad",
+    )(mid, w_attn, attn_out)
+
+
+def weight_grads_kernel(x_ref, pre_ref, output_ref, grad_ref, total):
+    i = pl.program_id(0)
+    width = pre_ref.shape[1]
+
+    @pl.when(i == 0)
+    def _():
+        total[...] = jnp.zeros_like(total)
+
+    total[...] += dot_tn(x_ref[...], pre_ref[...])
+
+    @pl.when(i == pl.num_programs(0) - 1)
+    def _():
+        grad_ref[:, :width] = total[...].astype(BF16)
+        grad_ref[:, width:] = output_ref[...]
+
+
+def attention_weight_grads(attn_in, pre_grads, output_grad):
+    tokens, depth = attn_in.shape
+    width, last = pre_grads.shape[1], output_grad.shape[1]
+    if width % 128 or last % 128:
+        return jnp.concatenate([dot_tn(attn_in, pre_grads).astype(BF16), output_grad], axis=1)
+    block = 1024
+    return pl.pallas_call(
+        weight_grads_kernel,
+        grid=(tokens // block,),
+        in_specs=[
+            pl.BlockSpec((block, depth), lambda i: (i, 0)),
+            pl.BlockSpec((block, width), lambda i: (i, 0)),
+            pl.BlockSpec((depth, last), lambda i: (0, 0)),
+        ],
+        out_specs=pl.BlockSpec((depth, width + last), lambda i: (0, 0)),
+        out_shape=jax.ShapeDtypeStruct((depth, width + last), BF16),
+        scratch_shapes=[pltpu.VMEM((depth, width), F32)],
+        compiler_params=pltpu.CompilerParams(vmem_limit_bytes=48 << 20),
+        cost_estimate=small_cost(),
+        name="attention_weight_grads",
+    )(attn_in, pre_grads, output_grad)
 
 
 def is_plane():
@@ -1345,7 +1420,7 @@
         [gate_weight, down_weight, up_weight],
     )
     w_gate, w_down, w_up = [gather_weight(own) for own in cuts]
-    w_qkv, w_out = w_attn[:, : 3 * width], w_attn[:, 3 * width :]
+    w_qkv = w_attn[:, : 3 * width]
 
     qkv = jnp.dot(attn_in, w_qkv, preferred_element_type=F32)
     if is_plane():
@@ -1374,8 +1449,7 @@
     up_grad = scatter_weight(up_part)
     gate_grad = scatter_weight(gate_part)
 
-    out_heads_grad = jnp.dot(mid_all, w_out, preferred_element_type=F32).astype(BF16)
-    output_grad = dot_tn(mid_all, attn_out).astype(BF16)
+    out_heads_grad, output_grad = heads_and_output_grad(mid_all, w_attn, attn_out)
     out_heads_grad, down_grad = lax.optimization_barrier((out_heads_grad, down_grad))
     if is_plane():
         pre_grads, down_rows = attention_backward(
@@ -1392,7 +1466,7 @@
         (pre_grads, up_grad, gate_grad, swap_rows(down_grad))
     )
     swapped = swap_rows(jnp.concatenate([gate_grad, up_grad], axis=1))
-    attn_part = jnp.concatenate([dot_tn(attn_in, pre_grads).astype(BF16), output_grad], axis=1)
+    attn_part = attention_weight_grads(attn_in, pre_grads, output_grad)
     pre_grads, attn_part, swapped = lax.optimization_barrier((pre_grads, attn_part, swapped))
     attn_grad = scatter_weight(attn_part)
     (attn_in_grad,) = product_scatter([pre_grads], [w_attn], 2)

time: 933 us -> 912 us (0.977)
  matrix products: 62.6 us -> 19.2 us
  Pallas kernels: 760 us -> 781 us
    dot_general x3 -> x0, matrix products: 43.4 us -> none  [the longest x2 30.7 us: dot_tn(): lax.dot_general(a, b, (((0,), (0,)), ((), ())), preferred_element_type=F32)]
    pallas_call x0 -> x2, Pallas kernels: none -> 31.1 us  [the longest x1 18.2 us: attention_weight_grads(): pl.pallas_call(weight_grads_kernel, grid=(tokens // block,), in_specs=[pl...]
  transfers between devices with their start and end apart: 12 -> 12, of which waited for: 3 -> 4; matrix products, arithmetic and copies ran while one was open for 10% -> 5% of each run, Pallas kernels for 67% -> 71%
where the time goes in v9:
time: 912 us; the launch traced here: 904 us
  Pallas kernels  781 us (86%)
  other arithmetic  42.7 us (5%)
  matrix products  19.2 us (2%)
  local copies, waits for them, and re-layouts  19 us (2%)
  waiting for transfers between devices  15.6 us (2%)
  between operations  14.7 us (2%)
  starting transfers between devices  11.8 us (1%)
    pallas_call x3, Pallas kernels, plane_scatter(): pl.pallas_call(functools.partial(scatter_kernel, rows, offsets, len(jobs)...  256 us
    pallas_call x3, Pallas kernels, plane_gather(): pl.pallas_call(functools.partial(gather_kernel, [job[0] for job in jobs],...  227 us
    pallas_call x1, Pallas kernels, attention_backward(): pl.pallas_call(functools.partial(bwd_kernel, heads, hosts), grid=(groups,...  134 us
    pallas_call x1, Pallas kernels, attention_forward(): pl.pallas_call(functools.partial(fwd_kernel, heads, hosts), grid=(groups,...  88.6 us
    pallas_call x1, Pallas kernels, gated_rows(): pl.pallas_call(gated_kernel, grid=(tokens // block,), in_specs=[pl.BlockS...  44.5 us
    dot_general x1, matrix products, body(): qkv = jnp.dot(attn_in, w_qkv, preferred_element_type=F32)  19.2 us
  transfers between devices with their start and end apart: 12, of which 4 were waited for; matrix products, arithmetic and copies ran while one was open for 5% of the time, Pallas kernels for 71%

profile of v9, /device:TPU:0, one launch (start us, length us, event | category | flops | bytes accessed | tf_op | source)
XLA Modules:
  0.0 903.9 jit_solution(8261501039159803229)
XLA Ops:
  11.2 1.9 fusion.3.refs_0_
  13.1 77.3 %plane_gather.3 = (bf16[4096,2048]{1,0:T(8,128)(2,1)}, bf16[512,1024]{1,0:T(8,128)(2,1)}, bf16[512,1024]{1,0:T(8,128)(2,1)}, bf16[512,1024]{1,0:T(8,128)(2,1)}, ...) custom-call(bf16[512,2048]{1,0:T(8,128)(2,1)} %fusion.3.refs_0_, ...), custom_call_target="tpu_custom_call" | custom-call | flops 1048576 | bytes 1048576 | tf_op jit(solution)/shard_map/plane_gather/pallas_call | solution.py:971
  94.3 19.2 %fusion.10.refs_0_.refs_1_.refs_2_ = f32[4096,768]{1,0:T(8,128)} fusion(bf16[4096,2048]{1,0:T(8,128)(2,1)} %get-tuple-element.51.x_ref, bf16[2048,1024]{1,0:T(8,128)(2,1)} %all-gather.5.cloned.1.call-done.refs_1_.w_ref), kind=kOutput, calls=%fused_computation.18 | convolution fusion | flops 12884901888 | bytes 32505856 | tf_op jit(solution)/shard_map/dot_general | solution.py:1425
  113.5 88.6 %tree_attention_forward.1 = (bf16[4096,256]{1,0:T(8,128)(2,1)}, f32[2,2,4096]{2,1,0:T(2,128)}, bf16[4096,256]{1,0:T(8,128)(2,1)}, bf16[4096,256]{1,0:T(8,128)(2,...) custom-call(f32[4096,768]{1,0:T(8,128)} %fusion.10.refs_0_.refs_1_.refs_2_, ...), custom_call_target="tpu_custom_call" | custom-call | flops 1048576 | bytes 1048576 | tf_op jit(solution)/shard_map/tree_attention_forward/pallas_call | solution.py:655
  202.1 81.3 %plane_scatter.3 = f32[512,2048]{1,0:T(8,128)} custom-call(bf16[4096,256]{1,0:T(8,128)(2,1)} %get-tuple-element.56.refs_0_.out_ref.refs_3_, bf16[2048,1024]{1,0:T(8,128)(2,1)} %all-gather.5.cloned.1.call-done.refs_1_.w_ref), custom_call_target="tpu_custom_call" | custom-call | flops 1048576 | bytes 1048576 | tf_op jit(solution)/shard_map/plane_scatter/pallas_call | solution.py:1164
  283.4 3.0 multiply_reduce_fusion.1
  288.2 74.4 %plane_gather.4 = (bf16[4096,2048]{1,0:T(8,128)(2,1)}, bf16[4096,1024]{1,0:T(8,128)(2,1)}) custom-call(bf16[512,2048]{1,0:T(8,128)(2,1)S(1)} %multiply_convert_fusion.refs_0_, bf16[4096,2048]{1,0:T(8,128)(2,1)} %get-tuple-element.60.refs_1_.refs_4_, bf16[2048,1024]{1,0:T(8,128)(2,1)} %all-gather.7.cloned.1.call-done.refs_2_), custom_call_target="tpu_custom_call" | custom-call | flops 1048576 | bytes 1048576 | tf_op jit(solution)/shard_map/plane_gather/pallas_call | solution.py:971
  362.6 2.2 copy-done.3
  364.8 44.5 %gated_rows.1 = (bf16[4096,1024]{1,0:T(8,128)(2,1)}, bf16[4096,1024]{1,0:T(8,128)(2,1)}, bf16[4096,1024]{1,0:T(8,128)(2,1)}) custom-call(bf16[4096,2048]{1,0:T(8,128)(2,1)} %get-tuple-element.62.x_ref.refs_3_, bf16[4096,1024]{1,0:T(8,128)(2,1)} %get-tuple-element.63.grad_ref, bf16[2048,1024]{1,0:T(8,128)(2,1)S(1)} %copy-done.3, ...), custom_call_target="tpu_custom_call" | custom-call | flops 1048576 | bytes 1048576 | tf_op jit(solution)/shard_map/gated_rows/pallas_call | solution.py:1215
  409.3 91.2 %plane_scatter.4 = (f32[512,2048]{1,0:T(8,128)}, bf16[2048,1024]{1,0:T(8,128)(2,1)}) custom-call(bf16[4096,1024]{1,0:T(8,128)(2,1)} %get-tuple-element.66.refs_0_.refs_5_, bf16[4096,1024]{1,0:T(8,128)(2,1)} %get-tuple-element.67.refs_1_.refs_4_, bf16[2048,1024]{1,0:T(8,128)(2,1)} %all-gather.9.cloned.1.call-done.gate_ref.refs_2_, ...), custom_call_target="tpu_custom_call" | custom-call | flops 1048576 | bytes 1048576 | tf_op jit(solution)/shard_map/plane_scatter/pallas_call | solution.py:1164
  502.1 4.7 multiply_reduce_fusion
  511.0 75.4 %plane_gather.5 = (bf16[4096,2048]{1,0:T(8,128)(2,1)}, bf16[4096,2048]{1,0:T(8,128)(2,1)}, bf16[2048,1024]{1,0:T(8,128)(2,1)}, bf16[2048,1024]{1,0:T(8,128)(2,1)}) custom-call(bf16[512,2048]{1,0:T(8,128)(2,1)S(1)} %fusion.15.refs_0_, bf16[4096,1024]{1,0:T(8,128)(2,1)} %get-tuple-element.68.refs_5_.refs_1_, ...), custom_call_target="tpu_custom_call" | custom-call | flops 1048576 | bytes 1048576 | tf_op jit(solution)/shard_map/plane_gather/pallas_call | solution.py:971
  588.0 2.2 copy-done
  590.2 12.9 %heads_and_output_grad.1 = (bf16[4096,256]{1,0:T(8,128)(2,1)S(1)}, bf16[2048,256]{1,0:T(8,128)(2,1)S(1)}) custom-call(bf16[4096,2048]{1,0:T(8,128)(2,1)} %get-tuple-element.70.x_ref, bf16[2048,1024]{1,0:T(8,128)(2,1)S(1)} %copy-done, bf16[4096,256]{1,0:T(8,128)(2,1)S(1)} %copy-done.1), custom_call_target="tpu_custom_call" | custom-call | flops 1048576 | bytes 1048576 | tf_op jit(solution)/shard_map/heads_and_output_grad/pallas_call | solution.py:1249
  604.5 3.5 all-to-all-start
  608.0 133.8 %tree_attention_backward.1 = (bf16[4096,768]{1,0:T(8,128)(2,1)}, bf16[512,2048]{1,0:T(8,128)(2,1)}) custom-call(bf16[4096,256]{1,0:T(8,128)(2,1)} %get-tuple-element.57.refs_0_, bf16[4096,256]{1,0:T(8,128)(2,1)} %get-tuple-element.58.refs_1_, bf16[4096,256]{1,0:T(8,128)(2,1)} %get-tuple-element.59.refs_2_, ...), custom_call_target="tpu_custom_call" | custom-call | flops 1048576 | bytes 1048576 | tf_op jit(solution)/shard_map/tree_attention_backward/pallas_call | solution.py:697
  741.9 3.5 pad_maximum_fusion
  745.3 3.6 all-to-all-start.1
  749.0 18.2 %attention_weight_grads.1 = bf16[2048,1024]{1,0:T(8,128)(2,1)S(1)} custom-call(bf16[4096,2048]{1,0:T(8,128)(2,1)} %get-tuple-element.51.x_ref, bf16[4096,768]{1,0:T(8,128)(2,1)} %get-tuple-element.85.pre_ref.refs_0_, bf16[2048,256]{1,0:T(8,128)(2,1)S(1)} %get-tuple-element.82.output_ref), custom_call_target="tpu_custom_call" | custom-call | flops 1048576 | bytes 1048576 | tf_op jit(solution)/shard_map/attention_weight_grads/pallas_call | solution.py:1284
  767.2 2.0 copy-done.2
  769.2 5.4 all-to-all-done.1
  776.3 83.4 %plane_scatter.5 = f32[512,2048]{1,0:T(8,128)} custom-call(bf16[4096,768]{1,0:T(8,128)(2,1)} %get-tuple-element.85.pre_ref.refs_0_, bf16[2048,1024]{1,0:T(8,128)(2,1)} %all-gather.5.cloned.1.call-done.refs_1_.w_ref), custom_call_target="tpu_custom_call" | custom-call | flops 1048576 | bytes 1048576 | tf_op jit(solution)/shard_map/plane_scatter/pallas_call | solution.py:1164
  859.8 3.0 multiply_reduce_fusion.2
  862.8 2.8 multiply_reduce_fusion.3
  865.8 3.0 fusion.4
  868.8 3.7 all-to-all-start.2
  872.5 8.9 fusion.8
  881.5 5.5 all-to-all-done.2
  887.1 1.8 multiply_reduce_fusion.4
  888.9 1.8 multiply_reduce_fusion.5
  890.7 1.8 multiply_reduce_fusion.6
  894.1 2.1 collective-permute-done
  (88 shorter events, 22.6 us)
Async XLA Ops:
  7.2 3.6 copy-start.12
  7.2 4.1 copy-start.21
  7.2 87.1 %all-gather.5.cloned.1.call-start = ((), (), s32[]{:S(2)}) async-start(), calls=%async_computation.7 | async-start | bytes 5242880 | tf_op jit(solution)/shard_map/all_gather | solution.py:1354
  10.7 2.5 copy-start.7
  10.7 2.5 copy-start.8
  10.7 2.5 copy-start.9
  10.7 277.5 %all-gather.7.cloned.1.call-start = ((), (), s32[]{:S(2)}) async-start(), calls=%async_computation.8 | async-start | bytes 5242880 | tf_op jit(solution)/shard_map/all_gather | solution.py:1354
  90.4 1.3 copy-start.4
  92.4 270.1 %all-gather.9.cloned.1.call-start = ((), (), s32[]{:S(2)}) async-start(), calls=%async_computation.9 | async-start | bytes 5242880 | tf_op jit(solution)/shard_map/all_gather | solution.py:1354
  93.2 269.4 %all-gather.11.cloned.1.call-start = ((), (), s32[]{:S(2)}) async-start(), calls=%async_computation.10 | async-start | bytes 5242880 | tf_op jit(solution)/shard_map/all_gather | solution.py:1354
  93.8 510.7 %reduce-scatter.5.cloned.1.call-start = ((), (), s32[]{:S(2)}) async-start(), calls=%async_computation.11 | async-start | bytes 5242880 | tf_op jit(solution)/shard_map/reduce_scatter | solution.py:1358
  202.1 84.3 %copy-start.20 = (f32[2048]{0:T(1024)S(1)}, f32[2048]{0:T(1024)}, u32[]{:S(2)}) copy-start(f32[2048]{0:T(1024)} %param.20) | copy-start | bytes 24580
  283.3 3.5 copy-start.10
  283.4 4.1 copy-start.13
  362.6 2.2 copy-start.3
  500.5 1.6 copy-start.14
  500.6 241.3 %reduce-scatter.7.cloned.1.call-start = ((), (), s32[]{:S(2)}) async-start(), calls=%async_computation.12 | async-start | bytes 5242880 | tf_op jit(solution)/shard_map/reduce_scatter | solution.py:1358
  502.1 5.4 copy-start.11
  502.1 6.7 copy-start.16
  502.1 7.3 copy-start.17
  586.4 1.6 copy-start.1
  586.5 155.4 %reduce-scatter.9.cloned.1.call-start = ((), (), s32[]{:S(2)}) async-start(), calls=%async_computation.13 | async-start | bytes 5242880 | tf_op jit(solution)/shard_map/reduce_scatter | solution.py:1358
  588.0 2.2 copy-start
  604.5 137.4 %all-to-all-start = ((bf16[4,128,1024]{2,1,0:T(8,128)(2,1)}), bf16[4,128,1024]{2,1,0:T(8,128)(2,1)S(1)}, u32[]{:S(2)}, u32[]{:S(2)}) async-start(bf16[4,128,1024]{2,1,0:T(8,128)(2,1)} %bitcast.70), calls=%async_computation.3 | async-start | bytes 2097152 | tf_op jit(solution)/shard_map/all_to_all | solution.py:1363
  741.9 3.5 copy-start.18
  745.3 29.3 %all-to-all-start.1 = ((bf16[4,128,2048]{2,1,0:T(8,128)(2,1)}), bf16[4,128,2048]{2,1,0:T(8,128)(2,1)S(1)}, u32[]{:S(2)}, u32[]{:S(2)}) async-start(bf16[4,128,2048]{2,1,0:T(8,128)(2,1)} %bitcast.68), calls=%async_computation.4 | async-start | bytes 4194304 | tf_op jit(solution)/shard_map/all_to_all | solution.py:1363
  748.9 116.8 %reduce-scatter.11.cloned.1.call-start = ((), (), s32[]{:S(2)}) async-start(), calls=%async_computation.14 | async-start | bytes 5242880 | tf_op jit(solution)/shard_map/reduce_scatter | solution.py:1358
  767.2 2.0 copy-start.2
  769.2 5.4 copy-start.19
  859.8 5.9 copy-start.15
  868.8 18.2 %all-to-all-start.2 = ((bf16[4,128,1024]{2,1,0:T(8,128)(2,1)}), bf16[4,128,1024]{2,1,0:T(8,128)(2,1)S(1)}, u32[]{:S(2)}, u32[]{:S(2)}) async-start(bf16[4,128,1024]{2,1,0:T(8,128)(2,1)} %bitcast.69), calls=%async_computation.6 | async-start | bytes 2097152 | tf_op jit(solution)/shard_map/all_to_all | solution.py:1363
  892.7 3.6 collective-permute-start
  (2 other events, 2.0 us)
Sparse Core Ops, SparseCore 0:
  10.8 83.4 all-gather.4
  95.9 79.3 all-gather.6
  176.8 79.2 all-gather.8
  257.5 79.2 all-gather.10
  500.7 75.6 reduce-scatter.4
  586.6 75.6 reduce-scatter.6
  664.5 77.2 reduce-scatter.8
  774.8 76.3 reduce-scatter.10

commit v10 on v9

--- a/solution.py
+++ b/solution.py
@@ -376,37 +376,43 @@
     first_tree = base // BQ
     mixed_end = -(-(branch_end + MOST_SEG) // BQ)
     chunks = jnp.minimum(i * BQ, base) // BK
+    half = BQ // 2
 
     @pl.when(i < first_tree)
     def _():
         @pl.loop(0, chunks)
         def _(j):
             start = pl.multiple_of(j * BK, BK)
-            tile(start, BK, 0, start)
+            tile(start, BK, 0, start, 0, BQ)
 
     @pl.when(i >= first_tree)
     def _():
-        tile(0, base, 0, 0)
+        tile(0, base, 0, 0, 0, BQ)
 
     @pl.when(i < first_tree)
     def _():
         start = pl.multiple_of(chunks * BK, BK)
-        tile(start, BK, 1, start)
+        for part in range(2):
+            tile(start, (part + 1) * half, 1, start, part * half, half)
 
     for block in range(first_tree, mixed_end):
 
         @pl.when(i == block)
         def _(block=block):
-            tile(base, (block + 1) * BQ - base, 2, base)
+            for part in range(2):
+                tile(base, block * BQ + (part + 1) * half - base, 2, base, part * half, half)
 
     @pl.when(i >= mixed_end)
     def _():
-        tile(base, branch_end - base, 3, base)
-        tile(pl.multiple_of(i * BQ - MOST_SEG, MOST_SEG), BQ + MOST_SEG, 4, branch_end)
+        tile(base, branch_end - base, 3, base, 0, BQ)
+        for part in range(2):
+            start = pl.multiple_of(i * BQ + part * half - MOST_SEG, MOST_SEG)
+            tile(start, half + MOST_SEG, 4, branch_end, part * half, half)
 
 
 def most_keys():
-    return TRUNK + 4 * MOST_SEG + BQ + MOST_SEG
+    branch_end = TRUNK + 4 * MOST_SEG
+    return max(branch_end + BQ // 2 + MOST_SEG, -(-(branch_end + MOST_SEG) // BQ) * BQ)
 
 
 def seen_mask(kind, q_at, k_at, seg_q, par_q, seg_k):
@@ -463,40 +469,40 @@
     m_ref[...] = jnp.full_like(m_ref, NEG_LARGE)
     acc_ref[...] = jnp.zeros_like(acc_ref)
 
-    def score_tile(start, width, kind, place):
-        keys = pl.ds(start, width)
+    def score_tile(start, width, kind, place, first, count):
+        keys, rows = pl.ds(start, width), slice(first, first + count)
         k = kt_ref[:, keys]
         seen = None
         if kind != 0:
-            shape = (BQ, width)
+            shape = (count, width)
             seen = seen_mask(
                 kind,
-                lax.broadcasted_iota(jnp.int32, shape, 0) + i * BQ,
+                lax.broadcasted_iota(jnp.int32, shape, 0) + i * BQ + first,
                 lax.broadcasted_iota(jnp.int32, shape, 1) + start,
-                cols_ref[:, 0:1], cols_ref[:, 1:2], rows_ref[0:1, keys],
+                cols_ref[rows, 0:1], cols_ref[rows, 1:2], rows_ref[0:1, keys],
             )
         for h in range(heads):
-            s = dot_n(q_heads[h], k)
+            s = dot_n(q_heads[h][rows], k)
             if seen is not None:
                 s = jnp.where(seen, s, NEG_LARGE)
-            s_ref[h, :, pl.ds(place, width)] = s
-            largest = m_ref[h]
+            s_ref[h, rows, pl.ds(place, width)] = s
+            largest = m_ref[h, rows]
             for c in range(width // 128):
                 largest = jnp.maximum(largest, s[:, c * 128 : (c + 1) * 128])
-            m_ref[h] = largest
+            m_ref[h, rows] = largest
 
     key_plan(i, score_tile)
     for h in range(heads):
         m_ref[h] = jnp.broadcast_to(jnp.max(m_ref[h], axis=1, keepdims=True), (BQ, 128))
 
-    def value_tile(start, width, kind, place):
-        keys = pl.ds(start, width)
+    def value_tile(start, width, kind, place, first, count):
+        keys, rows = pl.ds(start, width), slice(first, first + count)
         for h in range(heads):
-            m = m_ref[h]
+            m = m_ref[h, rows]
             parts = [
-                jnp.exp(s_ref[h, :, pl.ds(place + c * 128, 128)] - m).astype(BF16) for c in range(width // 128)
+                jnp.exp(s_ref[h, rows, pl.ds(place + c * 128, 128)] - m).astype(BF16) for c in range(width // 128)
             ]
-            acc_ref[h] += dot_n(jnp.concatenate(parts, axis=1), va_ref[h, keys, :])
+            acc_ref[h, rows] += dot_n(jnp.concatenate(parts, axis=1), va_ref[h, keys, :])
 
     key_plan(i, value_tile)
     out, lse = None, None
@@ -559,37 +565,35 @@
     lses = [lse_ref[0, h : h + 1, :] for h in range(heads)]
     q_turned = [jnp.transpose(x) for x in q_heads]
     do_turned = [jnp.transpose(x) for x in do_heads]
-    q_stack = jnp.concatenate(q_heads, axis=0)
-    do_stack = jnp.concatenate(do_heads, axis=0)
     dq_acc[...] = jnp.zeros_like(dq_acc)
 
-    def tile(start, width, kind, place):
-        keys = pl.ds(start, width)
+    def tile(start, width, kind, place, first, count):
+        keys, part = pl.ds(start, width), slice(first, first + count)
         k = k_ref[keys, :]
         v = v_ref[keys, :]
         seen = None
         if kind != 0:
-            shape = (width, BQ)
+            shape = (width, count)
             seen = seen_mask(
                 kind,
-                lax.broadcasted_iota(jnp.int32, shape, 1) + i * BQ,
+                lax.broadcasted_iota(jnp.int32, shape, 1) + i * BQ + first,
                 lax.broadcasted_iota(jnp.int32, shape, 0) + start,
-                rows_ref[0:1, :], rows_ref[1:2, :], cols_ref[keys, 0:1],
+                rows_ref[0:1, part], rows_ref[1:2, part], cols_ref[keys, 0:1],
             )
         probs, grads, k_heads = [], [], []
         for h in range(heads):
-            s = dot_n(k, q_turned[h])
-            p = jnp.exp(s - lses[h])
+            s = dot_n(k, q_turned[h][:, part])
+            p = jnp.exp(s - lses[h][:, part])
             if seen is not None:
                 p = jnp.where(seen, p, 0.0)
-            dp = dot_n(v, do_turned[h])
+            dp = dot_n(v, do_turned[h][:, part])
             probs.append(p.astype(BF16))
-            grads.append((p * (dp - deltas[h])).astype(BF16))
+            grads.append((p * (dp - deltas[h][:, part])).astype(BF16))
             k_heads.append(jnp.where(head_mask(k.shape, h), k, jnp.zeros_like(k)))
         grad_row = jnp.concatenate(grads, axis=1)
-        dv_acc[keys, :] += dot_n(jnp.concatenate(probs, axis=1), do_stack)
-        dk_acc[keys, :] += dot_n(grad_row, q_stack)
-        dq_acc[...] += dot_tn(jnp.concatenate(grads, axis=0), jnp.concatenate(k_heads, axis=0))
+        dv_acc[keys, :] += dot_n(jnp.concatenate(probs, axis=1), jnp.concatenate([x[part] for x in do_heads], axis=0))
+        dk_acc[keys, :] += dot_n(grad_row, jnp.concatenate([x[part] for x in q_heads], axis=0))
+        dq_acc[part, :] += dot_tn(jnp.concatenate(grads, axis=0), jnp.concatenate(k_heads, axis=0))
 
     key_plan(i, tile)
     dq = dq_acc[...] * SCALE
@@ -677,7 +681,7 @@
         ]
         + (gather_sems() if hosts else []),
         compiler_params=pltpu.CompilerParams(
-            vmem_limit_bytes=56 << 20, collective_id=6 if hosts else None, has_side_effects=hosts
+            vmem_limit_bytes=60 << 20, collective_id=6 if hosts else None, has_side_effects=hosts
         ),
         cost_estimate=small_cost(),
         name="tree_attention_forward",
@@ -980,7 +984,7 @@
         out_shape=[jax.ShapeDtypeStruct((8 * count, width), rows.dtype)] + [out for job in jobs for out in job[3]],
         scratch_shapes=scratch,
         compiler_params=pltpu.CompilerParams(
-            collective_id=collective_id, has_side_effects=True, vmem_limit_bytes=(48 << 20) if jobs else None
+            collective_id=collective_id, has_side_effects=True, vmem_limit_bytes=(60 << 20) if jobs else None
         ),
         cost_estimate=small_cost(),
         name="plane_gather",
@@ -1179,7 +1183,7 @@
         + [pltpu.SemaphoreType.DMA((2, len(parts))), pltpu.SemaphoreType.DMA((len(parts),))]
         + (product_buffers(rights[0].shape[1]) if jobs else []),
         compiler_params=pltpu.CompilerParams(
-            collective_id=collective_id, has_side_effects=True, vmem_limit_bytes=(58 if jobs else 52) << 20
+            collective_id=collective_id, has_side_effects=True, vmem_limit_bytes=60 << 20
         ),
         cost_estimate=small_cost(),
         name="plane_scatter",
@@ -1218,7 +1222,7 @@
         in_specs=[pl.BlockSpec((block, depth), lambda i: (i, 0)), rows, weight, weight],
         out_specs=[rows] * 3,
         out_shape=[out] * 3,
-        compiler_params=pltpu.CompilerParams(vmem_limit_bytes=48 << 20),
+        compiler_params=pltpu.CompilerParams(vmem_limit_bytes=60 << 20),
         cost_estimate=small_cost(),
         name="gated_rows",
     )(x, hidden_grad, w_gate, w_up)
@@ -1253,7 +1257,7 @@
         out_specs=[rows, pl.BlockSpec((depth, width), lambda i: (0, 0))],
         out_shape=[jax.ShapeDtypeStruct((tokens, width), BF16), jax.ShapeDtypeStruct((depth, width), BF16)],
         scratch_shapes=[pltpu.VMEM((width, depth), F32)],
-        compiler_params=pltpu.CompilerParams(vmem_limit_bytes=40 << 20),
+        compiler_params=pltpu.CompilerParams(vmem_limit_bytes=60 << 20),
         cost_estimate=small_cost(),
         name="heads_and_output_grad",
     )(mid, w_attn, attn_out)
@@ -1292,7 +1296,7 @@
         out_specs=pl.BlockSpec((depth, width + last), lambda i: (0, 0)),
         out_shape=jax.ShapeDtypeStruct((depth, width + last), BF16),
         scratch_shapes=[pltpu.VMEM((depth, width), F32)],
-        compiler_params=pltpu.CompilerParams(vmem_limit_bytes=48 << 20),
+        compiler_params=pltpu.CompilerParams(vmem_limit_bytes=60 << 20),
         cost_estimate=small_cost(),
         name="attention_weight_grads",
     )(attn_in, pre_grads, output_grad)

time: 912 us -> 907 us (level)
  local copies, waits for them, and re-layouts: 19 us -> 7.99 us
  waiting for transfers between devices: 15.6 us -> 25.9 us
    unnamed x44 -> x14, local copies, waits for them, and re-layouts: 15.8 us -> 3.25 us
    reduce_scatter x4, waiting for transfers between devices: 0.06 us -> 9.8 us  [scatter_weight(): lax.psum_scatter(grad.astype(BF16), 'fsdp', scatter_dimension=0, tiled=True)]
  transfers between devices with their start and end apart: 12 -> 12, of which waited for: 4 -> 5; matrix products, arithmetic and copies ran while one was open for 5% -> 6% of each run, Pallas kernels for 71% -> 71%
where the time goes in v10:
time: 907 us; the launch traced here: 900 us
  Pallas kernels  775 us (85%)
  other arithmetic  44.8 us (5%)
  waiting for transfers between devices  25.9 us (3%)
  matrix products  19.2 us (2%)
  between operations  14.6 us (2%)
  starting transfers between devices  12.6 us (1%)
    pallas_call x3, Pallas kernels, plane_scatter(): pl.pallas_call(functools.partial(scatter_kernel, rows, offsets, len(jobs)...  256 us
    pallas_call x3, Pallas kernels, plane_gather(): pl.pallas_call(functools.partial(gather_kernel, [job[0] for job in jobs],...  228 us
    pallas_call x1, Pallas kernels, attention_backward(): pl.pallas_call(functools.partial(bwd_kernel, heads, hosts), grid=(groups,...  126 us
    pallas_call x1, Pallas kernels, attention_forward(): pl.pallas_call(functools.partial(fwd_kernel, heads, hosts), grid=(groups,...  85 us
    pallas_call x1, Pallas kernels, gated_rows(): pl.pallas_call(gated_kernel, grid=(tokens // block,), in_specs=[pl.BlockS...  45.7 us
    pallas_call x1, Pallas kernels, attention_weight_grads(): pl.pallas_call(weight_grads_kernel, grid=(tokens // block,), in_specs=[pl...  20.4 us
    dot_general x1, matrix products, body(): qkv = jnp.dot(attn_in, w_qkv, preferred_element_type=F32)  19.2 us
  transfers between devices with their start and end apart: 12, of which 5 were waited for; matrix products, arithmetic and copies ran while one was open for 6% of the time, Pallas kernels for 71%

profile of v10, /device:TPU:0, one launch (start us, length us, event | category | flops | bytes accessed | tf_op | source)
XLA Modules:
  0.0 899.8 jit_solution(13886163164193618294)
XLA Ops:
  11.2 1.9 fusion.3.refs_0_
  13.1 78.6 %plane_gather.3 = (bf16[4096,2048]{1,0:T(8,128)(2,1)}, bf16[512,1024]{1,0:T(8,128)(2,1)}, bf16[512,1024]{1,0:T(8,128)(2,1)}, bf16[512,1024]{1,0:T(8,128)(2,1)}, ...) custom-call(bf16[512,2048]{1,0:T(8,128)(2,1)} %fusion.3.refs_0_, ...), custom_call_target="tpu_custom_call" | custom-call | flops 1048576 | bytes 1048576 | tf_op jit(solution)/shard_map/plane_gather/pallas_call | solution.py:975
  94.3 19.2 %fusion.10.refs_0_.refs_1_.refs_2_ = f32[4096,768]{1,0:T(8,128)} fusion(bf16[4096,2048]{1,0:T(8,128)(2,1)} %get-tuple-element.51.x_ref, bf16[2048,1024]{1,0:T(8,128)(2,1)} %all-gather.5.cloned.1.call-done.refs_1_.w_ref), kind=kOutput, calls=%fused_computation.18 | convolution fusion | flops 12884901888 | bytes 32505856 | tf_op jit(solution)/shard_map/dot_general | solution.py:1429
  113.5 85.0 %tree_attention_forward.1 = (bf16[4096,256]{1,0:T(8,128)(2,1)}, f32[2,2,4096]{2,1,0:T(2,128)}, bf16[4096,256]{1,0:T(8,128)(2,1)}, bf16[4096,256]{1,0:T(8,128)(2,...) custom-call(f32[4096,768]{1,0:T(8,128)} %fusion.10.refs_0_.refs_1_.refs_2_, ...), custom_call_target="tpu_custom_call" | custom-call | flops 1048576 | bytes 1048576 | tf_op jit(solution)/shard_map/tree_attention_forward/pallas_call | solution.py:659
  198.4 81.3 %plane_scatter.3 = f32[512,2048]{1,0:T(8,128)} custom-call(bf16[4096,256]{1,0:T(8,128)(2,1)} %get-tuple-element.56.refs_0_.out_ref.refs_3_, bf16[2048,1024]{1,0:T(8,128)(2,1)} %all-gather.5.cloned.1.call-done.refs_1_.w_ref), custom_call_target="tpu_custom_call" | custom-call | flops 1048576 | bytes 1048576 | tf_op jit(solution)/shard_map/plane_scatter/pallas_call | solution.py:1168
  279.8 3.0 multiply_reduce_fusion.1
  283.3 2.0 multiply_convert_fusion.refs_0_
  285.3 74.5 %plane_gather.4 = (bf16[4096,2048]{1,0:T(8,128)(2,1)}, bf16[4096,1024]{1,0:T(8,128)(2,1)}) custom-call(bf16[512,2048]{1,0:T(8,128)(2,1)} %multiply_convert_fusion.refs_0_, bf16[4096,2048]{1,0:T(8,128)(2,1)} %get-tuple-element.60.refs_1_.refs_4_, bf16[2048,1024]{1,0:T(8,128)(2,1)} %all-gather.7.cloned.1.call-done.refs_2_), custom_call_target="tpu_custom_call" | custom-call | flops 1048576 | bytes 1048576 | tf_op jit(solution)/shard_map/plane_gather/pallas_call | solution.py:975
  359.8 45.7 %gated_rows.1 = (bf16[4096,1024]{1,0:T(8,128)(2,1)}, bf16[4096,1024]{1,0:T(8,128)(2,1)}, bf16[4096,1024]{1,0:T(8,128)(2,1)}) custom-call(bf16[4096,2048]{1,0:T(8,128)(2,1)} %get-tuple-element.62.x_ref.refs_3_, bf16[4096,1024]{1,0:T(8,128)(2,1)} %get-tuple-element.63.grad_ref, bf16[2048,1024]{1,0:T(8,128)(2,1)} %all-gather.9.cloned.1.call-done.gate_ref.refs_2_, ...), custom_call_target="tpu_custom_call" | custom-call | flops 1048576 | bytes 1048576 | tf_op jit(solution)/shard_map/gated_rows/pallas_call | solution.py:1219
  405.6 91.3 %plane_scatter.4 = (f32[512,2048]{1,0:T(8,128)}, bf16[2048,1024]{1,0:T(8,128)(2,1)}) custom-call(bf16[4096,1024]{1,0:T(8,128)(2,1)} %get-tuple-element.66.refs_0_.refs_5_, bf16[4096,1024]{1,0:T(8,128)(2,1)} %get-tuple-element.67.refs_1_.refs_4_, bf16[2048,1024]{1,0:T(8,128)(2,1)} %all-gather.9.cloned.1.call-done.gate_ref.refs_2_, ...), custom_call_target="tpu_custom_call" | custom-call | flops 1048576 | bytes 1048576 | tf_op jit(solution)/shard_map/plane_scatter/pallas_call | solution.py:1168
  497.0 4.5 multiply_reduce_fusion
  504.3 3.0 fusion.15.refs_0_
  507.3 74.6 %plane_gather.5 = (bf16[4096,2048]{1,0:T(8,128)(2,1)}, bf16[4096,2048]{1,0:T(8,128)(2,1)}, bf16[2048,1024]{1,0:T(8,128)(2,1)}, bf16[2048,1024]{1,0:T(8,128)(2,1)}) custom-call(bf16[512,2048]{1,0:T(8,128)(2,1)} %fusion.15.refs_0_, bf16[4096,1024]{1,0:T(8,128)(2,1)} %get-tuple-element.68.refs_5_.refs_1_, ...), custom_call_target="tpu_custom_call" | custom-call | flops 1048576 | bytes 1048576 | tf_op jit(solution)/shard_map/plane_gather/pallas_call | solution.py:975
  582.7 13.9 %heads_and_output_grad.1 = (bf16[4096,256]{1,0:T(8,128)(2,1)}, bf16[2048,256]{1,0:T(8,128)(2,1)}) custom-call(bf16[4096,2048]{1,0:T(8,128)(2,1)} %get-tuple-element.70.x_ref, bf16[2048,1024]{1,0:T(8,128)(2,1)} %all-gather.5.cloned.1.call-done.refs_1_.w_ref, bf16[4096,256]{1,0:T(8,128)(2,1)} %get-tuple-element.56.refs_0_.out_ref.refs_3_), custom_call_target="tpu_custom_call" | custom-call | flops 1048576 | bytes 1048576 | tf_op jit(solution)/shard_map/heads_and_output_grad/pallas_call | solution.py:1253
  596.6 3.5 all-to-all-start
  600.2 125.9 %tree_attention_backward.1 = (bf16[4096,768]{1,0:T(8,128)(2,1)}, bf16[512,2048]{1,0:T(8,128)(2,1)}) custom-call(bf16[4096,256]{1,0:T(8,128)(2,1)} %get-tuple-element.57.refs_0_, bf16[4096,256]{1,0:T(8,128)(2,1)} %get-tuple-element.58.refs_1_, bf16[4096,256]{1,0:T(8,128)(2,1)} %get-tuple-element.59.refs_2_, ...), custom_call_target="tpu_custom_call" | custom-call | flops 1048576 | bytes 1048576 | tf_op jit(solution)/shard_map/tree_attention_backward/pallas_call | solution.py:701
  726.1 9.8 %reduce-scatter.9.cloned.1.call-done = bf16[512,1024]{1,0:T(8,128)(2,1)} async-done(((bf16[2048,1024]{1,0:T(8,128)(2,1)}), bf16[512,1024]{1,0:T(8,128)(2,1)}) %reduce-scatter.9.cloned.1.call-update) | async-done | bytes 1048592 | tf_op jit(solution)/shard_map/reduce_scatter | solution.py:1362
  735.9 3.1 pad_maximum_fusion
  739.0 4.4 all-to-all-start.1
  743.5 20.4 %attention_weight_grads.1 = bf16[2048,1024]{1,0:T(8,128)(2,1)} custom-call(bf16[4096,2048]{1,0:T(8,128)(2,1)} %get-tuple-element.51.x_ref, bf16[4096,768]{1,0:T(8,128)(2,1)} %get-tuple-element.85.pre_ref.refs_0_, bf16[2048,256]{1,0:T(8,128)(2,1)} %get-tuple-element.82.output_ref), custom_call_target="tpu_custom_call" | custom-call | flops 1048576 | bytes 1048576 | tf_op jit(solution)/shard_map/attention_weight_grads/pallas_call | solution.py:1288
  763.9 5.3 all-to-all-done.1
  770.8 83.4 %plane_scatter.5 = f32[512,2048]{1,0:T(8,128)} custom-call(bf16[4096,768]{1,0:T(8,128)(2,1)} %get-tuple-element.85.pre_ref.refs_0_, bf16[2048,1024]{1,0:T(8,128)(2,1)} %all-gather.5.cloned.1.call-done.refs_1_.w_ref), custom_call_target="tpu_custom_call" | custom-call | flops 1048576 | bytes 1048576 | tf_op jit(solution)/shard_map/plane_scatter/pallas_call | solution.py:1168
  855.9 2.8 multiply_reduce_fusion.2
  858.7 2.8 multiply_reduce_fusion.3
  861.7 3.0 fusion.4
  864.7 3.7 all-to-all-start.2
  868.4 8.9 fusion.8
  877.4 5.5 all-to-all-done.2
  883.0 1.8 multiply_reduce_fusion.4
  884.8 1.8 multiply_reduce_fusion.5
  886.6 1.8 multiply_reduce_fusion.6
  890.0 2.2 collective-permute-done
  (58 shorter events, 16.3 us)
Async XLA Ops:
  7.2 3.6 copy-start.2
  7.2 4.0 copy-start.6
  7.2 87.1 %all-gather.5.cloned.1.call-start = ((), (), s32[]{:S(2)}) async-start(), calls=%async_computation.7 | async-start | bytes 5242880 | tf_op jit(solution)/shard_map/all_gather | solution.py:1358
  10.7 274.6 %all-gather.7.cloned.1.call-start = ((), (), s32[]{:S(2)}) async-start(), calls=%async_computation.8 | async-start | bytes 5242880 | tf_op jit(solution)/shard_map/all_gather | solution.py:1358
  91.7 268.1 %all-gather.9.cloned.1.call-start = ((), (), s32[]{:S(2)}) async-start(), calls=%async_computation.9 | async-start | bytes 5242880 | tf_op jit(solution)/shard_map/all_gather | solution.py:1358
  92.5 267.3 %all-gather.11.cloned.1.call-start = ((), (), s32[]{:S(2)}) async-start(), calls=%async_computation.10 | async-start | bytes 5242880 | tf_op jit(solution)/shard_map/all_gather | solution.py:1358
  93.1 503.6 %reduce-scatter.5.cloned.1.call-start = ((), (), s32[]{:S(2)}) async-start(), calls=%async_computation.11 | async-start | bytes 5242880 | tf_op jit(solution)/shard_map/reduce_scatter | solution.py:1362
  279.8 3.5 copy-start
  279.8 3.5 copy-start.5
  496.9 229.2 %reduce-scatter.7.cloned.1.call-start = ((), (), s32[]{:S(2)}) async-start(), calls=%async_computation.12 | async-start | bytes 5242880 | tf_op jit(solution)/shard_map/reduce_scatter | solution.py:1362
  497.0 5.1 copy-start.1
  497.0 6.7 copy-start.3
  497.0 7.3 copy-start.4
  581.9 154.0 %reduce-scatter.9.cloned.1.call-start = ((), (), s32[]{:S(2)}) async-start(), calls=%async_computation.13 | async-start | bytes 5242880 | tf_op jit(solution)/shard_map/reduce_scatter | solution.py:1362
  596.6 139.3 %all-to-all-start = ((bf16[4,128,1024]{2,1,0:T(8,128)(2,1)}), bf16[4,128,1024]{2,1,0:T(8,128)(2,1)S(1)}, u32[]{:S(2)}, u32[]{:S(2)}) async-start(bf16[4,128,1024]{2,1,0:T(8,128)(2,1)} %bitcast.70), calls=%async_computation.3 | async-start | bytes 2097152 | tf_op jit(solution)/shard_map/all_to_all | solution.py:1367
  739.0 30.2 %all-to-all-start.1 = ((bf16[4,128,2048]{2,1,0:T(8,128)(2,1)}), bf16[4,128,2048]{2,1,0:T(8,128)(2,1)}, u32[]{:S(2)}, u32[]{:S(2)}) async-start(bf16[4,128,2048]{2,1,0:T(8,128)(2,1)} %bitcast.68), calls=%async_computation.4 | async-start | bytes 4194304 | tf_op jit(solution)/shard_map/all_to_all | solution.py:1367
  743.4 118.2 %reduce-scatter.11.cloned.1.call-start = ((), (), s32[]{:S(2)}) async-start(), calls=%async_computation.14 | async-start | bytes 5242880 | tf_op jit(solution)/shard_map/reduce_scatter | solution.py:1362
  864.7 18.2 %all-to-all-start.2 = ((bf16[4,128,1024]{2,1,0:T(8,128)(2,1)}), bf16[4,128,1024]{2,1,0:T(8,128)(2,1)S(1)}, u32[]{:S(2)}, u32[]{:S(2)}) async-start(bf16[4,128,1024]{2,1,0:T(8,128)(2,1)} %bitcast.69), calls=%async_computation.6 | async-start | bytes 2097152 | tf_op jit(solution)/shard_map/all_to_all | solution.py:1367
  888.6 3.6 collective-permute-start
Sparse Core Ops, SparseCore 0:
  10.8 83.4 all-gather.4
  95.9 79.2 all-gather.6
  176.8 79.2 all-gather.8
  257.5 79.2 all-gather.10
  497.0 74.9 reduce-scatter.4
  582.0 74.1 reduce-scatter.6
  658.6 77.2 reduce-scatter.8
  769.3 76.3 reduce-scatter.10

commit v11 on v10

--- a/solution.py
+++ b/solution.py
@@ -1466,17 +1466,17 @@
         pre_grads = jnp.concatenate(pre_grads, axis=1)
         down_rows = scatter_rows(down_rows)
     block_out = (mid_rows + down_rows.astype(F32)).astype(BF16)
-    pre_grads, up_grad, gate_grad, down_swapped = lax.optimization_barrier(
-        (pre_grads, up_grad, gate_grad, swap_rows(down_grad))
+    pre_grads, up_grad, down_swapped = lax.optimization_barrier((pre_grads, up_grad, swap_rows(down_grad)))
+    up_swapped = swap_rows(up_grad)
+    attn_part = attention_weight_grads(attn_in, pre_grads, output_grad)
+    pre_grads, attn_part, up_swapped, gate_grad = lax.optimization_barrier(
+        (pre_grads, attn_part, up_swapped, gate_grad)
     )
-    swapped = swap_rows(jnp.concatenate([gate_grad, up_grad], axis=1))
-    attn_part = attention_weight_grads(attn_in, pre_grads, output_grad)
-    pre_grads, attn_part, swapped = lax.optimization_barrier((pre_grads, attn_part, swapped))
+    gate_swapped = swap_rows(gate_grad)
     attn_grad = scatter_weight(attn_part)
     (attn_in_grad,) = product_scatter([pre_grads], [w_attn], 2)
     attn_in_grad, attn_grad = lax.optimization_barrier((attn_in_grad, attn_grad))
-    gate_out, up_out = lay_side_by_side(swapped, 2)
-    (down_out,) = lay_side_by_side(down_swapped, 1)
+    (gate_out,), (up_out,), (down_out,) = [lay_side_by_side(got, 1) for got in (gate_swapped, up_swapped, down_swapped)]
     query_out, key_out, value_out, output_out = lay_side_by_side(swap_rows(attn_grad), 4)
 
     def gain_part(pairs, gain):

time: 907 us -> 894 us (0.986)
  waiting for transfers between devices: 25.9 us -> 10.3 us
    reduce_scatter x4, waiting for transfers between devices: 9.8 us -> 0.03 us  [scatter_weight(): lax.psum_scatter(grad.astype(BF16), 'fsdp', scatter_dimension=0, tiled=True)]
  transfers between devices with their start and end apart: 12 -> 13, of which waited for: 5 -> 3; matrix products, arithmetic and copies ran while one was open for 6% -> 6% of each run, Pallas kernels for 71% -> 72%
where the time goes in v11:
time: 894 us; the launch traced here: 887 us
  Pallas kernels  775 us (87%)
  other arithmetic  43.1 us (5%)
  matrix products  19.2 us (2%)
  starting transfers between devices  16.6 us (2%)
  between operations  14.6 us (2%)
  waiting for transfers between devices  10.3 us (1%)
    pallas_call x3, Pallas kernels, plane_scatter(): pl.pallas_call(functools.partial(scatter_kernel, rows, offsets, len(jobs)...  256 us
    pallas_call x3, Pallas kernels, plane_gather(): pl.pallas_call(functools.partial(gather_kernel, [job[0] for job in jobs],...  228 us
    pallas_call x1, Pallas kernels, attention_backward(): pl.pallas_call(functools.partial(bwd_kernel, heads, hosts), grid=(groups,...  126 us
    pallas_call x1, Pallas kernels, attention_forward(): pl.pallas_call(functools.partial(fwd_kernel, heads, hosts), grid=(groups,...  85 us
    pallas_call x1, Pallas kernels, gated_rows(): pl.pallas_call(gated_kernel, grid=(tokens // block,), in_specs=[pl.BlockS...  45.7 us
    pallas_call x1, Pallas kernels, attention_weight_grads(): pl.pallas_call(weight_grads_kernel, grid=(tokens // block,), in_specs=[pl...  20.6 us
    dot_general x1, matrix products, body(): qkv = jnp.dot(attn_in, w_qkv, preferred_element_type=F32)  19.2 us
  transfers between devices with their start and end apart: 13, of which 3 were waited for; matrix products, arithmetic and copies ran while one was open for 6% of the time, Pallas kernels for 72%

profile of v11, /device:TPU:0, one launch (start us, length us, event | category | flops | bytes accessed | tf_op | source)
XLA Modules:
  0.0 886.7 jit_solution(2429457305296845327)
XLA Ops:
  11.2 1.9 fusion.3.refs_0_
  13.1 78.6 %plane_gather.3 = (bf16[4096,2048]{1,0:T(8,128)(2,1)}, bf16[512,1024]{1,0:T(8,128)(2,1)}, bf16[512,1024]{1,0:T(8,128)(2,1)}, bf16[512,1024]{1,0:T(8,128)(2,1)}, ...) custom-call(bf16[512,2048]{1,0:T(8,128)(2,1)} %fusion.3.refs_0_, ...), custom_call_target="tpu_custom_call" | custom-call | flops 1048576 | bytes 1048576 | tf_op jit(solution)/shard_map/plane_gather/pallas_call | solution.py:975
  94.3 19.2 %fusion.10.refs_0_.refs_1_.refs_2_ = f32[4096,768]{1,0:T(8,128)} fusion(bf16[4096,2048]{1,0:T(8,128)(2,1)} %get-tuple-element.51.x_ref, bf16[2048,1024]{1,0:T(8,128)(2,1)} %all-gather.5.cloned.1.call-done.refs_1_.w_ref), kind=kOutput, calls=%fused_computation.18 | convolution fusion | flops 12884901888 | bytes 32505856 | tf_op jit(solution)/shard_map/dot_general | solution.py:1429
  113.5 85.0 %tree_attention_forward.1 = (bf16[4096,256]{1,0:T(8,128)(2,1)}, f32[2,2,4096]{2,1,0:T(2,128)}, bf16[4096,256]{1,0:T(8,128)(2,1)}, bf16[4096,256]{1,0:T(8,128)(2,...) custom-call(f32[4096,768]{1,0:T(8,128)} %fusion.10.refs_0_.refs_1_.refs_2_, ...), custom_call_target="tpu_custom_call" | custom-call | flops 1048576 | bytes 1048576 | tf_op jit(solution)/shard_map/tree_attention_forward/pallas_call | solution.py:659
  198.5 81.3 %plane_scatter.3 = f32[512,2048]{1,0:T(8,128)} custom-call(bf16[4096,256]{1,0:T(8,128)(2,1)} %get-tuple-element.56.refs_0_.out_ref.refs_3_, bf16[2048,1024]{1,0:T(8,128)(2,1)} %all-gather.5.cloned.1.call-done.refs_1_.w_ref), custom_call_target="tpu_custom_call" | custom-call | flops 1048576 | bytes 1048576 | tf_op jit(solution)/shard_map/plane_scatter/pallas_call | solution.py:1168
  279.8 3.0 multiply_reduce_fusion.1
  283.3 2.0 multiply_convert_fusion.refs_0_
  285.3 74.5 %plane_gather.4 = (bf16[4096,2048]{1,0:T(8,128)(2,1)}, bf16[4096,1024]{1,0:T(8,128)(2,1)}) custom-call(bf16[512,2048]{1,0:T(8,128)(2,1)} %multiply_convert_fusion.refs_0_, bf16[4096,2048]{1,0:T(8,128)(2,1)} %get-tuple-element.60.refs_1_.refs_4_, bf16[2048,1024]{1,0:T(8,128)(2,1)} %all-gather.7.cloned.1.call-done.refs_2_), custom_call_target="tpu_custom_call" | custom-call | flops 1048576 | bytes 1048576 | tf_op jit(solution)/shard_map/plane_gather/pallas_call | solution.py:975
  359.9 45.7 %gated_rows.1 = (bf16[4096,1024]{1,0:T(8,128)(2,1)}, bf16[4096,1024]{1,0:T(8,128)(2,1)}, bf16[4096,1024]{1,0:T(8,128)(2,1)}) custom-call(bf16[4096,2048]{1,0:T(8,128)(2,1)} %get-tuple-element.62.x_ref.refs_3_, bf16[4096,1024]{1,0:T(8,128)(2,1)} %get-tuple-element.63.grad_ref, bf16[2048,1024]{1,0:T(8,128)(2,1)} %all-gather.9.cloned.1.call-done.gate_ref.refs_2_, ...), custom_call_target="tpu_custom_call" | custom-call | flops 1048576 | bytes 1048576 | tf_op jit(solution)/shard_map/gated_rows/pallas_call | solution.py:1219
  405.6 91.3 %plane_scatter.4 = (f32[512,2048]{1,0:T(8,128)}, bf16[2048,1024]{1,0:T(8,128)(2,1)}) custom-call(bf16[4096,1024]{1,0:T(8,128)(2,1)} %get-tuple-element.66.refs_0_.refs_5_, bf16[4096,1024]{1,0:T(8,128)(2,1)} %get-tuple-element.67.refs_1_.refs_4_, bf16[2048,1024]{1,0:T(8,128)(2,1)} %all-gather.9.cloned.1.call-done.gate_ref.refs_2_, ...), custom_call_target="tpu_custom_call" | custom-call | flops 1048576 | bytes 1048576 | tf_op jit(solution)/shard_map/plane_scatter/pallas_call | solution.py:1168
  497.0 4.5 multiply_reduce_fusion
  502.1 1.6 copy-done.3
  504.3 3.0 fusion.15.refs_0_
  507.2 74.6 %plane_gather.5 = (bf16[4096,2048]{1,0:T(8,128)(2,1)}, bf16[4096,2048]{1,0:T(8,128)(2,1)}, bf16[2048,1024]{1,0:T(8,128)(2,1)}, bf16[2048,1024]{1,0:T(8,128)(2,1)}) custom-call(bf16[512,2048]{1,0:T(8,128)(2,1)} %fusion.15.refs_0_, bf16[4096,1024]{1,0:T(8,128)(2,1)} %get-tuple-element.68.refs_5_.refs_1_, ...), custom_call_target="tpu_custom_call" | custom-call | flops 1048576 | bytes 1048576 | tf_op jit(solution)/shard_map/plane_gather/pallas_call | solution.py:975
  582.7 13.9 %heads_and_output_grad.1 = (bf16[4096,256]{1,0:T(8,128)(2,1)}, bf16[2048,256]{1,0:T(8,128)(2,1)}) custom-call(bf16[4096,2048]{1,0:T(8,128)(2,1)} %get-tuple-element.70.x_ref, bf16[2048,1024]{1,0:T(8,128)(2,1)} %all-gather.5.cloned.1.call-done.refs_1_.w_ref, bf16[4096,256]{1,0:T(8,128)(2,1)} %get-tuple-element.56.refs_0_.out_ref.refs_3_), custom_call_target="tpu_custom_call" | custom-call | flops 1048576 | bytes 1048576 | tf_op jit(solution)/shard_map/heads_and_output_grad/pallas_call | solution.py:1253
  596.6 3.5 all-to-all-start
  600.1 125.9 %tree_attention_backward.1 = (bf16[4096,768]{1,0:T(8,128)(2,1)}, bf16[512,2048]{1,0:T(8,128)(2,1)}) custom-call(bf16[4096,256]{1,0:T(8,128)(2,1)} %get-tuple-element.57.refs_0_, bf16[4096,256]{1,0:T(8,128)(2,1)} %get-tuple-element.58.refs_1_, bf16[4096,256]{1,0:T(8,128)(2,1)} %get-tuple-element.59.refs_2_, ...), custom_call_target="tpu_custom_call" | custom-call | flops 1048576 | bytes 1048576 | tf_op jit(solution)/shard_map/tree_attention_backward/pallas_call | solution.py:701
  726.1 4.3 all-to-all-start.1
  730.4 20.6 %attention_weight_grads.1 = bf16[2048,1024]{1,0:T(8,128)(2,1)} custom-call(bf16[4096,2048]{1,0:T(8,128)(2,1)} %get-tuple-element.51.x_ref, bf16[4096,768]{1,0:T(8,128)(2,1)} %get-tuple-element.84.pre_ref.refs_0_, bf16[2048,256]{1,0:T(8,128)(2,1)} %get-tuple-element.81.output_ref), custom_call_target="tpu_custom_call" | custom-call | flops 1048576 | bytes 1048576 | tf_op jit(solution)/shard_map/attention_weight_grads/pallas_call | solution.py:1288
  751.9 3.5 all-to-all-start.3
  755.4 2.9 maximum_convert_fusion.2
  758.3 83.1 %plane_scatter.5 = f32[512,2048]{1,0:T(8,128)} custom-call(bf16[4096,768]{1,0:T(8,128)(2,1)} %get-tuple-element.84.pre_ref.refs_0_, bf16[2048,1024]{1,0:T(8,128)(2,1)} %all-gather.5.cloned.1.call-done.refs_1_.w_ref), custom_call_target="tpu_custom_call" | custom-call | flops 1048576 | bytes 1048576 | tf_op jit(solution)/shard_map/plane_scatter/pallas_call | solution.py:1168
  842.7 2.8 multiply_reduce_fusion.2
  845.7 2.8 multiply_reduce_fusion.3
  848.6 3.0 fusion.4
  851.6 3.7 all-to-all-start.2
  855.4 8.9 %fusion.8 = (bf16[512,2048]{1,0:T(8,128)(2,1)}, bf16[512,2048]{1,0:T(8,128)(2,1)}) fusion(bf16[512,2048]{1,0:T(8,128)(2,1)S(1)} %copy-done.2, f32[512,2048]{1,0:T(8,128)} %plane_scatter.5, f32[512]{0:T(512)S(1)} %broadcast_multiply_fusion, f32[2048]{0:T(1024)S(1)} %copy-done.6, f32[512]{0:T(512)S(1)} %add_rsqrt_fusion.1, ...), kind=kLoop, calls=%fused_computation.11 | loop fusion | flops 19922944 | bytes 23093248 | tf_op jit(solution)/shard_map/convert_element_type | solution.py:1506
  864.3 5.5 all-to-all-done.2
  869.9 1.8 multiply_reduce_fusion.4
  871.7 1.8 multiply_reduce_fusion.5
  873.5 1.8 multiply_reduce_fusion.6
  877.5 1.5 collective-permute-done
  (60 shorter events, 14.3 us)
Async XLA Ops:
  7.2 3.6 copy-start.2
  7.2 4.0 copy-start.6
  7.2 87.1 %all-gather.5.cloned.1.call-start = ((), (), s32[]{:S(2)}) async-start(), calls=%async_computation.8 | async-start | bytes 5242880 | tf_op jit(solution)/shard_map/all_gather | solution.py:1358
  10.7 274.6 %all-gather.7.cloned.1.call-start = ((), (), s32[]{:S(2)}) async-start(), calls=%async_computation.9 | async-start | bytes 5242880 | tf_op jit(solution)/shard_map/all_gather | solution.py:1358
  91.7 268.1 %all-gather.9.cloned.1.call-start = ((), (), s32[]{:S(2)}) async-start(), calls=%async_computation.10 | async-start | bytes 5242880 | tf_op jit(solution)/shard_map/all_gather | solution.py:1358
  92.5 267.4 %all-gather.11.cloned.1.call-start = ((), (), s32[]{:S(2)}) async-start(), calls=%async_computation.11 | async-start | bytes 5242880 | tf_op jit(solution)/shard_map/all_gather | solution.py:1358
  93.1 503.6 %reduce-scatter.5.cloned.1.call-start = ((), (), s32[]{:S(2)}) async-start(), calls=%async_computation.12 | async-start | bytes 5242880 | tf_op jit(solution)/shard_map/reduce_scatter | solution.py:1362
  279.8 3.5 copy-start
  279.8 3.5 copy-start.5
  496.9 229.2 %reduce-scatter.7.cloned.1.call-start = ((), (), s32[]{:S(2)}) async-start(), calls=%async_computation.13 | async-start | bytes 5242880 | tf_op jit(solution)/shard_map/reduce_scatter | solution.py:1362
  497.0 5.1 copy-start.1
  497.0 6.7 copy-start.3
  497.0 7.3 copy-start.4
  581.9 169.1 %reduce-scatter.9.cloned.1.call-start = ((), (), s32[]{:S(2)}) async-start(), calls=%async_computation.14 | async-start | bytes 5242880 | tf_op jit(solution)/shard_map/reduce_scatter | solution.py:1362
  596.6 129.5 %all-to-all-start = ((bf16[4,128,1024]{2,1,0:T(8,128)(2,1)}), bf16[4,128,1024]{2,1,0:T(8,128)(2,1)S(1)}, u32[]{:S(2)}, u32[]{:S(2)}) async-start(bf16[4,128,1024]{2,1,0:T(8,128)(2,1)} %bitcast.71), calls=%async_computation.2 | async-start | bytes 2097152 | tf_op jit(solution)/shard_map/all_to_all | solution.py:1367
  726.1 24.9 %all-to-all-start.1 = ((bf16[4,128,1024]{2,1,0:T(8,128)(2,1)}), bf16[4,128,1024]{2,1,0:T(8,128)(2,1)}, u32[]{:S(2)}, u32[]{:S(2)}) async-start(bf16[4,128,1024]{2,1,0:T(8,128)(2,1)} %bitcast.72), calls=%async_computation.3 | async-start | bytes 2097152 | tf_op jit(solution)/shard_map/all_to_all | solution.py:1367
  730.4 118.2 %reduce-scatter.11.cloned.1.call-start = ((), (), s32[]{:S(2)}) async-start(), calls=%async_computation.15 | async-start | bytes 5242880 | tf_op jit(solution)/shard_map/reduce_scatter | solution.py:1362
  751.9 93.7 %all-to-all-start.3 = ((bf16[4,128,1024]{2,1,0:T(8,128)(2,1)}), bf16[4,128,1024]{2,1,0:T(8,128)(2,1)S(1)}, u32[]{:S(2)}, u32[]{:S(2)}) async-start(bf16[4,128,1024]{2,1,0:T(8,128)(2,1)} %bitcast.69), calls=%async_computation.7 | async-start | bytes 2097152 | tf_op jit(solution)/shard_map/all_to_all | solution.py:1367
  851.6 18.2 %all-to-all-start.2 = ((bf16[4,128,1024]{2,1,0:T(8,128)(2,1)}), bf16[4,128,1024]{2,1,0:T(8,128)(2,1)S(1)}, u32[]{:S(2)}, u32[]{:S(2)}) async-start(bf16[4,128,1024]{2,1,0:T(8,128)(2,1)} %bitcast.70), calls=%async_computation.6 | async-start | bytes 2097152 | tf_op jit(solution)/shard_map/all_to_all | solution.py:1367
  875.5 3.6 collective-permute-start
Sparse Core Ops, SparseCore 0:
  10.8 83.4 all-gather.4
  95.9 79.2 all-gather.6
  176.8 79.2 all-gather.8
  257.5 79.2 all-gather.10
  497.0 74.9 reduce-scatter.4
  582.0 74.2 reduce-scatter.6
  658.6 77.2 reduce-scatter.8
  751.1 75.8 reduce-scatter.10

commit v12 on v11

--- a/solution.py
+++ b/solution.py
@@ -1375,6 +1375,62 @@
     ]
 
 
+def lay_out_kernel(plan, weighted, ctx_ref, *refs):
+    inputs = refs[: max(source for source, _ in plan) + 1]
+    refs = refs[len(inputs) :]
+    weights, outs, sums_ref, total = refs[:weighted], refs[weighted:-2], refs[-2], refs[-1]
+    j = pl.program_id(0)
+
+    @pl.when(j == 0)
+    def _():
+        total[...] = jnp.zeros_like(total)
+
+    for n, ((source, first), out_ref) in enumerate(zip(plan, outs)):
+        columns = out_ref.shape[1]
+        grad = inputs[source][0, :, first : first + columns].astype(F32)
+        out_ref[...] = grad
+        if n < weighted:
+            product = grad * weights[n][...].astype(F32)
+            part = product[:, :128]
+            for c in range(1, columns // 128):
+                part = part + product[:, c * 128 : (c + 1) * 128]
+            total[...] += part
+
+    @pl.when(j == pl.num_programs(0) - 1)
+    def _():
+        column = jnp.sum(total[...], axis=1, keepdims=True)
+        sums_ref[...] = jnp.transpose(jnp.broadcast_to(column, total.shape))[:8]
+
+
+def lay_out_grads(swapped, count, weights):
+    size, rows = swapped[0].shape[:2]
+    columns = swapped[0].shape[2] // count
+    if columns % 128 or rows != 128:
+        outs = [out for got in swapped for out in lay_side_by_side(got, count)]
+        ctx = lax.axis_index("ctx")
+        held = [lax.dynamic_slice_in_dim(weight, ctx * rows, rows, 0).astype(F32) for weight in weights]
+        return outs, sum(jnp.sum(weight * out, axis=1) for weight, out in zip(held, outs))
+    plan = [(n, c * columns) for n in range(len(swapped)) for c in range(count)]
+    result = pl.pallas_call(
+        functools.partial(lay_out_kernel, plan, len(weights)),
+        grid_spec=pltpu.PrefetchScalarGridSpec(
+            num_scalar_prefetch=1,
+            grid=(size,),
+            in_specs=[pl.BlockSpec((1, rows, count * columns), lambda j, ctx: (j, 0, 0)) for _ in swapped]
+            + [pl.BlockSpec((rows, columns), lambda j, ctx: (ctx[0], j)) for _ in weights],
+            out_specs=[pl.BlockSpec((rows, columns), lambda j, ctx: (0, j)) for _ in plan]
+            + [pl.BlockSpec((8, rows), lambda j, ctx: (0, 0))],
+            scratch_shapes=[pltpu.VMEM((rows, 128), F32)],
+        ),
+        out_shape=[jax.ShapeDtypeStruct((rows, size * columns), F32) for _ in plan]
+        + [jax.ShapeDtypeStruct((8, rows), F32)],
+        compiler_params=pltpu.CompilerParams(vmem_limit_bytes=60 << 20),
+        cost_estimate=small_cost(),
+        name="lay_out_grads",
+    )(lax.axis_index("ctx").reshape(1).astype(jnp.int32), *swapped, *weights)
+    return result[:-1], result[-1][0]
+
+
 def normalize(rows):
     norm_inv = lax.rsqrt(jnp.mean(rows * rows, axis=1, keepdims=True) + EPSILON)
     return (rows * norm_inv, norm_inv)
@@ -1476,22 +1532,22 @@
     attn_grad = scatter_weight(attn_part)
     (attn_in_grad,) = product_scatter([pre_grads], [w_attn], 2)
     attn_in_grad, attn_grad = lax.optimization_barrier((attn_in_grad, attn_grad))
-    (gate_out,), (up_out,), (down_out,) = [lay_side_by_side(got, 1) for got in (gate_swapped, up_swapped, down_swapped)]
-    query_out, key_out, value_out, output_out = lay_side_by_side(swap_rows(attn_grad), 4)
-
-    def gain_part(pairs, gain):
-        held = query_out.shape[0]
-        total = sum(
-            jnp.sum(lax.dynamic_slice_in_dim(weight, ctx * held, held, 0).astype(F32) * grad, axis=1)
-            for weight, grad in pairs
-        )
-        first = (lax.axis_index("fsdp") * parts + ctx) * held
-        return total / lax.dynamic_slice_in_dim(gain, first, held, 0)
-
+    (gate_out, up_out, down_out), mlp_sums = lay_out_grads(
+        [gate_swapped, up_swapped, down_swapped], 1, [gate_weight, up_weight]
+    )
+    attn_back = norm_backward(attn_in_grad, attn_scaled, attn_inv, attn_gain)
+    input_grad = (mid_grad + attn_back).astype(BF16)
+    attn_swapped, input_grad, mlp_sums = lax.optimization_barrier((swap_rows(attn_grad), input_grad, mlp_sums))
+    (query_out, key_out, value_out, output_out), attn_sums = lay_out_grads(
+        [attn_swapped], 4, [query_weight, key_weight, value_weight]
+    )
+
+    held = query_out.shape[0]
+    first = (lax.axis_index("fsdp") * parts + ctx) * held
     sums = jnp.stack(
         [
-            gain_part([(query_weight, query_out), (key_weight, key_out), (value_weight, value_out)], attn_gain),
-            gain_part([(gate_weight, gate_out), (up_weight, up_out)], mlp_gain),
+            total / lax.dynamic_slice_in_dim(gain, first, held, 0)
+            for total, gain in ((attn_sums, attn_gain), (mlp_sums, mlp_gain))
         ]
     )
     row, others = lax.axis_index("tensor"), lax.axis_size("tensor")
@@ -1502,8 +1558,6 @@
     else:
         gain_grads = lax.dynamic_slice_in_dim(lax.psum(sums, "tensor"), row * kept, kept, 1)
 
-    attn_back = norm_backward(attn_in_grad, attn_scaled, attn_inv, attn_gain)
-    input_grad = (mid_grad + attn_back).astype(BF16)
     return (
         block_out,
         input_grad,

time: 894 us -> 892 us (level)
  other arithmetic: 43.1 us -> 28.9 us
  Pallas kernels: 775 us -> 786 us
    reduce_sum x5 -> x0, other arithmetic: 11.1 us -> none  [gain_part(): jnp.sum(lax.dynamic_slice_in_dim(weight, ctx * held, held, 0).astype(F32)...]
    pallas_call x0 -> x2, Pallas kernels: none -> 9.93 us  [lay_out_grads(): pl.pallas_call(functools.partial(lay_out_kernel, plan, len(weights)), gri...]
  transfers between devices with their start and end apart: 13 -> 13, of which waited for: 3 -> 3; matrix products, arithmetic and copies ran while one was open for 6% -> 5% of each run, Pallas kernels for 72% -> 73%
where the time goes in v12:
time: 892 us; the launch traced here: 885 us
  Pallas kernels  786 us (88%)
  other arithmetic  28.9 us (3%)
  matrix products  19.2 us (2%)
  starting transfers between devices  16.2 us (2%)
  between operations  14.6 us (2%)
  waiting for transfers between devices  11.3 us (1%)
    pallas_call x3, Pallas kernels, plane_scatter(): pl.pallas_call(functools.partial(scatter_kernel, rows, offsets, len(jobs)...  257 us
    pallas_call x3, Pallas kernels, plane_gather(): pl.pallas_call(functools.partial(gather_kernel, [job[0] for job in jobs],...  228 us
    pallas_call x1, Pallas kernels, attention_backward(): pl.pallas_call(functools.partial(bwd_kernel, heads, hosts), grid=(groups,...  126 us
    pallas_call x1, Pallas kernels, attention_forward(): pl.pallas_call(functools.partial(fwd_kernel, heads, hosts), grid=(groups,...  84.9 us
    pallas_call x1, Pallas kernels, gated_rows(): pl.pallas_call(gated_kernel, grid=(tokens // block,), in_specs=[pl.BlockS...  45.7 us
    pallas_call x1, Pallas kernels, attention_weight_grads(): pl.pallas_call(weight_grads_kernel, grid=(tokens // block,), in_specs=[pl...  20.6 us
    dot_general x1, matrix products, body(): qkv = jnp.dot(attn_in, w_qkv, preferred_element_type=F32)  19.2 us
  transfers between devices with their start and end apart: 13, of which 3 were waited for; matrix products, arithmetic and copies ran while one was open for 5% of the time, Pallas kernels for 73%

profile of v12, /device:TPU:0, one launch (start us, length us, event | category | flops | bytes accessed | tf_op | source)
XLA Modules:
  0.0 884.8 jit_solution(1845309056940592377)
XLA Ops:
  7.2 1.2 constant_dynamic-slice_fusion.2
  8.5 1.1 constant_dynamic-slice_fusion.4
  9.5 1.1 pad_maximum_fusion
  11.2 1.9 fusion.3.refs_0_
  13.1 78.6 %plane_gather.3 = (bf16[4096,2048]{1,0:T(8,128)(2,1)}, bf16[512,1024]{1,0:T(8,128)(2,1)}, bf16[512,1024]{1,0:T(8,128)(2,1)}, bf16[512,1024]{1,0:T(8,128)(2,1)}, ...) custom-call(bf16[512,2048]{1,0:T(8,128)(2,1)} %fusion.3.refs_0_, ...), custom_call_target="tpu_custom_call" | custom-call | flops 1048576 | bytes 1048576 | tf_op jit(solution)/shard_map/plane_gather/pallas_call | solution.py:975
  93.1 1.2 all-gather.5.cloned.1.call-done.refs_1_.w_ref
  94.3 19.2 %fusion.10.refs_0_.refs_1_.refs_2_ = f32[4096,768]{1,0:T(8,128)} fusion(bf16[4096,2048]{1,0:T(8,128)(2,1)} %get-tuple-element.63.x_ref, bf16[2048,1024]{1,0:T(8,128)(2,1)} %all-gather.5.cloned.1.call-done.refs_1_.w_ref), kind=kOutput, calls=%fused_computation.18 | convolution fusion | flops 12884901888 | bytes 32505856 | tf_op jit(solution)/shard_map/dot_general | solution.py:1485
  113.5 84.9 %tree_attention_forward.1 = (bf16[4096,256]{1,0:T(8,128)(2,1)}, f32[2,2,4096]{2,1,0:T(2,128)}, bf16[4096,256]{1,0:T(8,128)(2,1)}, bf16[4096,256]{1,0:T(8,128)(2,...) custom-call(f32[4096,768]{1,0:T(8,128)} %fusion.10.refs_0_.refs_1_.refs_2_, ...), custom_call_target="tpu_custom_call" | custom-call | flops 1048576 | bytes 1048576 | tf_op jit(solution)/shard_map/tree_attention_forward/pallas_call | solution.py:659
  198.5 81.3 %plane_scatter.3 = f32[512,2048]{1,0:T(8,128)} custom-call(bf16[4096,256]{1,0:T(8,128)(2,1)} %get-tuple-element.68.refs_0_.out_ref.refs_3_, bf16[2048,1024]{1,0:T(8,128)(2,1)} %all-gather.5.cloned.1.call-done.refs_1_.w_ref), custom_call_target="tpu_custom_call" | custom-call | flops 1048576 | bytes 1048576 | tf_op jit(solution)/shard_map/plane_scatter/pallas_call | solution.py:1168
  279.8 3.0 multiply_reduce_fusion.1
  283.3 2.0 multiply_convert_fusion.refs_0_
  285.3 74.5 %plane_gather.4 = (bf16[4096,2048]{1,0:T(8,128)(2,1)}, bf16[4096,1024]{1,0:T(8,128)(2,1)}) custom-call(bf16[512,2048]{1,0:T(8,128)(2,1)} %multiply_convert_fusion.refs_0_, bf16[4096,2048]{1,0:T(8,128)(2,1)} %get-tuple-element.72.refs_1_.refs_4_, bf16[2048,1024]{1,0:T(8,128)(2,1)} %all-gather.7.cloned.1.call-done.refs_2_), custom_call_target="tpu_custom_call" | custom-call | flops 1048576 | bytes 1048576 | tf_op jit(solution)/shard_map/plane_gather/pallas_call | solution.py:975
  359.9 45.7 %gated_rows.1 = (bf16[4096,1024]{1,0:T(8,128)(2,1)}, bf16[4096,1024]{1,0:T(8,128)(2,1)}, bf16[4096,1024]{1,0:T(8,128)(2,1)}) custom-call(bf16[4096,2048]{1,0:T(8,128)(2,1)} %get-tuple-element.74.x_ref.refs_3_, bf16[4096,1024]{1,0:T(8,128)(2,1)} %get-tuple-element.75.grad_ref, bf16[2048,1024]{1,0:T(8,128)(2,1)} %all-gather.9.cloned.1.call-done.gate_ref.refs_2_, ...), custom_call_target="tpu_custom_call" | custom-call | flops 1048576 | bytes 1048576 | tf_op jit(solution)/shard_map/gated_rows/pallas_call | solution.py:1219
  405.6 91.3 %plane_scatter.4 = (f32[512,2048]{1,0:T(8,128)}, bf16[2048,1024]{1,0:T(8,128)(2,1)}) custom-call(bf16[4096,1024]{1,0:T(8,128)(2,1)} %get-tuple-element.78.refs_0_.refs_5_, bf16[4096,1024]{1,0:T(8,128)(2,1)} %get-tuple-element.79.refs_1_.refs_4_, bf16[2048,1024]{1,0:T(8,128)(2,1)} %all-gather.9.cloned.1.call-done.gate_ref.refs_2_, ...), custom_call_target="tpu_custom_call" | custom-call | flops 1048576 | bytes 1048576 | tf_op jit(solution)/shard_map/plane_scatter/pallas_call | solution.py:1168
  497.0 4.5 multiply_reduce_fusion
  502.1 1.6 copy-done.3
  504.3 3.0 fusion.15.refs_0_
  507.3 74.6 %plane_gather.5 = (bf16[4096,2048]{1,0:T(8,128)(2,1)}, bf16[4096,2048]{1,0:T(8,128)(2,1)}, bf16[2048,1024]{1,0:T(8,128)(2,1)}, bf16[2048,1024]{1,0:T(8,128)(2,1)}) custom-call(bf16[512,2048]{1,0:T(8,128)(2,1)} %fusion.15.refs_0_, bf16[4096,1024]{1,0:T(8,128)(2,1)} %get-tuple-element.80.refs_5_.refs_1_, ...), custom_call_target="tpu_custom_call" | custom-call | flops 1048576 | bytes 1048576 | tf_op jit(solution)/shard_map/plane_gather/pallas_call | solution.py:975
  582.7 14.0 %heads_and_output_grad.1 = (bf16[4096,256]{1,0:T(8,128)(2,1)}, bf16[2048,256]{1,0:T(8,128)(2,1)}) custom-call(bf16[4096,2048]{1,0:T(8,128)(2,1)} %get-tuple-element.82.x_ref, bf16[2048,1024]{1,0:T(8,128)(2,1)} %all-gather.5.cloned.1.call-done.refs_1_.w_ref, bf16[4096,256]{1,0:T(8,128)(2,1)} %get-tuple-element.68.refs_0_.out_ref.refs_3_), custom_call_target="tpu_custom_call" | custom-call | flops 1048576 | bytes 1048576 | tf_op jit(solution)/shard_map/heads_and_output_grad/pallas_call | solution.py:1253
  596.7 3.5 all-to-all-start
  600.2 125.9 %tree_attention_backward.1 = (bf16[4096,768]{1,0:T(8,128)(2,1)}, bf16[512,2048]{1,0:T(8,128)(2,1)}) custom-call(bf16[4096,256]{1,0:T(8,128)(2,1)} %get-tuple-element.69.refs_0_, bf16[4096,256]{1,0:T(8,128)(2,1)} %get-tuple-element.70.refs_1_, bf16[4096,256]{1,0:T(8,128)(2,1)} %get-tuple-element.71.refs_2_, ...), custom_call_target="tpu_custom_call" | custom-call | flops 1048576 | bytes 1048576 | tf_op jit(solution)/shard_map/tree_attention_backward/pallas_call | solution.py:701
  726.2 4.3 all-to-all-start.1
  730.5 20.6 %attention_weight_grads.1 = bf16[2048,1024]{1,0:T(8,128)(2,1)} custom-call(bf16[4096,2048]{1,0:T(8,128)(2,1)} %get-tuple-element.63.x_ref, bf16[4096,768]{1,0:T(8,128)(2,1)} %get-tuple-element.96.pre_ref.refs_0_, bf16[2048,256]{1,0:T(8,128)(2,1)} %get-tuple-element.93.output_ref), custom_call_target="tpu_custom_call" | custom-call | flops 1048576 | bytes 1048576 | tf_op jit(solution)/shard_map/attention_weight_grads/pallas_call | solution.py:1288
  751.1 3.5 all-to-all-start.3
  754.6 84.4 %plane_scatter.5 = f32[512,2048]{1,0:T(8,128)} custom-call(bf16[4096,768]{1,0:T(8,128)(2,1)} %get-tuple-element.96.pre_ref.refs_0_, bf16[2048,1024]{1,0:T(8,128)(2,1)} %all-gather.5.cloned.1.call-done.refs_1_.w_ref), custom_call_target="tpu_custom_call" | custom-call | flops 1048576 | bytes 1048576 | tf_op jit(solution)/shard_map/plane_scatter/pallas_call | solution.py:1168
  840.1 6.0 lay_out_grads.2
  846.8 3.0 fusion.4
  849.8 3.5 all-to-all-start.2
  853.4 8.9 %fusion.8 = (bf16[512,2048]{1,0:T(8,128)(2,1)}, bf16[512,2048]{1,0:T(8,128)(2,1)}) fusion(bf16[512,2048]{1,0:T(8,128)(2,1)S(1)} %copy-done.2, f32[512,2048]{1,0:T(8,128)} %plane_scatter.5, f32[512]{0:T(512)S(1)} %broadcast_multiply_fusion, f32[2048]{0:T(1024)S(1)} %copy-done.9, f32[512]{0:T(512)S(1)} %add_rsqrt_fusion.1, ...), kind=kLoop, calls=%fused_computation.11 | loop fusion | flops 19922944 | bytes 23093248 | tf_op jit(solution)/shard_map/convert_element_type | solution.py:1539
  862.3 5.5 all-to-all-done.2.refs_0_
  868.8 3.9 lay_out_grads.3
  874.6 2.6 collective-permute-done
  (58 shorter events, 9.7 us)
Async XLA Ops:
  7.2 3.6 copy-start.2
  7.2 4.0 copy-start.9
  7.2 87.1 %all-gather.5.cloned.1.call-start = ((), (), s32[]{:S(2)}) async-start(), calls=%async_computation.8 | async-start | bytes 5242880 | tf_op jit(solution)/shard_map/all_gather | solution.py:1358
  10.7 274.7 %all-gather.7.cloned.1.call-start = ((), (), s32[]{:S(2)}) async-start(), calls=%async_computation.9 | async-start | bytes 5242880 | tf_op jit(solution)/shard_map/all_gather | solution.py:1358
  91.7 268.1 %all-gather.9.cloned.1.call-start = ((), (), s32[]{:S(2)}) async-start(), calls=%async_computation.10 | async-start | bytes 5242880 | tf_op jit(solution)/shard_map/all_gather | solution.py:1358
  92.5 267.4 %all-gather.11.cloned.1.call-start = ((), (), s32[]{:S(2)}) async-start(), calls=%async_computation.11 | async-start | bytes 5242880 | tf_op jit(solution)/shard_map/all_gather | solution.py:1358
  93.0 503.6 %reduce-scatter.5.cloned.1.call-start = ((), (), s32[]{:S(2)}) async-start(), calls=%async_computation.12 | async-start | bytes 5242880 | tf_op jit(solution)/shard_map/reduce_scatter | solution.py:1362
  279.8 3.5 copy-start
  279.8 3.5 copy-start.8
  496.9 229.2 %reduce-scatter.7.cloned.1.call-start = ((), (), s32[]{:S(2)}) async-start(), calls=%async_computation.13 | async-start | bytes 5242880 | tf_op jit(solution)/shard_map/reduce_scatter | solution.py:1362
  497.0 5.1 copy-start.1
  497.0 6.7 copy-start.3
  497.0 7.3 copy-start.4
  581.9 169.1 %reduce-scatter.9.cloned.1.call-start = ((), (), s32[]{:S(2)}) async-start(), calls=%async_computation.14 | async-start | bytes 5242880 | tf_op jit(solution)/shard_map/reduce_scatter | solution.py:1362
  596.7 129.5 %all-to-all-start = ((bf16[4,128,1024]{2,1,0:T(8,128)(2,1)}), bf16[4,128,1024]{2,1,0:T(8,128)(2,1)S(1)}, u32[]{:S(2)}, u32[]{:S(2)}) async-start(bf16[4,128,1024]{2,1,0:T(8,128)(2,1)} %bitcast.22), calls=%async_computation.2 | async-start | bytes 2097152 | tf_op jit(solution)/shard_map/all_to_all | solution.py:1367
  726.2 24.9 %copy-start.5 = (bf16[4,128,1024]{2,1,0:T(8,128)(2,1)}, bf16[4,128,1024]{2,1,0:T(8,128)(2,1)S(1)}, u32[]{:S(2)}) copy-start(bf16[4,128,1024]{2,1,0:T(8,128)(2,1)S(1)} %all-to-all-done.refs_2_) | copy-start | bytes 3145732
  726.2 24.9 %all-to-all-start.1 = ((bf16[4,128,1024]{2,1,0:T(8,128)(2,1)}), bf16[4,128,1024]{2,1,0:T(8,128)(2,1)}, u32[]{:S(2)}, u32[]{:S(2)}) async-start(bf16[4,128,1024]{2,1,0:T(8,128)(2,1)} %bitcast.23), calls=%async_computation.3 | async-start | bytes 2097152 | tf_op jit(solution)/shard_map/all_to_all | solution.py:1367
  730.5 116.3 %reduce-scatter.11.cloned.1.call-start = ((), (), s32[]{:S(2)}) async-start(), calls=%async_computation.15 | async-start | bytes 5242880 | tf_op jit(solution)/shard_map/reduce_scatter | solution.py:1362
  751.1 88.0 %all-to-all-start.3 = ((bf16[4,128,1024]{2,1,0:T(8,128)(2,1)}), bf16[4,128,1024]{2,1,0:T(8,128)(2,1)S(1)}, u32[]{:S(2)}, u32[]{:S(2)}) async-start(bf16[4,128,1024]{2,1,0:T(8,128)(2,1)} %bitcast.20), calls=%async_computation.7 | async-start | bytes 2097152 | tf_op jit(solution)/shard_map/all_to_all | solution.py:1367
  839.1 1.0 copy-start.6
  849.8 18.0 %all-to-all-start.2 = ((bf16[4,128,1024]{2,1,0:T(8,128)(2,1)}), bf16[4,128,1024]{2,1,0:T(8,128)(2,1)S(1)}, u32[]{:S(2)}, u32[]{:S(2)}) async-start(bf16[4,128,1024]{2,1,0:T(8,128)(2,1)} %bitcast.21), calls=%async_computation.6 | async-start | bytes 2097152 | tf_op jit(solution)/shard_map/all_to_all | solution.py:1367
  867.8 1.0 copy-start.7
  873.6 3.6 collective-permute-start
Sparse Core Ops, SparseCore 0:
  10.8 83.4 all-gather.4
  95.9 79.2 all-gather.6
  176.8 79.2 all-gather.8
  257.5 79.2 all-gather.10
  497.1 74.9 reduce-scatter.4
  582.1 74.1 reduce-scatter.6
  658.5 77.2 reduce-scatter.8
  751.2 75.8 reduce-scatter.10

commit v13 on v12

--- a/solution.py
+++ b/solution.py
@@ -1532,11 +1532,12 @@
     attn_grad = scatter_weight(attn_part)
     (attn_in_grad,) = product_scatter([pre_grads], [w_attn], 2)
     attn_in_grad, attn_grad = lax.optimization_barrier((attn_in_grad, attn_grad))
+    attn_back = norm_backward(attn_in_grad, attn_scaled, attn_inv, attn_gain)
+    input_grad = (mid_grad + attn_back).astype(BF16)
+    gate_swapped, input_grad = lax.optimization_barrier((gate_swapped, input_grad))
     (gate_out, up_out, down_out), mlp_sums = lay_out_grads(
         [gate_swapped, up_swapped, down_swapped], 1, [gate_weight, up_weight]
     )
-    attn_back = norm_backward(attn_in_grad, attn_scaled, attn_inv, attn_gain)
-    input_grad = (mid_grad + attn_back).astype(BF16)
     attn_swapped, input_grad, mlp_sums = lax.optimization_barrier((swap_rows(attn_grad), input_grad, mlp_sums))
     (query_out, key_out, value_out, output_out), attn_sums = lay_out_grads(
         [attn_swapped], 4, [query_weight, key_weight, value_weight]

time: 892 us -> 886 us (level)
  transfers between devices with their start and end apart: 13 -> 13, of which waited for: 3 -> 2; matrix products, arithmetic and copies ran while one was open for 5% -> 5% of each run, Pallas kernels for 73% -> 73%
where the time goes in v13:
time: 886 us; the launch traced here: 878 us
  Pallas kernels  786 us (89%)
  other arithmetic  28.9 us (3%)
  matrix products  19.2 us (2%)
  starting transfers between devices  17.2 us (2%)
  between operations  14.6 us (2%)
    pallas_call x3, Pallas kernels, plane_scatter(): pl.pallas_call(functools.partial(scatter_kernel, rows, offsets, len(jobs)...  257 us
    pallas_call x3, Pallas kernels, plane_gather(): pl.pallas_call(functools.partial(gather_kernel, [job[0] for job in jobs],...  228 us
    pallas_call x1, Pallas kernels, attention_backward(): pl.pallas_call(functools.partial(bwd_kernel, heads, hosts), grid=(groups,...  126 us
    pallas_call x1, Pallas kernels, attention_forward(): pl.pallas_call(functools.partial(fwd_kernel, heads, hosts), grid=(groups,...  85 us
    pallas_call x1, Pallas kernels, gated_rows(): pl.pallas_call(gated_kernel, grid=(tokens // block,), in_specs=[pl.BlockS...  45.7 us
    pallas_call x1, Pallas kernels, attention_weight_grads(): pl.pallas_call(weight_grads_kernel, grid=(tokens // block,), in_specs=[pl...  20.6 us
    dot_general x1, matrix products, body(): qkv = jnp.dot(attn_in, w_qkv, preferred_element_type=F32)  19.2 us
  transfers between devices with their start and end apart: 13, of which 2 were waited for; matrix products, arithmetic and copies ran while one was open for 5% of the time, Pallas kernels for 73%

profile of v13, /device:TPU:0, one launch (start us, length us, event | category | flops | bytes accessed | tf_op | source)
XLA Modules:
  0.0 878.4 jit_solution(4275605777959139078)
XLA Ops:
  7.2 1.2 constant_dynamic-slice_fusion.2
  8.5 1.1 constant_dynamic-slice_fusion.4
  9.5 1.1 pad_maximum_fusion
  11.2 1.9 fusion.3.refs_0_
  13.1 78.6 %plane_gather.3 = (bf16[4096,2048]{1,0:T(8,128)(2,1)}, bf16[512,1024]{1,0:T(8,128)(2,1)}, bf16[512,1024]{1,0:T(8,128)(2,1)}, bf16[512,1024]{1,0:T(8,128)(2,1)}, ...) custom-call(bf16[512,2048]{1,0:T(8,128)(2,1)} %fusion.3.refs_0_, ...), custom_call_target="tpu_custom_call" | custom-call | flops 1048576 | bytes 1048576 | tf_op jit(solution)/shard_map/plane_gather/pallas_call | solution.py:975
  93.1 1.2 all-gather.5.cloned.1.call-done.refs_1_.w_ref
  94.3 19.2 %fusion.10.refs_0_.refs_1_.refs_2_ = f32[4096,768]{1,0:T(8,128)} fusion(bf16[4096,2048]{1,0:T(8,128)(2,1)} %get-tuple-element.65.x_ref, bf16[2048,1024]{1,0:T(8,128)(2,1)} %all-gather.5.cloned.1.call-done.refs_1_.w_ref), kind=kOutput, calls=%fused_computation.18 | convolution fusion | flops 12884901888 | bytes 32505856 | tf_op jit(solution)/shard_map/dot_general | solution.py:1485
  113.5 85.0 %tree_attention_forward.1 = (bf16[4096,256]{1,0:T(8,128)(2,1)}, f32[2,2,4096]{2,1,0:T(2,128)}, bf16[4096,256]{1,0:T(8,128)(2,1)}, bf16[4096,256]{1,0:T(8,128)(2,...) custom-call(f32[4096,768]{1,0:T(8,128)} %fusion.10.refs_0_.refs_1_.refs_2_, ...), custom_call_target="tpu_custom_call" | custom-call | flops 1048576 | bytes 1048576 | tf_op jit(solution)/shard_map/tree_attention_forward/pallas_call | solution.py:659
  198.5 81.3 %plane_scatter.3 = f32[512,2048]{1,0:T(8,128)} custom-call(bf16[4096,256]{1,0:T(8,128)(2,1)} %get-tuple-element.70.refs_0_.out_ref.refs_3_, bf16[2048,1024]{1,0:T(8,128)(2,1)} %all-gather.5.cloned.1.call-done.refs_1_.w_ref), custom_call_target="tpu_custom_call" | custom-call | flops 1048576 | bytes 1048576 | tf_op jit(solution)/shard_map/plane_scatter/pallas_call | solution.py:1168
  279.8 3.0 multiply_reduce_fusion.1
  283.3 2.0 multiply_convert_fusion.refs_0_
  285.3 74.5 %plane_gather.4 = (bf16[4096,2048]{1,0:T(8,128)(2,1)}, bf16[4096,1024]{1,0:T(8,128)(2,1)}) custom-call(bf16[512,2048]{1,0:T(8,128)(2,1)} %multiply_convert_fusion.refs_0_, bf16[4096,2048]{1,0:T(8,128)(2,1)} %get-tuple-element.74.refs_1_.refs_4_, bf16[2048,1024]{1,0:T(8,128)(2,1)} %all-gather.7.cloned.1.call-done.refs_2_), custom_call_target="tpu_custom_call" | custom-call | flops 1048576 | bytes 1048576 | tf_op jit(solution)/shard_map/plane_gather/pallas_call | solution.py:975
  359.9 45.7 %gated_rows.1 = (bf16[4096,1024]{1,0:T(8,128)(2,1)}, bf16[4096,1024]{1,0:T(8,128)(2,1)}, bf16[4096,1024]{1,0:T(8,128)(2,1)}) custom-call(bf16[4096,2048]{1,0:T(8,128)(2,1)} %get-tuple-element.76.x_ref.refs_3_, bf16[4096,1024]{1,0:T(8,128)(2,1)} %get-tuple-element.77.grad_ref, bf16[2048,1024]{1,0:T(8,128)(2,1)} %all-gather.9.cloned.1.call-done.gate_ref.refs_2_, ...), custom_call_target="tpu_custom_call" | custom-call | flops 1048576 | bytes 1048576 | tf_op jit(solution)/shard_map/gated_rows/pallas_call | solution.py:1219
  405.6 91.2 %plane_scatter.4 = (f32[512,2048]{1,0:T(8,128)}, bf16[2048,1024]{1,0:T(8,128)(2,1)}) custom-call(bf16[4096,1024]{1,0:T(8,128)(2,1)} %get-tuple-element.80.refs_0_.refs_5_, bf16[4096,1024]{1,0:T(8,128)(2,1)} %get-tuple-element.81.refs_1_.refs_4_, bf16[2048,1024]{1,0:T(8,128)(2,1)} %all-gather.9.cloned.1.call-done.gate_ref.refs_2_, ...), custom_call_target="tpu_custom_call" | custom-call | flops 1048576 | bytes 1048576 | tf_op jit(solution)/shard_map/plane_scatter/pallas_call | solution.py:1168
  497.0 4.5 multiply_reduce_fusion
  502.0 1.6 copy-done.3
  504.3 3.0 fusion.15.refs_0_
  507.2 74.6 %plane_gather.5 = (bf16[4096,2048]{1,0:T(8,128)(2,1)}, bf16[4096,2048]{1,0:T(8,128)(2,1)}, bf16[2048,1024]{1,0:T(8,128)(2,1)}, bf16[2048,1024]{1,0:T(8,128)(2,1)}) custom-call(bf16[512,2048]{1,0:T(8,128)(2,1)} %fusion.15.refs_0_, bf16[4096,1024]{1,0:T(8,128)(2,1)} %get-tuple-element.82.refs_5_.refs_1_, ...), custom_call_target="tpu_custom_call" | custom-call | flops 1048576 | bytes 1048576 | tf_op jit(solution)/shard_map/plane_gather/pallas_call | solution.py:975
  582.7 13.9 %heads_and_output_grad.1 = (bf16[4096,256]{1,0:T(8,128)(2,1)}, bf16[2048,256]{1,0:T(8,128)(2,1)}) custom-call(bf16[4096,2048]{1,0:T(8,128)(2,1)} %get-tuple-element.84.x_ref, bf16[2048,1024]{1,0:T(8,128)(2,1)} %all-gather.5.cloned.1.call-done.refs_1_.w_ref, bf16[4096,256]{1,0:T(8,128)(2,1)} %get-tuple-element.70.refs_0_.out_ref.refs_3_), custom_call_target="tpu_custom_call" | custom-call | flops 1048576 | bytes 1048576 | tf_op jit(solution)/shard_map/heads_and_output_grad/pallas_call | solution.py:1253
  596.6 3.5 all-to-all-start
  600.1 126.0 %tree_attention_backward.1 = (bf16[4096,768]{1,0:T(8,128)(2,1)}, bf16[512,2048]{1,0:T(8,128)(2,1)}) custom-call(bf16[4096,256]{1,0:T(8,128)(2,1)} %get-tuple-element.71.refs_0_, bf16[4096,256]{1,0:T(8,128)(2,1)} %get-tuple-element.72.refs_1_, bf16[4096,256]{1,0:T(8,128)(2,1)} %get-tuple-element.73.refs_2_, ...), custom_call_target="tpu_custom_call" | custom-call | flops 1048576 | bytes 1048576 | tf_op jit(solution)/shard_map/tree_attention_backward/pallas_call | solution.py:701
  726.2 4.3 all-to-all-start.1
  730.5 20.6 %attention_weight_grads.1 = bf16[2048,1024]{1,0:T(8,128)(2,1)} custom-call(bf16[4096,2048]{1,0:T(8,128)(2,1)} %get-tuple-element.65.x_ref, bf16[4096,768]{1,0:T(8,128)(2,1)} %get-tuple-element.98.pre_ref.refs_0_, bf16[2048,256]{1,0:T(8,128)(2,1)} %get-tuple-element.95.output_ref), custom_call_target="tpu_custom_call" | custom-call | flops 1048576 | bytes 1048576 | tf_op jit(solution)/shard_map/attention_weight_grads/pallas_call | solution.py:1288
  751.1 3.5 all-to-all-start.3
  754.6 84.4 %plane_scatter.5 = f32[512,2048]{1,0:T(8,128)} custom-call(bf16[4096,768]{1,0:T(8,128)(2,1)} %get-tuple-element.98.pre_ref.refs_0_, bf16[2048,1024]{1,0:T(8,128)(2,1)} %all-gather.5.cloned.1.call-done.refs_1_.w_ref), custom_call_target="tpu_custom_call" | custom-call | flops 1048576 | bytes 1048576 | tf_op jit(solution)/shard_map/plane_scatter/pallas_call | solution.py:1168
  839.1 3.0 fusion.4
  842.1 4.5 all-to-all-start.2
  846.6 8.9 %fusion.8 = (bf16[512,2048]{1,0:T(8,128)(2,1)}, bf16[512,2048]{1,0:T(8,128)(2,1)}) fusion(bf16[512,2048]{1,0:T(8,128)(2,1)S(1)} %copy-done.2, f32[512,2048]{1,0:T(8,128)} %plane_scatter.5, f32[512]{0:T(512)S(1)} %broadcast_multiply_fusion, f32[2048]{0:T(1024)S(1)} %copy-done.8, f32[512]{0:T(512)S(1)} %add_rsqrt_fusion.1, ...), kind=kLoop, calls=%fused_computation.11 | loop fusion | flops 19922944 | bytes 23093248 | tf_op jit(solution)/shard_map/convert_element_type | solution.py:1536
  855.6 6.0 lay_out_grads.2
  862.3 3.9 lay_out_grads.3
  867.1 1.1 collective-permute-start
  868.2 2.5 collective-permute-done
  (56 shorter events, 6.7 us)
Async XLA Ops:
  7.2 3.6 copy-start.2
  7.2 4.0 copy-start.8
  7.2 87.1 %all-gather.5.cloned.1.call-start = ((), (), s32[]{:S(2)}) async-start(), calls=%async_computation.8 | async-start | bytes 5242880 | tf_op jit(solution)/shard_map/all_gather | solution.py:1358
  10.7 274.7 %all-gather.7.cloned.1.call-start = ((), (), s32[]{:S(2)}) async-start(), calls=%async_computation.9 | async-start | bytes 5242880 | tf_op jit(solution)/shard_map/all_gather | solution.py:1358
  91.7 268.1 %all-gather.9.cloned.1.call-start = ((), (), s32[]{:S(2)}) async-start(), calls=%async_computation.10 | async-start | bytes 5242880 | tf_op jit(solution)/shard_map/all_gather | solution.py:1358
  92.5 267.4 %all-gather.11.cloned.1.call-start = ((), (), s32[]{:S(2)}) async-start(), calls=%async_computation.11 | async-start | bytes 5242880 | tf_op jit(solution)/shard_map/all_gather | solution.py:1358
  93.1 503.5 %reduce-scatter.5.cloned.1.call-start = ((), (), s32[]{:S(2)}) async-start(), calls=%async_computation.12 | async-start | bytes 5242880 | tf_op jit(solution)/shard_map/reduce_scatter | solution.py:1362
  279.8 3.5 copy-start
  279.8 3.5 copy-start.7
  496.9 229.2 %reduce-scatter.7.cloned.1.call-start = ((), (), s32[]{:S(2)}) async-start(), calls=%async_computation.13 | async-start | bytes 5242880 | tf_op jit(solution)/shard_map/reduce_scatter | solution.py:1362
  496.9 5.1 copy-start.1
  497.0 6.7 copy-start.3
  497.0 7.3 copy-start.4
  581.9 169.1 %reduce-scatter.9.cloned.1.call-start = ((), (), s32[]{:S(2)}) async-start(), calls=%async_computation.14 | async-start | bytes 5242880 | tf_op jit(solution)/shard_map/reduce_scatter | solution.py:1362
  596.6 129.6 %all-to-all-start = ((bf16[4,128,1024]{2,1,0:T(8,128)(2,1)}), bf16[4,128,1024]{2,1,0:T(8,128)(2,1)S(1)}, u32[]{:S(2)}, u32[]{:S(2)}) async-start(bf16[4,128,1024]{2,1,0:T(8,128)(2,1)} %bitcast.22), calls=%async_computation.2 | async-start | bytes 2097152 | tf_op jit(solution)/shard_map/all_to_all | solution.py:1367
  726.1 24.9 %copy-start.5 = (bf16[4,128,1024]{2,1,0:T(8,128)(2,1)}, bf16[4,128,1024]{2,1,0:T(8,128)(2,1)S(1)}, u32[]{:S(2)}) copy-start(bf16[4,128,1024]{2,1,0:T(8,128)(2,1)S(1)} %all-to-all-done.refs_2_) | copy-start | bytes 3145732
  726.2 24.9 %all-to-all-start.1 = ((bf16[4,128,1024]{2,1,0:T(8,128)(2,1)}), bf16[4,128,1024]{2,1,0:T(8,128)(2,1)}, u32[]{:S(2)}, u32[]{:S(2)}) async-start(bf16[4,128,1024]{2,1,0:T(8,128)(2,1)} %bitcast.23), calls=%async_computation.3 | async-start | bytes 2097152 | tf_op jit(solution)/shard_map/all_to_all | solution.py:1367
  730.4 108.7 %reduce-scatter.11.cloned.1.call-start = ((), (), s32[]{:S(2)}) async-start(), calls=%async_computation.15 | async-start | bytes 5242880 | tf_op jit(solution)/shard_map/reduce_scatter | solution.py:1362
  751.1 91.1 %all-to-all-start.3 = ((bf16[4,128,1024]{2,1,0:T(8,128)(2,1)}), bf16[4,128,1024]{2,1,0:T(8,128)(2,1)S(1)}, u32[]{:S(2)}, u32[]{:S(2)}) async-start(bf16[4,128,1024]{2,1,0:T(8,128)(2,1)} %bitcast.20), calls=%async_computation.7 | async-start | bytes 2097152 | tf_op jit(solution)/shard_map/all_to_all | solution.py:1367
  842.1 13.4 %copy-start.6 = (bf16[4,128,1024]{2,1,0:T(8,128)(2,1)}, bf16[4,128,1024]{2,1,0:T(8,128)(2,1)S(1)}, u32[]{:S(2)}) copy-start(bf16[4,128,1024]{2,1,0:T(8,128)(2,1)S(1)} %all-to-all-done.3.refs_0_) | copy-start | bytes 3145732
  842.1 20.1 %all-to-all-start.2 = ((bf16[4,128,1024]{2,1,0:T(8,128)(2,1)}), bf16[4,128,1024]{2,1,0:T(8,128)(2,1)}, u32[]{:S(2)}, u32[]{:S(2)}) async-start(bf16[4,128,1024]{2,1,0:T(8,128)(2,1)} %bitcast.21), calls=%async_computation.6 | async-start | bytes 2097152 | tf_op jit(solution)/shard_map/all_to_all | solution.py:1367
  867.1 3.6 collective-permute-start
Sparse Core Ops, SparseCore 0:
  10.8 83.4 all-gather.4
  95.9 79.2 all-gather.6
  176.8 79.2 all-gather.8
  257.5 79.2 all-gather.10
  497.0 74.9 reduce-scatter.4
  582.0 74.2 reduce-scatter.6
  658.6 77.2 reduce-scatter.8
  751.2 75.9 reduce-scatter.10
